TPU v7x, 32 devices: a whole 2x2x4 slice. The times are simulated.
32 devices in a mesh: groups: 2 (over x), pool: 8 (over z, y), head: 2 (over core).
Axes of the slice: x: 2, y: 2, z: 4, core: 2. Of those that a mesh axis runs over, the one named last changes fastest.
Arguments:
- queries: bfloat16 [2048, 32, 128], P(('groups', 'pool'), 'head'), parts along dimension 0, may hold values from -400 to 400
- new_kv: bfloat16 [2048, 2, 4, 128], P(('groups', 'pool'), None, 'head'), parts along dimension 0, may hold values from -4 to 4
- pool: bfloat16 [528, 2, 4, 128, 128], P(('groups', 'pool'), None, 'head'), parts along dimension 0, may hold values from -6 to 6
- block_table: int32 [8, 64], P('groups'), parts along dimension 0, may hold values from -1 to 263, as said below
- prefix_len: int32 [8], P('groups'), parts along dimension 0, may hold values from 2048 to 8192, as said below
- new_slots: int32 [16], P('groups'), parts along dimension 0, may hold values from 0 to 263, as said below
Outputs:
- attended: bfloat16 [2048, 32, 128], P(('groups', 'pool'), 'head'), parts along dimension 0
- updated_pool: bfloat16 [528, 2, 4, 128, 128], P(('groups', 'pool'), None, 'head'), parts along dimension 0
There are 2 independent parts, one for each index of `groups`. A program takes and returns all parts, laid end to end along the dimension named above; each array names one. Nothing has to cross between parts.
Inputs may be any that keep to these rules, and one draw needn't show every extreme that they name: `block_table`: entry [r, j] is the slot (owner times 33 plus local slot) of page j of request r for j < ceil(prefix_len[r] / 128), and -1 after. All named slots differ. No owner holds more than 8 pages of one request, and the request with the longest prefix has exactly 8 on every owner. `prefix_len`: the longest prefix is exactly 8192 tokens. `new_slots`: entry d is a slot of owner d (d * 33 to (d + 1) * 33 - 1) that block_table does not name.
All inputs are finite; a program needn't handle non-finite values.
Results may differ from a plain program's by a relative error of at most 0.012.
Values may be sent and summed in bfloat16 or wider, within the bound.
No kernel may reach another device: no remote copies, remote signals or barrier semaphores. Data moves between devices by JAX's collectives and lax.ppermute only.
A program may use at most 128 MiB of HBM per device.

v0:
```python
import functools

import jax
import jax.numpy as jnp
from jax import lax
from jax.experimental import pallas as pl
from jax.experimental.pallas import tpu as pltpu
from jax.sharding import PartitionSpec as P


log2_e = 1.4426950408889634
hidden_score = -2e30
lowest_top = -1e30
lanes = 128
block_rows = 128
kernel_bytes = 24 << 20


def moved(array, apart):
    count = lax.axis_size("pool")
    return lax.ppermute(array, "pool", [(i, i ^ apart) for i in range(count)])


def whole(array):
    return pl.BlockSpec(array.shape, lambda i, *_: (0,) * len(array.shape))


def diagonal():
    shape = (lanes, lanes)
    return lax.broadcasted_iota(jnp.int32, shape, 0) == lax.broadcasted_iota(jnp.int32, shape, 1)


def as_row(column, eye):
    spread = jnp.where(eye, jnp.broadcast_to(column, (lanes, lanes)), 0.0)
    return jnp.sum(spread, axis=0, keepdims=True)


def as_column(row, eye):
    spread = jnp.where(eye, jnp.broadcast_to(row, (lanes, lanes)), 0.0)
    return jnp.sum(spread, axis=1, keepdims=True)


def in_three(values):
    high = values.astype(jnp.bfloat16)
    rest = values - high.astype(jnp.float32)
    middle = rest.astype(jnp.bfloat16)
    low = (rest - middle.astype(jnp.float32)).astype(jnp.bfloat16)
    return (high, middle, low)


def from_three(ref, begin, count):
    parts = [
        ref[0, begin + i * count : begin + (i + 1) * count].astype(jnp.float32) for i in range(3)
    ]
    return parts[0] + parts[1] + parts[2]


def gather_body(owner_ref, table_ref, pool_ref, *refs, lists, kv_heads, cap):
    outs = refs[:-4]
    staged, slots, sem_in, sem_out = refs[-4:]
    owner = owner_ref[0]
    pair = owner >> 1
    slot_count = pool_ref.shape[0]
    base = owner * slot_count
    width = table_ref.shape[1]

    def look(j, found):
        following = []
        for at, which in enumerate(lists):
            slot = table_ref[pair ^ which, j] - base
            slots[at * (cap + 1) + jnp.minimum(found[at], cap)] = slot
            held = (slot >= 0) & (slot < slot_count)
            following.append(found[at] + held.astype(jnp.int32))
        return tuple(following)

    found = lax.fori_loop(0, width, look, (jnp.int32(0),) * len(lists), unroll=4)
    arriving = []
    for at in range(len(lists)):
        for k in range(kv_heads):
            for i in range(cap):
                slot = jnp.where(i < found[at], slots[at * (cap + 1) + i], 0)
                copy = pltpu.make_async_copy(
                    pool_ref.at[slot, :, k], staged.at[at, k, i], sem_in.at[at, k, i]
                )
                copy.start()
                arriving.append(copy)
    leaving = []
    for at in range(len(lists)):
        for k in range(kv_heads):
            for i in range(cap):
                arriving[(at * kv_heads + k) * cap + i].wait()
            copy = pltpu.make_async_copy(
                staged.at[at, k], outs[at * kv_heads + k].at[0], sem_out.at[at, k]
            )
            copy.start()
            leaving.append(copy)
    for copy in leaving:
        copy.wait()


def gather_pages(owner, table, pool, lists, cap):
    _, pair_of, kv_heads, page_len, head_dim = pool.shape
    shape = pltpu.HBM((1, cap, pair_of, page_len, head_dim), pool.dtype)
    count = len(lists) * kv_heads
    outs = pl.pallas_call(
        functools.partial(gather_body, lists=lists, kv_heads=kv_heads, cap=cap),
        out_shape=[shape] * count,
        grid_spec=pltpu.PrefetchScalarGridSpec(
            num_scalar_prefetch=2,
            grid=(1,),
            in_specs=[pl.BlockSpec(memory_space=pltpu.HBM)],
            out_specs=[pl.BlockSpec(memory_space=pltpu.HBM)] * count,
            scratch_shapes=[
                pltpu.VMEM((len(lists), kv_heads, cap, pair_of, page_len, head_dim), pool.dtype),
                pltpu.SMEM((len(lists) * (cap + 1),), jnp.int32),
                pltpu.SemaphoreType.DMA((len(lists), kv_heads, cap)),
                pltpu.SemaphoreType.DMA((len(lists), kv_heads)),
            ],
        ),
        compiler_params=pltpu.CompilerParams(vmem_limit_bytes=kernel_bytes),
        name="gather_pages",
    )(owner, table, pltpu.with_memory_space_constraint(pool, pltpu.HBM))
    return [outs[i * kv_heads : (i + 1) * kv_heads] for i in range(len(lists))]


def attend_body(
    owner_ref,
    seen_ref,
    fresh_ref,
    *refs,
    halves,
    seen_at,
    has_page,
    has_prev,
    packed,
    step_rows,
    tile_rows,
    group,
    scale,
    copies_pool,
    waits,
    page_at,
):
    refs = list(refs)
    q_refs = [refs.pop(0) for _ in range(halves)]
    kv_refs = [refs.pop(0) for _ in seen_at]
    page_ref = refs.pop(0) if has_page else None
    prev_refs = [(refs.pop(0), refs.pop(0)) for _ in range(halves)] if has_prev else None
    pool_ref = refs.pop(0) if copies_pool else None
    del refs[:waits]
    out_refs = []
    for h in range(halves):
        out_refs.append((refs.pop(0),) if packed[h] else (refs.pop(0), refs.pop(0)))
    new_pool = refs.pop(0) if copies_pool else None
    wide_values = refs.pop(0)
    tables = [refs.pop(0) if packed[h] else out_refs[h][1].at[0] for h in range(halves)]
    if copies_pool:
        staged, sem_in, sem_out = refs
    head = pl.program_id(0)
    step = pl.program_id(1)
    heads = pl.num_programs(0)
    steps = pl.num_programs(1)
    owner = owner_ref[0]
    half = 1 - ((owner & 1) ^ ((owner >> 1) & 1))
    page_len = kv_refs[0].shape[3]
    keys = [ref.shape[1] * page_len for ref in kv_refs]

    if copies_pool:

        @pl.when((head == 0) & (step == 0))
        def _():
            pltpu.make_async_copy(pool_ref, staged, sem_in).start()

        @pl.when((head == 0) & (step == jnp.minimum(1, steps - 1)))
        def _():
            pltpu.make_async_copy(pool_ref, staged, sem_in).wait()
            staged[fresh_ref[owner] - owner * staged.shape[0]] = page_ref[...]
            pltpu.make_async_copy(staged, new_pool, sem_out).start()

    @pl.when(step == 0)
    def _():
        ones = jnp.ones((page_len, lanes), jnp.bfloat16)
        begin = 0
        for ref in kv_refs:
            for p in range(ref.shape[1]):
                wide_values[begin : begin + page_len, :lanes] = ref[0, p, 1]
                wide_values[begin : begin + page_len, lanes:] = ones
                begin += page_len
        if has_page:
            wide_values[begin : begin + page_len, :lanes] = page_ref[1, page_at]
            wide_values[begin : begin + page_len, lanes:] = ones

    eye = diagonal()
    limits = []
    for s, at in enumerate(seen_at):
        position = lax.broadcasted_iota(jnp.int32, (1, keys[s]), 1)
        limit = jnp.where(position < seen_ref[at[0], at[1]], jnp.inf, hidden_score)
        limits.append(limit.astype(jnp.float32))

    def score(h, t):
        query = q_refs[h][0, t * tile_rows : (t + 1) * tile_rows]
        scores = []
        for s, ref in enumerate(kv_refs):
            key_rows = ref[0, :, 0].reshape(keys[s], lanes)
            product = lax.dot_general(
                query, key_rows, (((1,), (1,)), ((), ())), preferred_element_type=jnp.float32
            )
            scores.append(jnp.minimum(product, limits[s]))
        if has_page:
            product = lax.dot_general(
                query, page_ref[0, page_at], (((1,), (1,)), ((), ())), preferred_element_type=jnp.float32
            )
            key_at = lax.broadcasted_iota(jnp.int32, product.shape, 1)
            if h == 0:
                row_at = lax.broadcasted_iota(jnp.int32, product.shape, 0)
                token = (step * step_rows + t * tile_rows + row_at) // group
                shown = key_at <= token
            else:
                shown = key_at < jnp.where(half == 0, page_len, 0)
            scores.append(jnp.where(shown, product, hidden_score))
        return scores

    def finish(h, t, scores):
        top = jnp.full((tile_rows, 1), lowest_top, jnp.float32)
        for part in scores:
            top = jnp.maximum(top, jnp.max(part, axis=1, keepdims=True))
        scaled_top = top * scale
        weights = [jnp.exp2(part * scale - scaled_top).astype(jnp.bfloat16) for part in scores]
        mixed = jnp.dot(
            jnp.concatenate(weights, axis=1), wide_values[...], preferred_element_type=jnp.float32
        )
        total = mixed[:, lanes:]
        mixed = mixed[:, :lanes]
        first = step * (step_rows // block_rows) + t * (tile_rows // block_rows)
        count = tables[h].shape[0] // 2
        for u in range(tile_rows // block_rows):
            inner = slice(u * block_rows, (u + 1) * block_rows)
            outer = slice(t * tile_rows + u * block_rows, t * tile_rows + (u + 1) * block_rows)
            part_top, part_total, part_mixed = top[inner], total[inner], mixed[inner]
            row = first + u
            if has_prev:
                prev_mixed, prev_table = prev_refs[h]
                prev_top = as_column(prev_table[0, pl.ds(row, 1)], eye)
                prev_total = as_column(prev_table[0, pl.ds(count + row, 1)], eye)
                joint = jnp.maximum(part_top, prev_top)
                keep = jnp.exp2((part_top - joint) * scale)
                keep_prev = jnp.exp2((prev_top - joint) * scale)
                part_mixed = part_mixed * keep + prev_mixed[0, outer] * keep_prev
                part_total = part_total * keep + prev_total * keep_prev
                part_top = joint
            tables[h][pl.ds(row, 1)] = as_row(part_top, eye)
            tables[h][pl.ds(count + row, 1)] = as_row(part_total, eye)
            if packed[h]:
                at = pl.multiple_of(row * block_rows, block_rows)
                out_refs[h][0][0, pl.ds(at, block_rows)] = part_mixed.astype(jnp.bfloat16)
            else:
                out_refs[h][0][0, outer] = part_mixed

    chains = [(h, t) for t in range(step_rows // tile_rows) for h in range(halves)]
    scores = score(*chains[0])
    for i, chain in enumerate(chains):
        following = score(*chains[i + 1]) if i + 1 < len(chains) else None
        finish(*chain, scores)
        scores = following

    @pl.when(step == steps - 1)
    def _():
        for h in range(halves):
            if packed[h]:
                size = tables[h].shape[0]
                begin = out_refs[h][0].shape[1] - 3 * size
                for i, part in enumerate(in_three(tables[h][...])):
                    out_refs[h][0][0, begin + i * size : begin + (i + 1) * size] = part

    if copies_pool:

        @pl.when((head == heads - 1) & (step == steps - 1))
        def _():
            pltpu.make_async_copy(staged, new_pool, sem_out).wait()


def attend(
    scalars, queries, sources, seen_at, packed, scale, group, heads, page=None, prev=None, pool=None, after=()
):
    halves = len(queries)
    rows = queries[0][0].shape[1]
    size = 2 * (rows // block_rows)
    step_rows = min(rows, 1024 // halves)
    tile_rows = min(step_rows, 256)
    key_count = sum(s.shape[1] * s.shape[3] for s, _ in sources)

    def per_rows(offset):
        return pl.BlockSpec((1, step_rows, lanes), lambda k, i, *_: (k + offset, i, 0))

    def per_head(array, offset):
        tail = array.shape[1:]
        return pl.BlockSpec((1, *tail), lambda k, i, *_: (k + offset,) + (0,) * len(tail))

    anywhere = pl.BlockSpec(memory_space=pl.ANY)
    args = [q for q, _ in queries] + [s for s, _ in sources]
    in_specs = [per_rows(at) for _, at in queries] + [per_head(s, at) for s, at in sources]
    page_at = 0
    if page is not None:
        page, page_at = page
        args.append(page)
        in_specs.append(whole(page))
        key_count += page.shape[2]
    if prev is not None:
        for mixed, table, at in prev:
            args += [mixed, table]
            in_specs += [per_rows(at), per_head(table, at)]
    if pool is not None:
        args.append(pltpu.with_memory_space_constraint(pool, pltpu.HBM))
        in_specs.append(pl.BlockSpec(memory_space=pltpu.HBM))
    args += list(after)
    in_specs += [anywhere] * len(after)
    out_shape = []
    out_specs = []
    scratch = [pltpu.VMEM((key_count, 2 * lanes), jnp.bfloat16)]
    for h in range(halves):
        if packed[h]:
            shape = jax.ShapeDtypeStruct((heads, rows + 3 * size, lanes), jnp.bfloat16)
            out_shape.append(shape)
            out_specs.append(per_head(shape, 0))
            scratch.append(pltpu.VMEM((size, lanes), jnp.float32))
        else:
            table = jax.ShapeDtypeStruct((heads, size, lanes), jnp.float32)
            out_shape += [jax.ShapeDtypeStruct((heads, rows, lanes), jnp.float32), table]
            out_specs += [per_rows(0), per_head(table, 0)]
    if pool is not None:
        out_shape.append(jax.ShapeDtypeStruct(pool.shape, pool.dtype))
        out_specs.append(pl.BlockSpec(memory_space=pltpu.HBM))
        scratch.append(pltpu.VMEM(pool.shape, pool.dtype))
        scratch += [pltpu.SemaphoreType.DMA, pltpu.SemaphoreType.DMA]
    work = halves * heads * rows * key_count
    return pl.pallas_call(
        functools.partial(
            attend_body,
            halves=halves,
            seen_at=seen_at,
            has_page=page is not None,
            has_prev=prev is not None,
            packed=packed,
            step_rows=step_rows,
            tile_rows=tile_rows,
            group=group,
            scale=scale,
            copies_pool=pool is not None,
            waits=len(after),
            page_at=page_at,
        ),
        out_shape=out_shape,
        grid_spec=pltpu.PrefetchScalarGridSpec(
            num_scalar_prefetch=3,
            grid=(heads, rows // step_rows),
            in_specs=in_specs,
            out_specs=out_specs,
            scratch_shapes=scratch,
        ),
        cost_estimate=pl.CostEstimate(
            flops=4 * work * lanes,
            transcendentals=work,
            bytes_accessed=4 * heads * key_count * lanes,
        ),
        compiler_params=pltpu.CompilerParams(vmem_limit_bytes=kernel_bytes),
        name="attend",
    )(*scalars, *args)


def join_body(own_mixed, own_table, *refs, scale, packs, waits):
    refs = list(refs)
    out_ref = refs.pop()
    if waits:
        del refs[-waits:]
    size = own_table.shape[1]
    count = size // 2
    rows = count * block_rows
    eye = diagonal()
    tops = [own_table[0, :count]]
    totals = [own_table[0, count:]]
    for ref in refs:
        table = from_three(ref, rows, size)
        tops.append(table[:count])
        totals.append(table[count:])
    top = functools.reduce(jnp.maximum, tops)
    keeps = [jnp.exp2((t - top) * scale) for t in tops]
    total = sum(t * keep for t, keep in zip(totals, keeps))
    if not packs:
        keeps = [keep / total for keep in keeps]
    for t in range(count):
        at = slice(t * block_rows, (t + 1) * block_rows)
        mixed = own_mixed[0, at] * as_column(keeps[0][t : t + 1], eye)
        for ref, keep in zip(refs, keeps[1:]):
            mixed = mixed + ref[0, at].astype(jnp.float32) * as_column(keep[t : t + 1], eye)
        if packs:
            out_ref[0, at] = mixed.astype(jnp.bfloat16)
        else:
            heads = out_ref.shape[1]
            tokens = block_rows // heads
            shaped = mixed.reshape(tokens, heads, lanes)
            out_ref[t * tokens : (t + 1) * tokens] = shaped.astype(jnp.bfloat16)
    if packs:
        table = jnp.concatenate([top, total], axis=0)
        for i, part in enumerate(in_three(table)):
            out_ref[0, rows + i * size : rows + (i + 1) * size] = part


def join_packed(own, received, scale, after=()):
    mixed, table = own
    args = [mixed, table, received]
    return pl.pallas_call(
        functools.partial(join_body, scale=scale, packs=True, waits=len(after)),
        out_shape=jax.ShapeDtypeStruct(received.shape, received.dtype),
        grid=(1,),
        in_specs=[whole(a) for a in args] + [pl.BlockSpec(memory_space=pl.ANY)] * len(after),
        out_specs=whole(received),
        compiler_params=pltpu.CompilerParams(vmem_limit_bytes=kernel_bytes),
        name="join_packed",
    )(*args, *after)


def join_out(own, received, target, shape, index, group, scale):
    mixed, table = own
    args = [mixed, table, *received]
    in_specs = [whole(a) for a in args]
    aliases = {}
    if target is not None:
        aliases = {len(args): 0}
        args.append(target)
        in_specs.append(pl.BlockSpec(memory_space=pl.ANY))
    return pl.pallas_call(
        functools.partial(join_body, scale=scale, packs=False, waits=len(aliases)),
        out_shape=jax.ShapeDtypeStruct(shape, jnp.bfloat16),
        grid=(1,),
        in_specs=in_specs,
        out_specs=pl.BlockSpec((shape[0], group, shape[2]), lambda i: (0, index, 0)),
        input_output_aliases=aliases,
        compiler_params=pltpu.CompilerParams(vmem_limit_bytes=kernel_bytes),
        name="join_out",
    )(*args)


def visible_counts(table, lengths, owner, steps, slot_count, page_len):
    requests, width = table.shape
    holders = owner ^ (2 * jnp.arange(steps, dtype=jnp.int32))
    chosen = (owner >> 1) ^ (jnp.arange(2, dtype=jnp.int32) * steps)
    column = jnp.arange(width, dtype=jnp.int32)
    count = jnp.clip(lengths[:, None] - column[None, :] * page_len, 0, page_len)
    first = holders[None, :, None, None] * slot_count
    entry = table[None, None]
    held = (entry >= first) & (entry < first + slot_count)
    asked = jnp.arange(requests, dtype=jnp.int32)[None, :] == chosen[:, None]
    picked = held & asked[:, None, :, None]
    return jnp.sum(jnp.where(picked, count[None, None], 0), axis=(2, 3))


def on_device(queries, new_kv, pool, block_table, prefix_len, new_slots):
    owner_count = lax.axis_size("pool")
    owner = lax.axis_index("pool").astype(jnp.int32)
    slot_count, _, kv_heads, page_len, head_dim = pool.shape
    tokens, q_heads, _ = queries.shape
    group = q_heads // kv_heads
    rows = tokens * group
    pairs = owner_count // 2
    near = pairs // 2
    cap = block_table.shape[1] // owner_count
    scale = head_dim**-0.5 * log2_e
    each = range(kv_heads)

    split = [
        queries[:, k * group : (k + 1) * group].reshape(1, rows, head_dim) for k in each
    ]
    far_own = [moved(split[k], pairs) for k in each]
    other = [moved(split[k], 1) for k in each]
    owner_list = jnp.full((1,), owner, jnp.int32)
    lists = [near + k for k in range(1, near)] + list(range(1, near)) + [0, near]
    pages = gather_pages(owner_list, block_table, pool, lists, cap)

    def exchanged(sent):
        return [[moved(sent[i][k], 2 * (i + 1)) for i in range(near - 1)] for k in each]

    got_far = exchanged(pages)
    got_near = exchanged(pages[near - 1 :])
    local, local_far = pages[2 * near - 2 :]
    seen = visible_counts(block_table, prefix_len, owner, near, slot_count, page_len)
    scalars = (owner_list, seen, new_slots)
    new_page = new_kv.transpose(1, 2, 0, 3)

    started = []
    updated = None
    after = []
    for k in each:
        results = attend(
            scalars,
            [(split[k], 0), (other[k], 0)],
            [(local[k], 0)],
            [(0, 0)],
            (False, False),
            scale,
            group,
            1,
            page=(new_page, k),
            pool=pool if k == 0 else None,
            after=after,
        )
        if k == 0:
            updated = results[4]
        started.append(results[:4])
        after = [results[1]]
    far_other = [moved(far_own[k], 1) for k in each]
    far = []
    for k in each:
        results = attend(
            scalars,
            [(far_own[k], 0), (far_other[k], 0)],
            [(local_far[k], 0)] + [(a, 0) for a in got_far[k]],
            [(1, i) for i in range(near)],
            (False, True),
            scale,
            group,
            1,
            after=after,
        )
        far.append((results[:2], moved(results[2], 1)))
        after = [results[1]]
    back = []
    ready = []
    for k in each:
        joined = join_packed(*far[k], scale, after=after)
        back.append(moved(joined, pairs))
        mine, mine_table, theirs, theirs_table = started[k]
        results = attend(
            scalars,
            [(split[k], 0), (other[k], 0)],
            [(a, 0) for a in got_near[k]],
            [(0, i) for i in range(1, near)],
            (False, True),
            scale,
            group,
            1,
            prev=[(mine, mine_table, 0), (theirs, theirs_table, 0)],
            after=[joined],
        )
        ready.append((results[:2], moved(results[2], 1)))
        after = [results[1]]
    attended = None
    for k in each:
        own, received = ready[k]
        attended = join_out(
            own, [received, back[k]], attended, queries.shape, k, group, scale
        )
    return (attended, updated)


def solution(mesh):
    placed = (
        P(("groups", "pool"), "head", None),
        P(("groups", "pool"), None, "head", None),
        P(("groups", "pool"), None, "head", None, None),
        P("groups", None),
        P("groups"),
        P("groups"),
    )

    return jax.shard_map(
        on_device,
        mesh=mesh,
        in_specs=placed,
        out_specs=(
            P(("groups", "pool"), "head", None),
            P(("groups", "pool"), None, "head", None, None),
        ),
        check_vma=False,
    )
```

profile of v0, /device:TPU:0, one launch (start us, length us, event | category | flops | bytes accessed | tf_op | source)
XLA Modules:
  0.0 98.7 jit_solution(17685168202906778443)
XLA Ops:
  0.6 0.0 copy-start.2
  0.7 1.1 %slice_bitcast_fusion = (bf16[1,1024,128]{2,1,0:T(8,128)(2,1)S(1)}, bf16[1,1024,128]{2,1,0:T(8,128)(2,1)S(1)}) fusion(bf16[128,16,128]{2,1,0:T(8,128)(2,1)} %param.6), kind=kLoop, calls=%fused_computation | loop fusion | bytes 1048576 | tf_op jit(solution)/shard_map/reshape | solution.py:471
  1.8 3.1 %collective-permute-start.2 = (bf16[1,1024,128]{2,1,0:T(8,128)(2,1)S(1)}, bf16[1,1024,128]{2,1,0:T(8,128)(2,1)S(1)}, u32[]{:S(2)}, u32[]{:S(2)}) collective-permute-start(bf16[1,1024,128]{2,1,0:T(8,128)(2,1)S(1)} %get-tuple-element.60.refs_0_), channel_id=1, source_target_pairs={{0,2},{2,0},{4,6},{6,4},{8,10},{10,8},{12,14},{14,12},{1,3},{3,1},... | collective-permute-start | bytes 786440 | tf_op jit(solution)/shard_map/ppermute | solution.py:21
  4.8 2.6 %collective-permute-start.6 = (bf16[1,1024,128]{2,1,0:T(8,128)(2,1)S(1)}, bf16[1,1024,128]{2,1,0:T(8,128)(2,1)S(1)}, u32[]{:S(2)}, u32[]{:S(2)}) collective-permute-start(bf16[1,1024,128]{2,1,0:T(8,128)(2,1)S(1)} %get-tuple-element.60.refs_0_), channel_id=1, source_target_pairs={{0,8},{2,10},{4,12},{6,14},{8,0},{10,2},{12,4},{14,6},{1,9},{3,11}... | collective-permute-start | bytes 786440 | tf_op jit(solution)/shard_map/ppermute | solution.py:21
  7.4 0.5 collective-permute-start
  7.9 0.0 collective-permute-start.3
  7.9 0.7 copy-done.1
  8.6 6.1 %gather_pages.1 = (bf16[1,8,2,128,128]{4,3,2,1,0:T(8,128)(2,1)}, bf16[1,8,2,128,128]{4,3,2,1,0:T(8,128)(2,1)}, bf16[1,8,2,128,128]{4,3,2,1,0:T(8,128)(2,1)}, bf1...) custom-call(s32[1]{0:T(128)} %bitcast.owner_ref, ...), custom_call_target="tpu_custom_call" | custom-call | tf_op jit(solution)/shard_map/gather_pages/pallas_call | solution.py:105
  14.7 2.0 %collective-permute-start.8 = (bf16[1,8,2,128,128]{4,3,2,1,0:T(8,128)(2,1)}, bf16[1,8,2,128,128]{4,3,2,1,0:T(8,128)(2,1)S(1)}, u32[]{:S(2)}, u32[]{:S(2)}) collective-permute-start(bf16[1,8,2,128,128]{4,3,2,1,0:T(8,128)(2,1)} %get-tuple-element.42), channel_id=1, source_target_pairs={{0,4},{2,6},{4,0},{6,2},{8,12},{10,14},{12,8},{14,10},{1,5},{3,7},... | collective-permute-start | bytes 1572872 | tf_op jit(solution)/shard_map/ppermute | solution.py:21
  16.7 0.1 compare_and_fusion
  16.8 0.1 subtract_clamp_fusion
  16.9 0.1 iota_compare_fusion
  17.0 0.0 collective-permute-done.2.refs_1_
  17.0 0.1 collective-permute-start.5
  17.1 8.9 %collective-permute-done.6.refs_0_ = bf16[1,1024,128]{2,1,0:T(8,128)(2,1)S(1)} collective-permute-done((bf16[1,1024,128]{2,1,0:T(8,128)(2,1)S(1)}, bf16[1,1024,128]{2,1,0:T(8,128)(2,1)S(1)}, u32[]{:S(2)}, u32[]{:S(2)}) %collective-permute-start.6) | collective-permute-done | bytes 262176 | tf_op jit(solution)/shard_map/ppermute | solution.py:21
  26.0 0.5 collective-permute-start.7
  26.4 0.2 select_reduce_fusion.seen_ref
  26.7 0.0 copy-start
  26.7 1.0 %copy-done = bf16[1,8,2,128,128]{4,3,2,1,0:T(8,128)(2,1)S(1)} copy-done((bf16[1,8,2,128,128]{4,3,2,1,0:T(8,128)(2,1)S(1)}, bf16[1,8,2,128,128]{4,3,2,1,0:T(8,128)(2,1)}, u32[]{:S(2)}) %copy-start) | copy-done | bytes 524312
  27.7 4.9 %attend.6 = (f32[1,1024,128]{2,1,0:T(8,128)S(1)}, f32[1,16,128]{2,1,0:T(8,128)S(1)}, f32[1,1024,128]{2,1,0:T(8,128)S(1)}, f32[1,16,128]{2,1,0:T(8,128)S(1)}, bf16[33,2,2,128,128]{4,3,2,1,0:T(8,128)(2,1)}) custom-call(s32[1]{0:T(128)} %bitcast.owner_ref, s32[2,2]{1,0:T(2,128)S(1)} %select_reduce_fusion.seen_ref, s32[8]{0:T(128)S(1)} %copy-done.3, ...), custom_call_target="tpu_custom_call" | custom-call | flops 1207959552 | bytes 589824 | tf_op jit(solution)/shard_map/attend/pallas_call | solution.py:336
  32.7 0.0 collective-permute-done.refs_1_
  32.7 0.1 collective-permute-start.10
  32.8 1.6 %collective-permute-start.4 = (bf16[1,1024,128]{2,1,0:T(8,128)(2,1)S(1)}, bf16[1,1024,128]{2,1,0:T(8,128)(2,1)S(1)}, u32[]{:S(2)}, u32[]{:S(2)}) collective-permute-start(bf16[1,1024,128]{2,1,0:T(8,128)(2,1)S(1)} %collective-permute-done.3.refs_0_), channel_id=1, source_target_pairs={{0,2},{2,0},{4,6},{6,4},{8,10},{10,8},{12,14},{14,12},{1,3},{3,1},... | collective-permute-start | bytes 786440 | tf_op jit(solution)/shard_map/ppermute | solution.py:21
  34.4 4.8 %attend.7 = (f32[1,1024,128]{2,1,0:T(8,128)S(1)}, f32[1,16,128]{2,1,0:T(8,128)S(1)}, f32[1,1024,128]{2,1,0:T(8,128)S(1)}, f32[1,16,128]{2,1,0:T(8,128)S(1)}) custom-call(s32[1]{0:T(128)} %bitcast.owner_ref, s32[2,2]{1,0:T(2,128)S(1)} %select_reduce_fusion.seen_ref, s32[8]{0:T(128)S(1)} %copy-done.3, bf16[1,1024,128]{2,1,0:T(8,128)(2,1)S(1)} %get-tuple-element.61.refs_0_, ...), custom_call_target="tpu_custom_call" | custom-call | flops 1207959552 | bytes 589824 | tf_op jit(solution)/shard_map/attend/pallas_call | solution.py:336
  39.3 0.7 collective-permute-done.8.refs_3_
  39.9 1.4 %collective-permute-start.1 = (bf16[1,8,2,128,128]{4,3,2,1,0:T(8,128)(2,1)S(1)}, bf16[1,8,2,128,128]{4,3,2,1,0:T(8,128)(2,1)S(1)}, u32[]{:S(2)}, u32[]{:S(2)}) collective-permute-start(bf16[1,8,2,128,128]{4,3,2,1,0:T(8,128)(2,1)S(1)} %copy-done.9), channel_id=1, source_target_pairs={{0,4},{2,6},{4,0},{6,2},{8,12},{10,14},{12,8},{14,10},{1,5},{3,7},... | collective-permute-start | bytes 1572872 | tf_op jit(solution)/shard_map/ppermute | solution.py:21
  41.3 0.0 collective-permute-done.7.refs_1_
  41.3 6.7 %attend.8 = (f32[1,1024,128]{2,1,0:T(8,128)S(1)}, f32[1,16,128]{2,1,0:T(8,128)S(1)}, bf16[1,1072,128]{2,1,0:T(8,128)(2,1)S(1)}) custom-call(s32[1]{0:T(128)} %bitcast.owner_ref, s32[2,2]{1,0:T(2,128)S(1)} %select_reduce_fusion.seen_ref, s32[8]{0:T(128)S(1)} %copy-done.3, bf16[1,1024,128]{2,1,0:T(8,128)(2,1)S(1)} %collective-permute-done.6.refs_0_, ...), custom_call_target="tpu_custom_call" | custom-call | flops 2147483648 | bytes 1048576 | tf_op jit(solution)/shard_map/attend/pallas_call | solution.py:336
  48.0 0.5 collective-permute-start.11
  48.5 2.6 %collective-permute-done.5.refs_3_ = bf16[1,8,2,128,128]{4,3,2,1,0:T(8,128)(2,1)S(1)} collective-permute-done((bf16[1,8,2,128,128]{4,3,2,1,0:T(8,128)(2,1)}, bf16[1,8,2,128,128]{4,3,2,1,0:T(8,128)(2,1)S(1)}, u32[]{:S(2)}, u32[]{:S(2)}) %collective-permute-start.5) | collective-permute-done | bytes 524320 | tf_op jit(solution)/shard_map/ppermute | solution.py:21
  51.2 0.0 collective-permute-done.4.refs_1_
  51.2 6.7 %attend.9 = (f32[1,1024,128]{2,1,0:T(8,128)S(1)}, f32[1,16,128]{2,1,0:T(8,128)S(1)}, bf16[1,1072,128]{2,1,0:T(8,128)(2,1)S(1)}) custom-call(s32[1]{0:T(128)} %bitcast.owner_ref, s32[2,2]{1,0:T(2,128)S(1)} %select_reduce_fusion.seen_ref, s32[8]{0:T(128)S(1)} %copy-done.3, bf16[1,1024,128]{2,1,0:T(8,128)(2,1)S(1)} %collective-permute-done.3.refs_0_, ...), custom_call_target="tpu_custom_call" | custom-call | flops 2147483648 | bytes 1048576 | tf_op jit(solution)/shard_map/attend/pallas_call | solution.py:336
  57.9 1.8 %collective-permute-start.9 = (bf16[1,1072,128]{2,1,0:T(8,128)(2,1)S(1)}, bf16[1,1072,128]{2,1,0:T(8,128)(2,1)S(1)}, u32[]{:S(2)}, u32[]{:S(2)}) collective-permute-start(bf16[1,1072,128]{2,1,0:T(8,128)(2,1)S(1)} %get-tuple-element.46), channel_id=1, source_target_pairs={{0,2},{2,0},{4,6},{6,4},{8,10},{10,8},{12,14},{14,12},{1,3},{3,1},... | collective-permute-start | bytes 823304 | tf_op jit(solution)/shard_map/ppermute | solution.py:21
  59.7 0.4 join_packed.2.refs_7_
  60.0 1.9 %collective-permute-start.15 = (bf16[1,1072,128]{2,1,0:T(8,128)(2,1)S(1)}, bf16[1,1072,128]{2,1,0:T(8,128)(2,1)S(1)}, u32[]{:S(2)}, u32[]{:S(2)}) collective-permute-start(bf16[1,1072,128]{2,1,0:T(8,128)(2,1)S(1)} %join_packed.2.refs_7_), channel_id=1, source_target_pairs={{0,8},{2,10},{4,12},{6,14},{8,0},{10,2},{12,4},{14,6},{1,9},{3,11}... | collective-permute-start | bytes 823304 | tf_op jit(solution)/shard_map/ppermute | solution.py:21
  61.9 4.2 %collective-permute-done.10.refs_2_ = bf16[1,8,2,128,128]{4,3,2,1,0:T(8,128)(2,1)S(1)} collective-permute-done((bf16[1,8,2,128,128]{4,3,2,1,0:T(8,128)(2,1)S(1)}, bf16[1,8,2,128,128]{4,3,2,1,0:T(8,128)(2,1)S(1)}, u32[]{:S(2)}, u32[]{:S(2)}) %collective-permute-start.10) | collective-permute-done | bytes 524320 | tf_op jit(solution)/shard_map/ppermute | solution.py:21
  66.1 4.5 %attend.10 = (f32[1,1024,128]{2,1,0:T(8,128)S(1)}, f32[1,16,128]{2,1,0:T(8,128)S(1)}, bf16[1,1072,128]{2,1,0:T(8,128)(2,1)S(1)}) custom-call(s32[1]{0:T(128)} %bitcast.owner_ref, s32[2,2]{1,0:T(2,128)S(1)} %select_reduce_fusion.seen_ref, s32[8]{0:T(128)S(1)} %copy-done.3, bf16[1,1024,128]{2,1,0:T(8,128)(2,1)S(1)} %get-tuple-element.60.refs_0_, ...), custom_call_target="tpu_custom_call" | custom-call | flops 1073741824 | bytes 524288 | tf_op jit(solution)/shard_map/attend/pallas_call | solution.py:336
  70.6 2.4 %collective-permute-start.14 = (bf16[1,1072,128]{2,1,0:T(8,128)(2,1)S(1)}, bf16[1,1072,128]{2,1,0:T(8,128)(2,1)S(1)}, u32[]{:S(2)}, u32[]{:S(2)}) collective-permute-start(bf16[1,1072,128]{2,1,0:T(8,128)(2,1)S(1)} %get-tuple-element.58), channel_id=1, source_target_pairs={{0,2},{2,0},{4,6},{6,4},{8,10},{10,8},{12,14},{14,12},{1,3},{3,1},... | collective-permute-start | bytes 823304 | tf_op jit(solution)/shard_map/ppermute | solution.py:21
  73.0 0.0 collective-permute-done.9.refs_0_
  73.0 0.4 join_packed.3.refs_7_
  73.4 4.2 %collective-permute-done.1.refs_2_ = bf16[1,8,2,128,128]{4,3,2,1,0:T(8,128)(2,1)S(1)} collective-permute-done((bf16[1,8,2,128,128]{4,3,2,1,0:T(8,128)(2,1)S(1)}, bf16[1,8,2,128,128]{4,3,2,1,0:T(8,128)(2,1)S(1)}, u32[]{:S(2)}, u32[]{:S(2)}) %collective-permute-start.1) | collective-permute-done | bytes 524320 | tf_op jit(solution)/shard_map/ppermute | solution.py:21
  77.5 4.3 %attend.11 = (f32[1,1024,128]{2,1,0:T(8,128)S(1)}, f32[1,16,128]{2,1,0:T(8,128)S(1)}, bf16[1,1072,128]{2,1,0:T(8,128)(2,1)S(1)}) custom-call(s32[1]{0:T(128)} %bitcast.owner_ref, s32[2,2]{1,0:T(2,128)S(1)} %select_reduce_fusion.seen_ref, s32[8]{0:T(128)S(1)} %copy-done.3, bf16[1,1024,128]{2,1,0:T(8,128)(2,1)S(1)} %get-tuple-element.61.refs_0_, ...), custom_call_target="tpu_custom_call" | custom-call | flops 1073741824 | bytes 524288 | tf_op jit(solution)/shard_map/attend/pallas_call | solution.py:336
  81.9 1.6 %collective-permute-start.12 = (bf16[1,1072,128]{2,1,0:T(8,128)(2,1)S(1)}, bf16[1,1072,128]{2,1,0:T(8,128)(2,1)S(1)}, u32[]{:S(2)}, u32[]{:S(2)}) collective-permute-start(bf16[1,1072,128]{2,1,0:T(8,128)(2,1)S(1)} %get-tuple-element.56), channel_id=1, source_target_pairs={{0,2},{2,0},{4,6},{6,4},{8,10},{10,8},{12,14},{14,12},{1,3},{3,1},... | collective-permute-start | bytes 823304 | tf_op jit(solution)/shard_map/ppermute | solution.py:21
  83.5 2.8 %collective-permute-start.13 = (bf16[1,1072,128]{2,1,0:T(8,128)(2,1)S(1)}, bf16[1,1072,128]{2,1,0:T(8,128)(2,1)S(1)}, u32[]{:S(2)}, u32[]{:S(2)}) collective-permute-start(bf16[1,1072,128]{2,1,0:T(8,128)(2,1)S(1)} %join_packed.3.refs_7_), channel_id=1, source_target_pairs={{0,8},{2,10},{4,12},{6,14},{8,0},{10,2},{12,4},{14,6},{1,9},{3,11}... | collective-permute-start | bytes 823304 | tf_op jit(solution)/shard_map/ppermute | solution.py:21
  86.2 1.2 %join_out.2.refs_2_ = bf16[128,16,128]{2,1,0:T(8,128)(2,1)} custom-call(f32[1,1024,128]{2,1,0:T(8,128)S(1)} %get-tuple-element.57.own_mixed, f32[1,16,128]{2,1,0:T(8,128)S(1)} %get-tuple-element.53.refs_1_.own_table, bf16[1,1072,128]{2,1,0:T(8,128)(2,1)S(1)} %collective-permute-done.14.refs_0_, bf16[1,1072,128]{2,1,0:T(8,128)(2,1)S(1)} %collective-permute-done.15.refs_1_), custom_call_target="tpu_custom_call" | custom-call | tf_op jit(solution)/shard_map/join_out/pallas_call | solution.py:431
  87.5 1.1 %collective-permute-done.12.refs_0_ = bf16[1,1072,128]{2,1,0:T(8,128)(2,1)S(1)} collective-permute-done((bf16[1,1072,128]{2,1,0:T(8,128)(2,1)S(1)}, bf16[1,1072,128]{2,1,0:T(8,128)(2,1)S(1)}, u32[]{:S(2)}, u32[]{:S(2)}) %collective-permute-start.12) | collective-permute-done | bytes 274464 | tf_op jit(solution)/shard_map/ppermute | solution.py:21
  88.6 8.9 %collective-permute-done.13.refs_1_ = bf16[1,1072,128]{2,1,0:T(8,128)(2,1)S(1)} collective-permute-done((bf16[1,1072,128]{2,1,0:T(8,128)(2,1)S(1)}, bf16[1,1072,128]{2,1,0:T(8,128)(2,1)S(1)}, u32[]{:S(2)}, u32[]{:S(2)}) %collective-permute-start.13) | collective-permute-done | bytes 274464 | tf_op jit(solution)/shard_map/ppermute | solution.py:21
  97.5 1.2 %join_out.3 = bf16[128,16,128]{2,1,0:T(8,128)(2,1)} custom-call(f32[1,1024,128]{2,1,0:T(8,128)S(1)} %get-tuple-element.54.own_mixed, f32[1,16,128]{2,1,0:T(8,128)S(1)} %get-tuple-element.55.own_table, bf16[1,1072,128]{2,1,0:T(8,128)(2,1)S(1)} %collective-permute-done.12.refs_0_, ...), custom_call_target="tpu_custom_call", output_to_operand_aliasing={{}: (4, {})} | custom-call | tf_op jit(solution)/shard_map/join_out/pallas_call | solution.py:431
  (26 shorter events, 0.1 us)
Async XLA Ops:
  0.6 16.1 %copy-start.2 = (s32[4,64]{1,0:T(4,128)S(1)}, s32[4,64]{1,0:T(4,128)}, u32[]{:S(2)}) copy-start(s32[4,64]{1,0:T(4,128)} %table_ref.1) | copy-start | bytes 3076
  0.6 16.2 %copy-start.8 = (s32[4]{0:T(128)S(1)}, s32[4]{0:T(128)}, u32[]{:S(2)}) copy-start(s32[4]{0:T(128)} %param.10) | copy-start | bytes 52
  0.7 26.0 %copy-start.7 = (bf16[128,2,2,128]{3,2,1,0:T(2,128)(2,1)S(1)}, bf16[128,2,2,128]{3,2,1,0:T(2,128)(2,1)}, u32[]{:S(2)}) copy-start(bf16[128,2,2,128]{3,2,1,0:T(2,128)(2,1)} %param.7) | copy-start | bytes 393220
  0.7 26.0 %copy-start.3 = (s32[8]{0:T(128)S(1)}, s32[8]{0:T(128)}, u32[]{:S(2)}) copy-start(s32[8]{0:T(128)} %fresh_ref.11) | copy-start | bytes 100
  1.8 15.2 %collective-permute-start.2 = (bf16[1,1024,128]{2,1,0:T(8,128)(2,1)S(1)}, bf16[1,1024,128]{2,1,0:T(8,128)(2,1)S(1)}, u32[]{:S(2)}, u32[]{:S(2)}) collective-permute-start(bf16[1,1024,128]{2,1,0:T(8,128)(2,1)S(1)} %get-tuple-element.60.refs_0_), channel_id=1, source_target_pairs={{0,2},{2,0},{4,6},{6,4},{8,10},{10,8},{12,14},{14,12},{1,3},{3,1},... | collective-permute-start | bytes 786440 | tf_op jit(solution)/shard_map/ppermute | solution.py:21
  4.8 21.1 %collective-permute-start.6 = (bf16[1,1024,128]{2,1,0:T(8,128)(2,1)S(1)}, bf16[1,1024,128]{2,1,0:T(8,128)(2,1)S(1)}, u32[]{:S(2)}, u32[]{:S(2)}) collective-permute-start(bf16[1,1024,128]{2,1,0:T(8,128)(2,1)S(1)} %get-tuple-element.60.refs_0_), channel_id=1, source_target_pairs={{0,8},{2,10},{4,12},{6,14},{8,0},{10,2},{12,4},{14,6},{1,9},{3,11}... | collective-permute-start | bytes 786440 | tf_op jit(solution)/shard_map/ppermute | solution.py:21
  7.4 25.3 %collective-permute-start = (bf16[1,1024,128]{2,1,0:T(8,128)(2,1)S(1)}, bf16[1,1024,128]{2,1,0:T(8,128)(2,1)S(1)}, u32[]{:S(2)}, u32[]{:S(2)}) collective-permute-start(bf16[1,1024,128]{2,1,0:T(8,128)(2,1)S(1)} %get-tuple-element.61.refs_0_), channel_id=1, source_target_pairs={{0,2},{2,0},{4,6},{6,4},{8,10},{10,8},{12,14},{14,12},{1,3},{3,1},... | collective-permute-start | bytes 786440 | tf_op jit(solution)/shard_map/ppermute | solution.py:21
  7.9 24.9 %collective-permute-start.3 = (bf16[1,1024,128]{2,1,0:T(8,128)(2,1)S(1)}, bf16[1,1024,128]{2,1,0:T(8,128)(2,1)S(1)}, u32[]{:S(2)}, u32[]{:S(2)}) collective-permute-start(bf16[1,1024,128]{2,1,0:T(8,128)(2,1)S(1)} %get-tuple-element.61.refs_0_), channel_id=1, source_target_pairs={{0,8},{2,10},{4,12},{6,14},{8,0},{10,2},{12,4},{14,6},{1,9},{3,11}... | collective-permute-start | bytes 786440 | tf_op jit(solution)/shard_map/ppermute | solution.py:21
  7.9 0.7 copy-start.1
  14.7 25.2 %collective-permute-start.8 = (bf16[1,8,2,128,128]{4,3,2,1,0:T(8,128)(2,1)}, bf16[1,8,2,128,128]{4,3,2,1,0:T(8,128)(2,1)S(1)}, u32[]{:S(2)}, u32[]{:S(2)}) collective-permute-start(bf16[1,8,2,128,128]{4,3,2,1,0:T(8,128)(2,1)} %get-tuple-element.42), channel_id=1, source_target_pairs={{0,4},{2,6},{4,0},{6,2},{8,12},{10,14},{12,8},{14,10},{1,5},{3,7},... | collective-permute-start | bytes 1572872 | tf_op jit(solution)/shard_map/ppermute | solution.py:21
  17.0 34.2 %collective-permute-start.5 = (bf16[1,8,2,128,128]{4,3,2,1,0:T(8,128)(2,1)}, bf16[1,8,2,128,128]{4,3,2,1,0:T(8,128)(2,1)S(1)}, u32[]{:S(2)}, u32[]{:S(2)}) collective-permute-start(bf16[1,8,2,128,128]{4,3,2,1,0:T(8,128)(2,1)} %get-tuple-element.40), channel_id=1, source_target_pairs={{0,4},{2,6},{4,0},{6,2},{8,12},{10,14},{12,8},{14,10},{1,5},{3,7},... | collective-permute-start | bytes 1572872 | tf_op jit(solution)/shard_map/ppermute | solution.py:21
  26.0 15.3 %collective-permute-start.7 = (bf16[1,1024,128]{2,1,0:T(8,128)(2,1)S(1)}, bf16[1,1024,128]{2,1,0:T(8,128)(2,1)S(1)}, u32[]{:S(2)}, u32[]{:S(2)}) collective-permute-start(bf16[1,1024,128]{2,1,0:T(8,128)(2,1)S(1)} %collective-permute-done.6.refs_0_), channel_id=1, source_target_pairs={{0,2},{2,0},{4,6},{6,4},{8,10},{10,8},{12,14},{14,12},{1,3},{3,1},... | collective-permute-start | bytes 786440 | tf_op jit(solution)/shard_map/ppermute | solution.py:21
  26.7 1.0 %copy-start = (bf16[1,8,2,128,128]{4,3,2,1,0:T(8,128)(2,1)S(1)}, bf16[1,8,2,128,128]{4,3,2,1,0:T(8,128)(2,1)}, u32[]{:S(2)}) copy-start(bf16[1,8,2,128,128]{4,3,2,1,0:T(8,128)(2,1)} %get-tuple-element.33.refs_2_) | copy-start | bytes 1572868
  27.7 5.0 %copy-start.10 = (bf16[1,8,2,128,128]{4,3,2,1,0:T(8,128)(2,1)S(1)}, bf16[1,8,2,128,128]{4,3,2,1,0:T(8,128)(2,1)}, u32[]{:S(2)}) copy-start(bf16[1,8,2,128,128]{4,3,2,1,0:T(8,128)(2,1)} %get-tuple-element.47) | copy-start | bytes 1572868
  27.7 6.7 %copy-start.6 = (bf16[1,8,2,128,128]{4,3,2,1,0:T(8,128)(2,1)S(1)}, bf16[1,8,2,128,128]{4,3,2,1,0:T(8,128)(2,1)}, u32[]{:S(2)}) copy-start(bf16[1,8,2,128,128]{4,3,2,1,0:T(8,128)(2,1)} %get-tuple-element.32.refs_2_) | copy-start | bytes 1572868
  27.7 12.2 %copy-start.9 = (bf16[1,8,2,128,128]{4,3,2,1,0:T(8,128)(2,1)S(1)}, bf16[1,8,2,128,128]{4,3,2,1,0:T(8,128)(2,1)}, u32[]{:S(2)}) copy-start(bf16[1,8,2,128,128]{4,3,2,1,0:T(8,128)(2,1)} %get-tuple-element.31) | copy-start | bytes 1572868
  27.7 13.6 %copy-start.5 = (bf16[1,8,2,128,128]{4,3,2,1,0:T(8,128)(2,1)S(1)}, bf16[1,8,2,128,128]{4,3,2,1,0:T(8,128)(2,1)}, u32[]{:S(2)}) copy-start(bf16[1,8,2,128,128]{4,3,2,1,0:T(8,128)(2,1)} %get-tuple-element.41.refs_2_) | copy-start | bytes 1572868
  32.7 33.4 %collective-permute-start.10 = (bf16[1,8,2,128,128]{4,3,2,1,0:T(8,128)(2,1)S(1)}, bf16[1,8,2,128,128]{4,3,2,1,0:T(8,128)(2,1)S(1)}, u32[]{:S(2)}, u32[]{:S(2)}) collective-permute-start(bf16[1,8,2,128,128]{4,3,2,1,0:T(8,128)(2,1)S(1)} %copy-done.10), channel_id=1, source_target_pairs={{0,4},{2,6},{4,0},{6,2},{8,12},{10,14},{12,8},{14,10},{1,5},{3,7},... | collective-permute-start | bytes 1572872 | tf_op jit(solution)/shard_map/ppermute | solution.py:21
  32.8 18.4 %collective-permute-start.4 = (bf16[1,1024,128]{2,1,0:T(8,128)(2,1)S(1)}, bf16[1,1024,128]{2,1,0:T(8,128)(2,1)S(1)}, u32[]{:S(2)}, u32[]{:S(2)}) collective-permute-start(bf16[1,1024,128]{2,1,0:T(8,128)(2,1)S(1)} %collective-permute-done.3.refs_0_), channel_id=1, source_target_pairs={{0,2},{2,0},{4,6},{6,4},{8,10},{10,8},{12,14},{14,12},{1,3},{3,1},... | collective-permute-start | bytes 786440 | tf_op jit(solution)/shard_map/ppermute | solution.py:21
  39.3 11.9 %copy-start.4 = (bf16[1,8,2,128,128]{4,3,2,1,0:T(8,128)(2,1)S(1)}, bf16[1,8,2,128,128]{4,3,2,1,0:T(8,128)(2,1)}, u32[]{:S(2)}) copy-start(bf16[1,8,2,128,128]{4,3,2,1,0:T(8,128)(2,1)} %get-tuple-element.39.refs_2_) | copy-start | bytes 1572868
  39.9 37.6 %collective-permute-start.1 = (bf16[1,8,2,128,128]{4,3,2,1,0:T(8,128)(2,1)S(1)}, bf16[1,8,2,128,128]{4,3,2,1,0:T(8,128)(2,1)S(1)}, u32[]{:S(2)}, u32[]{:S(2)}) collective-permute-start(bf16[1,8,2,128,128]{4,3,2,1,0:T(8,128)(2,1)S(1)} %copy-done.9), channel_id=1, source_target_pairs={{0,4},{2,6},{4,0},{6,2},{8,12},{10,14},{12,8},{14,10},{1,5},{3,7},... | collective-permute-start | bytes 1572872 | tf_op jit(solution)/shard_map/ppermute | solution.py:21
  48.0 11.7 %collective-permute-start.11 = (bf16[1,1072,128]{2,1,0:T(8,128)(2,1)S(1)}, bf16[1,1072,128]{2,1,0:T(8,128)(2,1)S(1)}, u32[]{:S(2)}, u32[]{:S(2)}) collective-permute-start(bf16[1,1072,128]{2,1,0:T(8,128)(2,1)S(1)} %get-tuple-element.52), channel_id=1, source_target_pairs={{0,2},{2,0},{4,6},{6,4},{8,10},{10,8},{12,14},{14,12},{1,3},{3,1},... | collective-permute-start | bytes 823304 | tf_op jit(solution)/shard_map/ppermute | solution.py:21
  57.9 15.2 %collective-permute-start.9 = (bf16[1,1072,128]{2,1,0:T(8,128)(2,1)S(1)}, bf16[1,1072,128]{2,1,0:T(8,128)(2,1)S(1)}, u32[]{:S(2)}, u32[]{:S(2)}) collective-permute-start(bf16[1,1072,128]{2,1,0:T(8,128)(2,1)S(1)} %get-tuple-element.46), channel_id=1, source_target_pairs={{0,2},{2,0},{4,6},{6,4},{8,10},{10,8},{12,14},{14,12},{1,3},{3,1},... | collective-permute-start | bytes 823304 | tf_op jit(solution)/shard_map/ppermute | solution.py:21
  60.0 26.2 %collective-permute-start.15 = (bf16[1,1072,128]{2,1,0:T(8,128)(2,1)S(1)}, bf16[1,1072,128]{2,1,0:T(8,128)(2,1)S(1)}, u32[]{:S(2)}, u32[]{:S(2)}) collective-permute-start(bf16[1,1072,128]{2,1,0:T(8,128)(2,1)S(1)} %join_packed.2.refs_7_), channel_id=1, source_target_pairs={{0,8},{2,10},{4,12},{6,14},{8,0},{10,2},{12,4},{14,6},{1,9},{3,11}... | collective-permute-start | bytes 823304 | tf_op jit(solution)/shard_map/ppermute | solution.py:21
  70.6 15.6 %collective-permute-start.14 = (bf16[1,1072,128]{2,1,0:T(8,128)(2,1)S(1)}, bf16[1,1072,128]{2,1,0:T(8,128)(2,1)S(1)}, u32[]{:S(2)}, u32[]{:S(2)}) collective-permute-start(bf16[1,1072,128]{2,1,0:T(8,128)(2,1)S(1)} %get-tuple-element.58), channel_id=1, source_target_pairs={{0,2},{2,0},{4,6},{6,4},{8,10},{10,8},{12,14},{14,12},{1,3},{3,1},... | collective-permute-start | bytes 823304 | tf_op jit(solution)/shard_map/ppermute | solution.py:21
  81.9 6.7 %collective-permute-start.12 = (bf16[1,1072,128]{2,1,0:T(8,128)(2,1)S(1)}, bf16[1,1072,128]{2,1,0:T(8,128)(2,1)S(1)}, u32[]{:S(2)}, u32[]{:S(2)}) collective-permute-start(bf16[1,1072,128]{2,1,0:T(8,128)(2,1)S(1)} %get-tuple-element.56), channel_id=1, source_target_pairs={{0,2},{2,0},{4,6},{6,4},{8,10},{10,8},{12,14},{14,12},{1,3},{3,1},... | collective-permute-start | bytes 823304 | tf_op jit(solution)/shard_map/ppermute | solution.py:21
  83.5 14.0 %collective-permute-start.13 = (bf16[1,1072,128]{2,1,0:T(8,128)(2,1)S(1)}, bf16[1,1072,128]{2,1,0:T(8,128)(2,1)S(1)}, u32[]{:S(2)}, u32[]{:S(2)}) collective-permute-start(bf16[1,1072,128]{2,1,0:T(8,128)(2,1)S(1)} %join_packed.3.refs_7_), channel_id=1, source_target_pairs={{0,8},{2,10},{4,12},{6,14},{8,0},{10,2},{12,4},{14,6},{1,9},{3,11}... | collective-permute-start | bytes 823304 | tf_op jit(solution)/shard_map/ppermute | solution.py:21
where the time goes:
time: 99 us; the launch traced here: 98.7 us
  Pallas kernels  41.2 us (42%)
  waiting for transfers between devices  30.6 us (31%)
  starting transfers between devices  22.7 us (23%)
  local copies, waits for them, and re-layouts  2.88 us (3%)
    pallas_call x6, Pallas kernels, attend(): pl.pallas_call(functools.partial(attend_body, halves=halves, seen_at=seen...  32 us
    ppermute x16, waiting for transfers between devices, moved(): return lax.ppermute(array, 'pool', [(i, i ^ apart) for i in range(count)])  30.6 us
    ppermute x16, starting transfers between devices, moved(): return lax.ppermute(array, 'pool', [(i, i ^ apart) for i in range(count)])  22.7 us
    pallas_call x1, Pallas kernels, gather_pages(): pl.pallas_call(functools.partial(gather_body, lists=lists, kv_heads=kv_he...  6.11 us
    pallas_call x2, Pallas kernels, join_out(): pl.pallas_call(functools.partial(join_body, scale=scale, packs=False, wai...  2.43 us
  transfers between devices with their start and end apart: 16, of which 7 were waited for; matrix products, arithmetic and copies ran while one was open for 0% of the time, Pallas kernels for 41%

commit v1 on v0

--- a/solution.py
+++ b/solution.py
@@ -473,15 +473,17 @@
     far_own = [moved(split[k], pairs) for k in each]
     other = [moved(split[k], 1) for k in each]
     owner_list = jnp.full((1,), owner, jnp.int32)
-    lists = [near + k for k in range(1, near)] + list(range(1, near)) + [0, near]
-    pages = gather_pages(owner_list, block_table, pool, lists, cap)
+    far_lists = [near + k for k in range(1, near)]
+    sent_far = gather_pages(owner_list, block_table, pool, far_lists, cap)
+    rest_lists = list(range(1, near)) + [0, near]
+    pages = gather_pages(owner_list, block_table, pool, rest_lists, cap)
 
     def exchanged(sent):
         return [[moved(sent[i][k], 2 * (i + 1)) for i in range(near - 1)] for k in each]
 
-    got_far = exchanged(pages)
-    got_near = exchanged(pages[near - 1 :])
-    local, local_far = pages[2 * near - 2 :]
+    got_far = exchanged(sent_far)
+    got_near = exchanged(pages)
+    local, local_far = pages[near - 1 :]
     seen = visible_counts(block_table, prefix_len, owner, near, slot_count, page_len)
     scalars = (owner_list, seen, new_slots)
     new_page = new_kv.transpose(1, 2, 0, 3)

time: 99 us -> 94 us (0.949)
  waiting for transfers between devices: 30.6 us -> 25.8 us
  starting transfers between devices: 22.7 us -> 20.6 us
  Pallas kernels: 41.2 us -> 43 us
    ppermute x16, waiting for transfers between devices: 30.6 us -> 25.8 us  [moved(): return lax.ppermute(array, 'pool', [(i, i ^ apart) for i in range(count)])]
    ppermute x16, starting transfers between devices: 22.7 us -> 20.6 us  [moved(): return lax.ppermute(array, 'pool', [(i, i ^ apart) for i in range(count)])]
    pallas_call x1 -> x2, Pallas kernels: 6.11 us -> 7.94 us  [gather_pages(): pl.pallas_call(functools.partial(gather_body, lists=lists, kv_heads=kv_he...]
  transfers between devices with their start and end apart: 16 -> 16, of which waited for: 7 -> 4; matrix products, arithmetic and copies ran while one was open for 0% -> 1% of each run, Pallas kernels for 41% -> 45%
where the time goes in v1:
time: 94 us; the launch traced here: 93.6 us
  Pallas kernels  43 us (46%)
  waiting for transfers between devices  25.8 us (27%)
  starting transfers between devices  20.6 us (22%)
  local copies, waits for them, and re-layouts  2.85 us (3%)
    pallas_call x6, Pallas kernels, attend(): pl.pallas_call(functools.partial(attend_body, halves=halves, seen_at=seen...  32 us
    ppermute x16, waiting for transfers between devices, moved(): return lax.ppermute(array, 'pool', [(i, i ^ apart) for i in range(count)])  25.8 us
    ppermute x16, starting transfers between devices, moved(): return lax.ppermute(array, 'pool', [(i, i ^ apart) for i in range(count)])  20.6 us
    pallas_call x2, Pallas kernels, gather_pages(): pl.pallas_call(functools.partial(gather_body, lists=lists, kv_heads=kv_he...  7.94 us
    pallas_call x2, Pallas kernels, join_out(): pl.pallas_call(functools.partial(join_body, scale=scale, packs=False, wai...  2.43 us
  transfers between devices with their start and end apart: 16, of which 4 were waited for; matrix products, arithmetic and copies ran while one was open for 1% of the time, Pallas kernels for 45%

profile of v1, /device:TPU:0, one launch (start us, length us, event | category | flops | bytes accessed | tf_op | source)
XLA Modules:
  0.0 93.6 jit_solution(15286681214518612826)
XLA Ops:
  0.6 0.0 copy-start.2
  0.7 1.1 %slice_bitcast_fusion = (bf16[1,1024,128]{2,1,0:T(8,128)(2,1)S(1)}, bf16[1,1024,128]{2,1,0:T(8,128)(2,1)S(1)}) fusion(bf16[128,16,128]{2,1,0:T(8,128)(2,1)} %param.6), kind=kLoop, calls=%fused_computation | loop fusion | bytes 1048576 | tf_op jit(solution)/shard_map/reshape | solution.py:471
  1.7 3.1 %collective-permute-start.2 = (bf16[1,1024,128]{2,1,0:T(8,128)(2,1)S(1)}, bf16[1,1024,128]{2,1,0:T(8,128)(2,1)S(1)}, u32[]{:S(2)}, u32[]{:S(2)}) collective-permute-start(bf16[1,1024,128]{2,1,0:T(8,128)(2,1)S(1)} %get-tuple-element.60.refs_0_), channel_id=1, source_target_pairs={{0,2},{2,0},{4,6},{6,4},{8,10},{10,8},{12,14},{14,12},{1,3},{3,1},... | collective-permute-start | bytes 786440 | tf_op jit(solution)/shard_map/ppermute | solution.py:21
  4.8 2.6 %collective-permute-start.6 = (bf16[1,1024,128]{2,1,0:T(8,128)(2,1)S(1)}, bf16[1,1024,128]{2,1,0:T(8,128)(2,1)S(1)}, u32[]{:S(2)}, u32[]{:S(2)}) collective-permute-start(bf16[1,1024,128]{2,1,0:T(8,128)(2,1)S(1)} %get-tuple-element.60.refs_0_), channel_id=1, source_target_pairs={{0,8},{2,10},{4,12},{6,14},{8,0},{10,2},{12,4},{14,6},{1,9},{3,11}... | collective-permute-start | bytes 786440 | tf_op jit(solution)/shard_map/ppermute | solution.py:21
  7.4 0.5 collective-permute-start
  7.9 0.0 collective-permute-start.3
  7.9 0.7 copy-done.1
  8.6 3.2 %gather_pages.3 = (bf16[1,8,2,128,128]{4,3,2,1,0:T(8,128)(2,1)}, bf16[1,8,2,128,128]{4,3,2,1,0:T(8,128)(2,1)}) custom-call(s32[1]{0:T(128)} %bitcast.owner_ref, s32[4,64]{1,0:T(4,128)S(1)} %copy-done.1, bf16[33,2,2,128,128]{4,3,2,1,0:T(8,128)(2,1)} %pool_ref.3), custom_call_target="tpu_custom_call" | custom-call | tf_op jit(solution)/shard_map/gather_pages/pallas_call | solution.py:105
  11.8 2.0 %collective-permute-start.8 = (bf16[1,8,2,128,128]{4,3,2,1,0:T(8,128)(2,1)}, bf16[1,8,2,128,128]{4,3,2,1,0:T(8,128)(2,1)S(1)}, u32[]{:S(2)}, u32[]{:S(2)}) collective-permute-start(bf16[1,8,2,128,128]{4,3,2,1,0:T(8,128)(2,1)} %get-tuple-element.42), channel_id=1, source_target_pairs={{0,4},{2,6},{4,0},{6,2},{8,12},{10,14},{12,8},{14,10},{1,5},{3,7},... | collective-permute-start | bytes 1572872 | tf_op jit(solution)/shard_map/ppermute | solution.py:21
  13.8 0.1 compare_and_fusion
  13.8 0.1 subtract_clamp_fusion
  13.9 0.1 iota_compare_fusion
  14.0 0.0 collective-permute-done.2.refs_1_
  14.0 0.1 collective-permute-start.5
  14.1 11.8 %collective-permute-done.6.refs_0_ = bf16[1,1024,128]{2,1,0:T(8,128)(2,1)S(1)} collective-permute-done((bf16[1,1024,128]{2,1,0:T(8,128)(2,1)S(1)}, bf16[1,1024,128]{2,1,0:T(8,128)(2,1)S(1)}, u32[]{:S(2)}, u32[]{:S(2)}) %collective-permute-start.6) | collective-permute-done | bytes 262176 | tf_op jit(solution)/shard_map/ppermute | solution.py:21
  25.9 0.5 collective-permute-start.7
  26.4 0.2 select_reduce_fusion.seen_ref
  26.6 4.7 %gather_pages.2 = (bf16[1,8,2,128,128]{4,3,2,1,0:T(8,128)(2,1)}, bf16[1,8,2,128,128]{4,3,2,1,0:T(8,128)(2,1)}, bf16[1,8,2,128,128]{4,3,2,1,0:T(8,128)(2,1)}, bf1...) custom-call(s32[1]{0:T(128)} %bitcast.owner_ref, ...), custom_call_target="tpu_custom_call" | custom-call | tf_op jit(solution)/shard_map/gather_pages/pallas_call | solution.py:105
  31.4 0.0 copy-start
  31.4 1.0 %copy-done = bf16[1,8,2,128,128]{4,3,2,1,0:T(8,128)(2,1)S(1)} copy-done((bf16[1,8,2,128,128]{4,3,2,1,0:T(8,128)(2,1)S(1)}, bf16[1,8,2,128,128]{4,3,2,1,0:T(8,128)(2,1)}, u32[]{:S(2)}) %copy-start) | copy-done | bytes 524312
  32.4 4.9 %attend.6 = (f32[1,1024,128]{2,1,0:T(8,128)S(1)}, f32[1,16,128]{2,1,0:T(8,128)S(1)}, f32[1,1024,128]{2,1,0:T(8,128)S(1)}, f32[1,16,128]{2,1,0:T(8,128)S(1)}, bf16[33,2,2,128,128]{4,3,2,1,0:T(8,128)(2,1)}) custom-call(s32[1]{0:T(128)} %bitcast.owner_ref, s32[2,2]{1,0:T(2,128)S(1)} %select_reduce_fusion.seen_ref, s32[8]{0:T(128)S(1)} %copy-done.3, ...), custom_call_target="tpu_custom_call" | custom-call | flops 1207959552 | bytes 589824 | tf_op jit(solution)/shard_map/attend/pallas_call | solution.py:336
  37.4 0.0 collective-permute-done.refs_1_
  37.4 0.1 collective-permute-start.10
  37.5 0.0 collective-permute-done.3.refs_0_
  37.5 1.6 %collective-permute-start.4 = (bf16[1,1024,128]{2,1,0:T(8,128)(2,1)S(1)}, bf16[1,1024,128]{2,1,0:T(8,128)(2,1)S(1)}, u32[]{:S(2)}, u32[]{:S(2)}) collective-permute-start(bf16[1,1024,128]{2,1,0:T(8,128)(2,1)S(1)} %collective-permute-done.3.refs_0_), channel_id=1, source_target_pairs={{0,2},{2,0},{4,6},{6,4},{8,10},{10,8},{12,14},{14,12},{1,3},{3,1},... | collective-permute-start | bytes 786440 | tf_op jit(solution)/shard_map/ppermute | solution.py:21
  39.1 4.8 %attend.7 = (f32[1,1024,128]{2,1,0:T(8,128)S(1)}, f32[1,16,128]{2,1,0:T(8,128)S(1)}, f32[1,1024,128]{2,1,0:T(8,128)S(1)}, f32[1,16,128]{2,1,0:T(8,128)S(1)}) custom-call(s32[1]{0:T(128)} %bitcast.owner_ref, s32[2,2]{1,0:T(2,128)S(1)} %select_reduce_fusion.seen_ref, s32[8]{0:T(128)S(1)} %copy-done.3, bf16[1,1024,128]{2,1,0:T(8,128)(2,1)S(1)} %get-tuple-element.61.refs_0_, ...), custom_call_target="tpu_custom_call" | custom-call | flops 1207959552 | bytes 589824 | tf_op jit(solution)/shard_map/attend/pallas_call | solution.py:336
  44.0 0.0 collective-permute-done.8.refs_3_
  44.0 2.0 %collective-permute-start.1 = (bf16[1,8,2,128,128]{4,3,2,1,0:T(8,128)(2,1)S(1)}, bf16[1,8,2,128,128]{4,3,2,1,0:T(8,128)(2,1)S(1)}, u32[]{:S(2)}, u32[]{:S(2)}) collective-permute-start(bf16[1,8,2,128,128]{4,3,2,1,0:T(8,128)(2,1)S(1)} %copy-done.9), channel_id=1, source_target_pairs={{0,4},{2,6},{4,0},{6,2},{8,12},{10,14},{12,8},{14,10},{1,5},{3,7},... | collective-permute-start | bytes 1572872 | tf_op jit(solution)/shard_map/ppermute | solution.py:21
  46.0 0.0 collective-permute-done.7.refs_1_
  46.0 6.7 %attend.8 = (f32[1,1024,128]{2,1,0:T(8,128)S(1)}, f32[1,16,128]{2,1,0:T(8,128)S(1)}, bf16[1,1072,128]{2,1,0:T(8,128)(2,1)S(1)}) custom-call(s32[1]{0:T(128)} %bitcast.owner_ref, s32[2,2]{1,0:T(2,128)S(1)} %select_reduce_fusion.seen_ref, s32[8]{0:T(128)S(1)} %copy-done.3, bf16[1,1024,128]{2,1,0:T(8,128)(2,1)S(1)} %collective-permute-done.6.refs_0_, ...), custom_call_target="tpu_custom_call" | custom-call | flops 2147483648 | bytes 1048576 | tf_op jit(solution)/shard_map/attend/pallas_call | solution.py:336
  52.7 0.5 collective-permute-start.11
  53.2 0.0 collective-permute-done.4.refs_1_
  53.2 6.7 %attend.9 = (f32[1,1024,128]{2,1,0:T(8,128)S(1)}, f32[1,16,128]{2,1,0:T(8,128)S(1)}, bf16[1,1072,128]{2,1,0:T(8,128)(2,1)S(1)}) custom-call(s32[1]{0:T(128)} %bitcast.owner_ref, s32[2,2]{1,0:T(2,128)S(1)} %select_reduce_fusion.seen_ref, s32[8]{0:T(128)S(1)} %copy-done.3, bf16[1,1024,128]{2,1,0:T(8,128)(2,1)S(1)} %collective-permute-done.3.refs_0_, ...), custom_call_target="tpu_custom_call" | custom-call | flops 2147483648 | bytes 1048576 | tf_op jit(solution)/shard_map/attend/pallas_call | solution.py:336
  59.9 1.6 %collective-permute-start.9 = (bf16[1,1072,128]{2,1,0:T(8,128)(2,1)S(1)}, bf16[1,1072,128]{2,1,0:T(8,128)(2,1)S(1)}, u32[]{:S(2)}, u32[]{:S(2)}) collective-permute-start(bf16[1,1072,128]{2,1,0:T(8,128)(2,1)S(1)} %get-tuple-element.46), channel_id=1, source_target_pairs={{0,2},{2,0},{4,6},{6,4},{8,10},{10,8},{12,14},{14,12},{1,3},{3,1},... | collective-permute-start | bytes 823304 | tf_op jit(solution)/shard_map/ppermute | solution.py:21
  61.6 0.4 join_packed.2.refs_7_
  61.9 1.2 %collective-permute-start.15 = (bf16[1,1072,128]{2,1,0:T(8,128)(2,1)S(1)}, bf16[1,1072,128]{2,1,0:T(8,128)(2,1)S(1)}, u32[]{:S(2)}, u32[]{:S(2)}) collective-permute-start(bf16[1,1072,128]{2,1,0:T(8,128)(2,1)S(1)} %join_packed.2.refs_7_), channel_id=1, source_target_pairs={{0,8},{2,10},{4,12},{6,14},{8,0},{10,2},{12,4},{14,6},{1,9},{3,11}... | collective-permute-start | bytes 823304 | tf_op jit(solution)/shard_map/ppermute | solution.py:21
  63.1 4.5 %attend.10 = (f32[1,1024,128]{2,1,0:T(8,128)S(1)}, f32[1,16,128]{2,1,0:T(8,128)S(1)}, bf16[1,1072,128]{2,1,0:T(8,128)(2,1)S(1)}) custom-call(s32[1]{0:T(128)} %bitcast.owner_ref, s32[2,2]{1,0:T(2,128)S(1)} %select_reduce_fusion.seen_ref, s32[8]{0:T(128)S(1)} %copy-done.3, bf16[1,1024,128]{2,1,0:T(8,128)(2,1)S(1)} %get-tuple-element.60.refs_0_, ...), custom_call_target="tpu_custom_call" | custom-call | flops 1073741824 | bytes 524288 | tf_op jit(solution)/shard_map/attend/pallas_call | solution.py:336
  67.6 0.6 collective-permute-start.14
  68.2 0.0 collective-permute-done.9.refs_0_
  68.2 0.4 join_packed.3.refs_7_
  68.5 6.1 %collective-permute-done.1.refs_2_ = bf16[1,8,2,128,128]{4,3,2,1,0:T(8,128)(2,1)S(1)} collective-permute-done((bf16[1,8,2,128,128]{4,3,2,1,0:T(8,128)(2,1)S(1)}, bf16[1,8,2,128,128]{4,3,2,1,0:T(8,128)(2,1)S(1)}, u32[]{:S(2)}, u32[]{:S(2)}) %collective-permute-start.1) | collective-permute-done | bytes 524320 | tf_op jit(solution)/shard_map/ppermute | solution.py:21
  74.6 4.3 %attend.11 = (f32[1,1024,128]{2,1,0:T(8,128)S(1)}, f32[1,16,128]{2,1,0:T(8,128)S(1)}, bf16[1,1072,128]{2,1,0:T(8,128)(2,1)S(1)}) custom-call(s32[1]{0:T(128)} %bitcast.owner_ref, s32[2,2]{1,0:T(2,128)S(1)} %select_reduce_fusion.seen_ref, s32[8]{0:T(128)S(1)} %copy-done.3, bf16[1,1024,128]{2,1,0:T(8,128)(2,1)S(1)} %get-tuple-element.61.refs_0_, ...), custom_call_target="tpu_custom_call" | custom-call | flops 1073741824 | bytes 524288 | tf_op jit(solution)/shard_map/attend/pallas_call | solution.py:336
  78.9 1.6 %collective-permute-start.12 = (bf16[1,1072,128]{2,1,0:T(8,128)(2,1)S(1)}, bf16[1,1072,128]{2,1,0:T(8,128)(2,1)S(1)}, u32[]{:S(2)}, u32[]{:S(2)}) collective-permute-start(bf16[1,1072,128]{2,1,0:T(8,128)(2,1)S(1)} %get-tuple-element.56), channel_id=1, source_target_pairs={{0,2},{2,0},{4,6},{6,4},{8,10},{10,8},{12,14},{14,12},{1,3},{3,1},... | collective-permute-start | bytes 823304 | tf_op jit(solution)/shard_map/ppermute | solution.py:21
  80.5 2.8 %collective-permute-start.13 = (bf16[1,1072,128]{2,1,0:T(8,128)(2,1)S(1)}, bf16[1,1072,128]{2,1,0:T(8,128)(2,1)S(1)}, u32[]{:S(2)}, u32[]{:S(2)}) collective-permute-start(bf16[1,1072,128]{2,1,0:T(8,128)(2,1)S(1)} %join_packed.3.refs_7_), channel_id=1, source_target_pairs={{0,8},{2,10},{4,12},{6,14},{8,0},{10,2},{12,4},{14,6},{1,9},{3,11}... | collective-permute-start | bytes 823304 | tf_op jit(solution)/shard_map/ppermute | solution.py:21
  83.3 1.2 %join_out.2.refs_2_ = bf16[128,16,128]{2,1,0:T(8,128)(2,1)} custom-call(f32[1,1024,128]{2,1,0:T(8,128)S(1)} %get-tuple-element.57.own_mixed, f32[1,16,128]{2,1,0:T(8,128)S(1)} %get-tuple-element.53.refs_1_.own_table, bf16[1,1072,128]{2,1,0:T(8,128)(2,1)S(1)} %collective-permute-done.14.refs_0_, bf16[1,1072,128]{2,1,0:T(8,128)(2,1)S(1)} %collective-permute-done.15.refs_1_), custom_call_target="tpu_custom_call" | custom-call | tf_op jit(solution)/shard_map/join_out/pallas_call | solution.py:431
  84.5 1.0 %collective-permute-done.12.refs_0_ = bf16[1,1072,128]{2,1,0:T(8,128)(2,1)S(1)} collective-permute-done((bf16[1,1072,128]{2,1,0:T(8,128)(2,1)S(1)}, bf16[1,1072,128]{2,1,0:T(8,128)(2,1)S(1)}, u32[]{:S(2)}, u32[]{:S(2)}) %collective-permute-start.12) | collective-permute-done | bytes 274464 | tf_op jit(solution)/shard_map/ppermute | solution.py:21
  85.5 6.9 %collective-permute-done.13.refs_1_ = bf16[1,1072,128]{2,1,0:T(8,128)(2,1)S(1)} collective-permute-done((bf16[1,1072,128]{2,1,0:T(8,128)(2,1)S(1)}, bf16[1,1072,128]{2,1,0:T(8,128)(2,1)S(1)}, u32[]{:S(2)}, u32[]{:S(2)}) %collective-permute-start.13) | collective-permute-done | bytes 274464 | tf_op jit(solution)/shard_map/ppermute | solution.py:21
  92.4 1.2 %join_out.3 = bf16[128,16,128]{2,1,0:T(8,128)(2,1)} custom-call(f32[1,1024,128]{2,1,0:T(8,128)S(1)} %get-tuple-element.54.own_mixed, f32[1,16,128]{2,1,0:T(8,128)S(1)} %get-tuple-element.55.own_table, bf16[1,1072,128]{2,1,0:T(8,128)(2,1)S(1)} %collective-permute-done.12.refs_0_, ...), custom_call_target="tpu_custom_call", output_to_operand_aliasing={{}: (4, {})} | custom-call | tf_op jit(solution)/shard_map/join_out/pallas_call | solution.py:431
  (27 shorter events, 0.1 us)
Async XLA Ops:
  0.6 13.1 %copy-start.2 = (s32[4,64]{1,0:T(4,128)S(1)}, s32[4,64]{1,0:T(4,128)}, u32[]{:S(2)}) copy-start(s32[4,64]{1,0:T(4,128)} %table_ref.3) | copy-start | bytes 3076
  0.6 13.2 %copy-start.8 = (s32[4]{0:T(128)S(1)}, s32[4]{0:T(128)}, u32[]{:S(2)}) copy-start(s32[4]{0:T(128)} %param.10) | copy-start | bytes 52
  1.7 12.3 %collective-permute-start.2 = (bf16[1,1024,128]{2,1,0:T(8,128)(2,1)S(1)}, bf16[1,1024,128]{2,1,0:T(8,128)(2,1)S(1)}, u32[]{:S(2)}, u32[]{:S(2)}) collective-permute-start(bf16[1,1024,128]{2,1,0:T(8,128)(2,1)S(1)} %get-tuple-element.60.refs_0_), channel_id=1, source_target_pairs={{0,2},{2,0},{4,6},{6,4},{8,10},{10,8},{12,14},{14,12},{1,3},{3,1},... | collective-permute-start | bytes 786440 | tf_op jit(solution)/shard_map/ppermute | solution.py:21
  4.8 21.1 %collective-permute-start.6 = (bf16[1,1024,128]{2,1,0:T(8,128)(2,1)S(1)}, bf16[1,1024,128]{2,1,0:T(8,128)(2,1)S(1)}, u32[]{:S(2)}, u32[]{:S(2)}) collective-permute-start(bf16[1,1024,128]{2,1,0:T(8,128)(2,1)S(1)} %get-tuple-element.60.refs_0_), channel_id=1, source_target_pairs={{0,8},{2,10},{4,12},{6,14},{8,0},{10,2},{12,4},{14,6},{1,9},{3,11}... | collective-permute-start | bytes 786440 | tf_op jit(solution)/shard_map/ppermute | solution.py:21
  7.4 30.0 %collective-permute-start = (bf16[1,1024,128]{2,1,0:T(8,128)(2,1)S(1)}, bf16[1,1024,128]{2,1,0:T(8,128)(2,1)S(1)}, u32[]{:S(2)}, u32[]{:S(2)}) collective-permute-start(bf16[1,1024,128]{2,1,0:T(8,128)(2,1)S(1)} %get-tuple-element.61.refs_0_), channel_id=1, source_target_pairs={{0,2},{2,0},{4,6},{6,4},{8,10},{10,8},{12,14},{14,12},{1,3},{3,1},... | collective-permute-start | bytes 786440 | tf_op jit(solution)/shard_map/ppermute | solution.py:21
  7.9 29.6 %collective-permute-start.3 = (bf16[1,1024,128]{2,1,0:T(8,128)(2,1)S(1)}, bf16[1,1024,128]{2,1,0:T(8,128)(2,1)S(1)}, u32[]{:S(2)}, u32[]{:S(2)}) collective-permute-start(bf16[1,1024,128]{2,1,0:T(8,128)(2,1)S(1)} %get-tuple-element.61.refs_0_), channel_id=1, source_target_pairs={{0,8},{2,10},{4,12},{6,14},{8,0},{10,2},{12,4},{14,6},{1,9},{3,11}... | collective-permute-start | bytes 786440 | tf_op jit(solution)/shard_map/ppermute | solution.py:21
  7.9 0.7 copy-start.1
  8.6 22.8 %copy-start.7 = (bf16[128,2,2,128]{3,2,1,0:T(2,128)(2,1)S(1)}, bf16[128,2,2,128]{3,2,1,0:T(2,128)(2,1)}, u32[]{:S(2)}) copy-start(bf16[128,2,2,128]{3,2,1,0:T(2,128)(2,1)} %param.7) | copy-start | bytes 393220
  8.6 22.8 %copy-start.3 = (s32[8]{0:T(128)S(1)}, s32[8]{0:T(128)}, u32[]{:S(2)}) copy-start(s32[8]{0:T(128)} %fresh_ref.11) | copy-start | bytes 100
  11.8 32.2 %collective-permute-start.8 = (bf16[1,8,2,128,128]{4,3,2,1,0:T(8,128)(2,1)}, bf16[1,8,2,128,128]{4,3,2,1,0:T(8,128)(2,1)S(1)}, u32[]{:S(2)}, u32[]{:S(2)}) collective-permute-start(bf16[1,8,2,128,128]{4,3,2,1,0:T(8,128)(2,1)} %get-tuple-element.42), channel_id=1, source_target_pairs={{0,4},{2,6},{4,0},{6,2},{8,12},{10,14},{12,8},{14,10},{1,5},{3,7},... | collective-permute-start | bytes 1572872 | tf_op jit(solution)/shard_map/ppermute | solution.py:21
  14.0 39.2 %collective-permute-start.5 = (bf16[1,8,2,128,128]{4,3,2,1,0:T(8,128)(2,1)}, bf16[1,8,2,128,128]{4,3,2,1,0:T(8,128)(2,1)S(1)}, u32[]{:S(2)}, u32[]{:S(2)}) collective-permute-start(bf16[1,8,2,128,128]{4,3,2,1,0:T(8,128)(2,1)} %get-tuple-element.40), channel_id=1, source_target_pairs={{0,4},{2,6},{4,0},{6,2},{8,12},{10,14},{12,8},{14,10},{1,5},{3,7},... | collective-permute-start | bytes 1572872 | tf_op jit(solution)/shard_map/ppermute | solution.py:21
  25.9 20.1 %collective-permute-start.7 = (bf16[1,1024,128]{2,1,0:T(8,128)(2,1)S(1)}, bf16[1,1024,128]{2,1,0:T(8,128)(2,1)S(1)}, u32[]{:S(2)}, u32[]{:S(2)}) collective-permute-start(bf16[1,1024,128]{2,1,0:T(8,128)(2,1)S(1)} %collective-permute-done.6.refs_0_), channel_id=1, source_target_pairs={{0,2},{2,0},{4,6},{6,4},{8,10},{10,8},{12,14},{14,12},{1,3},{3,1},... | collective-permute-start | bytes 786440 | tf_op jit(solution)/shard_map/ppermute | solution.py:21
  31.4 1.0 %copy-start = (bf16[1,8,2,128,128]{4,3,2,1,0:T(8,128)(2,1)S(1)}, bf16[1,8,2,128,128]{4,3,2,1,0:T(8,128)(2,1)}, u32[]{:S(2)}) copy-start(bf16[1,8,2,128,128]{4,3,2,1,0:T(8,128)(2,1)} %get-tuple-element.33.refs_2_) | copy-start | bytes 1572868
  32.4 5.0 %copy-start.10 = (bf16[1,8,2,128,128]{4,3,2,1,0:T(8,128)(2,1)S(1)}, bf16[1,8,2,128,128]{4,3,2,1,0:T(8,128)(2,1)}, u32[]{:S(2)}) copy-start(bf16[1,8,2,128,128]{4,3,2,1,0:T(8,128)(2,1)} %get-tuple-element.47) | copy-start | bytes 1572868
  32.4 6.7 %copy-start.6 = (bf16[1,8,2,128,128]{4,3,2,1,0:T(8,128)(2,1)S(1)}, bf16[1,8,2,128,128]{4,3,2,1,0:T(8,128)(2,1)}, u32[]{:S(2)}) copy-start(bf16[1,8,2,128,128]{4,3,2,1,0:T(8,128)(2,1)} %get-tuple-element.32.refs_2_) | copy-start | bytes 1572868
  32.4 11.5 %copy-start.9 = (bf16[1,8,2,128,128]{4,3,2,1,0:T(8,128)(2,1)S(1)}, bf16[1,8,2,128,128]{4,3,2,1,0:T(8,128)(2,1)}, u32[]{:S(2)}) copy-start(bf16[1,8,2,128,128]{4,3,2,1,0:T(8,128)(2,1)} %get-tuple-element.31) | copy-start | bytes 1572868
  32.4 13.6 %copy-start.5 = (bf16[1,8,2,128,128]{4,3,2,1,0:T(8,128)(2,1)S(1)}, bf16[1,8,2,128,128]{4,3,2,1,0:T(8,128)(2,1)}, u32[]{:S(2)}) copy-start(bf16[1,8,2,128,128]{4,3,2,1,0:T(8,128)(2,1)} %get-tuple-element.41.refs_2_) | copy-start | bytes 1572868
  37.4 25.7 %collective-permute-start.10 = (bf16[1,8,2,128,128]{4,3,2,1,0:T(8,128)(2,1)S(1)}, bf16[1,8,2,128,128]{4,3,2,1,0:T(8,128)(2,1)S(1)}, u32[]{:S(2)}, u32[]{:S(2)}) collective-permute-start(bf16[1,8,2,128,128]{4,3,2,1,0:T(8,128)(2,1)S(1)} %copy-done.10), channel_id=1, source_target_pairs={{0,4},{2,6},{4,0},{6,2},{8,12},{10,14},{12,8},{14,10},{1,5},{3,7},... | collective-permute-start | bytes 1572872 | tf_op jit(solution)/shard_map/ppermute | solution.py:21
  37.5 15.7 %collective-permute-start.4 = (bf16[1,1024,128]{2,1,0:T(8,128)(2,1)S(1)}, bf16[1,1024,128]{2,1,0:T(8,128)(2,1)S(1)}, u32[]{:S(2)}, u32[]{:S(2)}) collective-permute-start(bf16[1,1024,128]{2,1,0:T(8,128)(2,1)S(1)} %collective-permute-done.3.refs_0_), channel_id=1, source_target_pairs={{0,2},{2,0},{4,6},{6,4},{8,10},{10,8},{12,14},{14,12},{1,3},{3,1},... | collective-permute-start | bytes 786440 | tf_op jit(solution)/shard_map/ppermute | solution.py:21
  44.0 9.3 %copy-start.4 = (bf16[1,8,2,128,128]{4,3,2,1,0:T(8,128)(2,1)S(1)}, bf16[1,8,2,128,128]{4,3,2,1,0:T(8,128)(2,1)}, u32[]{:S(2)}) copy-start(bf16[1,8,2,128,128]{4,3,2,1,0:T(8,128)(2,1)} %get-tuple-element.39.refs_2_) | copy-start | bytes 1572868
  44.0 30.6 %collective-permute-start.1 = (bf16[1,8,2,128,128]{4,3,2,1,0:T(8,128)(2,1)S(1)}, bf16[1,8,2,128,128]{4,3,2,1,0:T(8,128)(2,1)S(1)}, u32[]{:S(2)}, u32[]{:S(2)}) collective-permute-start(bf16[1,8,2,128,128]{4,3,2,1,0:T(8,128)(2,1)S(1)} %copy-done.9), channel_id=1, source_target_pairs={{0,4},{2,6},{4,0},{6,2},{8,12},{10,14},{12,8},{14,10},{1,5},{3,7},... | collective-permute-start | bytes 1572872 | tf_op jit(solution)/shard_map/ppermute | solution.py:21
  52.7 8.9 %collective-permute-start.11 = (bf16[1,1072,128]{2,1,0:T(8,128)(2,1)S(1)}, bf16[1,1072,128]{2,1,0:T(8,128)(2,1)S(1)}, u32[]{:S(2)}, u32[]{:S(2)}) collective-permute-start(bf16[1,1072,128]{2,1,0:T(8,128)(2,1)S(1)} %get-tuple-element.52), channel_id=1, source_target_pairs={{0,2},{2,0},{4,6},{6,4},{8,10},{10,8},{12,14},{14,12},{1,3},{3,1},... | collective-permute-start | bytes 823304 | tf_op jit(solution)/shard_map/ppermute | solution.py:21
  59.9 8.2 %collective-permute-start.9 = (bf16[1,1072,128]{2,1,0:T(8,128)(2,1)S(1)}, bf16[1,1072,128]{2,1,0:T(8,128)(2,1)S(1)}, u32[]{:S(2)}, u32[]{:S(2)}) collective-permute-start(bf16[1,1072,128]{2,1,0:T(8,128)(2,1)S(1)} %get-tuple-element.46), channel_id=1, source_target_pairs={{0,2},{2,0},{4,6},{6,4},{8,10},{10,8},{12,14},{14,12},{1,3},{3,1},... | collective-permute-start | bytes 823304 | tf_op jit(solution)/shard_map/ppermute | solution.py:21
  61.9 21.4 %collective-permute-start.15 = (bf16[1,1072,128]{2,1,0:T(8,128)(2,1)S(1)}, bf16[1,1072,128]{2,1,0:T(8,128)(2,1)S(1)}, u32[]{:S(2)}, u32[]{:S(2)}) collective-permute-start(bf16[1,1072,128]{2,1,0:T(8,128)(2,1)S(1)} %join_packed.2.refs_7_), channel_id=1, source_target_pairs={{0,8},{2,10},{4,12},{6,14},{8,0},{10,2},{12,4},{14,6},{1,9},{3,11}... | collective-permute-start | bytes 823304 | tf_op jit(solution)/shard_map/ppermute | solution.py:21
  67.6 15.7 %collective-permute-start.14 = (bf16[1,1072,128]{2,1,0:T(8,128)(2,1)S(1)}, bf16[1,1072,128]{2,1,0:T(8,128)(2,1)S(1)}, u32[]{:S(2)}, u32[]{:S(2)}) collective-permute-start(bf16[1,1072,128]{2,1,0:T(8,128)(2,1)S(1)} %get-tuple-element.58), channel_id=1, source_target_pairs={{0,2},{2,0},{4,6},{6,4},{8,10},{10,8},{12,14},{14,12},{1,3},{3,1},... | collective-permute-start | bytes 823304 | tf_op jit(solution)/shard_map/ppermute | solution.py:21
  78.9 6.6 %collective-permute-start.12 = (bf16[1,1072,128]{2,1,0:T(8,128)(2,1)S(1)}, bf16[1,1072,128]{2,1,0:T(8,128)(2,1)S(1)}, u32[]{:S(2)}, u32[]{:S(2)}) collective-permute-start(bf16[1,1072,128]{2,1,0:T(8,128)(2,1)S(1)} %get-tuple-element.56), channel_id=1, source_target_pairs={{0,2},{2,0},{4,6},{6,4},{8,10},{10,8},{12,14},{14,12},{1,3},{3,1},... | collective-permute-start | bytes 823304 | tf_op jit(solution)/shard_map/ppermute | solution.py:21
  80.5 11.9 %collective-permute-start.13 = (bf16[1,1072,128]{2,1,0:T(8,128)(2,1)S(1)}, bf16[1,1072,128]{2,1,0:T(8,128)(2,1)S(1)}, u32[]{:S(2)}, u32[]{:S(2)}) collective-permute-start(bf16[1,1072,128]{2,1,0:T(8,128)(2,1)S(1)} %join_packed.3.refs_7_), channel_id=1, source_target_pairs={{0,8},{2,10},{4,12},{6,14},{8,0},{10,2},{12,4},{14,6},{1,9},{3,11}... | collective-permute-start | bytes 823304 | tf_op jit(solution)/shard_map/ppermute | solution.py:21

commit v2 on v1

--- a/solution.py
+++ b/solution.py
@@ -119,7 +119,7 @@
         ),
         compiler_params=pltpu.CompilerParams(vmem_limit_bytes=kernel_bytes),
         name="gather_pages",
-    )(owner, table, pltpu.with_memory_space_constraint(pool, pltpu.HBM))
+    )(owner, pltpu.with_memory_space_constraint(table, pltpu.HBM), pltpu.with_memory_space_constraint(pool, pltpu.HBM))
     return [outs[i * kv_heads : (i + 1) * kv_heads] for i in range(len(lists))]
 
 
@@ -531,20 +531,51 @@
         joined = join_packed(*far[k], scale, after=after)
         back.append(moved(joined, pairs))
         mine, mine_table, theirs, theirs_table = started[k]
-        results = attend(
-            scalars,
-            [(split[k], 0), (other[k], 0)],
-            [(a, 0) for a in got_near[k]],
-            [(0, i) for i in range(1, near)],
-            (False, True),
-            scale,
-            group,
-            1,
-            prev=[(mine, mine_table, 0), (theirs, theirs_table, 0)],
-            after=[joined],
-        )
-        ready.append((results[:2], moved(results[2], 1)))
-        after = [results[1]]
+        near_keys = [(a, 0) for a in got_near[k]]
+        near_at = [(0, i) for i in range(1, near)]
+        mine, theirs = (mine, mine_table, 0), (theirs, theirs_table, 0)
+        if k + 1 < kv_heads:
+            results = attend(
+                scalars,
+                [(split[k], 0), (other[k], 0)],
+                near_keys,
+                near_at,
+                (False, True),
+                scale,
+                group,
+                1,
+                prev=[mine, theirs],
+                after=[joined],
+            )
+            own_part = results[:2]
+            other_part = results[2]
+        else:
+            (other_part,) = attend(
+                scalars,
+                [(other[k], 0)],
+                near_keys,
+                near_at,
+                (True,),
+                scale,
+                group,
+                1,
+                prev=[theirs],
+                after=[joined],
+            )
+            own_part = attend(
+                scalars,
+                [(split[k], 0)],
+                near_keys,
+                near_at,
+                (False,),
+                scale,
+                group,
+                1,
+                prev=[mine],
+                after=[other_part],
+            )
+        ready.append((own_part, moved(other_part, 1)))
+        after = [own_part[1]]
     attended = None
     for k in each:
         own, received = ready[k]

time: 94 us -> 90.1 us (0.959)
  waiting for transfers between devices: 25.8 us -> 18.2 us
  starting transfers between devices: 20.6 us -> 24.3 us
    ppermute x16, waiting for transfers between devices: 25.8 us -> 18.2 us  [moved(): return lax.ppermute(array, 'pool', [(i, i ^ apart) for i in range(count)])]
    ppermute x16, starting transfers between devices: 20.6 us -> 24.3 us  [moved(): return lax.ppermute(array, 'pool', [(i, i ^ apart) for i in range(count)])]
    pallas_call x6 -> x7, Pallas kernels: 32 us -> 32.4 us  [attend(): pl.pallas_call(functools.partial(attend_body, halves=halves, seen_at=seen...]
  transfers between devices with their start and end apart: 16 -> 16, of which waited for: 4 -> 3; matrix products, arithmetic and copies ran while one was open for 1% -> 1% of each run, Pallas kernels for 45% -> 48%
where the time goes in v2:
time: 90.1 us; the launch traced here: 89.7 us
  Pallas kernels  43.8 us (49%)
  starting transfers between devices  24.3 us (27%)
  waiting for transfers between devices  18.2 us (20%)
  local copies, waits for them, and re-layouts  2.17 us (2%)
    pallas_call x7, Pallas kernels, attend(): pl.pallas_call(functools.partial(attend_body, halves=halves, seen_at=seen...  32.4 us
    ppermute x16, starting transfers between devices, moved(): return lax.ppermute(array, 'pool', [(i, i ^ apart) for i in range(count)])  24.3 us
    ppermute x16, waiting for transfers between devices, moved(): return lax.ppermute(array, 'pool', [(i, i ^ apart) for i in range(count)])  18.2 us
    pallas_call x2, Pallas kernels, gather_pages(): pl.pallas_call(functools.partial(gather_body, lists=lists, kv_heads=kv_he...  8.31 us
    pallas_call x2, Pallas kernels, join_out(): pl.pallas_call(functools.partial(join_body, scale=scale, packs=False, wai...  2.43 us
  transfers between devices with their start and end apart: 16, of which 3 were waited for; matrix products, arithmetic and copies ran while one was open for 1% of the time, Pallas kernels for 48%

profile of v2, /device:TPU:0, one launch (start us, length us, event | category | flops | bytes accessed | tf_op | source)
XLA Modules:
  0.0 89.7 jit_solution(18386951123480698458)
XLA Ops:
  0.6 0.0 copy-start.6
  0.7 1.1 %slice_bitcast_fusion = (bf16[1,1024,128]{2,1,0:T(8,128)(2,1)S(1)}, bf16[1,1024,128]{2,1,0:T(8,128)(2,1)S(1)}) fusion(bf16[128,16,128]{2,1,0:T(8,128)(2,1)} %param.6), kind=kLoop, calls=%fused_computation | loop fusion | bytes 1048576 | tf_op jit(solution)/shard_map/reshape | solution.py:471
  1.7 3.1 %collective-permute-start.2 = (bf16[1,1024,128]{2,1,0:T(8,128)(2,1)S(1)}, bf16[1,1024,128]{2,1,0:T(8,128)(2,1)S(1)}, u32[]{:S(2)}, u32[]{:S(2)}) collective-permute-start(bf16[1,1024,128]{2,1,0:T(8,128)(2,1)S(1)} %get-tuple-element.58.refs_0_), channel_id=1, source_target_pairs={{0,2},{2,0},{4,6},{6,4},{8,10},{10,8},{12,14},{14,12},{1,3},{3,1},... | collective-permute-start | bytes 786440 | tf_op jit(solution)/shard_map/ppermute | solution.py:21
  4.8 2.6 %collective-permute-start.6 = (bf16[1,1024,128]{2,1,0:T(8,128)(2,1)S(1)}, bf16[1,1024,128]{2,1,0:T(8,128)(2,1)S(1)}, u32[]{:S(2)}, u32[]{:S(2)}) collective-permute-start(bf16[1,1024,128]{2,1,0:T(8,128)(2,1)S(1)} %get-tuple-element.58.refs_0_), channel_id=1, source_target_pairs={{0,8},{2,10},{4,12},{6,14},{8,0},{10,2},{12,4},{14,6},{1,9},{3,11}... | collective-permute-start | bytes 786440 | tf_op jit(solution)/shard_map/ppermute | solution.py:21
  7.4 0.5 collective-permute-start.1
  7.9 0.0 collective-permute-start.3
  7.9 3.4 %gather_pages.3 = (bf16[1,8,2,128,128]{4,3,2,1,0:T(8,128)(2,1)}, bf16[1,8,2,128,128]{4,3,2,1,0:T(8,128)(2,1)}) custom-call(s32[1]{0:T(128)} %bitcast.owner_ref, s32[4,64]{1,0:T(4,128)} %table_ref.3, bf16[33,2,2,128,128]{4,3,2,1,0:T(8,128)(2,1)} %pool_ref.3), custom_call_target="tpu_custom_call" | custom-call | tf_op jit(solution)/shard_map/gather_pages/pallas_call | solution.py:105
  11.3 2.0 %collective-permute-start.8 = (bf16[1,8,2,128,128]{4,3,2,1,0:T(8,128)(2,1)}, bf16[1,8,2,128,128]{4,3,2,1,0:T(8,128)(2,1)S(1)}, u32[]{:S(2)}, u32[]{:S(2)}) collective-permute-start(bf16[1,8,2,128,128]{4,3,2,1,0:T(8,128)(2,1)} %get-tuple-element.41), channel_id=1, source_target_pairs={{0,4},{2,6},{4,0},{6,2},{8,12},{10,14},{12,8},{14,10},{1,5},{3,7},... | collective-permute-start | bytes 1572872 | tf_op jit(solution)/shard_map/ppermute | solution.py:21
  13.3 0.1 compare_and_fusion
  13.4 0.1 subtract_clamp_fusion
  13.5 0.1 iota_compare_fusion
  13.6 0.0 collective-permute-done.2.refs_1_
  13.6 0.5 collective-permute-start.5
  14.0 11.9 %collective-permute-done.6.refs_0_ = bf16[1,1024,128]{2,1,0:T(8,128)(2,1)S(1)} collective-permute-done((bf16[1,1024,128]{2,1,0:T(8,128)(2,1)S(1)}, bf16[1,1024,128]{2,1,0:T(8,128)(2,1)S(1)}, u32[]{:S(2)}, u32[]{:S(2)}) %collective-permute-start.6) | collective-permute-done | bytes 262176 | tf_op jit(solution)/shard_map/ppermute | solution.py:21
  25.9 0.5 collective-permute-start.7
  26.4 0.2 select_reduce_fusion.seen_ref
  26.6 4.9 %gather_pages.2 = (bf16[1,8,2,128,128]{4,3,2,1,0:T(8,128)(2,1)}, bf16[1,8,2,128,128]{4,3,2,1,0:T(8,128)(2,1)}, bf16[1,8,2,128,128]{4,3,2,1,0:T(8,128)(2,1)}, bf1...) custom-call(s32[1]{0:T(128)} %bitcast.owner_ref, ...), custom_call_target="tpu_custom_call" | custom-call | tf_op jit(solution)/shard_map/gather_pages/pallas_call | solution.py:105
  31.5 0.0 copy-start
  31.5 1.0 %copy-done = bf16[1,8,2,128,128]{4,3,2,1,0:T(8,128)(2,1)S(1)} copy-done((bf16[1,8,2,128,128]{4,3,2,1,0:T(8,128)(2,1)S(1)}, bf16[1,8,2,128,128]{4,3,2,1,0:T(8,128)(2,1)}, u32[]{:S(2)}) %copy-start) | copy-done | bytes 524312
  32.6 4.9 %attend.7 = (f32[1,1024,128]{2,1,0:T(8,128)S(1)}, f32[1,16,128]{2,1,0:T(8,128)S(1)}, f32[1,1024,128]{2,1,0:T(8,128)S(1)}, f32[1,16,128]{2,1,0:T(8,128)S(1)}, bf16[33,2,2,128,128]{4,3,2,1,0:T(8,128)(2,1)}) custom-call(s32[1]{0:T(128)} %bitcast.owner_ref, s32[2,2]{1,0:T(2,128)S(1)} %select_reduce_fusion.seen_ref, s32[8]{0:T(128)S(1)} %copy-done.1, ...), custom_call_target="tpu_custom_call" | custom-call | flops 1207959552 | bytes 589824 | tf_op jit(solution)/shard_map/attend/pallas_call | solution.py:336
  37.5 0.0 collective-permute-done.1.refs_1_.refs_0_
  37.5 0.1 collective-permute-start.10
  37.6 1.6 %collective-permute-start.4 = (bf16[1,1024,128]{2,1,0:T(8,128)(2,1)S(1)}, bf16[1,1024,128]{2,1,0:T(8,128)(2,1)S(1)}, u32[]{:S(2)}, u32[]{:S(2)}) collective-permute-start(bf16[1,1024,128]{2,1,0:T(8,128)(2,1)S(1)} %collective-permute-done.3.refs_0_), channel_id=1, source_target_pairs={{0,2},{2,0},{4,6},{6,4},{8,10},{10,8},{12,14},{14,12},{1,3},{3,1},... | collective-permute-start | bytes 786440 | tf_op jit(solution)/shard_map/ppermute | solution.py:21
  39.3 4.8 %attend.8 = (f32[1,1024,128]{2,1,0:T(8,128)S(1)}, f32[1,16,128]{2,1,0:T(8,128)S(1)}, f32[1,1024,128]{2,1,0:T(8,128)S(1)}, f32[1,16,128]{2,1,0:T(8,128)S(1)}) custom-call(s32[1]{0:T(128)} %bitcast.owner_ref, s32[2,2]{1,0:T(2,128)S(1)} %select_reduce_fusion.seen_ref, s32[8]{0:T(128)S(1)} %copy-done.1, bf16[1,1024,128]{2,1,0:T(8,128)(2,1)S(1)} %get-tuple-element.59.refs_0_, ...), custom_call_target="tpu_custom_call" | custom-call | flops 1207959552 | bytes 589824 | tf_op jit(solution)/shard_map/attend/pallas_call | solution.py:336
  44.0 0.0 collective-permute-done.8.refs_3_
  44.1 2.0 %collective-permute-start = (bf16[1,8,2,128,128]{4,3,2,1,0:T(8,128)(2,1)S(1)}, bf16[1,8,2,128,128]{4,3,2,1,0:T(8,128)(2,1)S(1)}, u32[]{:S(2)}, u32[]{:S(2)}) collective-permute-start(bf16[1,8,2,128,128]{4,3,2,1,0:T(8,128)(2,1)S(1)} %copy-done.8), channel_id=1, source_target_pairs={{0,4},{2,6},{4,0},{6,2},{8,12},{10,14},{12,8},{14,10},{1,5},{3,7},... | collective-permute-start | bytes 1572872 | tf_op jit(solution)/shard_map/ppermute | solution.py:21
  46.1 6.7 %attend.9 = (f32[1,1024,128]{2,1,0:T(8,128)S(1)}, f32[1,16,128]{2,1,0:T(8,128)S(1)}, bf16[1,1072,128]{2,1,0:T(8,128)(2,1)S(1)}) custom-call(s32[1]{0:T(128)} %bitcast.owner_ref, s32[2,2]{1,0:T(2,128)S(1)} %select_reduce_fusion.seen_ref, s32[8]{0:T(128)S(1)} %copy-done.1, bf16[1,1024,128]{2,1,0:T(8,128)(2,1)S(1)} %collective-permute-done.6.refs_0_, ...), custom_call_target="tpu_custom_call" | custom-call | flops 2147483648 | bytes 1048576 | tf_op jit(solution)/shard_map/attend/pallas_call | solution.py:336
  52.8 0.5 collective-permute-start.11
  53.3 0.0 collective-permute-done.5.refs_3_
  53.3 6.7 %attend.10 = (f32[1,1024,128]{2,1,0:T(8,128)S(1)}, f32[1,16,128]{2,1,0:T(8,128)S(1)}, bf16[1,1072,128]{2,1,0:T(8,128)(2,1)S(1)}) custom-call(s32[1]{0:T(128)} %bitcast.owner_ref, s32[2,2]{1,0:T(2,128)S(1)} %select_reduce_fusion.seen_ref, s32[8]{0:T(128)S(1)} %copy-done.1, bf16[1,1024,128]{2,1,0:T(8,128)(2,1)S(1)} %collective-permute-done.3.refs_0_, ...), custom_call_target="tpu_custom_call" | custom-call | flops 2147483648 | bytes 1048576 | tf_op jit(solution)/shard_map/attend/pallas_call | solution.py:336
  60.0 1.6 %collective-permute-start.9 = (bf16[1,1072,128]{2,1,0:T(8,128)(2,1)S(1)}, bf16[1,1072,128]{2,1,0:T(8,128)(2,1)S(1)}, u32[]{:S(2)}, u32[]{:S(2)}) collective-permute-start(bf16[1,1072,128]{2,1,0:T(8,128)(2,1)S(1)} %get-tuple-element.45), channel_id=1, source_target_pairs={{0,2},{2,0},{4,6},{6,4},{8,10},{10,8},{12,14},{14,12},{1,3},{3,1},... | collective-permute-start | bytes 823304 | tf_op jit(solution)/shard_map/ppermute | solution.py:21
  61.6 0.0 collective-permute-done.11.refs_0_
  61.6 0.4 join_packed.2.refs_7_
  62.0 1.2 %collective-permute-start.15 = (bf16[1,1072,128]{2,1,0:T(8,128)(2,1)S(1)}, bf16[1,1072,128]{2,1,0:T(8,128)(2,1)S(1)}, u32[]{:S(2)}, u32[]{:S(2)}) collective-permute-start(bf16[1,1072,128]{2,1,0:T(8,128)(2,1)S(1)} %join_packed.2.refs_7_), channel_id=1, source_target_pairs={{0,8},{2,10},{4,12},{6,14},{8,0},{10,2},{12,4},{14,6},{1,9},{3,11}... | collective-permute-start | bytes 823304 | tf_op jit(solution)/shard_map/ppermute | solution.py:21
  63.2 4.4 %attend.11 = (f32[1,1024,128]{2,1,0:T(8,128)S(1)}, f32[1,16,128]{2,1,0:T(8,128)S(1)}, bf16[1,1072,128]{2,1,0:T(8,128)(2,1)S(1)}) custom-call(s32[1]{0:T(128)} %bitcast.owner_ref, s32[2,2]{1,0:T(2,128)S(1)} %select_reduce_fusion.seen_ref, s32[8]{0:T(128)S(1)} %copy-done.1, bf16[1,1024,128]{2,1,0:T(8,128)(2,1)S(1)} %get-tuple-element.58.refs_0_, ...), custom_call_target="tpu_custom_call" | custom-call | flops 1073741824 | bytes 524288 | tf_op jit(solution)/shard_map/attend/pallas_call | solution.py:336
  67.6 0.6 collective-permute-start.14
  68.2 0.0 collective-permute-done.9.refs_0_
  68.2 0.4 join_packed.3.refs_4_
  68.5 2.4 %collective-permute-done.refs_1_ = bf16[1,8,2,128,128]{4,3,2,1,0:T(8,128)(2,1)S(1)} collective-permute-done((bf16[1,8,2,128,128]{4,3,2,1,0:T(8,128)(2,1)S(1)}, bf16[1,8,2,128,128]{4,3,2,1,0:T(8,128)(2,1)S(1)}, u32[]{:S(2)}, u32[]{:S(2)}) %collective-permute-start) | collective-permute-done | bytes 524320 | tf_op jit(solution)/shard_map/ppermute | solution.py:21
  70.9 2.5 %attend.12.refs_4_ = bf16[1,1072,128]{2,1,0:T(8,128)(2,1)S(1)} custom-call(s32[1]{0:T(128)} %bitcast.owner_ref, s32[2,2]{1,0:T(2,128)S(1)} %select_reduce_fusion.seen_ref, s32[8]{0:T(128)S(1)} %copy-done.1, bf16[1,1024,128]{2,1,0:T(8,128)(2,1)S(1)} %collective-permute-done.1.refs_1_.refs_0_, bf16[1,8,2,128,128]{4,3,2,1,0:T(8,128)(2,1)S(1)} %collective-permute-done.refs_1_, ...), custom_call_target="tpu_custom_call" | custom-call | flops 536870912 | bytes 524288 | tf_op jit(solution)/shard_map/attend/pallas_call | solution.py:336
  73.4 4.8 %collective-permute-start.12 = (bf16[1,1072,128]{2,1,0:T(8,128)(2,1)S(1)}, bf16[1,1072,128]{2,1,0:T(8,128)(2,1)S(1)}, u32[]{:S(2)}, u32[]{:S(2)}) collective-permute-start(bf16[1,1072,128]{2,1,0:T(8,128)(2,1)S(1)} %attend.12.refs_4_), channel_id=1, source_target_pairs={{0,2},{2,0},{4,6},{6,4},{8,10},{10,8},{12,14},{14,12},{1,3},{3,1},... | collective-permute-start | bytes 823304 | tf_op jit(solution)/shard_map/ppermute | solution.py:21
  78.2 2.8 %collective-permute-start.13 = (bf16[1,1072,128]{2,1,0:T(8,128)(2,1)S(1)}, bf16[1,1072,128]{2,1,0:T(8,128)(2,1)S(1)}, u32[]{:S(2)}, u32[]{:S(2)}) collective-permute-start(bf16[1,1072,128]{2,1,0:T(8,128)(2,1)S(1)} %join_packed.3.refs_4_), channel_id=1, source_target_pairs={{0,8},{2,10},{4,12},{6,14},{8,0},{10,2},{12,4},{14,6},{1,9},{3,11}... | collective-permute-start | bytes 823304 | tf_op jit(solution)/shard_map/ppermute | solution.py:21
  81.0 2.4 %attend.13 = (f32[1,1024,128]{2,1,0:T(8,128)S(1)}, f32[1,16,128]{2,1,0:T(8,128)S(1)}) custom-call(s32[1]{0:T(128)} %bitcast.owner_ref, s32[2,2]{1,0:T(2,128)S(1)} %select_reduce_fusion.seen_ref, s32[8]{0:T(128)S(1)} %copy-done.1, bf16[1,1024,128]{2,1,0:T(8,128)(2,1)S(1)} %get-tuple-element.59.refs_0_, ...), custom_call_target="tpu_custom_call" | custom-call | flops 536870912 | bytes 524288 | tf_op jit(solution)/shard_map/attend/pallas_call | solution.py:336
  83.4 0.0 collective-permute-done.14.refs_0_
  83.4 1.2 %join_out.2.refs_2_ = bf16[128,16,128]{2,1,0:T(8,128)(2,1)} custom-call(f32[1,1024,128]{2,1,0:T(8,128)S(1)} %get-tuple-element.55.own_mixed, f32[1,16,128]{2,1,0:T(8,128)S(1)} %get-tuple-element.52.refs_1_.own_table, bf16[1,1072,128]{2,1,0:T(8,128)(2,1)S(1)} %collective-permute-done.14.refs_0_, bf16[1,1072,128]{2,1,0:T(8,128)(2,1)S(1)} %collective-permute-done.15.refs_1_), custom_call_target="tpu_custom_call" | custom-call | tf_op jit(solution)/shard_map/join_out/pallas_call | solution.py:431
  84.6 0.0 collective-permute-done.12.refs_0_
  84.7 3.9 %collective-permute-done.13.refs_1_ = bf16[1,1072,128]{2,1,0:T(8,128)(2,1)S(1)} collective-permute-done((bf16[1,1072,128]{2,1,0:T(8,128)(2,1)S(1)}, bf16[1,1072,128]{2,1,0:T(8,128)(2,1)S(1)}, u32[]{:S(2)}, u32[]{:S(2)}) %collective-permute-start.13) | collective-permute-done | bytes 274464 | tf_op jit(solution)/shard_map/ppermute | solution.py:21
  88.5 1.2 %join_out.3 = bf16[128,16,128]{2,1,0:T(8,128)(2,1)} custom-call(f32[1,1024,128]{2,1,0:T(8,128)S(1)} %get-tuple-element.53.own_mixed, f32[1,16,128]{2,1,0:T(8,128)S(1)} %get-tuple-element.54.own_table, bf16[1,1072,128]{2,1,0:T(8,128)(2,1)S(1)} %collective-permute-done.12.refs_0_, ...), custom_call_target="tpu_custom_call", output_to_operand_aliasing={{}: (4, {})} | custom-call | tf_op jit(solution)/shard_map/join_out/pallas_call | solution.py:431
  (26 shorter events, 0.1 us)
Async XLA Ops:
  0.6 12.7 %copy-start.6 = (s32[4,64]{1,0:T(4,128)S(1)}, s32[4,64]{1,0:T(4,128)}, u32[]{:S(2)}) copy-start(s32[4,64]{1,0:T(4,128)} %table_ref.3) | copy-start | bytes 3076
  0.6 12.8 %copy-start.7 = (s32[4]{0:T(128)S(1)}, s32[4]{0:T(128)}, u32[]{:S(2)}) copy-start(s32[4]{0:T(128)} %param.10) | copy-start | bytes 52
  1.7 11.8 %collective-permute-start.2 = (bf16[1,1024,128]{2,1,0:T(8,128)(2,1)S(1)}, bf16[1,1024,128]{2,1,0:T(8,128)(2,1)S(1)}, u32[]{:S(2)}, u32[]{:S(2)}) collective-permute-start(bf16[1,1024,128]{2,1,0:T(8,128)(2,1)S(1)} %get-tuple-element.58.refs_0_), channel_id=1, source_target_pairs={{0,2},{2,0},{4,6},{6,4},{8,10},{10,8},{12,14},{14,12},{1,3},{3,1},... | collective-permute-start | bytes 786440 | tf_op jit(solution)/shard_map/ppermute | solution.py:21
  4.8 21.1 %collective-permute-start.6 = (bf16[1,1024,128]{2,1,0:T(8,128)(2,1)S(1)}, bf16[1,1024,128]{2,1,0:T(8,128)(2,1)S(1)}, u32[]{:S(2)}, u32[]{:S(2)}) collective-permute-start(bf16[1,1024,128]{2,1,0:T(8,128)(2,1)S(1)} %get-tuple-element.58.refs_0_), channel_id=1, source_target_pairs={{0,8},{2,10},{4,12},{6,14},{8,0},{10,2},{12,4},{14,6},{1,9},{3,11}... | collective-permute-start | bytes 786440 | tf_op jit(solution)/shard_map/ppermute | solution.py:21
  7.4 30.1 %collective-permute-start.1 = (bf16[1,1024,128]{2,1,0:T(8,128)(2,1)S(1)}, bf16[1,1024,128]{2,1,0:T(8,128)(2,1)S(1)}, u32[]{:S(2)}, u32[]{:S(2)}) collective-permute-start(bf16[1,1024,128]{2,1,0:T(8,128)(2,1)S(1)} %get-tuple-element.59.refs_0_), channel_id=1, source_target_pairs={{0,2},{2,0},{4,6},{6,4},{8,10},{10,8},{12,14},{14,12},{1,3},{3,1},... | collective-permute-start | bytes 786440 | tf_op jit(solution)/shard_map/ppermute | solution.py:21
  7.9 29.7 %collective-permute-start.3 = (bf16[1,1024,128]{2,1,0:T(8,128)(2,1)S(1)}, bf16[1,1024,128]{2,1,0:T(8,128)(2,1)S(1)}, u32[]{:S(2)}, u32[]{:S(2)}) collective-permute-start(bf16[1,1024,128]{2,1,0:T(8,128)(2,1)S(1)} %get-tuple-element.59.refs_0_), channel_id=1, source_target_pairs={{0,8},{2,10},{4,12},{6,14},{8,0},{10,2},{12,4},{14,6},{1,9},{3,11}... | collective-permute-start | bytes 786440 | tf_op jit(solution)/shard_map/ppermute | solution.py:21
  7.9 23.6 %copy-start.5 = (bf16[128,2,2,128]{3,2,1,0:T(2,128)(2,1)S(1)}, bf16[128,2,2,128]{3,2,1,0:T(2,128)(2,1)}, u32[]{:S(2)}) copy-start(bf16[128,2,2,128]{3,2,1,0:T(2,128)(2,1)} %param.7) | copy-start | bytes 393220
  7.9 23.6 %copy-start.1 = (s32[8]{0:T(128)S(1)}, s32[8]{0:T(128)}, u32[]{:S(2)}) copy-start(s32[8]{0:T(128)} %fresh_ref.13) | copy-start | bytes 100
  11.3 32.7 %collective-permute-start.8 = (bf16[1,8,2,128,128]{4,3,2,1,0:T(8,128)(2,1)}, bf16[1,8,2,128,128]{4,3,2,1,0:T(8,128)(2,1)S(1)}, u32[]{:S(2)}, u32[]{:S(2)}) collective-permute-start(bf16[1,8,2,128,128]{4,3,2,1,0:T(8,128)(2,1)} %get-tuple-element.41), channel_id=1, source_target_pairs={{0,4},{2,6},{4,0},{6,2},{8,12},{10,14},{12,8},{14,10},{1,5},{3,7},... | collective-permute-start | bytes 1572872 | tf_op jit(solution)/shard_map/ppermute | solution.py:21
  13.6 39.7 %collective-permute-start.5 = (bf16[1,8,2,128,128]{4,3,2,1,0:T(8,128)(2,1)}, bf16[1,8,2,128,128]{4,3,2,1,0:T(8,128)(2,1)S(1)}, u32[]{:S(2)}, u32[]{:S(2)}) collective-permute-start(bf16[1,8,2,128,128]{4,3,2,1,0:T(8,128)(2,1)} %get-tuple-element.39), channel_id=1, source_target_pairs={{0,4},{2,6},{4,0},{6,2},{8,12},{10,14},{12,8},{14,10},{1,5},{3,7},... | collective-permute-start | bytes 1572872 | tf_op jit(solution)/shard_map/ppermute | solution.py:21
  25.9 20.2 %collective-permute-start.7 = (bf16[1,1024,128]{2,1,0:T(8,128)(2,1)S(1)}, bf16[1,1024,128]{2,1,0:T(8,128)(2,1)S(1)}, u32[]{:S(2)}, u32[]{:S(2)}) collective-permute-start(bf16[1,1024,128]{2,1,0:T(8,128)(2,1)S(1)} %collective-permute-done.6.refs_0_), channel_id=1, source_target_pairs={{0,2},{2,0},{4,6},{6,4},{8,10},{10,8},{12,14},{14,12},{1,3},{3,1},... | collective-permute-start | bytes 786440 | tf_op jit(solution)/shard_map/ppermute | solution.py:21
  31.5 1.0 %copy-start = (bf16[1,8,2,128,128]{4,3,2,1,0:T(8,128)(2,1)S(1)}, bf16[1,8,2,128,128]{4,3,2,1,0:T(8,128)(2,1)}, u32[]{:S(2)}) copy-start(bf16[1,8,2,128,128]{4,3,2,1,0:T(8,128)(2,1)} %get-tuple-element.32.refs_2_) | copy-start | bytes 1572868
  32.6 5.0 %copy-start.9 = (bf16[1,8,2,128,128]{4,3,2,1,0:T(8,128)(2,1)S(1)}, bf16[1,8,2,128,128]{4,3,2,1,0:T(8,128)(2,1)}, u32[]{:S(2)}) copy-start(bf16[1,8,2,128,128]{4,3,2,1,0:T(8,128)(2,1)} %get-tuple-element.46) | copy-start | bytes 1572868
  32.6 6.7 %copy-start.4 = (bf16[1,8,2,128,128]{4,3,2,1,0:T(8,128)(2,1)S(1)}, bf16[1,8,2,128,128]{4,3,2,1,0:T(8,128)(2,1)}, u32[]{:S(2)}) copy-start(bf16[1,8,2,128,128]{4,3,2,1,0:T(8,128)(2,1)} %get-tuple-element.31.refs_2_) | copy-start | bytes 1572868
  32.6 11.5 %copy-start.8 = (bf16[1,8,2,128,128]{4,3,2,1,0:T(8,128)(2,1)S(1)}, bf16[1,8,2,128,128]{4,3,2,1,0:T(8,128)(2,1)}, u32[]{:S(2)}) copy-start(bf16[1,8,2,128,128]{4,3,2,1,0:T(8,128)(2,1)} %get-tuple-element.30) | copy-start | bytes 1572868
  32.6 13.5 %copy-start.3 = (bf16[1,8,2,128,128]{4,3,2,1,0:T(8,128)(2,1)S(1)}, bf16[1,8,2,128,128]{4,3,2,1,0:T(8,128)(2,1)}, u32[]{:S(2)}) copy-start(bf16[1,8,2,128,128]{4,3,2,1,0:T(8,128)(2,1)} %get-tuple-element.40.refs_2_) | copy-start | bytes 1572868
  37.5 25.6 %collective-permute-start.10 = (bf16[1,8,2,128,128]{4,3,2,1,0:T(8,128)(2,1)S(1)}, bf16[1,8,2,128,128]{4,3,2,1,0:T(8,128)(2,1)S(1)}, u32[]{:S(2)}, u32[]{:S(2)}) collective-permute-start(bf16[1,8,2,128,128]{4,3,2,1,0:T(8,128)(2,1)S(1)} %copy-done.9), channel_id=1, source_target_pairs={{0,4},{2,6},{4,0},{6,2},{8,12},{10,14},{12,8},{14,10},{1,5},{3,7},... | collective-permute-start | bytes 1572872 | tf_op jit(solution)/shard_map/ppermute | solution.py:21
  37.6 15.7 %collective-permute-start.4 = (bf16[1,1024,128]{2,1,0:T(8,128)(2,1)S(1)}, bf16[1,1024,128]{2,1,0:T(8,128)(2,1)S(1)}, u32[]{:S(2)}, u32[]{:S(2)}) collective-permute-start(bf16[1,1024,128]{2,1,0:T(8,128)(2,1)S(1)} %collective-permute-done.3.refs_0_), channel_id=1, source_target_pairs={{0,2},{2,0},{4,6},{6,4},{8,10},{10,8},{12,14},{14,12},{1,3},{3,1},... | collective-permute-start | bytes 786440 | tf_op jit(solution)/shard_map/ppermute | solution.py:21
  44.0 9.3 %copy-start.2 = (bf16[1,8,2,128,128]{4,3,2,1,0:T(8,128)(2,1)S(1)}, bf16[1,8,2,128,128]{4,3,2,1,0:T(8,128)(2,1)}, u32[]{:S(2)}) copy-start(bf16[1,8,2,128,128]{4,3,2,1,0:T(8,128)(2,1)} %get-tuple-element.38.refs_2_) | copy-start | bytes 1572868
  44.1 26.9 %collective-permute-start = (bf16[1,8,2,128,128]{4,3,2,1,0:T(8,128)(2,1)S(1)}, bf16[1,8,2,128,128]{4,3,2,1,0:T(8,128)(2,1)S(1)}, u32[]{:S(2)}, u32[]{:S(2)}) collective-permute-start(bf16[1,8,2,128,128]{4,3,2,1,0:T(8,128)(2,1)S(1)} %copy-done.8), channel_id=1, source_target_pairs={{0,4},{2,6},{4,0},{6,2},{8,12},{10,14},{12,8},{14,10},{1,5},{3,7},... | collective-permute-start | bytes 1572872 | tf_op jit(solution)/shard_map/ppermute | solution.py:21
  52.8 8.9 %collective-permute-start.11 = (bf16[1,1072,128]{2,1,0:T(8,128)(2,1)S(1)}, bf16[1,1072,128]{2,1,0:T(8,128)(2,1)S(1)}, u32[]{:S(2)}, u32[]{:S(2)}) collective-permute-start(bf16[1,1072,128]{2,1,0:T(8,128)(2,1)S(1)} %get-tuple-element.51), channel_id=1, source_target_pairs={{0,2},{2,0},{4,6},{6,4},{8,10},{10,8},{12,14},{14,12},{1,3},{3,1},... | collective-permute-start | bytes 823304 | tf_op jit(solution)/shard_map/ppermute | solution.py:21
  60.0 8.2 %collective-permute-start.9 = (bf16[1,1072,128]{2,1,0:T(8,128)(2,1)S(1)}, bf16[1,1072,128]{2,1,0:T(8,128)(2,1)S(1)}, u32[]{:S(2)}, u32[]{:S(2)}) collective-permute-start(bf16[1,1072,128]{2,1,0:T(8,128)(2,1)S(1)} %get-tuple-element.45), channel_id=1, source_target_pairs={{0,2},{2,0},{4,6},{6,4},{8,10},{10,8},{12,14},{14,12},{1,3},{3,1},... | collective-permute-start | bytes 823304 | tf_op jit(solution)/shard_map/ppermute | solution.py:21
  62.0 21.4 %collective-permute-start.15 = (bf16[1,1072,128]{2,1,0:T(8,128)(2,1)S(1)}, bf16[1,1072,128]{2,1,0:T(8,128)(2,1)S(1)}, u32[]{:S(2)}, u32[]{:S(2)}) collective-permute-start(bf16[1,1072,128]{2,1,0:T(8,128)(2,1)S(1)} %join_packed.2.refs_7_), channel_id=1, source_target_pairs={{0,8},{2,10},{4,12},{6,14},{8,0},{10,2},{12,4},{14,6},{1,9},{3,11}... | collective-permute-start | bytes 823304 | tf_op jit(solution)/shard_map/ppermute | solution.py:21
  67.6 15.8 %collective-permute-start.14 = (bf16[1,1072,128]{2,1,0:T(8,128)(2,1)S(1)}, bf16[1,1072,128]{2,1,0:T(8,128)(2,1)S(1)}, u32[]{:S(2)}, u32[]{:S(2)}) collective-permute-start(bf16[1,1072,128]{2,1,0:T(8,128)(2,1)S(1)} %get-tuple-element.56), channel_id=1, source_target_pairs={{0,2},{2,0},{4,6},{6,4},{8,10},{10,8},{12,14},{14,12},{1,3},{3,1},... | collective-permute-start | bytes 823304 | tf_op jit(solution)/shard_map/ppermute | solution.py:21
  73.4 11.3 %collective-permute-start.12 = (bf16[1,1072,128]{2,1,0:T(8,128)(2,1)S(1)}, bf16[1,1072,128]{2,1,0:T(8,128)(2,1)S(1)}, u32[]{:S(2)}, u32[]{:S(2)}) collective-permute-start(bf16[1,1072,128]{2,1,0:T(8,128)(2,1)S(1)} %attend.12.refs_4_), channel_id=1, source_target_pairs={{0,2},{2,0},{4,6},{6,4},{8,10},{10,8},{12,14},{14,12},{1,3},{3,1},... | collective-permute-start | bytes 823304 | tf_op jit(solution)/shard_map/ppermute | solution.py:21
  78.2 10.3 %collective-permute-start.13 = (bf16[1,1072,128]{2,1,0:T(8,128)(2,1)S(1)}, bf16[1,1072,128]{2,1,0:T(8,128)(2,1)S(1)}, u32[]{:S(2)}, u32[]{:S(2)}) collective-permute-start(bf16[1,1072,128]{2,1,0:T(8,128)(2,1)S(1)} %join_packed.3.refs_4_), channel_id=1, source_target_pairs={{0,8},{2,10},{4,12},{6,14},{8,0},{10,2},{12,4},{14,6},{1,9},{3,11}... | collective-permute-start | bytes 823304 | tf_op jit(solution)/shard_map/ppermute | solution.py:21

commit v3 on v2

--- a/solution.py
+++ b/solution.py
@@ -55,9 +55,10 @@
     return parts[0] + parts[1] + parts[2]
 
 
-def gather_body(owner_ref, table_ref, pool_ref, *refs, lists, kv_heads, cap):
-    outs = refs[:-4]
-    staged, slots, sem_in, sem_out = refs[-4:]
+def gather_body(owner_ref, table_ref, pool_ref, *refs, lists, resident, kv_heads, cap):
+    outs = refs[: len(lists) * kv_heads]
+    staged = refs[len(lists) * kv_heads] if resident < len(lists) else None
+    slots, sem, sem_out = refs[-3:]
     owner = owner_ref[0]
     pair = owner >> 1
     slot_count = pool_ref.shape[0]
@@ -73,24 +74,26 @@
             following.append(found[at] + held.astype(jnp.int32))
         return tuple(following)
 
-    found = lax.fori_loop(0, width, look, (jnp.int32(0),) * len(lists), unroll=4)
-    arriving = []
-    for at in range(len(lists)):
+    found = lax.fori_loop(0, width, look, (jnp.int32(0),) * len(lists), unroll=16)
+    arriving = {}
+    for at in reversed(range(len(lists))):
         for k in range(kv_heads):
+            out = outs[at * kv_heads + k].at[0] if at < resident else staged.at[at - resident, k]
+            arriving[at, k] = []
             for i in range(cap):
                 slot = jnp.where(i < found[at], slots[at * (cap + 1) + i], 0)
                 copy = pltpu.make_async_copy(
-                    pool_ref.at[slot, :, k], staged.at[at, k, i], sem_in.at[at, k, i]
+                    pool_ref.at[slot, :, k], out.at[i], sem.at[at, k, i]
                 )
                 copy.start()
-                arriving.append(copy)
+                arriving[at, k].append(copy)
     leaving = []
-    for at in range(len(lists)):
-        for k in range(kv_heads):
-            for i in range(cap):
-                arriving[(at * kv_heads + k) * cap + i].wait()
+    for (at, k), copies in arriving.items():
+        for copy in copies:
+            copy.wait()
+        if at >= resident:
             copy = pltpu.make_async_copy(
-                staged.at[at, k], outs[at * kv_heads + k].at[0], sem_out.at[at, k]
+                staged.at[at - resident, k], outs[at * kv_heads + k].at[0], sem_out.at[at, k]
             )
             copy.start()
             leaving.append(copy)
@@ -98,20 +101,30 @@
         copy.wait()
 
 
-def gather_pages(owner, table, pool, lists, cap):
+def gather_pages(owner, table, pool, lists, resident, cap):
     _, pair_of, kv_heads, page_len, head_dim = pool.shape
-    shape = pltpu.HBM((1, cap, pair_of, page_len, head_dim), pool.dtype)
-    count = len(lists) * kv_heads
-    outs = pl.pallas_call(
-        functools.partial(gather_body, lists=lists, kv_heads=kv_heads, cap=cap),
-        out_shape=[shape] * count,
+    outs = []
+    specs = []
+    for at in range(len(lists)):
+        space = pltpu.VMEM if at < resident else pltpu.HBM
+        outs += [space((1, cap, pair_of, page_len, head_dim), pool.dtype)] * kv_heads
+        specs += [pl.BlockSpec(memory_space=space)] * kv_heads
+    scratch = []
+    if resident < len(lists):
+        size = (len(lists) - resident, kv_heads, cap, pair_of, page_len, head_dim)
+        scratch.append(pltpu.VMEM(size, pool.dtype))
+    pages = pl.pallas_call(
+        functools.partial(
+            gather_body, lists=lists, resident=resident, kv_heads=kv_heads, cap=cap
+        ),
+        out_shape=outs,
         grid_spec=pltpu.PrefetchScalarGridSpec(
             num_scalar_prefetch=2,
             grid=(1,),
             in_specs=[pl.BlockSpec(memory_space=pltpu.HBM)],
-            out_specs=[pl.BlockSpec(memory_space=pltpu.HBM)] * count,
-            scratch_shapes=[
-                pltpu.VMEM((len(lists), kv_heads, cap, pair_of, page_len, head_dim), pool.dtype),
+            out_specs=specs,
+            scratch_shapes=scratch
+            + [
                 pltpu.SMEM((len(lists) * (cap + 1),), jnp.int32),
                 pltpu.SemaphoreType.DMA((len(lists), kv_heads, cap)),
                 pltpu.SemaphoreType.DMA((len(lists), kv_heads)),
@@ -119,8 +132,12 @@
         ),
         compiler_params=pltpu.CompilerParams(vmem_limit_bytes=kernel_bytes),
         name="gather_pages",
-    )(owner, pltpu.with_memory_space_constraint(table, pltpu.HBM), pltpu.with_memory_space_constraint(pool, pltpu.HBM))
-    return [outs[i * kv_heads : (i + 1) * kv_heads] for i in range(len(lists))]
+    )(
+        owner,
+        pltpu.with_memory_space_constraint(table, pltpu.HBM),
+        pltpu.with_memory_space_constraint(pool, pltpu.HBM),
+    )
+    return [pages[i * kv_heads : (i + 1) * kv_heads] for i in range(len(lists))]
 
 
 def attend_body(
@@ -474,9 +491,9 @@
     other = [moved(split[k], 1) for k in each]
     owner_list = jnp.full((1,), owner, jnp.int32)
     far_lists = [near + k for k in range(1, near)]
-    sent_far = gather_pages(owner_list, block_table, pool, far_lists, cap)
+    sent_far = gather_pages(owner_list, block_table, pool, far_lists, near - 1, cap)
     rest_lists = list(range(1, near)) + [0, near]
-    pages = gather_pages(owner_list, block_table, pool, rest_lists, cap)
+    pages = gather_pages(owner_list, block_table, pool, rest_lists, near - 1, cap)
 
     def exchanged(sent):
         return [[moved(sent[i][k], 2 * (i + 1)) for i in range(near - 1)] for k in each]
@@ -495,7 +512,7 @@
         results = attend(
             scalars,
             [(split[k], 0), (other[k], 0)],
-            [(local[k], 0)],
+            [(local[k] if k else pltpu.with_memory_space_constraint(local[k], pltpu.HBM), 0)],
             [(0, 0)],
             (False, False),
             scale,

time: 90.1 us -> 88.9 us (0.987)
  local copies, waits for them, and re-layouts: 2.17 us -> 1.13 us
    pallas_call x2, Pallas kernels: 8.31 us -> 7.05 us  [gather_pages(): pl.pallas_call(functools.partial(gather_body, lists=lists, resident=resid...]
    unnamed x21 -> x15, local copies, waits for them, and re-layouts: 1.09 us -> 0.05 us
    pallas_call x7, Pallas kernels: 32.4 us -> 33.3 us  [attend(): pl.pallas_call(functools.partial(attend_body, halves=halves, seen_at=seen...]
where the time goes in v3:
time: 88.9 us; the launch traced here: 88.5 us
  Pallas kernels  43.5 us (49%)
  starting transfers between devices  24.8 us (28%)
  waiting for transfers between devices  17.8 us (20%)
  local copies, waits for them, and re-layouts  1.13 us (1%)
    pallas_call x7, Pallas kernels, attend(): pl.pallas_call(functools.partial(attend_body, halves=halves, seen_at=seen...  33.3 us
    ppermute x16, starting transfers between devices, moved(): return lax.ppermute(array, 'pool', [(i, i ^ apart) for i in range(count)])  24.8 us
    ppermute x16, waiting for transfers between devices, moved(): return lax.ppermute(array, 'pool', [(i, i ^ apart) for i in range(count)])  17.8 us
    pallas_call x2, Pallas kernels, gather_pages(): pl.pallas_call(functools.partial(gather_body, lists=lists, resident=resid...  7.05 us
    pallas_call x2, Pallas kernels, join_out(): pl.pallas_call(functools.partial(join_body, scale=scale, packs=False, wai...  2.43 us
  transfers between devices with their start and end apart: 16, of which 3 were waited for; matrix products, arithmetic and copies ran while one was open for 1% of the time, Pallas kernels for 48%

profile of v3, /device:TPU:0, one launch (start us, length us, event | category | flops | bytes accessed | tf_op | source)
XLA Modules:
  0.0 88.5 jit_solution(6088367216050103256)
XLA Ops:
  0.6 0.0 copy-start.5
  0.7 1.1 %slice_bitcast_fusion = (bf16[1,1024,128]{2,1,0:T(8,128)(2,1)S(1)}, bf16[1,1024,128]{2,1,0:T(8,128)(2,1)S(1)}) fusion(bf16[128,16,128]{2,1,0:T(8,128)(2,1)} %param.6), kind=kLoop, calls=%fused_computation | loop fusion | bytes 1048576 | tf_op jit(solution)/shard_map/reshape | solution.py:488
  1.7 3.1 %collective-permute-start.2 = (bf16[1,1024,128]{2,1,0:T(8,128)(2,1)S(1)}, bf16[1,1024,128]{2,1,0:T(8,128)(2,1)S(1)}, u32[]{:S(2)}, u32[]{:S(2)}) collective-permute-start(bf16[1,1024,128]{2,1,0:T(8,128)(2,1)S(1)} %get-tuple-element.58.refs_0_), channel_id=1, source_target_pairs={{0,2},{2,0},{4,6},{6,4},{8,10},{10,8},{12,14},{14,12},{1,3},{3,1},... | collective-permute-start | bytes 786440 | tf_op jit(solution)/shard_map/ppermute | solution.py:21
  4.8 2.6 %collective-permute-start.6 = (bf16[1,1024,128]{2,1,0:T(8,128)(2,1)S(1)}, bf16[1,1024,128]{2,1,0:T(8,128)(2,1)S(1)}, u32[]{:S(2)}, u32[]{:S(2)}) collective-permute-start(bf16[1,1024,128]{2,1,0:T(8,128)(2,1)S(1)} %get-tuple-element.58.refs_0_), channel_id=1, source_target_pairs={{0,8},{2,10},{4,12},{6,14},{8,0},{10,2},{12,4},{14,6},{1,9},{3,11}... | collective-permute-start | bytes 786440 | tf_op jit(solution)/shard_map/ppermute | solution.py:21
  7.4 0.5 collective-permute-start.1
  7.9 0.0 collective-permute-start.3
  7.9 2.6 %gather_pages.3 = (bf16[1,8,2,128,128]{4,3,2,1,0:T(8,128)(2,1)S(1)}, bf16[1,8,2,128,128]{4,3,2,1,0:T(8,128)(2,1)S(1)}) custom-call(s32[1]{0:T(128)} %bitcast.owner_ref, s32[4,64]{1,0:T(4,128)} %table_ref.3, bf16[33,2,2,128,128]{4,3,2,1,0:T(8,128)(2,1)} %pool_ref.3), custom_call_target="tpu_custom_call" | custom-call | tf_op jit(solution)/shard_map/gather_pages/pallas_call | solution.py:116
  10.5 2.0 %collective-permute-start.8 = (bf16[1,8,2,128,128]{4,3,2,1,0:T(8,128)(2,1)S(1)}, bf16[1,8,2,128,128]{4,3,2,1,0:T(8,128)(2,1)S(1)}, u32[]{:S(2)}, u32[]{:S(2)}) collective-permute-start(bf16[1,8,2,128,128]{4,3,2,1,0:T(8,128)(2,1)S(1)} %get-tuple-element.41), channel_id=1, source_target_pairs={{0,4},{2,6},{4,0},{6,2},{8,12},{10,14},{12,8},{14,10},{1,5},{3,7},... | collective-permute-start | bytes 1572872 | tf_op jit(solution)/shard_map/ppermute | solution.py:21
  12.4 0.1 compare_and_fusion
  12.5 0.1 subtract_clamp_fusion
  12.6 0.1 iota_compare_fusion
  12.7 0.0 collective-permute-done.2.refs_1_
  12.7 1.3 %collective-permute-start.5 = (bf16[1,8,2,128,128]{4,3,2,1,0:T(8,128)(2,1)S(1)}, bf16[1,8,2,128,128]{4,3,2,1,0:T(8,128)(2,1)S(1)}, u32[]{:S(2)}, u32[]{:S(2)}) collective-permute-start(bf16[1,8,2,128,128]{4,3,2,1,0:T(8,128)(2,1)S(1)} %get-tuple-element.39), channel_id=1, source_target_pairs={{0,4},{2,6},{4,0},{6,2},{8,12},{10,14},{12,8},{14,10},{1,5},{3,7},... | collective-permute-start | bytes 1572872 | tf_op jit(solution)/shard_map/ppermute | solution.py:21
  14.0 11.9 %collective-permute-done.6.refs_0_ = bf16[1,1024,128]{2,1,0:T(8,128)(2,1)S(1)} collective-permute-done((bf16[1,1024,128]{2,1,0:T(8,128)(2,1)S(1)}, bf16[1,1024,128]{2,1,0:T(8,128)(2,1)S(1)}, u32[]{:S(2)}, u32[]{:S(2)}) %collective-permute-start.6) | collective-permute-done | bytes 262176 | tf_op jit(solution)/shard_map/ppermute | solution.py:21
  25.9 0.5 collective-permute-start.7
  26.4 0.2 select_reduce_fusion.seen_ref
  26.6 4.5 %gather_pages.2 = (bf16[1,8,2,128,128]{4,3,2,1,0:T(8,128)(2,1)S(1)}, bf16[1,8,2,128,128]{4,3,2,1,0:T(8,128)(2,1)S(1)}, bf16[1,8,2,128,128]{4,3,2,1,0:T(8,128)(2,...) custom-call(s32[1]{0:T(128)} %bitcast.owner_ref, ...), custom_call_target="tpu_custom_call" | custom-call | tf_op jit(solution)/shard_map/gather_pages/pallas_call | solution.py:116
  31.2 5.9 %attend.7 = (f32[1,1024,128]{2,1,0:T(8,128)S(1)}, f32[1,16,128]{2,1,0:T(8,128)S(1)}, f32[1,1024,128]{2,1,0:T(8,128)S(1)}, f32[1,16,128]{2,1,0:T(8,128)S(1)}, bf16[33,2,2,128,128]{4,3,2,1,0:T(8,128)(2,1)}) custom-call(s32[1]{0:T(128)} %bitcast.owner_ref, s32[2,2]{1,0:T(2,128)S(1)} %select_reduce_fusion.seen_ref, s32[8]{0:T(128)S(1)} %copy-done, ...), custom_call_target="tpu_custom_call" | custom-call | flops 1207959552 | bytes 589824 | tf_op jit(solution)/shard_map/attend/pallas_call | solution.py:353
  37.1 0.0 collective-permute-done.1.refs_1_.refs_0_
  37.1 0.1 collective-permute-start.10
  37.2 0.0 collective-permute-done.3.refs_0_
  37.2 1.6 %collective-permute-start.4 = (bf16[1,1024,128]{2,1,0:T(8,128)(2,1)S(1)}, bf16[1,1024,128]{2,1,0:T(8,128)(2,1)S(1)}, u32[]{:S(2)}, u32[]{:S(2)}) collective-permute-start(bf16[1,1024,128]{2,1,0:T(8,128)(2,1)S(1)} %collective-permute-done.3.refs_0_), channel_id=1, source_target_pairs={{0,2},{2,0},{4,6},{6,4},{8,10},{10,8},{12,14},{14,12},{1,3},{3,1},... | collective-permute-start | bytes 786440 | tf_op jit(solution)/shard_map/ppermute | solution.py:21
  38.8 4.8 %attend.8 = (f32[1,1024,128]{2,1,0:T(8,128)S(1)}, f32[1,16,128]{2,1,0:T(8,128)S(1)}, f32[1,1024,128]{2,1,0:T(8,128)S(1)}, f32[1,16,128]{2,1,0:T(8,128)S(1)}) custom-call(s32[1]{0:T(128)} %bitcast.owner_ref, s32[2,2]{1,0:T(2,128)S(1)} %select_reduce_fusion.seen_ref, s32[8]{0:T(128)S(1)} %copy-done, bf16[1,1024,128]{2,1,0:T(8,128)(2,1)S(1)} %get-tuple-element.59.refs_0_, ...), custom_call_target="tpu_custom_call" | custom-call | flops 1207959552 | bytes 589824 | tf_op jit(solution)/shard_map/attend/pallas_call | solution.py:353
  43.6 2.0 %collective-permute-start = (bf16[1,8,2,128,128]{4,3,2,1,0:T(8,128)(2,1)S(1)}, bf16[1,8,2,128,128]{4,3,2,1,0:T(8,128)(2,1)S(1)}, u32[]{:S(2)}, u32[]{:S(2)}) collective-permute-start(bf16[1,8,2,128,128]{4,3,2,1,0:T(8,128)(2,1)S(1)} %get-tuple-element.30), channel_id=1, source_target_pairs={{0,4},{2,6},{4,0},{6,2},{8,12},{10,14},{12,8},{14,10},{1,5},{3,7},... | collective-permute-start | bytes 1572872 | tf_op jit(solution)/shard_map/ppermute | solution.py:21
  45.6 6.7 %attend.9 = (f32[1,1024,128]{2,1,0:T(8,128)S(1)}, f32[1,16,128]{2,1,0:T(8,128)S(1)}, bf16[1,1072,128]{2,1,0:T(8,128)(2,1)S(1)}) custom-call(s32[1]{0:T(128)} %bitcast.owner_ref, s32[2,2]{1,0:T(2,128)S(1)} %select_reduce_fusion.seen_ref, s32[8]{0:T(128)S(1)} %copy-done, bf16[1,1024,128]{2,1,0:T(8,128)(2,1)S(1)} %collective-permute-done.6.refs_0_, ...), custom_call_target="tpu_custom_call" | custom-call | flops 2147483648 | bytes 1048576 | tf_op jit(solution)/shard_map/attend/pallas_call | solution.py:353
  52.3 0.5 collective-permute-start.11
  52.8 0.0 collective-permute-done.5.refs_3_
  52.9 0.0 collective-permute-done.4.refs_1_
  52.9 6.8 %attend.10 = (f32[1,1024,128]{2,1,0:T(8,128)S(1)}, f32[1,16,128]{2,1,0:T(8,128)S(1)}, bf16[1,1072,128]{2,1,0:T(8,128)(2,1)S(1)}) custom-call(s32[1]{0:T(128)} %bitcast.owner_ref, s32[2,2]{1,0:T(2,128)S(1)} %select_reduce_fusion.seen_ref, s32[8]{0:T(128)S(1)} %copy-done, bf16[1,1024,128]{2,1,0:T(8,128)(2,1)S(1)} %collective-permute-done.3.refs_0_, ...), custom_call_target="tpu_custom_call" | custom-call | flops 2147483648 | bytes 1048576 | tf_op jit(solution)/shard_map/attend/pallas_call | solution.py:353
  59.7 1.6 %collective-permute-start.9 = (bf16[1,1072,128]{2,1,0:T(8,128)(2,1)S(1)}, bf16[1,1072,128]{2,1,0:T(8,128)(2,1)S(1)}, u32[]{:S(2)}, u32[]{:S(2)}) collective-permute-start(bf16[1,1072,128]{2,1,0:T(8,128)(2,1)S(1)} %get-tuple-element.45), channel_id=1, source_target_pairs={{0,2},{2,0},{4,6},{6,4},{8,10},{10,8},{12,14},{14,12},{1,3},{3,1},... | collective-permute-start | bytes 823304 | tf_op jit(solution)/shard_map/ppermute | solution.py:21
  61.3 0.0 collective-permute-done.11.refs_0_
  61.3 0.4 join_packed.2.refs_7_
  61.7 1.2 %collective-permute-start.15 = (bf16[1,1072,128]{2,1,0:T(8,128)(2,1)S(1)}, bf16[1,1072,128]{2,1,0:T(8,128)(2,1)S(1)}, u32[]{:S(2)}, u32[]{:S(2)}) collective-permute-start(bf16[1,1072,128]{2,1,0:T(8,128)(2,1)S(1)} %join_packed.2.refs_7_), channel_id=1, source_target_pairs={{0,8},{2,10},{4,12},{6,14},{8,0},{10,2},{12,4},{14,6},{1,9},{3,11}... | collective-permute-start | bytes 823304 | tf_op jit(solution)/shard_map/ppermute | solution.py:21
  62.8 0.0 collective-permute-done.10.refs_2_
  62.8 4.2 %attend.11 = (f32[1,1024,128]{2,1,0:T(8,128)S(1)}, f32[1,16,128]{2,1,0:T(8,128)S(1)}, bf16[1,1072,128]{2,1,0:T(8,128)(2,1)S(1)}) custom-call(s32[1]{0:T(128)} %bitcast.owner_ref, s32[2,2]{1,0:T(2,128)S(1)} %select_reduce_fusion.seen_ref, s32[8]{0:T(128)S(1)} %copy-done, bf16[1,1024,128]{2,1,0:T(8,128)(2,1)S(1)} %get-tuple-element.58.refs_0_, ...), custom_call_target="tpu_custom_call" | custom-call | flops 1073741824 | bytes 524288 | tf_op jit(solution)/shard_map/attend/pallas_call | solution.py:353
  67.1 0.6 collective-permute-start.14
  67.7 0.0 collective-permute-done.9.refs_0_
  67.7 0.4 join_packed.3.refs_4_
  68.0 2.1 %collective-permute-done.refs_1_ = bf16[1,8,2,128,128]{4,3,2,1,0:T(8,128)(2,1)S(1)} collective-permute-done((bf16[1,8,2,128,128]{4,3,2,1,0:T(8,128)(2,1)S(1)}, bf16[1,8,2,128,128]{4,3,2,1,0:T(8,128)(2,1)S(1)}, u32[]{:S(2)}, u32[]{:S(2)}) %collective-permute-start) | collective-permute-done | bytes 524320 | tf_op jit(solution)/shard_map/ppermute | solution.py:21
  70.1 2.4 %attend.12.refs_4_ = bf16[1,1072,128]{2,1,0:T(8,128)(2,1)S(1)} custom-call(s32[1]{0:T(128)} %bitcast.owner_ref, s32[2,2]{1,0:T(2,128)S(1)} %select_reduce_fusion.seen_ref, s32[8]{0:T(128)S(1)} %copy-done, bf16[1,1024,128]{2,1,0:T(8,128)(2,1)S(1)} %collective-permute-done.1.refs_1_.refs_0_, bf16[1,8,2,128,128]{4,3,2,1,0:T(8,128)(2,1)S(1)} %collective-permute-done.refs_1_, ...), custom_call_target="tpu_custom_call" | custom-call | flops 536870912 | bytes 524288 | tf_op jit(solution)/shard_map/attend/pallas_call | solution.py:353
  72.6 1.6 %collective-permute-start.12 = (bf16[1,1072,128]{2,1,0:T(8,128)(2,1)S(1)}, bf16[1,1072,128]{2,1,0:T(8,128)(2,1)S(1)}, u32[]{:S(2)}, u32[]{:S(2)}) collective-permute-start(bf16[1,1072,128]{2,1,0:T(8,128)(2,1)S(1)} %attend.12.refs_4_), channel_id=1, source_target_pairs={{0,2},{2,0},{4,6},{6,4},{8,10},{10,8},{12,14},{14,12},{1,3},{3,1},... | collective-permute-start | bytes 823304 | tf_op jit(solution)/shard_map/ppermute | solution.py:21
  74.2 5.7 %collective-permute-start.13 = (bf16[1,1072,128]{2,1,0:T(8,128)(2,1)S(1)}, bf16[1,1072,128]{2,1,0:T(8,128)(2,1)S(1)}, u32[]{:S(2)}, u32[]{:S(2)}) collective-permute-start(bf16[1,1072,128]{2,1,0:T(8,128)(2,1)S(1)} %join_packed.3.refs_4_), channel_id=1, source_target_pairs={{0,8},{2,10},{4,12},{6,14},{8,0},{10,2},{12,4},{14,6},{1,9},{3,11}... | collective-permute-start | bytes 823304 | tf_op jit(solution)/shard_map/ppermute | solution.py:21
  79.9 2.4 %attend.13 = (f32[1,1024,128]{2,1,0:T(8,128)S(1)}, f32[1,16,128]{2,1,0:T(8,128)S(1)}) custom-call(s32[1]{0:T(128)} %bitcast.owner_ref, s32[2,2]{1,0:T(2,128)S(1)} %select_reduce_fusion.seen_ref, s32[8]{0:T(128)S(1)} %copy-done, bf16[1,1024,128]{2,1,0:T(8,128)(2,1)S(1)} %get-tuple-element.59.refs_0_, ...), custom_call_target="tpu_custom_call" | custom-call | flops 536870912 | bytes 524288 | tf_op jit(solution)/shard_map/attend/pallas_call | solution.py:353
  82.3 0.0 collective-permute-done.14.refs_0_
  82.3 0.0 collective-permute-done.15.refs_1_
  82.3 1.2 %join_out.2.refs_2_ = bf16[128,16,128]{2,1,0:T(8,128)(2,1)} custom-call(f32[1,1024,128]{2,1,0:T(8,128)S(1)} %get-tuple-element.55.own_mixed, f32[1,16,128]{2,1,0:T(8,128)S(1)} %get-tuple-element.52.refs_1_.own_table, bf16[1,1072,128]{2,1,0:T(8,128)(2,1)S(1)} %collective-permute-done.14.refs_0_, bf16[1,1072,128]{2,1,0:T(8,128)(2,1)S(1)} %collective-permute-done.15.refs_1_), custom_call_target="tpu_custom_call" | custom-call | tf_op jit(solution)/shard_map/join_out/pallas_call | solution.py:448
  83.5 3.8 %collective-permute-done.13.refs_1_ = bf16[1,1072,128]{2,1,0:T(8,128)(2,1)S(1)} collective-permute-done((bf16[1,1072,128]{2,1,0:T(8,128)(2,1)S(1)}, bf16[1,1072,128]{2,1,0:T(8,128)(2,1)S(1)}, u32[]{:S(2)}, u32[]{:S(2)}) %collective-permute-start.13) | collective-permute-done | bytes 274464 | tf_op jit(solution)/shard_map/ppermute | solution.py:21
  87.3 1.2 %join_out.3 = bf16[128,16,128]{2,1,0:T(8,128)(2,1)} custom-call(f32[1,1024,128]{2,1,0:T(8,128)S(1)} %get-tuple-element.53.own_mixed, f32[1,16,128]{2,1,0:T(8,128)S(1)} %get-tuple-element.54.own_table, bf16[1,1072,128]{2,1,0:T(8,128)(2,1)S(1)} %collective-permute-done.12.refs_0_, ...), custom_call_target="tpu_custom_call", output_to_operand_aliasing={{}: (4, {})} | custom-call | tf_op jit(solution)/shard_map/join_out/pallas_call | solution.py:448
  (20 shorter events, 0.1 us)
Async XLA Ops:
  0.6 11.8 %copy-start.5 = (s32[4,64]{1,0:T(4,128)S(1)}, s32[4,64]{1,0:T(4,128)}, u32[]{:S(2)}) copy-start(s32[4,64]{1,0:T(4,128)} %table_ref.3) | copy-start | bytes 3076
  0.6 11.9 %copy-start.6 = (s32[4]{0:T(128)S(1)}, s32[4]{0:T(128)}, u32[]{:S(2)}) copy-start(s32[4]{0:T(128)} %param.10) | copy-start | bytes 52
  1.7 10.9 %collective-permute-start.2 = (bf16[1,1024,128]{2,1,0:T(8,128)(2,1)S(1)}, bf16[1,1024,128]{2,1,0:T(8,128)(2,1)S(1)}, u32[]{:S(2)}, u32[]{:S(2)}) collective-permute-start(bf16[1,1024,128]{2,1,0:T(8,128)(2,1)S(1)} %get-tuple-element.58.refs_0_), channel_id=1, source_target_pairs={{0,2},{2,0},{4,6},{6,4},{8,10},{10,8},{12,14},{14,12},{1,3},{3,1},... | collective-permute-start | bytes 786440 | tf_op jit(solution)/shard_map/ppermute | solution.py:21
  4.8 21.1 %collective-permute-start.6 = (bf16[1,1024,128]{2,1,0:T(8,128)(2,1)S(1)}, bf16[1,1024,128]{2,1,0:T(8,128)(2,1)S(1)}, u32[]{:S(2)}, u32[]{:S(2)}) collective-permute-start(bf16[1,1024,128]{2,1,0:T(8,128)(2,1)S(1)} %get-tuple-element.58.refs_0_), channel_id=1, source_target_pairs={{0,8},{2,10},{4,12},{6,14},{8,0},{10,2},{12,4},{14,6},{1,9},{3,11}... | collective-permute-start | bytes 786440 | tf_op jit(solution)/shard_map/ppermute | solution.py:21
  7.4 29.7 %collective-permute-start.1 = (bf16[1,1024,128]{2,1,0:T(8,128)(2,1)S(1)}, bf16[1,1024,128]{2,1,0:T(8,128)(2,1)S(1)}, u32[]{:S(2)}, u32[]{:S(2)}) collective-permute-start(bf16[1,1024,128]{2,1,0:T(8,128)(2,1)S(1)} %get-tuple-element.59.refs_0_), channel_id=1, source_target_pairs={{0,2},{2,0},{4,6},{6,4},{8,10},{10,8},{12,14},{14,12},{1,3},{3,1},... | collective-permute-start | bytes 786440 | tf_op jit(solution)/shard_map/ppermute | solution.py:21
  7.9 29.3 %collective-permute-start.3 = (bf16[1,1024,128]{2,1,0:T(8,128)(2,1)S(1)}, bf16[1,1024,128]{2,1,0:T(8,128)(2,1)S(1)}, u32[]{:S(2)}, u32[]{:S(2)}) collective-permute-start(bf16[1,1024,128]{2,1,0:T(8,128)(2,1)S(1)} %get-tuple-element.59.refs_0_), channel_id=1, source_target_pairs={{0,8},{2,10},{4,12},{6,14},{8,0},{10,2},{12,4},{14,6},{1,9},{3,11}... | collective-permute-start | bytes 786440 | tf_op jit(solution)/shard_map/ppermute | solution.py:21
  7.9 23.2 %copy-start.4 = (bf16[128,2,2,128]{3,2,1,0:T(2,128)(2,1)S(1)}, bf16[128,2,2,128]{3,2,1,0:T(2,128)(2,1)}, u32[]{:S(2)}) copy-start(bf16[128,2,2,128]{3,2,1,0:T(2,128)(2,1)} %param.7) | copy-start | bytes 393220
  7.9 23.2 %copy-start = (s32[8]{0:T(128)S(1)}, s32[8]{0:T(128)}, u32[]{:S(2)}) copy-start(s32[8]{0:T(128)} %fresh_ref.13) | copy-start | bytes 100
  10.5 33.1 %collective-permute-start.8 = (bf16[1,8,2,128,128]{4,3,2,1,0:T(8,128)(2,1)S(1)}, bf16[1,8,2,128,128]{4,3,2,1,0:T(8,128)(2,1)S(1)}, u32[]{:S(2)}, u32[]{:S(2)}) collective-permute-start(bf16[1,8,2,128,128]{4,3,2,1,0:T(8,128)(2,1)S(1)} %get-tuple-element.41), channel_id=1, source_target_pairs={{0,4},{2,6},{4,0},{6,2},{8,12},{10,14},{12,8},{14,10},{1,5},{3,7},... | collective-permute-start | bytes 1572872 | tf_op jit(solution)/shard_map/ppermute | solution.py:21
  12.7 40.2 %collective-permute-start.5 = (bf16[1,8,2,128,128]{4,3,2,1,0:T(8,128)(2,1)S(1)}, bf16[1,8,2,128,128]{4,3,2,1,0:T(8,128)(2,1)S(1)}, u32[]{:S(2)}, u32[]{:S(2)}) collective-permute-start(bf16[1,8,2,128,128]{4,3,2,1,0:T(8,128)(2,1)S(1)} %get-tuple-element.39), channel_id=1, source_target_pairs={{0,4},{2,6},{4,0},{6,2},{8,12},{10,14},{12,8},{14,10},{1,5},{3,7},... | collective-permute-start | bytes 1572872 | tf_op jit(solution)/shard_map/ppermute | solution.py:21
  25.9 19.7 %collective-permute-start.7 = (bf16[1,1024,128]{2,1,0:T(8,128)(2,1)S(1)}, bf16[1,1024,128]{2,1,0:T(8,128)(2,1)S(1)}, u32[]{:S(2)}, u32[]{:S(2)}) collective-permute-start(bf16[1,1024,128]{2,1,0:T(8,128)(2,1)S(1)} %collective-permute-done.6.refs_0_), channel_id=1, source_target_pairs={{0,2},{2,0},{4,6},{6,4},{8,10},{10,8},{12,14},{14,12},{1,3},{3,1},... | collective-permute-start | bytes 786440 | tf_op jit(solution)/shard_map/ppermute | solution.py:21
  31.1 7.7 %copy-start.3 = (bf16[1,8,2,128,128]{4,3,2,1,0:T(8,128)(2,1)S(1)}, bf16[1,8,2,128,128]{4,3,2,1,0:T(8,128)(2,1)}, u32[]{:S(2)}) copy-start(bf16[1,8,2,128,128]{4,3,2,1,0:T(8,128)(2,1)} %get-tuple-element.31.refs_2_) | copy-start | bytes 1572868
  31.1 14.5 %copy-start.2 = (bf16[1,8,2,128,128]{4,3,2,1,0:T(8,128)(2,1)S(1)}, bf16[1,8,2,128,128]{4,3,2,1,0:T(8,128)(2,1)}, u32[]{:S(2)}) copy-start(bf16[1,8,2,128,128]{4,3,2,1,0:T(8,128)(2,1)} %get-tuple-element.40.refs_2_) | copy-start | bytes 1572868
  37.1 25.7 %collective-permute-start.10 = (bf16[1,8,2,128,128]{4,3,2,1,0:T(8,128)(2,1)S(1)}, bf16[1,8,2,128,128]{4,3,2,1,0:T(8,128)(2,1)S(1)}, u32[]{:S(2)}, u32[]{:S(2)}) collective-permute-start(bf16[1,8,2,128,128]{4,3,2,1,0:T(8,128)(2,1)S(1)} %get-tuple-element.46), channel_id=1, source_target_pairs={{0,4},{2,6},{4,0},{6,2},{8,12},{10,14},{12,8},{14,10},{1,5},{3,7},... | collective-permute-start | bytes 1572872 | tf_op jit(solution)/shard_map/ppermute | solution.py:21
  37.2 15.7 %collective-permute-start.4 = (bf16[1,1024,128]{2,1,0:T(8,128)(2,1)S(1)}, bf16[1,1024,128]{2,1,0:T(8,128)(2,1)S(1)}, u32[]{:S(2)}, u32[]{:S(2)}) collective-permute-start(bf16[1,1024,128]{2,1,0:T(8,128)(2,1)S(1)} %collective-permute-done.3.refs_0_), channel_id=1, source_target_pairs={{0,2},{2,0},{4,6},{6,4},{8,10},{10,8},{12,14},{14,12},{1,3},{3,1},... | collective-permute-start | bytes 786440 | tf_op jit(solution)/shard_map/ppermute | solution.py:21
  43.6 9.3 %copy-start.1 = (bf16[1,8,2,128,128]{4,3,2,1,0:T(8,128)(2,1)S(1)}, bf16[1,8,2,128,128]{4,3,2,1,0:T(8,128)(2,1)}, u32[]{:S(2)}) copy-start(bf16[1,8,2,128,128]{4,3,2,1,0:T(8,128)(2,1)} %get-tuple-element.38.refs_2_) | copy-start | bytes 1572868
  43.6 26.5 %collective-permute-start = (bf16[1,8,2,128,128]{4,3,2,1,0:T(8,128)(2,1)S(1)}, bf16[1,8,2,128,128]{4,3,2,1,0:T(8,128)(2,1)S(1)}, u32[]{:S(2)}, u32[]{:S(2)}) collective-permute-start(bf16[1,8,2,128,128]{4,3,2,1,0:T(8,128)(2,1)S(1)} %get-tuple-element.30), channel_id=1, source_target_pairs={{0,4},{2,6},{4,0},{6,2},{8,12},{10,14},{12,8},{14,10},{1,5},{3,7},... | collective-permute-start | bytes 1572872 | tf_op jit(solution)/shard_map/ppermute | solution.py:21
  52.3 9.0 %collective-permute-start.11 = (bf16[1,1072,128]{2,1,0:T(8,128)(2,1)S(1)}, bf16[1,1072,128]{2,1,0:T(8,128)(2,1)S(1)}, u32[]{:S(2)}, u32[]{:S(2)}) collective-permute-start(bf16[1,1072,128]{2,1,0:T(8,128)(2,1)S(1)} %get-tuple-element.51), channel_id=1, source_target_pairs={{0,2},{2,0},{4,6},{6,4},{8,10},{10,8},{12,14},{14,12},{1,3},{3,1},... | collective-permute-start | bytes 823304 | tf_op jit(solution)/shard_map/ppermute | solution.py:21
  59.7 8.0 %collective-permute-start.9 = (bf16[1,1072,128]{2,1,0:T(8,128)(2,1)S(1)}, bf16[1,1072,128]{2,1,0:T(8,128)(2,1)S(1)}, u32[]{:S(2)}, u32[]{:S(2)}) collective-permute-start(bf16[1,1072,128]{2,1,0:T(8,128)(2,1)S(1)} %get-tuple-element.45), channel_id=1, source_target_pairs={{0,2},{2,0},{4,6},{6,4},{8,10},{10,8},{12,14},{14,12},{1,3},{3,1},... | collective-permute-start | bytes 823304 | tf_op jit(solution)/shard_map/ppermute | solution.py:21
  61.7 20.6 %collective-permute-start.15 = (bf16[1,1072,128]{2,1,0:T(8,128)(2,1)S(1)}, bf16[1,1072,128]{2,1,0:T(8,128)(2,1)S(1)}, u32[]{:S(2)}, u32[]{:S(2)}) collective-permute-start(bf16[1,1072,128]{2,1,0:T(8,128)(2,1)S(1)} %join_packed.2.refs_7_), channel_id=1, source_target_pairs={{0,8},{2,10},{4,12},{6,14},{8,0},{10,2},{12,4},{14,6},{1,9},{3,11}... | collective-permute-start | bytes 823304 | tf_op jit(solution)/shard_map/ppermute | solution.py:21
  67.1 15.2 %collective-permute-start.14 = (bf16[1,1072,128]{2,1,0:T(8,128)(2,1)S(1)}, bf16[1,1072,128]{2,1,0:T(8,128)(2,1)S(1)}, u32[]{:S(2)}, u32[]{:S(2)}) collective-permute-start(bf16[1,1072,128]{2,1,0:T(8,128)(2,1)S(1)} %get-tuple-element.56), channel_id=1, source_target_pairs={{0,2},{2,0},{4,6},{6,4},{8,10},{10,8},{12,14},{14,12},{1,3},{3,1},... | collective-permute-start | bytes 823304 | tf_op jit(solution)/shard_map/ppermute | solution.py:21
  72.6 10.9 %collective-permute-start.12 = (bf16[1,1072,128]{2,1,0:T(8,128)(2,1)S(1)}, bf16[1,1072,128]{2,1,0:T(8,128)(2,1)S(1)}, u32[]{:S(2)}, u32[]{:S(2)}) collective-permute-start(bf16[1,1072,128]{2,1,0:T(8,128)(2,1)S(1)} %attend.12.refs_4_), channel_id=1, source_target_pairs={{0,2},{2,0},{4,6},{6,4},{8,10},{10,8},{12,14},{14,12},{1,3},{3,1},... | collective-permute-start | bytes 823304 | tf_op jit(solution)/shard_map/ppermute | solution.py:21
  74.2 13.1 %collective-permute-start.13 = (bf16[1,1072,128]{2,1,0:T(8,128)(2,1)S(1)}, bf16[1,1072,128]{2,1,0:T(8,128)(2,1)S(1)}, u32[]{:S(2)}, u32[]{:S(2)}) collective-permute-start(bf16[1,1072,128]{2,1,0:T(8,128)(2,1)S(1)} %join_packed.3.refs_4_), channel_id=1, source_target_pairs={{0,8},{2,10},{4,12},{6,14},{8,0},{10,2},{12,4},{14,6},{1,9},{3,11}... | collective-permute-start | bytes 823304 | tf_op jit(solution)/shard_map/ppermute | solution.py:21

commit v4 on v2

--- a/solution.py
+++ b/solution.py
@@ -55,72 +55,93 @@
     return parts[0] + parts[1] + parts[2]
 
 
-def gather_body(owner_ref, table_ref, pool_ref, *refs, lists, kv_heads, cap):
-    outs = refs[:-4]
-    staged, slots, sem_in, sem_out = refs[-4:]
+def gather_body(owner_ref, table_ref, length_ref, pool_ref, *refs, lists, near, waits, kv_heads, cap):
+    refs = refs[waits:]
+    outs = refs[: len(lists) * kv_heads]
+    seen_ref = refs[len(lists) * kv_heads] if near else None
+    slots, sem = refs[-2:]
     owner = owner_ref[0]
     pair = owner >> 1
-    slot_count = pool_ref.shape[0]
-    base = owner * slot_count
+    slot_count, _, _, page_len, _ = pool_ref.shape
     width = table_ref.shape[1]
+
+    def held(request, holder, j):
+        slot = table_ref[request, j] - holder * slot_count
+        return slot, (slot >= 0) & (slot < slot_count)
 
     def look(j, found):
         following = []
         for at, which in enumerate(lists):
-            slot = table_ref[pair ^ which, j] - base
+            slot, here = held(pair ^ which, owner, j)
             slots[at * (cap + 1) + jnp.minimum(found[at], cap)] = slot
-            held = (slot >= 0) & (slot < slot_count)
-            following.append(found[at] + held.astype(jnp.int32))
+            following.append(found[at] + here.astype(jnp.int32))
         return tuple(following)
 
-    found = lax.fori_loop(0, width, look, (jnp.int32(0),) * len(lists), unroll=4)
-    arriving = []
+    found = lax.fori_loop(0, width, look, (jnp.int32(0),) * len(lists), unroll=16)
+    copies = []
     for at in range(len(lists)):
         for k in range(kv_heads):
             for i in range(cap):
                 slot = jnp.where(i < found[at], slots[at * (cap + 1) + i], 0)
                 copy = pltpu.make_async_copy(
-                    pool_ref.at[slot, :, k], staged.at[at, k, i], sem_in.at[at, k, i]
+                    pool_ref.at[slot, :, k], outs[at * kv_heads + k].at[0, i], sem.at[at, k, i]
                 )
                 copy.start()
-                arriving.append(copy)
-    leaving = []
-    for at in range(len(lists)):
-        for k in range(kv_heads):
-            for i in range(cap):
-                arriving[(at * kv_heads + k) * cap + i].wait()
-            copy = pltpu.make_async_copy(
-                staged.at[at, k], outs[at * kv_heads + k].at[0], sem_out.at[at, k]
-            )
-            copy.start()
-            leaving.append(copy)
-    for copy in leaving:
+                copies.append(copy)
+    if near:
+        asked = [(t, s) for t in range(2) for s in range(near)]
+
+        def count(j, seen):
+            following = []
+            for (t, s), so_far in zip(asked, seen):
+                request = pair ^ (t * near)
+                _, there = held(request, owner ^ (2 * s), j)
+                inside = jnp.clip(length_ref[request] - j * page_len, 0, page_len)
+                following.append(so_far + jnp.where(there, inside, 0))
+            return tuple(following)
+
+        seen = lax.fori_loop(0, width, count, (jnp.int32(0),) * len(asked), unroll=8)
+        for (t, s), total in zip(asked, seen):
+            seen_ref[t, s] = total
+    for copy in copies:
         copy.wait()
 
 
-def gather_pages(owner, table, pool, lists, cap):
+def gather_pages(owner, table, lengths, pool, lists, near, cap, after=()):
     _, pair_of, kv_heads, page_len, head_dim = pool.shape
-    shape = pltpu.HBM((1, cap, pair_of, page_len, head_dim), pool.dtype)
     count = len(lists) * kv_heads
-    outs = pl.pallas_call(
-        functools.partial(gather_body, lists=lists, kv_heads=kv_heads, cap=cap),
-        out_shape=[shape] * count,
+    outs = [pltpu.VMEM((1, cap, pair_of, page_len, head_dim), pool.dtype)] * count
+    specs = [pl.BlockSpec(memory_space=pltpu.VMEM)] * count
+    if near:
+        outs.append(jax.ShapeDtypeStruct((2, near), jnp.int32))
+        specs.append(pl.BlockSpec(memory_space=pltpu.SMEM))
+    results = pl.pallas_call(
+        functools.partial(
+            gather_body, lists=lists, near=near, waits=len(after), kv_heads=kv_heads, cap=cap
+        ),
+        out_shape=outs,
         grid_spec=pltpu.PrefetchScalarGridSpec(
-            num_scalar_prefetch=2,
+            num_scalar_prefetch=3,
             grid=(1,),
-            in_specs=[pl.BlockSpec(memory_space=pltpu.HBM)],
-            out_specs=[pl.BlockSpec(memory_space=pltpu.HBM)] * count,
+            in_specs=[pl.BlockSpec(memory_space=pltpu.HBM)]
+            + [pl.BlockSpec(memory_space=pl.ANY)] * len(after),
+            out_specs=specs,
             scratch_shapes=[
-                pltpu.VMEM((len(lists), kv_heads, cap, pair_of, page_len, head_dim), pool.dtype),
                 pltpu.SMEM((len(lists) * (cap + 1),), jnp.int32),
                 pltpu.SemaphoreType.DMA((len(lists), kv_heads, cap)),
-                pltpu.SemaphoreType.DMA((len(lists), kv_heads)),
             ],
         ),
         compiler_params=pltpu.CompilerParams(vmem_limit_bytes=kernel_bytes),
         name="gather_pages",
-    )(owner, pltpu.with_memory_space_constraint(table, pltpu.HBM), pltpu.with_memory_space_constraint(pool, pltpu.HBM))
-    return [outs[i * kv_heads : (i + 1) * kv_heads] for i in range(len(lists))]
+    )(
+        owner,
+        pltpu.with_memory_space_constraint(table, pltpu.HBM),
+        pltpu.with_memory_space_constraint(lengths, pltpu.HBM),
+        pltpu.with_memory_space_constraint(pool, pltpu.HBM),
+        *after,
+    )
+    pages = [results[i * kv_heads : (i + 1) * kv_heads] for i in range(len(lists))]
+    return pages, results[-1]
 
 
 def attend_body(
@@ -440,24 +461,10 @@
     )(*args)
 
 
-def visible_counts(table, lengths, owner, steps, slot_count, page_len):
-    requests, width = table.shape
-    holders = owner ^ (2 * jnp.arange(steps, dtype=jnp.int32))
-    chosen = (owner >> 1) ^ (jnp.arange(2, dtype=jnp.int32) * steps)
-    column = jnp.arange(width, dtype=jnp.int32)
-    count = jnp.clip(lengths[:, None] - column[None, :] * page_len, 0, page_len)
-    first = holders[None, :, None, None] * slot_count
-    entry = table[None, None]
-    held = (entry >= first) & (entry < first + slot_count)
-    asked = jnp.arange(requests, dtype=jnp.int32)[None, :] == chosen[:, None]
-    picked = held & asked[:, None, :, None]
-    return jnp.sum(jnp.where(picked, count[None, None], 0), axis=(2, 3))
-
-
 def on_device(queries, new_kv, pool, block_table, prefix_len, new_slots):
     owner_count = lax.axis_size("pool")
     owner = lax.axis_index("pool").astype(jnp.int32)
-    slot_count, _, kv_heads, page_len, head_dim = pool.shape
+    _, _, kv_heads, _, head_dim = pool.shape
     tokens, q_heads, _ = queries.shape
     group = q_heads // kv_heads
     rows = tokens * group
@@ -467,16 +474,17 @@
     scale = head_dim**-0.5 * log2_e
     each = range(kv_heads)
 
+    owner_list = jnp.full((1,), owner, jnp.int32)
     split = [
         queries[:, k * group : (k + 1) * group].reshape(1, rows, head_dim) for k in each
     ]
+    new_page = new_kv.transpose(1, 2, 0, 3)
     far_own = [moved(split[k], pairs) for k in each]
     other = [moved(split[k], 1) for k in each]
-    owner_list = jnp.full((1,), owner, jnp.int32)
-    far_lists = [near + k for k in range(1, near)]
-    sent_far = gather_pages(owner_list, block_table, pool, far_lists, cap)
+    lookup = (owner_list, block_table, prefix_len, pool)
+    sent_far, _ = gather_pages(*lookup, [near + k for k in range(1, near)], 0, cap)
     rest_lists = list(range(1, near)) + [0, near]
-    pages = gather_pages(owner_list, block_table, pool, rest_lists, cap)
+    pages, seen = gather_pages(*lookup, rest_lists, near, cap, after=[new_page])
 
     def exchanged(sent):
         return [[moved(sent[i][k], 2 * (i + 1)) for i in range(near - 1)] for k in each]
@@ -484,9 +492,7 @@
     got_far = exchanged(sent_far)
     got_near = exchanged(pages)
     local, local_far = pages[near - 1 :]
-    seen = visible_counts(block_table, prefix_len, owner, near, slot_count, page_len)
     scalars = (owner_list, seen, new_slots)
-    new_page = new_kv.transpose(1, 2, 0, 3)
 
     started = []
     updated = None

time: 90.1 us -> 89.2 us (0.990)
  waiting for transfers between devices: 18.2 us -> 22.1 us
  starting transfers between devices: 24.3 us -> 22.1 us
  Pallas kernels: 43.8 us -> 42.7 us
  local copies, waits for them, and re-layouts: 2.17 us -> 1.13 us
    ppermute x16, waiting for transfers between devices: 18.2 us -> 22.1 us  [moved(): return lax.ppermute(array, 'pool', [(i, i ^ apart) for i in range(count)])]
    ppermute x16, starting transfers between devices: 24.3 us -> 22.1 us  [moved(): return lax.ppermute(array, 'pool', [(i, i ^ apart) for i in range(count)])]
    pallas_call x2, Pallas kernels: 8.31 us -> 7.07 us  [gather_pages(): pl.pallas_call(functools.partial(gather_body, lists=lists, near=near, wai...]
    unnamed x21 -> x5, local copies, waits for them, and re-layouts: 1.09 us -> 0.03 us
  transfers between devices with their start and end apart: 16 -> 16, of which waited for: 3 -> 3; matrix products, arithmetic and copies ran while one was open for 1% -> 0% of each run, Pallas kernels for 48% -> 47%
where the time goes in v4:
time: 89.2 us; the launch traced here: 88.8 us
  Pallas kernels  42.7 us (48%)
  starting transfers between devices  22.1 us (25%)
  waiting for transfers between devices  22.1 us (25%)
  local copies, waits for them, and re-layouts  1.13 us (1%)
    pallas_call x7, Pallas kernels, attend(): pl.pallas_call(functools.partial(attend_body, halves=halves, seen_at=seen...  32.5 us
    ppermute x16, starting transfers between devices, moved(): return lax.ppermute(array, 'pool', [(i, i ^ apart) for i in range(count)])  22.1 us
    ppermute x16, waiting for transfers between devices, moved(): return lax.ppermute(array, 'pool', [(i, i ^ apart) for i in range(count)])  22.1 us
    pallas_call x2, Pallas kernels, gather_pages(): pl.pallas_call(functools.partial(gather_body, lists=lists, near=near, wai...  7.07 us
    pallas_call x2, Pallas kernels, join_out(): pl.pallas_call(functools.partial(join_body, scale=scale, packs=False, wai...  2.43 us
  transfers between devices with their start and end apart: 16, of which 3 were waited for; matrix products, arithmetic and copies ran while one was open for 0% of the time, Pallas kernels for 47%

profile of v4, /device:TPU:0, one launch (start us, length us, event | category | flops | bytes accessed | tf_op | source)
XLA Modules:
  0.0 88.8 jit_solution(8508156702886848261)
XLA Ops:
  0.6 0.0 copy-start.1
  0.6 1.1 %slice_bitcast_fusion = (bf16[1,1024,128]{2,1,0:T(8,128)(2,1)S(1)}, bf16[1,1024,128]{2,1,0:T(8,128)(2,1)S(1)}) fusion(bf16[128,16,128]{2,1,0:T(8,128)(2,1)} %param.6), kind=kLoop, calls=%fused_computation | loop fusion | bytes 1048576 | tf_op jit(solution)/shard_map/reshape | solution.py:479
  1.7 3.1 %collective-permute-start.2 = (bf16[1,1024,128]{2,1,0:T(8,128)(2,1)S(1)}, bf16[1,1024,128]{2,1,0:T(8,128)(2,1)S(1)}, u32[]{:S(2)}, u32[]{:S(2)}) collective-permute-start(bf16[1,1024,128]{2,1,0:T(8,128)(2,1)S(1)} %get-tuple-element.60.refs_0_), channel_id=1, source_target_pairs={{0,2},{2,0},{4,6},{6,4},{8,10},{10,8},{12,14},{14,12},{1,3},{3,1},... | collective-permute-start | bytes 786440 | tf_op jit(solution)/shard_map/ppermute | solution.py:21
  4.8 2.5 %gather_pages.3 = (bf16[1,8,2,128,128]{4,3,2,1,0:T(8,128)(2,1)S(1)}, bf16[1,8,2,128,128]{4,3,2,1,0:T(8,128)(2,1)S(1)}) custom-call(s32[1]{0:T(128)} %bitcast.owner_ref, s32[4,64]{1,0:T(4,128)} %table_ref.3, s32[4]{0:T(128)} %length_ref.3, bf16[33,2,2,128,128]{4,3,2,1,0:T(8,128)(2,1)} %pool_ref.3), custom_call_target="tpu_custom_call" | custom-call | tf_op jit(solution)/shard_map/gather_pages/pallas_call | solution.py:118
  7.4 1.6 %collective-permute-start.8 = (bf16[1,8,2,128,128]{4,3,2,1,0:T(8,128)(2,1)S(1)}, bf16[1,8,2,128,128]{4,3,2,1,0:T(8,128)(2,1)S(1)}, u32[]{:S(2)}, u32[]{:S(2)}) collective-permute-start(bf16[1,8,2,128,128]{4,3,2,1,0:T(8,128)(2,1)S(1)} %get-tuple-element.43), channel_id=1, source_target_pairs={{0,4},{2,6},{4,0},{6,2},{8,12},{10,14},{12,8},{14,10},{1,5},{3,7},... | collective-permute-start | bytes 1572872 | tf_op jit(solution)/shard_map/ppermute | solution.py:21
  9.0 2.7 %collective-permute-start.6 = (bf16[1,1024,128]{2,1,0:T(8,128)(2,1)S(1)}, bf16[1,1024,128]{2,1,0:T(8,128)(2,1)S(1)}, u32[]{:S(2)}, u32[]{:S(2)}) collective-permute-start(bf16[1,1024,128]{2,1,0:T(8,128)(2,1)S(1)} %get-tuple-element.60.refs_0_), channel_id=1, source_target_pairs={{0,8},{2,10},{4,12},{6,14},{8,0},{10,2},{12,4},{14,6},{1,9},{3,11}... | collective-permute-start | bytes 786440 | tf_op jit(solution)/shard_map/ppermute | solution.py:21
  11.7 0.4 collective-permute-start.1
  12.1 0.3 collective-permute-start.3
  12.4 0.0 collective-permute-done.2.refs_1_
  12.4 0.5 collective-permute-start.5
  12.9 14.1 %collective-permute-done.6.refs_0_ = bf16[1,1024,128]{2,1,0:T(8,128)(2,1)S(1)} collective-permute-done((bf16[1,1024,128]{2,1,0:T(8,128)(2,1)S(1)}, bf16[1,1024,128]{2,1,0:T(8,128)(2,1)S(1)}, u32[]{:S(2)}, u32[]{:S(2)}) %collective-permute-start.6) | collective-permute-done | bytes 262176 | tf_op jit(solution)/shard_map/ppermute | solution.py:21
  27.0 0.5 collective-permute-start.7
  27.5 0.0 copy-done.1
  27.5 4.5 %gather_pages.2 = (bf16[1,8,2,128,128]{4,3,2,1,0:T(8,128)(2,1)S(1)}, bf16[1,8,2,128,128]{4,3,2,1,0:T(8,128)(2,1)S(1)}, bf16[1,8,2,128,128]{4,3,2,1,0:T(8,128)(2,...) custom-call(s32[1]{0:T(128)} %bitcast.owner_ref, ...), custom_call_target="tpu_custom_call" | custom-call | tf_op jit(solution)/shard_map/gather_pages/pallas_call | solution.py:118
  32.0 4.9 %attend.7 = (f32[1,1024,128]{2,1,0:T(8,128)S(1)}, f32[1,16,128]{2,1,0:T(8,128)S(1)}, f32[1,1024,128]{2,1,0:T(8,128)S(1)}, f32[1,16,128]{2,1,0:T(8,128)S(1)}, bf16[33,2,2,128,128]{4,3,2,1,0:T(8,128)(2,1)}) custom-call(s32[1]{0:T(128)} %bitcast.owner_ref, s32[2,2]{1,0:T(2,128)S(1)} %get-tuple-element.31.seen_ref, s32[8]{0:T(128)S(1)} %copy-done, ...), custom_call_target="tpu_custom_call" | custom-call | flops 1207959552 | bytes 589824 | tf_op jit(solution)/shard_map/attend/pallas_call | solution.py:357
  37.0 0.0 collective-permute-done.1.refs_1_.refs_0_
  37.0 3.6 %collective-permute-start.10 = (bf16[1,8,2,128,128]{4,3,2,1,0:T(8,128)(2,1)S(1)}, bf16[1,8,2,128,128]{4,3,2,1,0:T(8,128)(2,1)S(1)}, u32[]{:S(2)}, u32[]{:S(2)}) collective-permute-start(bf16[1,8,2,128,128]{4,3,2,1,0:T(8,128)(2,1)S(1)} %get-tuple-element.48), channel_id=1, source_target_pairs={{0,4},{2,6},{4,0},{6,2},{8,12},{10,14},{12,8},{14,10},{1,5},{3,7},... | collective-permute-start | bytes 1572872 | tf_op jit(solution)/shard_map/ppermute | solution.py:21
  40.6 0.0 collective-permute-done.3.refs_0_
  40.6 1.5 %collective-permute-start.4 = (bf16[1,1024,128]{2,1,0:T(8,128)(2,1)S(1)}, bf16[1,1024,128]{2,1,0:T(8,128)(2,1)S(1)}, u32[]{:S(2)}, u32[]{:S(2)}) collective-permute-start(bf16[1,1024,128]{2,1,0:T(8,128)(2,1)S(1)} %collective-permute-done.3.refs_0_), channel_id=1, source_target_pairs={{0,2},{2,0},{4,6},{6,4},{8,10},{10,8},{12,14},{14,12},{1,3},{3,1},... | collective-permute-start | bytes 786440 | tf_op jit(solution)/shard_map/ppermute | solution.py:21
  42.1 4.8 %attend.8 = (f32[1,1024,128]{2,1,0:T(8,128)S(1)}, f32[1,16,128]{2,1,0:T(8,128)S(1)}, f32[1,1024,128]{2,1,0:T(8,128)S(1)}, f32[1,16,128]{2,1,0:T(8,128)S(1)}) custom-call(s32[1]{0:T(128)} %bitcast.owner_ref, s32[2,2]{1,0:T(2,128)S(1)} %get-tuple-element.31.seen_ref, s32[8]{0:T(128)S(1)} %copy-done, bf16[1,1024,128]{2,1,0:T(8,128)(2,1)S(1)} %get-tuple-element.61.refs_0_, ...), custom_call_target="tpu_custom_call" | custom-call | flops 1207959552 | bytes 589824 | tf_op jit(solution)/shard_map/attend/pallas_call | solution.py:357
  46.9 0.0 collective-permute-done.8.refs_3_
  46.9 0.2 collective-permute-start
  47.1 0.0 collective-permute-done.7.refs_1_
  47.1 6.7 %attend.9 = (f32[1,1024,128]{2,1,0:T(8,128)S(1)}, f32[1,16,128]{2,1,0:T(8,128)S(1)}, bf16[1,1072,128]{2,1,0:T(8,128)(2,1)S(1)}) custom-call(s32[1]{0:T(128)} %bitcast.owner_ref, s32[2,2]{1,0:T(2,128)S(1)} %get-tuple-element.31.seen_ref, s32[8]{0:T(128)S(1)} %copy-done, bf16[1,1024,128]{2,1,0:T(8,128)(2,1)S(1)} %collective-permute-done.6.refs_0_, ...), custom_call_target="tpu_custom_call" | custom-call | flops 2147483648 | bytes 1048576 | tf_op jit(solution)/shard_map/attend/pallas_call | solution.py:357
  53.8 0.6 collective-permute-start.11
  54.3 0.0 collective-permute-done.5.refs_3_
  54.4 0.0 collective-permute-done.4.refs_1_
  54.4 6.8 %attend.10 = (f32[1,1024,128]{2,1,0:T(8,128)S(1)}, f32[1,16,128]{2,1,0:T(8,128)S(1)}, bf16[1,1072,128]{2,1,0:T(8,128)(2,1)S(1)}) custom-call(s32[1]{0:T(128)} %bitcast.owner_ref, s32[2,2]{1,0:T(2,128)S(1)} %get-tuple-element.31.seen_ref, s32[8]{0:T(128)S(1)} %copy-done, bf16[1,1024,128]{2,1,0:T(8,128)(2,1)S(1)} %collective-permute-done.3.refs_0_, ...), custom_call_target="tpu_custom_call" | custom-call | flops 2147483648 | bytes 1048576 | tf_op jit(solution)/shard_map/attend/pallas_call | solution.py:357
  61.2 1.6 %collective-permute-start.9 = (bf16[1,1072,128]{2,1,0:T(8,128)(2,1)S(1)}, bf16[1,1072,128]{2,1,0:T(8,128)(2,1)S(1)}, u32[]{:S(2)}, u32[]{:S(2)}) collective-permute-start(bf16[1,1072,128]{2,1,0:T(8,128)(2,1)S(1)} %get-tuple-element.47), channel_id=1, source_target_pairs={{0,2},{2,0},{4,6},{6,4},{8,10},{10,8},{12,14},{14,12},{1,3},{3,1},... | collective-permute-start | bytes 823304 | tf_op jit(solution)/shard_map/ppermute | solution.py:21
  62.8 0.0 collective-permute-done.11.refs_0_
  62.8 0.4 join_packed.2.refs_7_
  63.2 1.9 %collective-permute-start.15 = (bf16[1,1072,128]{2,1,0:T(8,128)(2,1)S(1)}, bf16[1,1072,128]{2,1,0:T(8,128)(2,1)S(1)}, u32[]{:S(2)}, u32[]{:S(2)}) collective-permute-start(bf16[1,1072,128]{2,1,0:T(8,128)(2,1)S(1)} %join_packed.2.refs_7_), channel_id=1, source_target_pairs={{0,8},{2,10},{4,12},{6,14},{8,0},{10,2},{12,4},{14,6},{1,9},{3,11}... | collective-permute-start | bytes 823304 | tf_op jit(solution)/shard_map/ppermute | solution.py:21
  65.1 0.0 collective-permute-done.10.refs_2_
  65.1 4.3 %attend.11 = (f32[1,1024,128]{2,1,0:T(8,128)S(1)}, f32[1,16,128]{2,1,0:T(8,128)S(1)}, bf16[1,1072,128]{2,1,0:T(8,128)(2,1)S(1)}) custom-call(s32[1]{0:T(128)} %bitcast.owner_ref, s32[2,2]{1,0:T(2,128)S(1)} %get-tuple-element.31.seen_ref, s32[8]{0:T(128)S(1)} %copy-done, bf16[1,1024,128]{2,1,0:T(8,128)(2,1)S(1)} %get-tuple-element.60.refs_0_, ...), custom_call_target="tpu_custom_call" | custom-call | flops 1073741824 | bytes 524288 | tf_op jit(solution)/shard_map/attend/pallas_call | solution.py:357
  69.4 0.6 collective-permute-start.14
  70.0 0.0 collective-permute-done.9.refs_0_
  70.0 0.4 join_packed.3.refs_4_
  70.3 0.0 collective-permute-done.refs_1_
  70.3 2.5 %attend.12.refs_4_ = bf16[1,1072,128]{2,1,0:T(8,128)(2,1)S(1)} custom-call(s32[1]{0:T(128)} %bitcast.owner_ref, s32[2,2]{1,0:T(2,128)S(1)} %get-tuple-element.31.seen_ref, s32[8]{0:T(128)S(1)} %copy-done, bf16[1,1024,128]{2,1,0:T(8,128)(2,1)S(1)} %collective-permute-done.1.refs_1_.refs_0_, bf16[1,8,2,128,128]{4,3,2,1,0:T(8,128)(2,1)S(1)} %collective-permute-done.refs_1_, ...), custom_call_target="tpu_custom_call" | custom-call | flops 536870912 | bytes 524288 | tf_op jit(solution)/shard_map/attend/pallas_call | solution.py:357
  72.8 1.6 %collective-permute-start.12 = (bf16[1,1072,128]{2,1,0:T(8,128)(2,1)S(1)}, bf16[1,1072,128]{2,1,0:T(8,128)(2,1)S(1)}, u32[]{:S(2)}, u32[]{:S(2)}) collective-permute-start(bf16[1,1072,128]{2,1,0:T(8,128)(2,1)S(1)} %attend.12.refs_4_), channel_id=1, source_target_pairs={{0,2},{2,0},{4,6},{6,4},{8,10},{10,8},{12,14},{14,12},{1,3},{3,1},... | collective-permute-start | bytes 823304 | tf_op jit(solution)/shard_map/ppermute | solution.py:21
  74.4 1.5 %collective-permute-start.13 = (bf16[1,1072,128]{2,1,0:T(8,128)(2,1)S(1)}, bf16[1,1072,128]{2,1,0:T(8,128)(2,1)S(1)}, u32[]{:S(2)}, u32[]{:S(2)}) collective-permute-start(bf16[1,1072,128]{2,1,0:T(8,128)(2,1)S(1)} %join_packed.3.refs_4_), channel_id=1, source_target_pairs={{0,8},{2,10},{4,12},{6,14},{8,0},{10,2},{12,4},{14,6},{1,9},{3,11}... | collective-permute-start | bytes 823304 | tf_op jit(solution)/shard_map/ppermute | solution.py:21
  75.9 2.4 %attend.13 = (f32[1,1024,128]{2,1,0:T(8,128)S(1)}, f32[1,16,128]{2,1,0:T(8,128)S(1)}) custom-call(s32[1]{0:T(128)} %bitcast.owner_ref, s32[2,2]{1,0:T(2,128)S(1)} %get-tuple-element.31.seen_ref, s32[8]{0:T(128)S(1)} %copy-done, bf16[1,1024,128]{2,1,0:T(8,128)(2,1)S(1)} %get-tuple-element.61.refs_0_, ...), custom_call_target="tpu_custom_call" | custom-call | flops 536870912 | bytes 524288 | tf_op jit(solution)/shard_map/attend/pallas_call | solution.py:357
  78.4 0.0 collective-permute-done.14.refs_0_
  78.4 2.4 %collective-permute-done.15.refs_1_ = bf16[1,1072,128]{2,1,0:T(8,128)(2,1)S(1)} collective-permute-done((bf16[1,1072,128]{2,1,0:T(8,128)(2,1)S(1)}, bf16[1,1072,128]{2,1,0:T(8,128)(2,1)S(1)}, u32[]{:S(2)}, u32[]{:S(2)}) %collective-permute-start.15) | collective-permute-done | bytes 274464 | tf_op jit(solution)/shard_map/ppermute | solution.py:21
  80.8 1.2 %join_out.2.refs_2_ = bf16[128,16,128]{2,1,0:T(8,128)(2,1)} custom-call(f32[1,1024,128]{2,1,0:T(8,128)S(1)} %get-tuple-element.57.own_mixed, f32[1,16,128]{2,1,0:T(8,128)S(1)} %get-tuple-element.54.refs_1_.own_table, bf16[1,1072,128]{2,1,0:T(8,128)(2,1)S(1)} %collective-permute-done.14.refs_0_, bf16[1,1072,128]{2,1,0:T(8,128)(2,1)S(1)} %collective-permute-done.15.refs_1_), custom_call_target="tpu_custom_call" | custom-call | tf_op jit(solution)/shard_map/join_out/pallas_call | solution.py:452
  82.0 0.0 collective-permute-done.12.refs_0_
  82.0 5.6 %collective-permute-done.13.refs_1_ = bf16[1,1072,128]{2,1,0:T(8,128)(2,1)S(1)} collective-permute-done((bf16[1,1072,128]{2,1,0:T(8,128)(2,1)S(1)}, bf16[1,1072,128]{2,1,0:T(8,128)(2,1)S(1)}, u32[]{:S(2)}, u32[]{:S(2)}) %collective-permute-start.13) | collective-permute-done | bytes 274464 | tf_op jit(solution)/shard_map/ppermute | solution.py:21
  87.6 1.2 %join_out.3 = bf16[128,16,128]{2,1,0:T(8,128)(2,1)} custom-call(f32[1,1024,128]{2,1,0:T(8,128)S(1)} %get-tuple-element.55.own_mixed, f32[1,16,128]{2,1,0:T(8,128)S(1)} %get-tuple-element.56.own_table, bf16[1,1072,128]{2,1,0:T(8,128)(2,1)S(1)} %collective-permute-done.12.refs_0_, ...), custom_call_target="tpu_custom_call", output_to_operand_aliasing={{}: (4, {})} | custom-call | tf_op jit(solution)/shard_map/join_out/pallas_call | solution.py:452
  (3 shorter events, 0.0 us)
Async XLA Ops:
  0.6 26.9 %copy-start.1 = (bf16[128,2,2,128]{3,2,1,0:T(2,128)(2,1)S(1)}, bf16[128,2,2,128]{3,2,1,0:T(2,128)(2,1)}, u32[]{:S(2)}) copy-start(bf16[128,2,2,128]{3,2,1,0:T(2,128)(2,1)} %param.7) | copy-start | bytes 393220
  1.7 10.7 %collective-permute-start.2 = (bf16[1,1024,128]{2,1,0:T(8,128)(2,1)S(1)}, bf16[1,1024,128]{2,1,0:T(8,128)(2,1)S(1)}, u32[]{:S(2)}, u32[]{:S(2)}) collective-permute-start(bf16[1,1024,128]{2,1,0:T(8,128)(2,1)S(1)} %get-tuple-element.60.refs_0_), channel_id=1, source_target_pairs={{0,2},{2,0},{4,6},{6,4},{8,10},{10,8},{12,14},{14,12},{1,3},{3,1},... | collective-permute-start | bytes 786440 | tf_op jit(solution)/shard_map/ppermute | solution.py:21
  4.8 27.2 %copy-start = (s32[8]{0:T(128)S(1)}, s32[8]{0:T(128)}, u32[]{:S(2)}) copy-start(s32[8]{0:T(128)} %fresh_ref.13) | copy-start | bytes 100
  7.4 39.6 %collective-permute-start.8 = (bf16[1,8,2,128,128]{4,3,2,1,0:T(8,128)(2,1)S(1)}, bf16[1,8,2,128,128]{4,3,2,1,0:T(8,128)(2,1)S(1)}, u32[]{:S(2)}, u32[]{:S(2)}) collective-permute-start(bf16[1,8,2,128,128]{4,3,2,1,0:T(8,128)(2,1)S(1)} %get-tuple-element.43), channel_id=1, source_target_pairs={{0,4},{2,6},{4,0},{6,2},{8,12},{10,14},{12,8},{14,10},{1,5},{3,7},... | collective-permute-start | bytes 1572872 | tf_op jit(solution)/shard_map/ppermute | solution.py:21
  9.0 18.0 %collective-permute-start.6 = (bf16[1,1024,128]{2,1,0:T(8,128)(2,1)S(1)}, bf16[1,1024,128]{2,1,0:T(8,128)(2,1)S(1)}, u32[]{:S(2)}, u32[]{:S(2)}) collective-permute-start(bf16[1,1024,128]{2,1,0:T(8,128)(2,1)S(1)} %get-tuple-element.60.refs_0_), channel_id=1, source_target_pairs={{0,8},{2,10},{4,12},{6,14},{8,0},{10,2},{12,4},{14,6},{1,9},{3,11}... | collective-permute-start | bytes 786440 | tf_op jit(solution)/shard_map/ppermute | solution.py:21
  11.7 25.3 %collective-permute-start.1 = (bf16[1,1024,128]{2,1,0:T(8,128)(2,1)S(1)}, bf16[1,1024,128]{2,1,0:T(8,128)(2,1)S(1)}, u32[]{:S(2)}, u32[]{:S(2)}) collective-permute-start(bf16[1,1024,128]{2,1,0:T(8,128)(2,1)S(1)} %get-tuple-element.61.refs_0_), channel_id=1, source_target_pairs={{0,2},{2,0},{4,6},{6,4},{8,10},{10,8},{12,14},{14,12},{1,3},{3,1},... | collective-permute-start | bytes 786440 | tf_op jit(solution)/shard_map/ppermute | solution.py:21
  12.1 28.5 %collective-permute-start.3 = (bf16[1,1024,128]{2,1,0:T(8,128)(2,1)S(1)}, bf16[1,1024,128]{2,1,0:T(8,128)(2,1)S(1)}, u32[]{:S(2)}, u32[]{:S(2)}) collective-permute-start(bf16[1,1024,128]{2,1,0:T(8,128)(2,1)S(1)} %get-tuple-element.61.refs_0_), channel_id=1, source_target_pairs={{0,8},{2,10},{4,12},{6,14},{8,0},{10,2},{12,4},{14,6},{1,9},{3,11}... | collective-permute-start | bytes 786440 | tf_op jit(solution)/shard_map/ppermute | solution.py:21
  12.4 41.9 %collective-permute-start.5 = (bf16[1,8,2,128,128]{4,3,2,1,0:T(8,128)(2,1)S(1)}, bf16[1,8,2,128,128]{4,3,2,1,0:T(8,128)(2,1)S(1)}, u32[]{:S(2)}, u32[]{:S(2)}) collective-permute-start(bf16[1,8,2,128,128]{4,3,2,1,0:T(8,128)(2,1)S(1)} %get-tuple-element.41), channel_id=1, source_target_pairs={{0,4},{2,6},{4,0},{6,2},{8,12},{10,14},{12,8},{14,10},{1,5},{3,7},... | collective-permute-start | bytes 1572872 | tf_op jit(solution)/shard_map/ppermute | solution.py:21
  27.0 20.1 %collective-permute-start.7 = (bf16[1,1024,128]{2,1,0:T(8,128)(2,1)S(1)}, bf16[1,1024,128]{2,1,0:T(8,128)(2,1)S(1)}, u32[]{:S(2)}, u32[]{:S(2)}) collective-permute-start(bf16[1,1024,128]{2,1,0:T(8,128)(2,1)S(1)} %collective-permute-done.6.refs_0_), channel_id=1, source_target_pairs={{0,2},{2,0},{4,6},{6,4},{8,10},{10,8},{12,14},{14,12},{1,3},{3,1},... | collective-permute-start | bytes 786440 | tf_op jit(solution)/shard_map/ppermute | solution.py:21
  37.0 28.1 %collective-permute-start.10 = (bf16[1,8,2,128,128]{4,3,2,1,0:T(8,128)(2,1)S(1)}, bf16[1,8,2,128,128]{4,3,2,1,0:T(8,128)(2,1)S(1)}, u32[]{:S(2)}, u32[]{:S(2)}) collective-permute-start(bf16[1,8,2,128,128]{4,3,2,1,0:T(8,128)(2,1)S(1)} %get-tuple-element.48), channel_id=1, source_target_pairs={{0,4},{2,6},{4,0},{6,2},{8,12},{10,14},{12,8},{14,10},{1,5},{3,7},... | collective-permute-start | bytes 1572872 | tf_op jit(solution)/shard_map/ppermute | solution.py:21
  40.6 13.8 %collective-permute-start.4 = (bf16[1,1024,128]{2,1,0:T(8,128)(2,1)S(1)}, bf16[1,1024,128]{2,1,0:T(8,128)(2,1)S(1)}, u32[]{:S(2)}, u32[]{:S(2)}) collective-permute-start(bf16[1,1024,128]{2,1,0:T(8,128)(2,1)S(1)} %collective-permute-done.3.refs_0_), channel_id=1, source_target_pairs={{0,2},{2,0},{4,6},{6,4},{8,10},{10,8},{12,14},{14,12},{1,3},{3,1},... | collective-permute-start | bytes 786440 | tf_op jit(solution)/shard_map/ppermute | solution.py:21
  46.9 23.4 %collective-permute-start = (bf16[1,8,2,128,128]{4,3,2,1,0:T(8,128)(2,1)S(1)}, bf16[1,8,2,128,128]{4,3,2,1,0:T(8,128)(2,1)S(1)}, u32[]{:S(2)}, u32[]{:S(2)}) collective-permute-start(bf16[1,8,2,128,128]{4,3,2,1,0:T(8,128)(2,1)S(1)} %get-tuple-element.32), channel_id=1, source_target_pairs={{0,4},{2,6},{4,0},{6,2},{8,12},{10,14},{12,8},{14,10},{1,5},{3,7},... | collective-permute-start | bytes 1572872 | tf_op jit(solution)/shard_map/ppermute | solution.py:21
  53.8 9.0 %collective-permute-start.11 = (bf16[1,1072,128]{2,1,0:T(8,128)(2,1)S(1)}, bf16[1,1072,128]{2,1,0:T(8,128)(2,1)S(1)}, u32[]{:S(2)}, u32[]{:S(2)}) collective-permute-start(bf16[1,1072,128]{2,1,0:T(8,128)(2,1)S(1)} %get-tuple-element.53), channel_id=1, source_target_pairs={{0,2},{2,0},{4,6},{6,4},{8,10},{10,8},{12,14},{14,12},{1,3},{3,1},... | collective-permute-start | bytes 823304 | tf_op jit(solution)/shard_map/ppermute | solution.py:21
  61.2 8.8 %collective-permute-start.9 = (bf16[1,1072,128]{2,1,0:T(8,128)(2,1)S(1)}, bf16[1,1072,128]{2,1,0:T(8,128)(2,1)S(1)}, u32[]{:S(2)}, u32[]{:S(2)}) collective-permute-start(bf16[1,1072,128]{2,1,0:T(8,128)(2,1)S(1)} %get-tuple-element.47), channel_id=1, source_target_pairs={{0,2},{2,0},{4,6},{6,4},{8,10},{10,8},{12,14},{14,12},{1,3},{3,1},... | collective-permute-start | bytes 823304 | tf_op jit(solution)/shard_map/ppermute | solution.py:21
  63.2 17.7 %collective-permute-start.15 = (bf16[1,1072,128]{2,1,0:T(8,128)(2,1)S(1)}, bf16[1,1072,128]{2,1,0:T(8,128)(2,1)S(1)}, u32[]{:S(2)}, u32[]{:S(2)}) collective-permute-start(bf16[1,1072,128]{2,1,0:T(8,128)(2,1)S(1)} %join_packed.2.refs_7_), channel_id=1, source_target_pairs={{0,8},{2,10},{4,12},{6,14},{8,0},{10,2},{12,4},{14,6},{1,9},{3,11}... | collective-permute-start | bytes 823304 | tf_op jit(solution)/shard_map/ppermute | solution.py:21
  69.4 9.0 %collective-permute-start.14 = (bf16[1,1072,128]{2,1,0:T(8,128)(2,1)S(1)}, bf16[1,1072,128]{2,1,0:T(8,128)(2,1)S(1)}, u32[]{:S(2)}, u32[]{:S(2)}) collective-permute-start(bf16[1,1072,128]{2,1,0:T(8,128)(2,1)S(1)} %get-tuple-element.58), channel_id=1, source_target_pairs={{0,2},{2,0},{4,6},{6,4},{8,10},{10,8},{12,14},{14,12},{1,3},{3,1},... | collective-permute-start | bytes 823304 | tf_op jit(solution)/shard_map/ppermute | solution.py:21
  72.8 9.2 %collective-permute-start.12 = (bf16[1,1072,128]{2,1,0:T(8,128)(2,1)S(1)}, bf16[1,1072,128]{2,1,0:T(8,128)(2,1)S(1)}, u32[]{:S(2)}, u32[]{:S(2)}) collective-permute-start(bf16[1,1072,128]{2,1,0:T(8,128)(2,1)S(1)} %attend.12.refs_4_), channel_id=1, source_target_pairs={{0,2},{2,0},{4,6},{6,4},{8,10},{10,8},{12,14},{14,12},{1,3},{3,1},... | collective-permute-start | bytes 823304 | tf_op jit(solution)/shard_map/ppermute | solution.py:21
  74.4 13.2 %collective-permute-start.13 = (bf16[1,1072,128]{2,1,0:T(8,128)(2,1)S(1)}, bf16[1,1072,128]{2,1,0:T(8,128)(2,1)S(1)}, u32[]{:S(2)}, u32[]{:S(2)}) collective-permute-start(bf16[1,1072,128]{2,1,0:T(8,128)(2,1)S(1)} %join_packed.3.refs_4_), channel_id=1, source_target_pairs={{0,8},{2,10},{4,12},{6,14},{8,0},{10,2},{12,4},{14,6},{1,9},{3,11}... | collective-permute-start | bytes 823304 | tf_op jit(solution)/shard_map/ppermute | solution.py:21

commit v5 on v4

--- a/solution.py
+++ b/solution.py
@@ -55,10 +55,14 @@
     return parts[0] + parts[1] + parts[2]
 
 
-def gather_body(owner_ref, table_ref, length_ref, pool_ref, *refs, lists, near, waits, kv_heads, cap):
+def last_pages(cap):
+    return max(1, cap // 4)
+
+
+def gather_body(owner_ref, table_ref, length_ref, pool_ref, *refs, lists, near, waits, ranges, cap):
     refs = refs[waits:]
-    outs = refs[: len(lists) * kv_heads]
-    seen_ref = refs[len(lists) * kv_heads] if near else None
+    outs = refs[: len(ranges)]
+    seen_ref = refs[len(ranges)] if near else None
     slots, sem = refs[-2:]
     owner = owner_ref[0]
     pair = owner >> 1
@@ -79,15 +83,14 @@
 
     found = lax.fori_loop(0, width, look, (jnp.int32(0),) * len(lists), unroll=16)
     copies = []
-    for at in range(len(lists)):
-        for k in range(kv_heads):
-            for i in range(cap):
-                slot = jnp.where(i < found[at], slots[at * (cap + 1) + i], 0)
-                copy = pltpu.make_async_copy(
-                    pool_ref.at[slot, :, k], outs[at * kv_heads + k].at[0, i], sem.at[at, k, i]
-                )
-                copy.start()
-                copies.append(copy)
+    for (at, k, begin, end), out in zip(ranges, outs):
+        for i in range(begin, end):
+            slot = jnp.where(i < found[at], slots[at * (cap + 1) + i], 0)
+            copy = pltpu.make_async_copy(
+                pool_ref.at[slot, :, k], out.at[0, i - begin], sem.at[at, k, i]
+            )
+            copy.start()
+            copies.append(copy)
     if near:
         asked = [(t, s) for t in range(2) for s in range(near)]
 
@@ -109,15 +112,24 @@
 
 def gather_pages(owner, table, lengths, pool, lists, near, cap, after=()):
     _, pair_of, kv_heads, page_len, head_dim = pool.shape
-    count = len(lists) * kv_heads
-    outs = [pltpu.VMEM((1, cap, pair_of, page_len, head_dim), pool.dtype)] * count
-    specs = [pl.BlockSpec(memory_space=pltpu.VMEM)] * count
+    ranges = []
+    for at in range(len(lists)):
+        for k in range(kv_heads):
+            cuts = [0, cap]
+            if near and at < near - 1 and k == kv_heads - 1:
+                cuts.insert(1, cap - last_pages(cap))
+            ranges += [(at, k, begin, end) for begin, end in zip(cuts, cuts[1:])]
+    outs = [
+        pltpu.VMEM((1, end - begin, pair_of, page_len, head_dim), pool.dtype)
+        for _, _, begin, end in ranges
+    ]
+    specs = [pl.BlockSpec(memory_space=pltpu.VMEM)] * len(outs)
     if near:
         outs.append(jax.ShapeDtypeStruct((2, near), jnp.int32))
         specs.append(pl.BlockSpec(memory_space=pltpu.SMEM))
     results = pl.pallas_call(
         functools.partial(
-            gather_body, lists=lists, near=near, waits=len(after), kv_heads=kv_heads, cap=cap
+            gather_body, lists=lists, near=near, waits=len(after), ranges=ranges, cap=cap
         ),
         out_shape=outs,
         grid_spec=pltpu.PrefetchScalarGridSpec(
@@ -140,7 +152,9 @@
         pltpu.with_memory_space_constraint(pool, pltpu.HBM),
         *after,
     )
-    pages = [results[i * kv_heads : (i + 1) * kv_heads] for i in range(len(lists))]
+    pages = [[[] for _ in range(kv_heads)] for _ in lists]
+    for (at, k, _, _), part in zip(ranges, results):
+        pages[at][k].append(part)
     return pages, results[-1]
 
 
@@ -215,7 +229,7 @@
     limits = []
     for s, at in enumerate(seen_at):
         position = lax.broadcasted_iota(jnp.int32, (1, keys[s]), 1)
-        limit = jnp.where(position < seen_ref[at[0], at[1]], jnp.inf, hidden_score)
+        limit = jnp.where(position + at[2] < seen_ref[at[0], at[1]], jnp.inf, hidden_score)
         limits.append(limit.astype(jnp.float32))
 
     def score(h, t):
@@ -464,7 +478,7 @@
 def on_device(queries, new_kv, pool, block_table, prefix_len, new_slots):
     owner_count = lax.axis_size("pool")
     owner = lax.axis_index("pool").astype(jnp.int32)
-    _, _, kv_heads, _, head_dim = pool.shape
+    _, _, kv_heads, page_len, head_dim = pool.shape
     tokens, q_heads, _ = queries.shape
     group = q_heads // kv_heads
     rows = tokens * group
@@ -486,12 +500,13 @@
     rest_lists = list(range(1, near)) + [0, near]
     pages, seen = gather_pages(*lookup, rest_lists, near, cap, after=[new_page])
 
-    def exchanged(sent):
-        return [[moved(sent[i][k], 2 * (i + 1)) for i in range(near - 1)] for k in each]
-
-    got_far = exchanged(sent_far)
-    got_near = exchanged(pages)
-    local, local_far = pages[near - 1 :]
+    def exchanged(sent, k, part):
+        return [moved(sent[i][k][part], 2 * (i + 1)) for i in range(near - 1)]
+
+    got_far = [exchanged(sent_far, k, 0) for k in each]
+    got_near = [exchanged(pages, k, 0) for k in each]
+    got_late = exchanged(pages, kv_heads - 1, 1)
+    local, local_far = [[part[0] for part in pages[i]] for i in (near - 1, near)]
     scalars = (owner_list, seen, new_slots)
 
     started = []
@@ -502,7 +517,7 @@
             scalars,
             [(split[k], 0), (other[k], 0)],
             [(local[k], 0)],
-            [(0, 0)],
+            [(0, 0, 0)],
             (False, False),
             scale,
             group,
@@ -522,7 +537,7 @@
             scalars,
             [(far_own[k], 0), (far_other[k], 0)],
             [(local_far[k], 0)] + [(a, 0) for a in got_far[k]],
-            [(1, i) for i in range(near)],
+            [(1, i, 0) for i in range(near)],
             (False, True),
             scale,
             group,
@@ -538,7 +553,7 @@
         back.append(moved(joined, pairs))
         mine, mine_table, theirs, theirs_table = started[k]
         near_keys = [(a, 0) for a in got_near[k]]
-        near_at = [(0, i) for i in range(1, near)]
+        near_at = [(0, i, 0) for i in range(1, near)]
         mine, theirs = (mine, mine_table, 0), (theirs, theirs_table, 0)
         if k + 1 < kv_heads:
             results = attend(
@@ -556,23 +571,37 @@
             own_part = results[:2]
             other_part = results[2]
         else:
-            (other_part,) = attend(
+            late_keys = [(a, 0) for a in got_late]
+            skipped = (cap - last_pages(cap)) * page_len
+            late_at = [(0, i, skipped) for i in range(1, near)]
+            early = attend(
                 scalars,
                 [(other[k], 0)],
                 near_keys,
                 near_at,
-                (True,),
+                (False,),
                 scale,
                 group,
                 1,
                 prev=[theirs],
                 after=[joined],
             )
+            (other_part,) = attend(
+                scalars,
+                [(other[k], 0)],
+                late_keys,
+                late_at,
+                (True,),
+                scale,
+                group,
+                1,
+                prev=[(*early, 0)],
+            )
             own_part = attend(
                 scalars,
                 [(split[k], 0)],
-                near_keys,
-                near_at,
+                near_keys + late_keys,
+                near_at + late_at,
                 (False,),
                 scale,
                 group,

time: 89.2 us -> 89.6 us (level)
  waiting for transfers between devices: 22.1 us -> 20 us
  starting transfers between devices: 22.1 us -> 23.6 us
  Pallas kernels: 42.7 us -> 43.7 us
    ppermute x16 -> x17, waiting for transfers between devices: 22.1 us -> 20 us  [moved(): return lax.ppermute(array, 'pool', [(i, i ^ apart) for i in range(count)])]
    ppermute x16 -> x17, starting transfers between devices: 22.1 us -> 23.6 us  [moved(): return lax.ppermute(array, 'pool', [(i, i ^ apart) for i in range(count)])]
    pallas_call x7 -> x8, Pallas kernels: 32.5 us -> 33.5 us  [attend(): pl.pallas_call(functools.partial(attend_body, halves=halves, seen_at=seen...]
  transfers between devices with their start and end apart: 16 -> 17, of which waited for: 3 -> 3; matrix products, arithmetic and copies ran while one was open for 0% -> 0% of each run, Pallas kernels for 47% -> 48%
where the time goes in v5:
time: 89.6 us; the launch traced here: 89.3 us
  Pallas kernels  43.7 us (49%)
  starting transfers between devices  23.6 us (26%)
  waiting for transfers between devices  20 us (22%)
  local copies, waits for them, and re-layouts  1.13 us (1%)
    pallas_call x8, Pallas kernels, attend(): pl.pallas_call(functools.partial(attend_body, halves=halves, seen_at=seen...  33.5 us
    ppermute x17, starting transfers between devices, moved(): return lax.ppermute(array, 'pool', [(i, i ^ apart) for i in range(count)])  23.6 us
    ppermute x17, waiting for transfers between devices, moved(): return lax.ppermute(array, 'pool', [(i, i ^ apart) for i in range(count)])  20 us
    pallas_call x2, Pallas kernels, gather_pages(): pl.pallas_call(functools.partial(gather_body, lists=lists, near=near, wai...  7.07 us
    pallas_call x2, Pallas kernels, join_out(): pl.pallas_call(functools.partial(join_body, scale=scale, packs=False, wai...  2.43 us
  transfers between devices with their start and end apart: 17, of which 3 were waited for; matrix products, arithmetic and copies ran while one was open for 0% of the time, Pallas kernels for 48%

profile of v5, /device:TPU:0, one launch (start us, length us, event | category | flops | bytes accessed | tf_op | source)
XLA Modules:
  0.0 89.3 jit_solution(3076960601312767576)
XLA Ops:
  0.6 1.1 %slice_bitcast_fusion = (bf16[1,1024,128]{2,1,0:T(8,128)(2,1)S(1)}, bf16[1,1024,128]{2,1,0:T(8,128)(2,1)S(1)}) fusion(bf16[128,16,128]{2,1,0:T(8,128)(2,1)} %param.6), kind=kLoop, calls=%fused_computation | loop fusion | bytes 1048576 | tf_op jit(solution)/shard_map/reshape | solution.py:493
  1.7 3.1 %collective-permute-start.3 = (bf16[1,1024,128]{2,1,0:T(8,128)(2,1)S(1)}, bf16[1,1024,128]{2,1,0:T(8,128)(2,1)S(1)}, u32[]{:S(2)}, u32[]{:S(2)}) collective-permute-start(bf16[1,1024,128]{2,1,0:T(8,128)(2,1)S(1)} %get-tuple-element.66.refs_0_), channel_id=1, source_target_pairs={{0,2},{2,0},{4,6},{6,4},{8,10},{10,8},{12,14},{14,12},{1,3},{3,1},... | collective-permute-start | bytes 786440 | tf_op jit(solution)/shard_map/ppermute | solution.py:21
  4.8 2.5 %gather_pages.3 = (bf16[1,8,2,128,128]{4,3,2,1,0:T(8,128)(2,1)S(1)}, bf16[1,8,2,128,128]{4,3,2,1,0:T(8,128)(2,1)S(1)}) custom-call(s32[1]{0:T(128)} %bitcast.owner_ref, s32[4,64]{1,0:T(4,128)} %table_ref.3, s32[4]{0:T(128)} %length_ref.3, bf16[33,2,2,128,128]{4,3,2,1,0:T(8,128)(2,1)} %pool_ref.3), custom_call_target="tpu_custom_call" | custom-call | tf_op jit(solution)/shard_map/gather_pages/pallas_call | solution.py:130
  7.4 1.6 %collective-permute-start.9 = (bf16[1,8,2,128,128]{4,3,2,1,0:T(8,128)(2,1)S(1)}, bf16[1,8,2,128,128]{4,3,2,1,0:T(8,128)(2,1)S(1)}, u32[]{:S(2)}, u32[]{:S(2)}) collective-permute-start(bf16[1,8,2,128,128]{4,3,2,1,0:T(8,128)(2,1)S(1)} %get-tuple-element.47), channel_id=1, source_target_pairs={{0,4},{2,6},{4,0},{6,2},{8,12},{10,14},{12,8},{14,10},{1,5},{3,7},... | collective-permute-start | bytes 1572872 | tf_op jit(solution)/shard_map/ppermute | solution.py:21
  9.0 2.7 %collective-permute-start.7 = (bf16[1,1024,128]{2,1,0:T(8,128)(2,1)S(1)}, bf16[1,1024,128]{2,1,0:T(8,128)(2,1)S(1)}, u32[]{:S(2)}, u32[]{:S(2)}) collective-permute-start(bf16[1,1024,128]{2,1,0:T(8,128)(2,1)S(1)} %get-tuple-element.66.refs_0_), channel_id=1, source_target_pairs={{0,8},{2,10},{4,12},{6,14},{8,0},{10,2},{12,4},{14,6},{1,9},{3,11}... | collective-permute-start | bytes 786440 | tf_op jit(solution)/shard_map/ppermute | solution.py:21
  11.7 0.4 collective-permute-start.2
  12.1 0.3 collective-permute-start.4
  12.4 0.0 collective-permute-done.3.refs_1_
  12.4 0.5 collective-permute-start.6
  12.9 14.1 %collective-permute-done.7.refs_0_ = bf16[1,1024,128]{2,1,0:T(8,128)(2,1)S(1)} collective-permute-done((bf16[1,1024,128]{2,1,0:T(8,128)(2,1)S(1)}, bf16[1,1024,128]{2,1,0:T(8,128)(2,1)S(1)}, u32[]{:S(2)}, u32[]{:S(2)}) %collective-permute-start.7) | collective-permute-done | bytes 262176 | tf_op jit(solution)/shard_map/ppermute | solution.py:21
  27.0 0.5 collective-permute-start.8
  27.5 4.5 %gather_pages.2 = (bf16[1,8,2,128,128]{4,3,2,1,0:T(8,128)(2,1)S(1)}, bf16[1,6,2,128,128]{4,3,2,1,0:T(8,128)(2,1)S(1)}, bf16[1,2,2,128,128]{4,3,2,1,0:T(8,128)(2,...) custom-call(s32[1]{0:T(128)} %bitcast.owner_ref, ...), custom_call_target="tpu_custom_call" | custom-call | tf_op jit(solution)/shard_map/gather_pages/pallas_call | solution.py:130
  32.1 4.9 %attend.8 = (f32[1,1024,128]{2,1,0:T(8,128)S(1)}, f32[1,16,128]{2,1,0:T(8,128)S(1)}, f32[1,1024,128]{2,1,0:T(8,128)S(1)}, f32[1,16,128]{2,1,0:T(8,128)S(1)}, bf16[33,2,2,128,128]{4,3,2,1,0:T(8,128)(2,1)}) custom-call(s32[1]{0:T(128)} %bitcast.owner_ref, s32[2,2]{1,0:T(2,128)S(1)} %get-tuple-element.34.seen_ref, s32[8]{0:T(128)S(1)} %copy-done, ...), custom_call_target="tpu_custom_call" | custom-call | flops 1207959552 | bytes 589824 | tf_op jit(solution)/shard_map/attend/pallas_call | solution.py:371
  37.0 0.0 collective-permute-done.2.refs_1_.refs_0_
  37.0 3.6 %collective-permute-start.11 = (bf16[1,8,2,128,128]{4,3,2,1,0:T(8,128)(2,1)S(1)}, bf16[1,8,2,128,128]{4,3,2,1,0:T(8,128)(2,1)S(1)}, u32[]{:S(2)}, u32[]{:S(2)}) collective-permute-start(bf16[1,8,2,128,128]{4,3,2,1,0:T(8,128)(2,1)S(1)} %get-tuple-element.52), channel_id=1, source_target_pairs={{0,4},{2,6},{4,0},{6,2},{8,12},{10,14},{12,8},{14,10},{1,5},{3,7},... | collective-permute-start | bytes 1572872 | tf_op jit(solution)/shard_map/ppermute | solution.py:21
  40.6 0.0 collective-permute-done.4.refs_0_
  40.6 1.5 %collective-permute-start.5 = (bf16[1,1024,128]{2,1,0:T(8,128)(2,1)S(1)}, bf16[1,1024,128]{2,1,0:T(8,128)(2,1)S(1)}, u32[]{:S(2)}, u32[]{:S(2)}) collective-permute-start(bf16[1,1024,128]{2,1,0:T(8,128)(2,1)S(1)} %collective-permute-done.4.refs_0_), channel_id=1, source_target_pairs={{0,2},{2,0},{4,6},{6,4},{8,10},{10,8},{12,14},{14,12},{1,3},{3,1},... | collective-permute-start | bytes 786440 | tf_op jit(solution)/shard_map/ppermute | solution.py:21
  42.1 4.8 %attend.9 = (f32[1,1024,128]{2,1,0:T(8,128)S(1)}, f32[1,16,128]{2,1,0:T(8,128)S(1)}, f32[1,1024,128]{2,1,0:T(8,128)S(1)}, f32[1,16,128]{2,1,0:T(8,128)S(1)}) custom-call(s32[1]{0:T(128)} %bitcast.owner_ref, s32[2,2]{1,0:T(2,128)S(1)} %get-tuple-element.34.seen_ref, s32[8]{0:T(128)S(1)} %copy-done, bf16[1,1024,128]{2,1,0:T(8,128)(2,1)S(1)} %get-tuple-element.67.refs_0_, ...), custom_call_target="tpu_custom_call" | custom-call | flops 1207959552 | bytes 589824 | tf_op jit(solution)/shard_map/attend/pallas_call | solution.py:371
  46.9 0.0 collective-permute-done.9.refs_3_
  46.9 0.1 collective-permute-start
  47.1 0.0 collective-permute-done.8.refs_1_
  47.1 6.7 %attend.10 = (f32[1,1024,128]{2,1,0:T(8,128)S(1)}, f32[1,16,128]{2,1,0:T(8,128)S(1)}, bf16[1,1072,128]{2,1,0:T(8,128)(2,1)S(1)}) custom-call(s32[1]{0:T(128)} %bitcast.owner_ref, s32[2,2]{1,0:T(2,128)S(1)} %get-tuple-element.34.seen_ref, s32[8]{0:T(128)S(1)} %copy-done, bf16[1,1024,128]{2,1,0:T(8,128)(2,1)S(1)} %collective-permute-done.7.refs_0_, ...), custom_call_target="tpu_custom_call" | custom-call | flops 2147483648 | bytes 1048576 | tf_op jit(solution)/shard_map/attend/pallas_call | solution.py:371
  53.8 0.6 collective-permute-start.12
  54.4 0.0 collective-permute-done.6.refs_3_
  54.4 0.0 collective-permute-done.5.refs_1_
  54.4 6.9 %attend.11 = (f32[1,1024,128]{2,1,0:T(8,128)S(1)}, f32[1,16,128]{2,1,0:T(8,128)S(1)}, bf16[1,1072,128]{2,1,0:T(8,128)(2,1)S(1)}) custom-call(s32[1]{0:T(128)} %bitcast.owner_ref, s32[2,2]{1,0:T(2,128)S(1)} %get-tuple-element.34.seen_ref, s32[8]{0:T(128)S(1)} %copy-done, bf16[1,1024,128]{2,1,0:T(8,128)(2,1)S(1)} %collective-permute-done.4.refs_0_, ...), custom_call_target="tpu_custom_call" | custom-call | flops 2147483648 | bytes 1048576 | tf_op jit(solution)/shard_map/attend/pallas_call | solution.py:371
  61.2 1.6 %collective-permute-start.10 = (bf16[1,1072,128]{2,1,0:T(8,128)(2,1)S(1)}, bf16[1,1072,128]{2,1,0:T(8,128)(2,1)S(1)}, u32[]{:S(2)}, u32[]{:S(2)}) collective-permute-start(bf16[1,1072,128]{2,1,0:T(8,128)(2,1)S(1)} %get-tuple-element.51), channel_id=1, source_target_pairs={{0,2},{2,0},{4,6},{6,4},{8,10},{10,8},{12,14},{14,12},{1,3},{3,1},... | collective-permute-start | bytes 823304 | tf_op jit(solution)/shard_map/ppermute | solution.py:21
  62.8 1.9 %collective-permute-start.1 = (bf16[1,2,2,128,128]{4,3,2,1,0:T(8,128)(2,1)S(1)}, bf16[1,2,2,128,128]{4,3,2,1,0:T(8,128)(2,1)S(1)}, u32[]{:S(2)}, u32[]{:S(2)}) collective-permute-start(bf16[1,2,2,128,128]{4,3,2,1,0:T(8,128)(2,1)S(1)} %get-tuple-element.36), channel_id=1, source_target_pairs={{0,4},{2,6},{4,0},{6,2},{8,12},{10,14},{12,8},{14,10},{1,5},{3,7},... | collective-permute-start | bytes 393224 | tf_op jit(solution)/shard_map/ppermute | solution.py:21
  64.8 0.0 collective-permute-done.12.refs_0_
  64.8 0.4 join_packed.2.refs_7_
  65.1 0.1 collective-permute-start.16
  65.2 0.0 collective-permute-done.11.refs_2_
  65.2 4.3 %attend.12 = (f32[1,1024,128]{2,1,0:T(8,128)S(1)}, f32[1,16,128]{2,1,0:T(8,128)S(1)}, bf16[1,1072,128]{2,1,0:T(8,128)(2,1)S(1)}) custom-call(s32[1]{0:T(128)} %bitcast.owner_ref, s32[2,2]{1,0:T(2,128)S(1)} %get-tuple-element.34.seen_ref, s32[8]{0:T(128)S(1)} %copy-done, bf16[1,1024,128]{2,1,0:T(8,128)(2,1)S(1)} %get-tuple-element.66.refs_0_, ...), custom_call_target="tpu_custom_call" | custom-call | flops 1073741824 | bytes 524288 | tf_op jit(solution)/shard_map/attend/pallas_call | solution.py:371
  69.5 0.6 collective-permute-start.15
  70.1 0.0 collective-permute-done.10.refs_0_
  70.1 0.4 join_packed.3.refs_4_
  70.5 0.0 collective-permute-done.refs_1_
  70.5 2.1 %attend.13 = (f32[1,1024,128]{2,1,0:T(8,128)S(1)}, f32[1,16,128]{2,1,0:T(8,128)S(1)}) custom-call(s32[1]{0:T(128)} %bitcast.owner_ref, s32[2,2]{1,0:T(2,128)S(1)} %get-tuple-element.34.seen_ref, s32[8]{0:T(128)S(1)} %copy-done, bf16[1,1024,128]{2,1,0:T(8,128)(2,1)S(1)} %collective-permute-done.2.refs_1_.refs_0_, ...), custom_call_target="tpu_custom_call" | custom-call | flops 402653184 | bytes 393216 | tf_op jit(solution)/shard_map/attend/pallas_call | solution.py:371
  72.6 1.4 %attend.14.refs_5_ = bf16[1,1072,128]{2,1,0:T(8,128)(2,1)S(1)} custom-call(s32[1]{0:T(128)} %bitcast.owner_ref, s32[2,2]{1,0:T(2,128)S(1)} %get-tuple-element.34.seen_ref, s32[8]{0:T(128)S(1)} %copy-done, bf16[1,1024,128]{2,1,0:T(8,128)(2,1)S(1)} %collective-permute-done.2.refs_1_.refs_0_, ...), custom_call_target="tpu_custom_call" | custom-call | flops 134217728 | bytes 131072 | tf_op jit(solution)/shard_map/attend/pallas_call | solution.py:371
  74.0 1.6 %collective-permute-start.13 = (bf16[1,1072,128]{2,1,0:T(8,128)(2,1)S(1)}, bf16[1,1072,128]{2,1,0:T(8,128)(2,1)S(1)}, u32[]{:S(2)}, u32[]{:S(2)}) collective-permute-start(bf16[1,1072,128]{2,1,0:T(8,128)(2,1)S(1)} %attend.14.refs_5_), channel_id=1, source_target_pairs={{0,2},{2,0},{4,6},{6,4},{8,10},{10,8},{12,14},{14,12},{1,3},{3,1},... | collective-permute-start | bytes 823304 | tf_op jit(solution)/shard_map/ppermute | solution.py:21
  75.6 2.9 %collective-permute-start.14 = (bf16[1,1072,128]{2,1,0:T(8,128)(2,1)S(1)}, bf16[1,1072,128]{2,1,0:T(8,128)(2,1)S(1)}, u32[]{:S(2)}, u32[]{:S(2)}) collective-permute-start(bf16[1,1072,128]{2,1,0:T(8,128)(2,1)S(1)} %join_packed.3.refs_4_), channel_id=1, source_target_pairs={{0,8},{2,10},{4,12},{6,14},{8,0},{10,2},{12,4},{14,6},{1,9},{3,11}... | collective-permute-start | bytes 823304 | tf_op jit(solution)/shard_map/ppermute | solution.py:21
  78.5 2.4 %attend.15 = (f32[1,1024,128]{2,1,0:T(8,128)S(1)}, f32[1,16,128]{2,1,0:T(8,128)S(1)}) custom-call(s32[1]{0:T(128)} %bitcast.owner_ref, s32[2,2]{1,0:T(2,128)S(1)} %get-tuple-element.34.seen_ref, s32[8]{0:T(128)S(1)} %copy-done, bf16[1,1024,128]{2,1,0:T(8,128)(2,1)S(1)} %get-tuple-element.67.refs_0_, ...), custom_call_target="tpu_custom_call" | custom-call | flops 536870912 | bytes 524288 | tf_op jit(solution)/shard_map/attend/pallas_call | solution.py:371
  80.9 0.0 collective-permute-done.15.refs_0_
  80.9 3.8 %collective-permute-done.16.refs_1_ = bf16[1,1072,128]{2,1,0:T(8,128)(2,1)S(1)} collective-permute-done((bf16[1,1072,128]{2,1,0:T(8,128)(2,1)S(1)}, bf16[1,1072,128]{2,1,0:T(8,128)(2,1)S(1)}, u32[]{:S(2)}, u32[]{:S(2)}) %collective-permute-start.16) | collective-permute-done | bytes 274464 | tf_op jit(solution)/shard_map/ppermute | solution.py:21
  84.7 1.2 %join_out.2.refs_2_ = bf16[128,16,128]{2,1,0:T(8,128)(2,1)} custom-call(f32[1,1024,128]{2,1,0:T(8,128)S(1)} %get-tuple-element.63.own_mixed, f32[1,16,128]{2,1,0:T(8,128)S(1)} %get-tuple-element.58.refs_1_.own_table, bf16[1,1072,128]{2,1,0:T(8,128)(2,1)S(1)} %collective-permute-done.15.refs_0_, bf16[1,1072,128]{2,1,0:T(8,128)(2,1)S(1)} %collective-permute-done.16.refs_1_), custom_call_target="tpu_custom_call" | custom-call | tf_op jit(solution)/shard_map/join_out/pallas_call | solution.py:466
  85.9 0.0 collective-permute-done.13.refs_0_
  85.9 2.2 %collective-permute-done.14.refs_1_ = bf16[1,1072,128]{2,1,0:T(8,128)(2,1)S(1)} collective-permute-done((bf16[1,1072,128]{2,1,0:T(8,128)(2,1)S(1)}, bf16[1,1072,128]{2,1,0:T(8,128)(2,1)S(1)}, u32[]{:S(2)}, u32[]{:S(2)}) %collective-permute-start.14) | collective-permute-done | bytes 274464 | tf_op jit(solution)/shard_map/ppermute | solution.py:21
  88.0 1.2 %join_out.3 = bf16[128,16,128]{2,1,0:T(8,128)(2,1)} custom-call(f32[1,1024,128]{2,1,0:T(8,128)S(1)} %get-tuple-element.61.own_mixed, f32[1,16,128]{2,1,0:T(8,128)S(1)} %get-tuple-element.62.own_table, bf16[1,1072,128]{2,1,0:T(8,128)(2,1)S(1)} %collective-permute-done.13.refs_0_, ...), custom_call_target="tpu_custom_call", output_to_operand_aliasing={{}: (4, {})} | custom-call | tf_op jit(solution)/shard_map/join_out/pallas_call | solution.py:466
  (6 shorter events, 0.0 us)
Async XLA Ops:
  0.6 26.9 %copy-start.1 = (bf16[128,2,2,128]{3,2,1,0:T(2,128)(2,1)S(1)}, bf16[128,2,2,128]{3,2,1,0:T(2,128)(2,1)}, u32[]{:S(2)}) copy-start(bf16[128,2,2,128]{3,2,1,0:T(2,128)(2,1)} %param.7) | copy-start | bytes 393220
  1.7 10.7 %collective-permute-start.3 = (bf16[1,1024,128]{2,1,0:T(8,128)(2,1)S(1)}, bf16[1,1024,128]{2,1,0:T(8,128)(2,1)S(1)}, u32[]{:S(2)}, u32[]{:S(2)}) collective-permute-start(bf16[1,1024,128]{2,1,0:T(8,128)(2,1)S(1)} %get-tuple-element.66.refs_0_), channel_id=1, source_target_pairs={{0,2},{2,0},{4,6},{6,4},{8,10},{10,8},{12,14},{14,12},{1,3},{3,1},... | collective-permute-start | bytes 786440 | tf_op jit(solution)/shard_map/ppermute | solution.py:21
  4.8 27.2 %copy-start = (s32[8]{0:T(128)S(1)}, s32[8]{0:T(128)}, u32[]{:S(2)}) copy-start(s32[8]{0:T(128)} %fresh_ref.15) | copy-start | bytes 100
  7.4 39.6 %collective-permute-start.9 = (bf16[1,8,2,128,128]{4,3,2,1,0:T(8,128)(2,1)S(1)}, bf16[1,8,2,128,128]{4,3,2,1,0:T(8,128)(2,1)S(1)}, u32[]{:S(2)}, u32[]{:S(2)}) collective-permute-start(bf16[1,8,2,128,128]{4,3,2,1,0:T(8,128)(2,1)S(1)} %get-tuple-element.47), channel_id=1, source_target_pairs={{0,4},{2,6},{4,0},{6,2},{8,12},{10,14},{12,8},{14,10},{1,5},{3,7},... | collective-permute-start | bytes 1572872 | tf_op jit(solution)/shard_map/ppermute | solution.py:21
  9.0 18.0 %collective-permute-start.7 = (bf16[1,1024,128]{2,1,0:T(8,128)(2,1)S(1)}, bf16[1,1024,128]{2,1,0:T(8,128)(2,1)S(1)}, u32[]{:S(2)}, u32[]{:S(2)}) collective-permute-start(bf16[1,1024,128]{2,1,0:T(8,128)(2,1)S(1)} %get-tuple-element.66.refs_0_), channel_id=1, source_target_pairs={{0,8},{2,10},{4,12},{6,14},{8,0},{10,2},{12,4},{14,6},{1,9},{3,11}... | collective-permute-start | bytes 786440 | tf_op jit(solution)/shard_map/ppermute | solution.py:21
  11.7 25.3 %collective-permute-start.2 = (bf16[1,1024,128]{2,1,0:T(8,128)(2,1)S(1)}, bf16[1,1024,128]{2,1,0:T(8,128)(2,1)S(1)}, u32[]{:S(2)}, u32[]{:S(2)}) collective-permute-start(bf16[1,1024,128]{2,1,0:T(8,128)(2,1)S(1)} %get-tuple-element.67.refs_0_), channel_id=1, source_target_pairs={{0,2},{2,0},{4,6},{6,4},{8,10},{10,8},{12,14},{14,12},{1,3},{3,1},... | collective-permute-start | bytes 786440 | tf_op jit(solution)/shard_map/ppermute | solution.py:21
  12.1 28.5 %collective-permute-start.4 = (bf16[1,1024,128]{2,1,0:T(8,128)(2,1)S(1)}, bf16[1,1024,128]{2,1,0:T(8,128)(2,1)S(1)}, u32[]{:S(2)}, u32[]{:S(2)}) collective-permute-start(bf16[1,1024,128]{2,1,0:T(8,128)(2,1)S(1)} %get-tuple-element.67.refs_0_), channel_id=1, source_target_pairs={{0,8},{2,10},{4,12},{6,14},{8,0},{10,2},{12,4},{14,6},{1,9},{3,11}... | collective-permute-start | bytes 786440 | tf_op jit(solution)/shard_map/ppermute | solution.py:21
  12.4 41.9 %collective-permute-start.6 = (bf16[1,8,2,128,128]{4,3,2,1,0:T(8,128)(2,1)S(1)}, bf16[1,8,2,128,128]{4,3,2,1,0:T(8,128)(2,1)S(1)}, u32[]{:S(2)}, u32[]{:S(2)}) collective-permute-start(bf16[1,8,2,128,128]{4,3,2,1,0:T(8,128)(2,1)S(1)} %get-tuple-element.45), channel_id=1, source_target_pairs={{0,4},{2,6},{4,0},{6,2},{8,12},{10,14},{12,8},{14,10},{1,5},{3,7},... | collective-permute-start | bytes 1572872 | tf_op jit(solution)/shard_map/ppermute | solution.py:21
  27.0 20.1 %collective-permute-start.8 = (bf16[1,1024,128]{2,1,0:T(8,128)(2,1)S(1)}, bf16[1,1024,128]{2,1,0:T(8,128)(2,1)S(1)}, u32[]{:S(2)}, u32[]{:S(2)}) collective-permute-start(bf16[1,1024,128]{2,1,0:T(8,128)(2,1)S(1)} %collective-permute-done.7.refs_0_), channel_id=1, source_target_pairs={{0,2},{2,0},{4,6},{6,4},{8,10},{10,8},{12,14},{14,12},{1,3},{3,1},... | collective-permute-start | bytes 786440 | tf_op jit(solution)/shard_map/ppermute | solution.py:21
  37.0 28.2 %collective-permute-start.11 = (bf16[1,8,2,128,128]{4,3,2,1,0:T(8,128)(2,1)S(1)}, bf16[1,8,2,128,128]{4,3,2,1,0:T(8,128)(2,1)S(1)}, u32[]{:S(2)}, u32[]{:S(2)}) collective-permute-start(bf16[1,8,2,128,128]{4,3,2,1,0:T(8,128)(2,1)S(1)} %get-tuple-element.52), channel_id=1, source_target_pairs={{0,4},{2,6},{4,0},{6,2},{8,12},{10,14},{12,8},{14,10},{1,5},{3,7},... | collective-permute-start | bytes 1572872 | tf_op jit(solution)/shard_map/ppermute | solution.py:21
  40.6 13.8 %collective-permute-start.5 = (bf16[1,1024,128]{2,1,0:T(8,128)(2,1)S(1)}, bf16[1,1024,128]{2,1,0:T(8,128)(2,1)S(1)}, u32[]{:S(2)}, u32[]{:S(2)}) collective-permute-start(bf16[1,1024,128]{2,1,0:T(8,128)(2,1)S(1)} %collective-permute-done.4.refs_0_), channel_id=1, source_target_pairs={{0,2},{2,0},{4,6},{6,4},{8,10},{10,8},{12,14},{14,12},{1,3},{3,1},... | collective-permute-start | bytes 786440 | tf_op jit(solution)/shard_map/ppermute | solution.py:21
  46.9 23.5 %collective-permute-start = (bf16[1,6,2,128,128]{4,3,2,1,0:T(8,128)(2,1)S(1)}, bf16[1,6,2,128,128]{4,3,2,1,0:T(8,128)(2,1)S(1)}, u32[]{:S(2)}, u32[]{:S(2)}) collective-permute-start(bf16[1,6,2,128,128]{4,3,2,1,0:T(8,128)(2,1)S(1)} %get-tuple-element.35), channel_id=1, source_target_pairs={{0,4},{2,6},{4,0},{6,2},{8,12},{10,14},{12,8},{14,10},{1,5},{3,7},... | collective-permute-start | bytes 1179656 | tf_op jit(solution)/shard_map/ppermute | solution.py:21
  53.8 11.0 %collective-permute-start.12 = (bf16[1,1072,128]{2,1,0:T(8,128)(2,1)S(1)}, bf16[1,1072,128]{2,1,0:T(8,128)(2,1)S(1)}, u32[]{:S(2)}, u32[]{:S(2)}) collective-permute-start(bf16[1,1072,128]{2,1,0:T(8,128)(2,1)S(1)} %get-tuple-element.57), channel_id=1, source_target_pairs={{0,2},{2,0},{4,6},{6,4},{8,10},{10,8},{12,14},{14,12},{1,3},{3,1},... | collective-permute-start | bytes 823304 | tf_op jit(solution)/shard_map/ppermute | solution.py:21
  61.2 8.9 %collective-permute-start.10 = (bf16[1,1072,128]{2,1,0:T(8,128)(2,1)S(1)}, bf16[1,1072,128]{2,1,0:T(8,128)(2,1)S(1)}, u32[]{:S(2)}, u32[]{:S(2)}) collective-permute-start(bf16[1,1072,128]{2,1,0:T(8,128)(2,1)S(1)} %get-tuple-element.51), channel_id=1, source_target_pairs={{0,2},{2,0},{4,6},{6,4},{8,10},{10,8},{12,14},{14,12},{1,3},{3,1},... | collective-permute-start | bytes 823304 | tf_op jit(solution)/shard_map/ppermute | solution.py:21
  62.8 9.8 %collective-permute-start.1 = (bf16[1,2,2,128,128]{4,3,2,1,0:T(8,128)(2,1)S(1)}, bf16[1,2,2,128,128]{4,3,2,1,0:T(8,128)(2,1)S(1)}, u32[]{:S(2)}, u32[]{:S(2)}) collective-permute-start(bf16[1,2,2,128,128]{4,3,2,1,0:T(8,128)(2,1)S(1)} %get-tuple-element.36), channel_id=1, source_target_pairs={{0,4},{2,6},{4,0},{6,2},{8,12},{10,14},{12,8},{14,10},{1,5},{3,7},... | collective-permute-start | bytes 393224 | tf_op jit(solution)/shard_map/ppermute | solution.py:21
  65.1 19.5 %collective-permute-start.16 = (bf16[1,1072,128]{2,1,0:T(8,128)(2,1)S(1)}, bf16[1,1072,128]{2,1,0:T(8,128)(2,1)S(1)}, u32[]{:S(2)}, u32[]{:S(2)}) collective-permute-start(bf16[1,1072,128]{2,1,0:T(8,128)(2,1)S(1)} %join_packed.2.refs_7_), channel_id=1, source_target_pairs={{0,8},{2,10},{4,12},{6,14},{8,0},{10,2},{12,4},{14,6},{1,9},{3,11}... | collective-permute-start | bytes 823304 | tf_op jit(solution)/shard_map/ppermute | solution.py:21
  69.5 11.3 %collective-permute-start.15 = (bf16[1,1072,128]{2,1,0:T(8,128)(2,1)S(1)}, bf16[1,1072,128]{2,1,0:T(8,128)(2,1)S(1)}, u32[]{:S(2)}, u32[]{:S(2)}) collective-permute-start(bf16[1,1072,128]{2,1,0:T(8,128)(2,1)S(1)} %get-tuple-element.64), channel_id=1, source_target_pairs={{0,2},{2,0},{4,6},{6,4},{8,10},{10,8},{12,14},{14,12},{1,3},{3,1},... | collective-permute-start | bytes 823304 | tf_op jit(solution)/shard_map/ppermute | solution.py:21
  74.0 11.9 %collective-permute-start.13 = (bf16[1,1072,128]{2,1,0:T(8,128)(2,1)S(1)}, bf16[1,1072,128]{2,1,0:T(8,128)(2,1)S(1)}, u32[]{:S(2)}, u32[]{:S(2)}) collective-permute-start(bf16[1,1072,128]{2,1,0:T(8,128)(2,1)S(1)} %attend.14.refs_5_), channel_id=1, source_target_pairs={{0,2},{2,0},{4,6},{6,4},{8,10},{10,8},{12,14},{14,12},{1,3},{3,1},... | collective-permute-start | bytes 823304 | tf_op jit(solution)/shard_map/ppermute | solution.py:21
  75.6 12.5 %collective-permute-start.14 = (bf16[1,1072,128]{2,1,0:T(8,128)(2,1)S(1)}, bf16[1,1072,128]{2,1,0:T(8,128)(2,1)S(1)}, u32[]{:S(2)}, u32[]{:S(2)}) collective-permute-start(bf16[1,1072,128]{2,1,0:T(8,128)(2,1)S(1)} %join_packed.3.refs_4_), channel_id=1, source_target_pairs={{0,8},{2,10},{4,12},{6,14},{8,0},{10,2},{12,4},{14,6},{1,9},{3,11}... | collective-permute-start | bytes 823304 | tf_op jit(solution)/shard_map/ppermute | solution.py:21

commit v6 on v5

--- a/solution.py
+++ b/solution.py
@@ -59,11 +59,12 @@
     return max(1, cap // 4)
 
 
-def gather_body(owner_ref, table_ref, length_ref, pool_ref, *refs, lists, near, waits, ranges, cap):
+def gather_body(owner_ref, table_ref, length_ref, pool_ref, *refs, near, waits, ranges, cap):
     refs = refs[waits:]
     outs = refs[: len(ranges)]
     seen_ref = refs[len(ranges)] if near else None
     slots, sem = refs[-2:]
+    lists = sorted({which for which, _, _, _ in ranges})
     owner = owner_ref[0]
     pair = owner >> 1
     slot_count, _, _, page_len, _ = pool_ref.shape
@@ -83,11 +84,12 @@
 
     found = lax.fori_loop(0, width, look, (jnp.int32(0),) * len(lists), unroll=16)
     copies = []
-    for (at, k, begin, end), out in zip(ranges, outs):
+    for (which, k, begin, end), out in zip(ranges, outs):
+        at = lists.index(which)
         for i in range(begin, end):
             slot = jnp.where(i < found[at], slots[at * (cap + 1) + i], 0)
             copy = pltpu.make_async_copy(
-                pool_ref.at[slot, :, k], out.at[0, i - begin], sem.at[at, k, i]
+                pool_ref.at[slot, :, k], out.at[0, i - begin], sem.at[len(copies)]
             )
             copy.start()
             copies.append(copy)
@@ -110,27 +112,20 @@
         copy.wait()
 
 
-def gather_pages(owner, table, lengths, pool, lists, near, cap, after=()):
-    _, pair_of, kv_heads, page_len, head_dim = pool.shape
-    ranges = []
-    for at in range(len(lists)):
-        for k in range(kv_heads):
-            cuts = [0, cap]
-            if near and at < near - 1 and k == kv_heads - 1:
-                cuts.insert(1, cap - last_pages(cap))
-            ranges += [(at, k, begin, end) for begin, end in zip(cuts, cuts[1:])]
+def gather_pages(owner, table, lengths, pool, ranges, near, cap, after=()):
+    _, pair_of, _, page_len, head_dim = pool.shape
     outs = [
         pltpu.VMEM((1, end - begin, pair_of, page_len, head_dim), pool.dtype)
         for _, _, begin, end in ranges
     ]
+    copy_count = sum(end - begin for _, _, begin, end in ranges)
+    list_count = len({which for which, _, _, _ in ranges})
     specs = [pl.BlockSpec(memory_space=pltpu.VMEM)] * len(outs)
     if near:
         outs.append(jax.ShapeDtypeStruct((2, near), jnp.int32))
         specs.append(pl.BlockSpec(memory_space=pltpu.SMEM))
     results = pl.pallas_call(
-        functools.partial(
-            gather_body, lists=lists, near=near, waits=len(after), ranges=ranges, cap=cap
-        ),
+        functools.partial(gather_body, near=near, waits=len(after), ranges=ranges, cap=cap),
         out_shape=outs,
         grid_spec=pltpu.PrefetchScalarGridSpec(
             num_scalar_prefetch=3,
@@ -139,8 +134,8 @@
             + [pl.BlockSpec(memory_space=pl.ANY)] * len(after),
             out_specs=specs,
             scratch_shapes=[
-                pltpu.SMEM((len(lists) * (cap + 1),), jnp.int32),
-                pltpu.SemaphoreType.DMA((len(lists), kv_heads, cap)),
+                pltpu.SMEM((list_count * (cap + 1),), jnp.int32),
+                pltpu.SemaphoreType.DMA((copy_count,)),
             ],
         ),
         compiler_params=pltpu.CompilerParams(vmem_limit_bytes=kernel_bytes),
@@ -152,9 +147,7 @@
         pltpu.with_memory_space_constraint(pool, pltpu.HBM),
         *after,
     )
-    pages = [[[] for _ in range(kv_heads)] for _ in lists]
-    for (at, k, _, _), part in zip(ranges, results):
-        pages[at][k].append(part)
+    pages = {(which, k, begin): part for (which, k, begin, _), part in zip(ranges, results)}
     return pages, results[-1]
 
 
@@ -175,20 +168,26 @@
     copies_pool,
     waits,
     page_at,
+    row_count,
 ):
     refs = list(refs)
     q_refs = [refs.pop(0) for _ in range(halves)]
     kv_refs = [refs.pop(0) for _ in seen_at]
     page_ref = refs.pop(0) if has_page else None
-    prev_refs = [(refs.pop(0), refs.pop(0)) for _ in range(halves)] if has_prev else None
+    prev_refs = [[refs.pop(0) for _ in range(has_prev)] for _ in range(halves)]
     pool_ref = refs.pop(0) if copies_pool else None
     del refs[:waits]
     out_refs = []
     for h in range(halves):
-        out_refs.append((refs.pop(0),) if packed[h] else (refs.pop(0), refs.pop(0)))
+        out_refs.append([refs.pop(0) for _ in range({True: 1, False: 2, None: 3}[packed[h]])])
     new_pool = refs.pop(0) if copies_pool else None
     wide_values = refs.pop(0)
-    tables = [refs.pop(0) if packed[h] else out_refs[h][1].at[0] for h in range(halves)]
+    tables = []
+    for h in range(halves):
+        if packed[h] is None:
+            tables.append(None)
+        else:
+            tables.append(refs.pop(0) if packed[h] else out_refs[h][1].at[0])
     if copies_pool:
         staged, sem_in, sem_out = refs
     head = pl.program_id(0)
@@ -226,6 +225,7 @@
             wide_values[begin : begin + page_len, lanes:] = ones
 
     eye = diagonal()
+    q_count = row_count // block_rows
     limits = []
     for s, at in enumerate(seen_at):
         position = lax.broadcasted_iota(jnp.int32, (1, keys[s]), 1)
@@ -267,24 +267,33 @@
         total = mixed[:, lanes:]
         mixed = mixed[:, :lanes]
         first = step * (step_rows // block_rows) + t * (tile_rows // block_rows)
-        count = tables[h].shape[0] // 2
+        count = q_count
         for u in range(tile_rows // block_rows):
             inner = slice(u * block_rows, (u + 1) * block_rows)
             outer = slice(t * tile_rows + u * block_rows, t * tile_rows + (u + 1) * block_rows)
             part_top, part_total, part_mixed = top[inner], total[inner], mixed[inner]
             row = first + u
             if has_prev:
-                prev_mixed, prev_table = prev_refs[h]
-                prev_top = as_column(prev_table[0, pl.ds(row, 1)], eye)
-                prev_total = as_column(prev_table[0, pl.ds(count + row, 1)], eye)
+                if has_prev == 3:
+                    prev_mixed, prev_tops, prev_totals = prev_refs[h]
+                    prev_top = prev_tops[0, outer]
+                    prev_total = prev_totals[0, outer]
+                else:
+                    prev_mixed, prev_table = prev_refs[h]
+                    prev_top = as_column(prev_table[0, pl.ds(row, 1)], eye)
+                    prev_total = as_column(prev_table[0, pl.ds(count + row, 1)], eye)
                 joint = jnp.maximum(part_top, prev_top)
                 keep = jnp.exp2((part_top - joint) * scale)
                 keep_prev = jnp.exp2((prev_top - joint) * scale)
                 part_mixed = part_mixed * keep + prev_mixed[0, outer] * keep_prev
                 part_total = part_total * keep + prev_total * keep_prev
                 part_top = joint
-            tables[h][pl.ds(row, 1)] = as_row(part_top, eye)
-            tables[h][pl.ds(count + row, 1)] = as_row(part_total, eye)
+            if packed[h] is None:
+                out_refs[h][1][0, outer] = jnp.broadcast_to(part_top, (block_rows, lanes))
+                out_refs[h][2][0, outer] = jnp.broadcast_to(part_total, (block_rows, lanes))
+            else:
+                tables[h][pl.ds(row, 1)] = as_row(part_top, eye)
+                tables[h][pl.ds(count + row, 1)] = as_row(part_total, eye)
             if packed[h]:
                 at = pl.multiple_of(row * block_rows, block_rows)
                 out_refs[h][0][0, pl.ds(at, block_rows)] = part_mixed.astype(jnp.bfloat16)
@@ -341,9 +350,12 @@
         in_specs.append(whole(page))
         key_count += page.shape[2]
     if prev is not None:
-        for mixed, table, at in prev:
-            args += [mixed, table]
-            in_specs += [per_rows(at), per_head(table, at)]
+        for *state, at in prev:
+            args += state
+            if len(state) == 3:
+                in_specs += [per_rows(at)] * 3
+            else:
+                in_specs += [per_rows(at), per_head(state[1], at)]
     if pool is not None:
         args.append(pltpu.with_memory_space_constraint(pool, pltpu.HBM))
         in_specs.append(pl.BlockSpec(memory_space=pltpu.HBM))
@@ -358,6 +370,9 @@
             out_shape.append(shape)
             out_specs.append(per_head(shape, 0))
             scratch.append(pltpu.VMEM((size, lanes), jnp.float32))
+        elif packed[h] is None:
+            out_shape += [jax.ShapeDtypeStruct((heads, rows, lanes), jnp.float32)] * 3
+            out_specs += [per_rows(0)] * 3
         else:
             table = jax.ShapeDtypeStruct((heads, size, lanes), jnp.float32)
             out_shape += [jax.ShapeDtypeStruct((heads, rows, lanes), jnp.float32), table]
@@ -374,7 +389,7 @@
             halves=halves,
             seen_at=seen_at,
             has_page=page is not None,
-            has_prev=prev is not None,
+            has_prev=len(prev[0]) - 1 if prev else 0,
             packed=packed,
             step_rows=step_rows,
             tile_rows=tile_rows,
@@ -383,6 +398,7 @@
             copies_pool=pool is not None,
             waits=len(after),
             page_at=page_at,
+            row_count=rows,
         ),
         out_shape=out_shape,
         grid_spec=pltpu.PrefetchScalarGridSpec(
@@ -404,29 +420,43 @@
 
 def join_body(own_mixed, own_table, *refs, scale, packs, waits):
     refs = list(refs)
+    shares = refs.pop()
     out_ref = refs.pop()
     if waits:
         del refs[-waits:]
     size = own_table.shape[1]
     count = size // 2
     rows = count * block_rows
+    step = pl.program_id(0)
+    blocks = own_mixed.shape[1] // block_rows
     eye = diagonal()
-    tops = [own_table[0, :count]]
-    totals = [own_table[0, count:]]
-    for ref in refs:
-        table = from_three(ref, rows, size)
-        tops.append(table[:count])
-        totals.append(table[count:])
-    top = functools.reduce(jnp.maximum, tops)
-    keeps = [jnp.exp2((t - top) * scale) for t in tops]
-    total = sum(t * keep for t, keep in zip(totals, keeps))
-    if not packs:
-        keeps = [keep / total for keep in keeps]
-    for t in range(count):
+
+    @pl.when(step == 0)
+    def _():
+        tops = [own_table[0, :count]]
+        totals = [own_table[0, count:]]
+        for ref in refs:
+            table = from_three(ref, rows, size)
+            tops.append(table[:count])
+            totals.append(table[count:])
+        top = functools.reduce(jnp.maximum, tops)
+        keeps = [jnp.exp2((t - top) * scale) for t in tops]
+        total = sum(t * keep for t, keep in zip(totals, keeps))
+        for i, keep in enumerate(keeps):
+            shares[i] = keep if packs else keep / total
+        if packs:
+            table = jnp.concatenate([top, total], axis=0)
+            for i, part in enumerate(in_three(table)):
+                out_ref[0, rows + i * size : rows + (i + 1) * size] = part
+
+    for t in range(blocks):
+        row = step * blocks + t
         at = slice(t * block_rows, (t + 1) * block_rows)
-        mixed = own_mixed[0, at] * as_column(keeps[0][t : t + 1], eye)
-        for ref, keep in zip(refs, keeps[1:]):
-            mixed = mixed + ref[0, at].astype(jnp.float32) * as_column(keep[t : t + 1], eye)
+        begin = pl.multiple_of(row * block_rows, block_rows)
+        mixed = own_mixed[0, at] * as_column(shares[0, pl.ds(row, 1)], eye)
+        for i, ref in enumerate(refs):
+            part = ref[0, pl.ds(begin, block_rows)].astype(jnp.float32)
+            mixed = mixed + part * as_column(shares[i + 1, pl.ds(row, 1)], eye)
         if packs:
             out_ref[0, at] = mixed.astype(jnp.bfloat16)
         else:
@@ -434,10 +464,6 @@
             tokens = block_rows // heads
             shaped = mixed.reshape(tokens, heads, lanes)
             out_ref[t * tokens : (t + 1) * tokens] = shaped.astype(jnp.bfloat16)
-    if packs:
-        table = jnp.concatenate([top, total], axis=0)
-        for i, part in enumerate(in_three(table)):
-            out_ref[0, rows + i * size : rows + (i + 1) * size] = part
 
 
 def join_packed(own, received, scale, after=()):
@@ -449,6 +475,7 @@
         grid=(1,),
         in_specs=[whole(a) for a in args] + [pl.BlockSpec(memory_space=pl.ANY)] * len(after),
         out_specs=whole(received),
+        scratch_shapes=[pltpu.VMEM((2, table.shape[1] // 2, lanes), jnp.float32)],
         compiler_params=pltpu.CompilerParams(vmem_limit_bytes=kernel_bytes),
         name="join_packed",
     )(*args, *after)
@@ -458,6 +485,9 @@
     mixed, table = own
     args = [mixed, table, *received]
     in_specs = [whole(a) for a in args]
+    steps = 2
+    rows = mixed.shape[1] // steps
+    in_specs[0] = pl.BlockSpec((1, rows, lanes), lambda i: (0, i, 0))
     aliases = {}
     if target is not None:
         aliases = {len(args): 0}
@@ -466,9 +496,10 @@
     return pl.pallas_call(
         functools.partial(join_body, scale=scale, packs=False, waits=len(aliases)),
         out_shape=jax.ShapeDtypeStruct(shape, jnp.bfloat16),
-        grid=(1,),
+        grid=(steps,),
         in_specs=in_specs,
-        out_specs=pl.BlockSpec((shape[0], group, shape[2]), lambda i: (0, index, 0)),
+        out_specs=pl.BlockSpec((shape[0] // steps, group, shape[2]), lambda i: (i, index, 0)),
+        scratch_shapes=[pltpu.VMEM((len(received) + 1, table.shape[1] // 2, lanes), jnp.float32)],
         input_output_aliases=aliases,
         compiler_params=pltpu.CompilerParams(vmem_limit_bytes=kernel_bytes),
         name="join_out",
@@ -496,17 +527,25 @@
     far_own = [moved(split[k], pairs) for k in each]
     other = [moved(split[k], 1) for k in each]
     lookup = (owner_list, block_table, prefix_len, pool)
-    sent_far, _ = gather_pages(*lookup, [near + k for k in range(1, near)], 0, cap)
-    rest_lists = list(range(1, near)) + [0, near]
-    pages, seen = gather_pages(*lookup, rest_lists, near, cap, after=[new_page])
-
-    def exchanged(sent, k, part):
-        return [moved(sent[i][k][part], 2 * (i + 1)) for i in range(near - 1)]
-
-    got_far = [exchanged(sent_far, k, 0) for k in each]
-    got_near = [exchanged(pages, k, 0) for k in each]
-    got_late = exchanged(pages, kv_heads - 1, 1)
-    local, local_far = [[part[0] for part in pages[i]] for i in (near - 1, near)]
+    last = kv_heads - 1
+    cut = cap - last_pages(cap)
+    ring = range(1, near)
+    ranges = [(near + i, 0, 0, cap) for i in ring]
+    pages, _ = gather_pages(*lookup, ranges, 0, cap)
+    ranges = [(near + i, k, 0, cap) for k in each if k for i in ring]
+    ranges += [(i, k, 0, cut if k == last else cap) for k in each for i in ring]
+    ranges += [(i, last, cut, cap) for i in ring]
+    ranges += [(i, k, 0, cap) for i in (0, near) for k in each]
+    more, seen = gather_pages(*lookup, ranges, near, cap, after=[new_page])
+    pages = {**pages, **more}
+
+    def exchanged(first, k, begin):
+        return [moved(pages[first + i, k, begin], 2 * i) for i in ring]
+
+    got_far = [exchanged(near, k, 0) for k in each]
+    got_near = [exchanged(0, k, 0) for k in each]
+    got_late = exchanged(0, last, cut)
+    local, local_far = [[pages[i, k, 0] for k in each] for i in (0, near)]
     scalars = (owner_list, seen, new_slots)
 
     started = []
@@ -572,14 +611,13 @@
             other_part = results[2]
         else:
             late_keys = [(a, 0) for a in got_late]
-            skipped = (cap - last_pages(cap)) * page_len
-            late_at = [(0, i, skipped) for i in range(1, near)]
+            late_at = [(0, i, cut * page_len) for i in range(1, near)]
             early = attend(
                 scalars,
                 [(other[k], 0)],
                 near_keys,
                 near_at,
-                (False,),
+                (None,),
                 scale,
                 group,
                 1,

time: 89.6 us -> 88.6 us (0.989)
  starting transfers between devices: 23.6 us -> 20.9 us
  waiting for transfers between devices: 20 us -> 21.4 us
    ppermute x17, starting transfers between devices: 23.6 us -> 20.9 us  [moved(): return lax.ppermute(array, 'pool', [(i, i ^ apart) for i in range(count)])]
    ppermute x17, waiting for transfers between devices: 20 us -> 21.4 us  [moved(): return lax.ppermute(array, 'pool', [(i, i ^ apart) for i in range(count)])]
  transfers between devices with their start and end apart: 17 -> 17, of which waited for: 3 -> 4; matrix products, arithmetic and copies ran while one was open for 0% -> 0% of each run, Pallas kernels for 48% -> 48%
where the time goes in v6:
time: 88.6 us; the launch traced here: 88.3 us
  Pallas kernels  44.1 us (50%)
  waiting for transfers between devices  21.4 us (24%)
  starting transfers between devices  20.9 us (24%)
  local copies, waits for them, and re-layouts  1.13 us (1%)
    pallas_call x8, Pallas kernels, attend(): pl.pallas_call(functools.partial(attend_body, halves=halves, seen_at=seen...  33.4 us
    ppermute x17, waiting for transfers between devices, moved(): return lax.ppermute(array, 'pool', [(i, i ^ apart) for i in range(count)])  21.4 us
    ppermute x17, starting transfers between devices, moved(): return lax.ppermute(array, 'pool', [(i, i ^ apart) for i in range(count)])  20.9 us
    pallas_call x2, Pallas kernels, gather_pages(): pl.pallas_call(functools.partial(gather_body, near=near, waits=len(after)...  7.35 us
    pallas_call x2, Pallas kernels, join_out(): pl.pallas_call(functools.partial(join_body, scale=scale, packs=False, wai...  2.58 us
  transfers between devices with their start and end apart: 17, of which 4 were waited for; matrix products, arithmetic and copies ran while one was open for 0% of the time, Pallas kernels for 48%

profile of v6, /device:TPU:0, one launch (start us, length us, event | category | flops | bytes accessed | tf_op | source)
XLA Modules:
  0.0 88.3 jit_solution(10148824342865665701)
XLA Ops:
  0.6 1.1 %slice_bitcast_fusion = (bf16[1,1024,128]{2,1,0:T(8,128)(2,1)S(1)}, bf16[1,1024,128]{2,1,0:T(8,128)(2,1)S(1)}) fusion(bf16[128,16,128]{2,1,0:T(8,128)(2,1)} %param.6), kind=kLoop, calls=%fused_computation | loop fusion | bytes 1048576 | tf_op jit(solution)/shard_map/reshape | solution.py:524
  1.7 3.1 %collective-permute-start.3 = (bf16[1,1024,128]{2,1,0:T(8,128)(2,1)S(1)}, bf16[1,1024,128]{2,1,0:T(8,128)(2,1)S(1)}, u32[]{:S(2)}, u32[]{:S(2)}) collective-permute-start(bf16[1,1024,128]{2,1,0:T(8,128)(2,1)S(1)} %get-tuple-element.66.refs_0_), channel_id=1, source_target_pairs={{0,2},{2,0},{4,6},{6,4},{8,10},{10,8},{12,14},{14,12},{1,3},{3,1},... | collective-permute-start | bytes 786440 | tf_op jit(solution)/shard_map/ppermute | solution.py:21
  4.8 2.3 %gather_pages.3 = bf16[1,8,2,128,128]{4,3,2,1,0:T(8,128)(2,1)S(1)} custom-call(s32[1]{0:T(128)} %bitcast.owner_ref, s32[4,64]{1,0:T(4,128)} %table_ref.3, s32[4]{0:T(128)} %length_ref.3, bf16[33,2,2,128,128]{4,3,2,1,0:T(8,128)(2,1)} %pool_ref.3), custom_call_target="tpu_custom_call" | custom-call | tf_op jit(solution)/shard_map/gather_pages/pallas_call | solution.py:127
  7.1 1.6 %collective-permute-start.9 = (bf16[1,8,2,128,128]{4,3,2,1,0:T(8,128)(2,1)S(1)}, bf16[1,8,2,128,128]{4,3,2,1,0:T(8,128)(2,1)S(1)}, u32[]{:S(2)}, u32[]{:S(2)}) collective-permute-start(bf16[1,8,2,128,128]{4,3,2,1,0:T(8,128)(2,1)S(1)} %gather_pages.3), channel_id=1, source_target_pairs={{0,4},{2,6},{4,0},{6,2},{8,12},{10,14},{12,8},{14,10},{1,5},{3,7},... | collective-permute-start | bytes 1572872 | tf_op jit(solution)/shard_map/ppermute | solution.py:21
  8.8 2.6 %collective-permute-start.7 = (bf16[1,1024,128]{2,1,0:T(8,128)(2,1)S(1)}, bf16[1,1024,128]{2,1,0:T(8,128)(2,1)S(1)}, u32[]{:S(2)}, u32[]{:S(2)}) collective-permute-start(bf16[1,1024,128]{2,1,0:T(8,128)(2,1)S(1)} %get-tuple-element.66.refs_0_), channel_id=1, source_target_pairs={{0,8},{2,10},{4,12},{6,14},{8,0},{10,2},{12,4},{14,6},{1,9},{3,11}... | collective-permute-start | bytes 786440 | tf_op jit(solution)/shard_map/ppermute | solution.py:21
  11.4 0.5 collective-permute-start.2
  11.9 0.3 collective-permute-start.4
  12.2 5.0 %gather_pages.2 = (bf16[1,8,2,128,128]{4,3,2,1,0:T(8,128)(2,1)S(1)}, bf16[1,8,2,128,128]{4,3,2,1,0:T(8,128)(2,1)S(1)}, bf16[1,6,2,128,128]{4,3,2,1,0:T(8,128)(2,...) custom-call(s32[1]{0:T(128)} %bitcast.owner_ref, ...), custom_call_target="tpu_custom_call" | custom-call | tf_op jit(solution)/shard_map/gather_pages/pallas_call | solution.py:127
  17.3 0.0 collective-permute-done.3.refs_1_
  17.3 0.2 collective-permute-start.6
  17.5 9.3 %collective-permute-done.7.refs_0_ = bf16[1,1024,128]{2,1,0:T(8,128)(2,1)S(1)} collective-permute-done((bf16[1,1024,128]{2,1,0:T(8,128)(2,1)S(1)}, bf16[1,1024,128]{2,1,0:T(8,128)(2,1)S(1)}, u32[]{:S(2)}, u32[]{:S(2)}) %collective-permute-start.7) | collective-permute-done | bytes 262176 | tf_op jit(solution)/shard_map/ppermute | solution.py:21
  26.7 0.5 collective-permute-start.8
  27.2 4.9 %attend.8 = (f32[1,1024,128]{2,1,0:T(8,128)S(1)}, f32[1,16,128]{2,1,0:T(8,128)S(1)}, f32[1,1024,128]{2,1,0:T(8,128)S(1)}, f32[1,16,128]{2,1,0:T(8,128)S(1)}, bf16[33,2,2,128,128]{4,3,2,1,0:T(8,128)(2,1)}) custom-call(s32[1]{0:T(128)} %bitcast.owner_ref, s32[2,2]{1,0:T(2,128)S(1)} %get-tuple-element.34.seen_ref, s32[8]{0:T(128)S(1)} %copy-done, ...), custom_call_target="tpu_custom_call" | custom-call | flops 1207959552 | bytes 589824 | tf_op jit(solution)/shard_map/attend/pallas_call | solution.py:386
  32.1 0.0 collective-permute-done.2.refs_1_.refs_0_
  32.2 3.6 %collective-permute-start.11 = (bf16[1,8,2,128,128]{4,3,2,1,0:T(8,128)(2,1)S(1)}, bf16[1,8,2,128,128]{4,3,2,1,0:T(8,128)(2,1)S(1)}, u32[]{:S(2)}, u32[]{:S(2)}) collective-permute-start(bf16[1,8,2,128,128]{4,3,2,1,0:T(8,128)(2,1)S(1)} %get-tuple-element.51), channel_id=1, source_target_pairs={{0,4},{2,6},{4,0},{6,2},{8,12},{10,14},{12,8},{14,10},{1,5},{3,7},... | collective-permute-start | bytes 1572872 | tf_op jit(solution)/shard_map/ppermute | solution.py:21
  35.8 0.0 collective-permute-done.4.refs_0_
  35.8 1.5 %collective-permute-start.5 = (bf16[1,1024,128]{2,1,0:T(8,128)(2,1)S(1)}, bf16[1,1024,128]{2,1,0:T(8,128)(2,1)S(1)}, u32[]{:S(2)}, u32[]{:S(2)}) collective-permute-start(bf16[1,1024,128]{2,1,0:T(8,128)(2,1)S(1)} %collective-permute-done.4.refs_0_), channel_id=1, source_target_pairs={{0,2},{2,0},{4,6},{6,4},{8,10},{10,8},{12,14},{14,12},{1,3},{3,1},... | collective-permute-start | bytes 786440 | tf_op jit(solution)/shard_map/ppermute | solution.py:21
  37.3 4.8 %attend.9 = (f32[1,1024,128]{2,1,0:T(8,128)S(1)}, f32[1,16,128]{2,1,0:T(8,128)S(1)}, f32[1,1024,128]{2,1,0:T(8,128)S(1)}, f32[1,16,128]{2,1,0:T(8,128)S(1)}) custom-call(s32[1]{0:T(128)} %bitcast.owner_ref, s32[2,2]{1,0:T(2,128)S(1)} %get-tuple-element.34.seen_ref, s32[8]{0:T(128)S(1)} %copy-done, bf16[1,1024,128]{2,1,0:T(8,128)(2,1)S(1)} %get-tuple-element.67.refs_0_, ...), custom_call_target="tpu_custom_call" | custom-call | flops 1207959552 | bytes 589824 | tf_op jit(solution)/shard_map/attend/pallas_call | solution.py:386
  42.1 0.0 collective-permute-done.9.refs_3_
  42.1 0.1 collective-permute-start
  42.3 0.0 collective-permute-done.8.refs_1_
  42.3 6.7 %attend.10 = (f32[1,1024,128]{2,1,0:T(8,128)S(1)}, f32[1,16,128]{2,1,0:T(8,128)S(1)}, bf16[1,1072,128]{2,1,0:T(8,128)(2,1)S(1)}) custom-call(s32[1]{0:T(128)} %bitcast.owner_ref, s32[2,2]{1,0:T(2,128)S(1)} %get-tuple-element.34.seen_ref, s32[8]{0:T(128)S(1)} %copy-done, bf16[1,1024,128]{2,1,0:T(8,128)(2,1)S(1)} %collective-permute-done.7.refs_0_, ...), custom_call_target="tpu_custom_call" | custom-call | flops 2147483648 | bytes 1048576 | tf_op jit(solution)/shard_map/attend/pallas_call | solution.py:386
  48.9 0.6 collective-permute-start.12
  49.5 0.0 collective-permute-done.6.refs_3_
  49.5 0.0 collective-permute-done.5.refs_1_
  49.5 6.9 %attend.11 = (f32[1,1024,128]{2,1,0:T(8,128)S(1)}, f32[1,16,128]{2,1,0:T(8,128)S(1)}, bf16[1,1072,128]{2,1,0:T(8,128)(2,1)S(1)}) custom-call(s32[1]{0:T(128)} %bitcast.owner_ref, s32[2,2]{1,0:T(2,128)S(1)} %get-tuple-element.34.seen_ref, s32[8]{0:T(128)S(1)} %copy-done, bf16[1,1024,128]{2,1,0:T(8,128)(2,1)S(1)} %collective-permute-done.4.refs_0_, ...), custom_call_target="tpu_custom_call" | custom-call | flops 2147483648 | bytes 1048576 | tf_op jit(solution)/shard_map/attend/pallas_call | solution.py:386
  56.4 1.6 %collective-permute-start.10 = (bf16[1,1072,128]{2,1,0:T(8,128)(2,1)S(1)}, bf16[1,1072,128]{2,1,0:T(8,128)(2,1)S(1)}, u32[]{:S(2)}, u32[]{:S(2)}) collective-permute-start(bf16[1,1072,128]{2,1,0:T(8,128)(2,1)S(1)} %get-tuple-element.50), channel_id=1, source_target_pairs={{0,2},{2,0},{4,6},{6,4},{8,10},{10,8},{12,14},{14,12},{1,3},{3,1},... | collective-permute-start | bytes 823304 | tf_op jit(solution)/shard_map/ppermute | solution.py:21
  58.0 1.9 %collective-permute-start.1 = (bf16[1,2,2,128,128]{4,3,2,1,0:T(8,128)(2,1)S(1)}, bf16[1,2,2,128,128]{4,3,2,1,0:T(8,128)(2,1)S(1)}, u32[]{:S(2)}, u32[]{:S(2)}) collective-permute-start(bf16[1,2,2,128,128]{4,3,2,1,0:T(8,128)(2,1)S(1)} %get-tuple-element.36), channel_id=1, source_target_pairs={{0,4},{2,6},{4,0},{6,2},{8,12},{10,14},{12,8},{14,10},{1,5},{3,7},... | collective-permute-start | bytes 393224 | tf_op jit(solution)/shard_map/ppermute | solution.py:21
  59.9 0.0 collective-permute-done.12.refs_0_
  59.9 0.4 join_packed.2.refs_7_
  60.3 0.1 collective-permute-start.16
  60.4 0.0 collective-permute-done.11.refs_2_
  60.4 4.3 %attend.12 = (f32[1,1024,128]{2,1,0:T(8,128)S(1)}, f32[1,16,128]{2,1,0:T(8,128)S(1)}, bf16[1,1072,128]{2,1,0:T(8,128)(2,1)S(1)}) custom-call(s32[1]{0:T(128)} %bitcast.owner_ref, s32[2,2]{1,0:T(2,128)S(1)} %get-tuple-element.34.seen_ref, s32[8]{0:T(128)S(1)} %copy-done, bf16[1,1024,128]{2,1,0:T(8,128)(2,1)S(1)} %get-tuple-element.66.refs_0_, ...), custom_call_target="tpu_custom_call" | custom-call | flops 1073741824 | bytes 524288 | tf_op jit(solution)/shard_map/attend/pallas_call | solution.py:386
  64.7 0.6 collective-permute-start.15
  65.3 0.0 collective-permute-done.10.refs_0_
  65.3 0.4 join_packed.3.refs_4_
  65.7 4.2 %collective-permute-done.refs_1_ = bf16[1,6,2,128,128]{4,3,2,1,0:T(8,128)(2,1)S(1)} collective-permute-done((bf16[1,6,2,128,128]{4,3,2,1,0:T(8,128)(2,1)S(1)}, bf16[1,6,2,128,128]{4,3,2,1,0:T(8,128)(2,1)S(1)}, u32[]{:S(2)}, u32[]{:S(2)}) %collective-permute-start) | collective-permute-done | bytes 393248 | tf_op jit(solution)/shard_map/ppermute | solution.py:21
  69.8 2.0 %attend.13 = (f32[1,1024,128]{2,1,0:T(8,128)S(1)}, f32[1,1024,128]{2,1,0:T(8,128)S(1)}, f32[1,1024,128]{2,1,0:T(8,128)S(1)}) custom-call(s32[1]{0:T(128)} %bitcast.owner_ref, s32[2,2]{1,0:T(2,128)S(1)} %get-tuple-element.34.seen_ref, s32[8]{0:T(128)S(1)} %copy-done, bf16[1,1024,128]{2,1,0:T(8,128)(2,1)S(1)} %collective-permute-done.2.refs_1_.refs_0_, ...), custom_call_target="tpu_custom_call" | custom-call | flops 402653184 | bytes 393216 | tf_op jit(solution)/shard_map/attend/pallas_call | solution.py:386
  71.9 0.0 collective-permute-done.1.refs_1_.refs_2_
  71.9 1.4 %attend.14.refs_5_ = bf16[1,1072,128]{2,1,0:T(8,128)(2,1)S(1)} custom-call(s32[1]{0:T(128)} %bitcast.owner_ref, s32[2,2]{1,0:T(2,128)S(1)} %get-tuple-element.34.seen_ref, s32[8]{0:T(128)S(1)} %copy-done, bf16[1,1024,128]{2,1,0:T(8,128)(2,1)S(1)} %collective-permute-done.2.refs_1_.refs_0_, ...), custom_call_target="tpu_custom_call" | custom-call | flops 134217728 | bytes 131072 | tf_op jit(solution)/shard_map/attend/pallas_call | solution.py:386
  73.3 0.1 collective-permute-start.13
  73.4 1.9 %collective-permute-start.14 = (bf16[1,1072,128]{2,1,0:T(8,128)(2,1)S(1)}, bf16[1,1072,128]{2,1,0:T(8,128)(2,1)S(1)}, u32[]{:S(2)}, u32[]{:S(2)}) collective-permute-start(bf16[1,1072,128]{2,1,0:T(8,128)(2,1)S(1)} %join_packed.3.refs_4_), channel_id=1, source_target_pairs={{0,8},{2,10},{4,12},{6,14},{8,0},{10,2},{12,4},{14,6},{1,9},{3,11}... | collective-permute-start | bytes 823304 | tf_op jit(solution)/shard_map/ppermute | solution.py:21
  75.3 2.4 %attend.15 = (f32[1,1024,128]{2,1,0:T(8,128)S(1)}, f32[1,16,128]{2,1,0:T(8,128)S(1)}) custom-call(s32[1]{0:T(128)} %bitcast.owner_ref, s32[2,2]{1,0:T(2,128)S(1)} %get-tuple-element.34.seen_ref, s32[8]{0:T(128)S(1)} %copy-done, bf16[1,1024,128]{2,1,0:T(8,128)(2,1)S(1)} %get-tuple-element.67.refs_0_, ...), custom_call_target="tpu_custom_call" | custom-call | flops 536870912 | bytes 524288 | tf_op jit(solution)/shard_map/attend/pallas_call | solution.py:386
  77.8 0.0 collective-permute-done.15.refs_0_
  77.8 1.3 %join_out.2.refs_2_ = bf16[128,16,128]{2,1,0:T(8,128)(2,1)} custom-call(f32[1,1024,128]{2,1,0:T(8,128)S(1)} %get-tuple-element.63.own_mixed, f32[1,16,128]{2,1,0:T(8,128)S(1)} %get-tuple-element.57.refs_1_.own_table, bf16[1,1072,128]{2,1,0:T(8,128)(2,1)S(1)} %collective-permute-done.15.refs_0_, bf16[1,1072,128]{2,1,0:T(8,128)(2,1)S(1)} %collective-permute-done.16.refs_1_), custom_call_target="tpu_custom_call" | custom-call | tf_op jit(solution)/shard_map/join_out/pallas_call | solution.py:496
  79.1 0.8 collective-permute-done.13.refs_0_
  79.9 7.1 %collective-permute-done.14.refs_1_ = bf16[1,1072,128]{2,1,0:T(8,128)(2,1)S(1)} collective-permute-done((bf16[1,1072,128]{2,1,0:T(8,128)(2,1)S(1)}, bf16[1,1072,128]{2,1,0:T(8,128)(2,1)S(1)}, u32[]{:S(2)}, u32[]{:S(2)}) %collective-permute-start.14) | collective-permute-done | bytes 274464 | tf_op jit(solution)/shard_map/ppermute | solution.py:21
  87.0 1.3 %join_out.3 = bf16[128,16,128]{2,1,0:T(8,128)(2,1)} custom-call(f32[1,1024,128]{2,1,0:T(8,128)S(1)} %get-tuple-element.61.own_mixed, f32[1,16,128]{2,1,0:T(8,128)S(1)} %get-tuple-element.62.own_table, bf16[1,1072,128]{2,1,0:T(8,128)(2,1)S(1)} %collective-permute-done.13.refs_0_, ...), custom_call_target="tpu_custom_call", output_to_operand_aliasing={{}: (4, {})} | custom-call | tf_op jit(solution)/shard_map/join_out/pallas_call | solution.py:496
  (6 shorter events, 0.0 us)
Async XLA Ops:
  0.6 11.6 %copy-start.1 = (bf16[128,2,2,128]{3,2,1,0:T(2,128)(2,1)S(1)}, bf16[128,2,2,128]{3,2,1,0:T(2,128)(2,1)}, u32[]{:S(2)}) copy-start(bf16[128,2,2,128]{3,2,1,0:T(2,128)(2,1)} %param.7) | copy-start | bytes 393220
  1.7 15.5 %collective-permute-start.3 = (bf16[1,1024,128]{2,1,0:T(8,128)(2,1)S(1)}, bf16[1,1024,128]{2,1,0:T(8,128)(2,1)S(1)}, u32[]{:S(2)}, u32[]{:S(2)}) collective-permute-start(bf16[1,1024,128]{2,1,0:T(8,128)(2,1)S(1)} %get-tuple-element.66.refs_0_), channel_id=1, source_target_pairs={{0,2},{2,0},{4,6},{6,4},{8,10},{10,8},{12,14},{14,12},{1,3},{3,1},... | collective-permute-start | bytes 786440 | tf_op jit(solution)/shard_map/ppermute | solution.py:21
  4.8 22.4 %copy-start = (s32[8]{0:T(128)S(1)}, s32[8]{0:T(128)}, u32[]{:S(2)}) copy-start(s32[8]{0:T(128)} %fresh_ref.15) | copy-start | bytes 100
  7.1 35.0 %collective-permute-start.9 = (bf16[1,8,2,128,128]{4,3,2,1,0:T(8,128)(2,1)S(1)}, bf16[1,8,2,128,128]{4,3,2,1,0:T(8,128)(2,1)S(1)}, u32[]{:S(2)}, u32[]{:S(2)}) collective-permute-start(bf16[1,8,2,128,128]{4,3,2,1,0:T(8,128)(2,1)S(1)} %gather_pages.3), channel_id=1, source_target_pairs={{0,4},{2,6},{4,0},{6,2},{8,12},{10,14},{12,8},{14,10},{1,5},{3,7},... | collective-permute-start | bytes 1572872 | tf_op jit(solution)/shard_map/ppermute | solution.py:21
  8.8 18.0 %collective-permute-start.7 = (bf16[1,1024,128]{2,1,0:T(8,128)(2,1)S(1)}, bf16[1,1024,128]{2,1,0:T(8,128)(2,1)S(1)}, u32[]{:S(2)}, u32[]{:S(2)}) collective-permute-start(bf16[1,1024,128]{2,1,0:T(8,128)(2,1)S(1)} %get-tuple-element.66.refs_0_), channel_id=1, source_target_pairs={{0,8},{2,10},{4,12},{6,14},{8,0},{10,2},{12,4},{14,6},{1,9},{3,11}... | collective-permute-start | bytes 786440 | tf_op jit(solution)/shard_map/ppermute | solution.py:21
  11.4 20.8 %collective-permute-start.2 = (bf16[1,1024,128]{2,1,0:T(8,128)(2,1)S(1)}, bf16[1,1024,128]{2,1,0:T(8,128)(2,1)S(1)}, u32[]{:S(2)}, u32[]{:S(2)}) collective-permute-start(bf16[1,1024,128]{2,1,0:T(8,128)(2,1)S(1)} %get-tuple-element.67.refs_0_), channel_id=1, source_target_pairs={{0,2},{2,0},{4,6},{6,4},{8,10},{10,8},{12,14},{14,12},{1,3},{3,1},... | collective-permute-start | bytes 786440 | tf_op jit(solution)/shard_map/ppermute | solution.py:21
  11.9 23.9 %collective-permute-start.4 = (bf16[1,1024,128]{2,1,0:T(8,128)(2,1)S(1)}, bf16[1,1024,128]{2,1,0:T(8,128)(2,1)S(1)}, u32[]{:S(2)}, u32[]{:S(2)}) collective-permute-start(bf16[1,1024,128]{2,1,0:T(8,128)(2,1)S(1)} %get-tuple-element.67.refs_0_), channel_id=1, source_target_pairs={{0,8},{2,10},{4,12},{6,14},{8,0},{10,2},{12,4},{14,6},{1,9},{3,11}... | collective-permute-start | bytes 786440 | tf_op jit(solution)/shard_map/ppermute | solution.py:21
  17.3 32.2 %collective-permute-start.6 = (bf16[1,8,2,128,128]{4,3,2,1,0:T(8,128)(2,1)S(1)}, bf16[1,8,2,128,128]{4,3,2,1,0:T(8,128)(2,1)S(1)}, u32[]{:S(2)}, u32[]{:S(2)}) collective-permute-start(bf16[1,8,2,128,128]{4,3,2,1,0:T(8,128)(2,1)S(1)} %get-tuple-element.45), channel_id=1, source_target_pairs={{0,4},{2,6},{4,0},{6,2},{8,12},{10,14},{12,8},{14,10},{1,5},{3,7},... | collective-permute-start | bytes 1572872 | tf_op jit(solution)/shard_map/ppermute | solution.py:21
  26.7 15.5 %collective-permute-start.8 = (bf16[1,1024,128]{2,1,0:T(8,128)(2,1)S(1)}, bf16[1,1024,128]{2,1,0:T(8,128)(2,1)S(1)}, u32[]{:S(2)}, u32[]{:S(2)}) collective-permute-start(bf16[1,1024,128]{2,1,0:T(8,128)(2,1)S(1)} %collective-permute-done.7.refs_0_), channel_id=1, source_target_pairs={{0,2},{2,0},{4,6},{6,4},{8,10},{10,8},{12,14},{14,12},{1,3},{3,1},... | collective-permute-start | bytes 786440 | tf_op jit(solution)/shard_map/ppermute | solution.py:21
  32.2 28.2 %collective-permute-start.11 = (bf16[1,8,2,128,128]{4,3,2,1,0:T(8,128)(2,1)S(1)}, bf16[1,8,2,128,128]{4,3,2,1,0:T(8,128)(2,1)S(1)}, u32[]{:S(2)}, u32[]{:S(2)}) collective-permute-start(bf16[1,8,2,128,128]{4,3,2,1,0:T(8,128)(2,1)S(1)} %get-tuple-element.51), channel_id=1, source_target_pairs={{0,4},{2,6},{4,0},{6,2},{8,12},{10,14},{12,8},{14,10},{1,5},{3,7},... | collective-permute-start | bytes 1572872 | tf_op jit(solution)/shard_map/ppermute | solution.py:21
  35.8 13.7 %collective-permute-start.5 = (bf16[1,1024,128]{2,1,0:T(8,128)(2,1)S(1)}, bf16[1,1024,128]{2,1,0:T(8,128)(2,1)S(1)}, u32[]{:S(2)}, u32[]{:S(2)}) collective-permute-start(bf16[1,1024,128]{2,1,0:T(8,128)(2,1)S(1)} %collective-permute-done.4.refs_0_), channel_id=1, source_target_pairs={{0,2},{2,0},{4,6},{6,4},{8,10},{10,8},{12,14},{14,12},{1,3},{3,1},... | collective-permute-start | bytes 786440 | tf_op jit(solution)/shard_map/ppermute | solution.py:21
  42.1 27.7 %collective-permute-start = (bf16[1,6,2,128,128]{4,3,2,1,0:T(8,128)(2,1)S(1)}, bf16[1,6,2,128,128]{4,3,2,1,0:T(8,128)(2,1)S(1)}, u32[]{:S(2)}, u32[]{:S(2)}) collective-permute-start(bf16[1,6,2,128,128]{4,3,2,1,0:T(8,128)(2,1)S(1)} %get-tuple-element.35), channel_id=1, source_target_pairs={{0,4},{2,6},{4,0},{6,2},{8,12},{10,14},{12,8},{14,10},{1,5},{3,7},... | collective-permute-start | bytes 1179656 | tf_op jit(solution)/shard_map/ppermute | solution.py:21
  48.9 11.0 %collective-permute-start.12 = (bf16[1,1072,128]{2,1,0:T(8,128)(2,1)S(1)}, bf16[1,1072,128]{2,1,0:T(8,128)(2,1)S(1)}, u32[]{:S(2)}, u32[]{:S(2)}) collective-permute-start(bf16[1,1072,128]{2,1,0:T(8,128)(2,1)S(1)} %get-tuple-element.56), channel_id=1, source_target_pairs={{0,2},{2,0},{4,6},{6,4},{8,10},{10,8},{12,14},{14,12},{1,3},{3,1},... | collective-permute-start | bytes 823304 | tf_op jit(solution)/shard_map/ppermute | solution.py:21
  56.4 8.9 %collective-permute-start.10 = (bf16[1,1072,128]{2,1,0:T(8,128)(2,1)S(1)}, bf16[1,1072,128]{2,1,0:T(8,128)(2,1)S(1)}, u32[]{:S(2)}, u32[]{:S(2)}) collective-permute-start(bf16[1,1072,128]{2,1,0:T(8,128)(2,1)S(1)} %get-tuple-element.50), channel_id=1, source_target_pairs={{0,2},{2,0},{4,6},{6,4},{8,10},{10,8},{12,14},{14,12},{1,3},{3,1},... | collective-permute-start | bytes 823304 | tf_op jit(solution)/shard_map/ppermute | solution.py:21
  58.0 13.9 %collective-permute-start.1 = (bf16[1,2,2,128,128]{4,3,2,1,0:T(8,128)(2,1)S(1)}, bf16[1,2,2,128,128]{4,3,2,1,0:T(8,128)(2,1)S(1)}, u32[]{:S(2)}, u32[]{:S(2)}) collective-permute-start(bf16[1,2,2,128,128]{4,3,2,1,0:T(8,128)(2,1)S(1)} %get-tuple-element.36), channel_id=1, source_target_pairs={{0,4},{2,6},{4,0},{6,2},{8,12},{10,14},{12,8},{14,10},{1,5},{3,7},... | collective-permute-start | bytes 393224 | tf_op jit(solution)/shard_map/ppermute | solution.py:21
  60.3 17.5 %collective-permute-start.16 = (bf16[1,1072,128]{2,1,0:T(8,128)(2,1)S(1)}, bf16[1,1072,128]{2,1,0:T(8,128)(2,1)S(1)}, u32[]{:S(2)}, u32[]{:S(2)}) collective-permute-start(bf16[1,1072,128]{2,1,0:T(8,128)(2,1)S(1)} %join_packed.2.refs_7_), channel_id=1, source_target_pairs={{0,8},{2,10},{4,12},{6,14},{8,0},{10,2},{12,4},{14,6},{1,9},{3,11}... | collective-permute-start | bytes 823304 | tf_op jit(solution)/shard_map/ppermute | solution.py:21
  64.7 13.0 %collective-permute-start.15 = (bf16[1,1072,128]{2,1,0:T(8,128)(2,1)S(1)}, bf16[1,1072,128]{2,1,0:T(8,128)(2,1)S(1)}, u32[]{:S(2)}, u32[]{:S(2)}) collective-permute-start(bf16[1,1072,128]{2,1,0:T(8,128)(2,1)S(1)} %get-tuple-element.64), channel_id=1, source_target_pairs={{0,2},{2,0},{4,6},{6,4},{8,10},{10,8},{12,14},{14,12},{1,3},{3,1},... | collective-permute-start | bytes 823304 | tf_op jit(solution)/shard_map/ppermute | solution.py:21
  73.3 6.6 %collective-permute-start.13 = (bf16[1,1072,128]{2,1,0:T(8,128)(2,1)S(1)}, bf16[1,1072,128]{2,1,0:T(8,128)(2,1)S(1)}, u32[]{:S(2)}, u32[]{:S(2)}) collective-permute-start(bf16[1,1072,128]{2,1,0:T(8,128)(2,1)S(1)} %attend.14.refs_5_), channel_id=1, source_target_pairs={{0,2},{2,0},{4,6},{6,4},{8,10},{10,8},{12,14},{14,12},{1,3},{3,1},... | collective-permute-start | bytes 823304 | tf_op jit(solution)/shard_map/ppermute | solution.py:21
  73.4 13.6 %collective-permute-start.14 = (bf16[1,1072,128]{2,1,0:T(8,128)(2,1)S(1)}, bf16[1,1072,128]{2,1,0:T(8,128)(2,1)S(1)}, u32[]{:S(2)}, u32[]{:S(2)}) collective-permute-start(bf16[1,1072,128]{2,1,0:T(8,128)(2,1)S(1)} %join_packed.3.refs_4_), channel_id=1, source_target_pairs={{0,8},{2,10},{4,12},{6,14},{8,0},{10,2},{12,4},{14,6},{1,9},{3,11}... | collective-permute-start | bytes 823304 | tf_op jit(solution)/shard_map/ppermute | solution.py:21

commit v7 on v5

--- a/solution.py
+++ b/solution.py
@@ -59,11 +59,12 @@
     return max(1, cap // 4)
 
 
-def gather_body(owner_ref, table_ref, length_ref, pool_ref, *refs, lists, near, waits, ranges, cap):
+def gather_body(owner_ref, table_ref, length_ref, pool_ref, *refs, near, waits, ranges, cap):
     refs = refs[waits:]
     outs = refs[: len(ranges)]
     seen_ref = refs[len(ranges)] if near else None
     slots, sem = refs[-2:]
+    lists = sorted({which for which, _, _, _ in ranges})
     owner = owner_ref[0]
     pair = owner >> 1
     slot_count, _, _, page_len, _ = pool_ref.shape
@@ -83,22 +84,23 @@
 
     found = lax.fori_loop(0, width, look, (jnp.int32(0),) * len(lists), unroll=16)
     copies = []
-    for (at, k, begin, end), out in zip(ranges, outs):
+    for (which, k, begin, end), out in zip(ranges, outs):
+        at = lists.index(which)
         for i in range(begin, end):
             slot = jnp.where(i < found[at], slots[at * (cap + 1) + i], 0)
             copy = pltpu.make_async_copy(
-                pool_ref.at[slot, :, k], out.at[0, i - begin], sem.at[at, k, i]
+                pool_ref.at[slot, :, k], out.at[0, i - begin], sem.at[len(copies)]
             )
             copy.start()
             copies.append(copy)
     if near:
-        asked = [(t, s) for t in range(2) for s in range(near)]
+        asked = [(t, s) for t in range(3) for s in range(near)]
 
         def count(j, seen):
             following = []
             for (t, s), so_far in zip(asked, seen):
-                request = pair ^ (t * near)
-                _, there = held(request, owner ^ (2 * s), j)
+                request = pair ^ (near if t == 1 else 0)
+                _, there = held(request, owner ^ (2 * s + t // 2), j)
                 inside = jnp.clip(length_ref[request] - j * page_len, 0, page_len)
                 following.append(so_far + jnp.where(there, inside, 0))
             return tuple(following)
@@ -110,27 +112,20 @@
         copy.wait()
 
 
-def gather_pages(owner, table, lengths, pool, lists, near, cap, after=()):
-    _, pair_of, kv_heads, page_len, head_dim = pool.shape
-    ranges = []
-    for at in range(len(lists)):
-        for k in range(kv_heads):
-            cuts = [0, cap]
-            if near and at < near - 1 and k == kv_heads - 1:
-                cuts.insert(1, cap - last_pages(cap))
-            ranges += [(at, k, begin, end) for begin, end in zip(cuts, cuts[1:])]
+def gather_pages(owner, table, lengths, pool, ranges, near, cap, after=()):
+    _, pair_of, _, page_len, head_dim = pool.shape
     outs = [
         pltpu.VMEM((1, end - begin, pair_of, page_len, head_dim), pool.dtype)
         for _, _, begin, end in ranges
     ]
+    copy_count = sum(end - begin for _, _, begin, end in ranges)
+    list_count = len({which for which, _, _, _ in ranges})
     specs = [pl.BlockSpec(memory_space=pltpu.VMEM)] * len(outs)
     if near:
-        outs.append(jax.ShapeDtypeStruct((2, near), jnp.int32))
+        outs.append(jax.ShapeDtypeStruct((3, near), jnp.int32))
         specs.append(pl.BlockSpec(memory_space=pltpu.SMEM))
     results = pl.pallas_call(
-        functools.partial(
-            gather_body, lists=lists, near=near, waits=len(after), ranges=ranges, cap=cap
-        ),
+        functools.partial(gather_body, near=near, waits=len(after), ranges=ranges, cap=cap),
         out_shape=outs,
         grid_spec=pltpu.PrefetchScalarGridSpec(
             num_scalar_prefetch=3,
@@ -139,8 +134,8 @@
             + [pl.BlockSpec(memory_space=pl.ANY)] * len(after),
             out_specs=specs,
             scratch_shapes=[
-                pltpu.SMEM((len(lists) * (cap + 1),), jnp.int32),
-                pltpu.SemaphoreType.DMA((len(lists), kv_heads, cap)),
+                pltpu.SMEM((list_count * (cap + 1),), jnp.int32),
+                pltpu.SemaphoreType.DMA((copy_count,)),
             ],
         ),
         compiler_params=pltpu.CompilerParams(vmem_limit_bytes=kernel_bytes),
@@ -152,9 +147,7 @@
         pltpu.with_memory_space_constraint(pool, pltpu.HBM),
         *after,
     )
-    pages = [[[] for _ in range(kv_heads)] for _ in lists]
-    for (at, k, _, _), part in zip(ranges, results):
-        pages[at][k].append(part)
+    pages = {(which, k, begin): part for (which, k, begin, _), part in zip(ranges, results)}
     return pages, results[-1]
 
 
@@ -496,17 +489,27 @@
     far_own = [moved(split[k], pairs) for k in each]
     other = [moved(split[k], 1) for k in each]
     lookup = (owner_list, block_table, prefix_len, pool)
-    sent_far, _ = gather_pages(*lookup, [near + k for k in range(1, near)], 0, cap)
-    rest_lists = list(range(1, near)) + [0, near]
-    pages, seen = gather_pages(*lookup, rest_lists, near, cap, after=[new_page])
-
-    def exchanged(sent, k, part):
-        return [moved(sent[i][k][part], 2 * (i + 1)) for i in range(near - 1)]
-
-    got_far = [exchanged(sent_far, k, 0) for k in each]
-    got_near = [exchanged(pages, k, 0) for k in each]
-    got_late = exchanged(pages, kv_heads - 1, 1)
-    local, local_far = [[part[0] for part in pages[i]] for i in (near - 1, near)]
+    last = kv_heads - 1
+    cut = cap - last_pages(cap)
+    ring = range(1, near)
+    ranges = [(near + i, 0, 0, cap) for i in ring]
+    pages, _ = gather_pages(*lookup, ranges, 0, cap)
+    ranges = [(near + i, k, 0, cap) for k in each if k for i in ring]
+    ranges += [(i, k, 0, cut if k == last else cap) for k in each for i in ring]
+    ranges += [(i, last, cut, cap) for i in ring]
+    ranges += [(i, k, 0, cap) for i in (0, near) for k in each]
+    more, seen = gather_pages(*lookup, ranges, near, cap, after=[new_page])
+    pages = {**pages, **more}
+
+    def exchanged(first, k, begin):
+        return [moved(pages[first + i, k, begin], 2 * i) for i in ring]
+
+    got_far = [exchanged(near, k, 0) for k in each]
+    got_near = [exchanged(0, k, 0) for k in each]
+    got_late = [moved(pages[i, last, cut], 2 * i) for i in ring]
+    theirs_late = [moved(pages[i, last, cut], 1) for i in ring]
+    got_late += [moved(part, 2 * i) for i, part in zip(ring, theirs_late)]
+    local, local_far = [[pages[i, k, 0] for k in each] for i in (0, near)]
     scalars = (owner_list, seen, new_slots)
 
     started = []
@@ -572,42 +575,41 @@
             other_part = results[2]
         else:
             late_keys = [(a, 0) for a in got_late]
-            skipped = (cap - last_pages(cap)) * page_len
-            late_at = [(0, i, skipped) for i in range(1, near)]
+            late_at = [(t, i, cut * page_len) for t in (0, 2) for i in ring]
+            (other_part,) = attend(
+                scalars,
+                [(other[k], 0)],
+                near_keys,
+                near_at,
+                (True,),
+                scale,
+                group,
+                1,
+                prev=[theirs],
+                after=[joined],
+            )
             early = attend(
                 scalars,
-                [(other[k], 0)],
+                [(split[k], 0)],
                 near_keys,
                 near_at,
                 (False,),
                 scale,
                 group,
                 1,
-                prev=[theirs],
-                after=[joined],
+                prev=[mine],
+                after=[other_part],
             )
-            (other_part,) = attend(
+            own_part = attend(
                 scalars,
-                [(other[k], 0)],
+                [(split[k], 0)],
                 late_keys,
                 late_at,
-                (True,),
+                (False,),
                 scale,
                 group,
                 1,
                 prev=[(*early, 0)],
-            )
-            own_part = attend(
-                scalars,
-                [(split[k], 0)],
-                near_keys + late_keys,
-                near_at + late_at,
-                (False,),
-                scale,
-                group,
-                1,
-                prev=[mine],
-                after=[other_part],
             )
         ready.append((own_part, moved(other_part, 1)))
         after = [own_part[1]]

time: 89.6 us -> 87.5 us (0.977)
  waiting for transfers between devices: 20 us -> 16.7 us
    ppermute x17 -> x19, waiting for transfers between devices: 20 us -> 16.7 us  [moved(): return lax.ppermute(array, 'pool', [(i, i ^ apart) for i in range(count)])]
    ppermute x17 -> x19, starting transfers between devices: 23.6 us -> 24.4 us  [moved(): return lax.ppermute(array, 'pool', [(i, i ^ apart) for i in range(count)])]
  transfers between devices with their start and end apart: 17 -> 19, of which waited for: 3 -> 4; matrix products, arithmetic and copies ran while one was open for 0% -> 0% of each run, Pallas kernels for 48% -> 49%
where the time goes in v7:
time: 87.5 us; the launch traced here: 87.2 us
  Pallas kernels  44.2 us (51%)
  starting transfers between devices  24.4 us (28%)
  waiting for transfers between devices  16.7 us (19%)
  local copies, waits for them, and re-layouts  1.13 us (1%)
    pallas_call x8, Pallas kernels, attend(): pl.pallas_call(functools.partial(attend_body, halves=halves, seen_at=seen...  33.7 us
    ppermute x19, starting transfers between devices, moved(): return lax.ppermute(array, 'pool', [(i, i ^ apart) for i in range(count)])  24.4 us
    ppermute x19, waiting for transfers between devices, moved(): return lax.ppermute(array, 'pool', [(i, i ^ apart) for i in range(count)])  16.7 us
    pallas_call x2, Pallas kernels, gather_pages(): pl.pallas_call(functools.partial(gather_body, near=near, waits=len(after)...  7.36 us
    pallas_call x2, Pallas kernels, join_out(): pl.pallas_call(functools.partial(join_body, scale=scale, packs=False, wai...  2.44 us
  transfers between devices with their start and end apart: 19, of which 4 were waited for; matrix products, arithmetic and copies ran while one was open for 0% of the time, Pallas kernels for 49%

profile of v7, /device:TPU:0, one launch (start us, length us, event | category | flops | bytes accessed | tf_op | source)
XLA Modules:
  0.0 87.2 jit_solution(5937483433908696297)
XLA Ops:
  0.6 1.1 %slice_bitcast_fusion = (bf16[1,1024,128]{2,1,0:T(8,128)(2,1)S(1)}, bf16[1,1024,128]{2,1,0:T(8,128)(2,1)S(1)}) fusion(bf16[128,16,128]{2,1,0:T(8,128)(2,1)} %param.6), kind=kLoop, calls=%fused_computation | loop fusion | bytes 1048576 | tf_op jit(solution)/shard_map/reshape | solution.py:486
  1.7 3.1 %collective-permute-start.5 = (bf16[1,1024,128]{2,1,0:T(8,128)(2,1)S(1)}, bf16[1,1024,128]{2,1,0:T(8,128)(2,1)S(1)}, u32[]{:S(2)}, u32[]{:S(2)}) collective-permute-start(bf16[1,1024,128]{2,1,0:T(8,128)(2,1)S(1)} %get-tuple-element.64.refs_0_), channel_id=1, source_target_pairs={{0,2},{2,0},{4,6},{6,4},{8,10},{10,8},{12,14},{14,12},{1,3},{3,1},... | collective-permute-start | bytes 786440 | tf_op jit(solution)/shard_map/ppermute | solution.py:21
  4.8 2.3 %gather_pages.3 = bf16[1,8,2,128,128]{4,3,2,1,0:T(8,128)(2,1)S(1)} custom-call(s32[1]{0:T(128)} %bitcast.owner_ref, s32[4,64]{1,0:T(4,128)} %table_ref.3, s32[4]{0:T(128)} %length_ref.3, bf16[33,2,2,128,128]{4,3,2,1,0:T(8,128)(2,1)} %pool_ref.3), custom_call_target="tpu_custom_call" | custom-call | tf_op jit(solution)/shard_map/gather_pages/pallas_call | solution.py:127
  7.1 1.6 %collective-permute-start.11 = (bf16[1,8,2,128,128]{4,3,2,1,0:T(8,128)(2,1)S(1)}, bf16[1,8,2,128,128]{4,3,2,1,0:T(8,128)(2,1)S(1)}, u32[]{:S(2)}, u32[]{:S(2)}) collective-permute-start(bf16[1,8,2,128,128]{4,3,2,1,0:T(8,128)(2,1)S(1)} %gather_pages.3), channel_id=1, source_target_pairs={{0,4},{2,6},{4,0},{6,2},{8,12},{10,14},{12,8},{14,10},{1,5},{3,7},... | collective-permute-start | bytes 1572872 | tf_op jit(solution)/shard_map/ppermute | solution.py:21
  8.8 2.6 %collective-permute-start.9 = (bf16[1,1024,128]{2,1,0:T(8,128)(2,1)S(1)}, bf16[1,1024,128]{2,1,0:T(8,128)(2,1)S(1)}, u32[]{:S(2)}, u32[]{:S(2)}) collective-permute-start(bf16[1,1024,128]{2,1,0:T(8,128)(2,1)S(1)} %get-tuple-element.64.refs_0_), channel_id=1, source_target_pairs={{0,8},{2,10},{4,12},{6,14},{8,0},{10,2},{12,4},{14,6},{1,9},{3,11}... | collective-permute-start | bytes 786440 | tf_op jit(solution)/shard_map/ppermute | solution.py:21
  11.4 0.5 collective-permute-start.4
  11.9 0.3 collective-permute-start.6
  12.2 5.1 %gather_pages.2 = (bf16[1,8,2,128,128]{4,3,2,1,0:T(8,128)(2,1)S(1)}, bf16[1,8,2,128,128]{4,3,2,1,0:T(8,128)(2,1)S(1)}, bf16[1,6,2,128,128]{4,3,2,1,0:T(8,128)(2,...) custom-call(s32[1]{0:T(128)} %bitcast.owner_ref, ...), custom_call_target="tpu_custom_call" | custom-call | tf_op jit(solution)/shard_map/gather_pages/pallas_call | solution.py:127
  17.3 0.0 collective-permute-done.5.refs_1_
  17.3 0.2 collective-permute-start.8
  17.5 9.3 %collective-permute-done.9.refs_0_ = bf16[1,1024,128]{2,1,0:T(8,128)(2,1)S(1)} collective-permute-done((bf16[1,1024,128]{2,1,0:T(8,128)(2,1)S(1)}, bf16[1,1024,128]{2,1,0:T(8,128)(2,1)S(1)}, u32[]{:S(2)}, u32[]{:S(2)}) %collective-permute-start.9) | collective-permute-done | bytes 262176 | tf_op jit(solution)/shard_map/ppermute | solution.py:21
  26.7 0.5 collective-permute-start.10
  27.2 4.9 %attend.8 = (f32[1,1024,128]{2,1,0:T(8,128)S(1)}, f32[1,16,128]{2,1,0:T(8,128)S(1)}, f32[1,1024,128]{2,1,0:T(8,128)S(1)}, f32[1,16,128]{2,1,0:T(8,128)S(1)}, bf16[33,2,2,128,128]{4,3,2,1,0:T(8,128)(2,1)}) custom-call(s32[1]{0:T(128)} %bitcast.owner_ref, s32[3,2]{1,0:T(4,128)S(1)} %get-tuple-element.33.seen_ref, s32[8]{0:T(128)S(1)} %copy-done, ...), custom_call_target="tpu_custom_call" | custom-call | flops 1207959552 | bytes 589824 | tf_op jit(solution)/shard_map/attend/pallas_call | solution.py:364
  32.2 0.0 collective-permute-done.4.refs_1_.refs_0_
  32.2 3.6 %collective-permute-start.13 = (bf16[1,8,2,128,128]{4,3,2,1,0:T(8,128)(2,1)S(1)}, bf16[1,8,2,128,128]{4,3,2,1,0:T(8,128)(2,1)S(1)}, u32[]{:S(2)}, u32[]{:S(2)}) collective-permute-start(bf16[1,8,2,128,128]{4,3,2,1,0:T(8,128)(2,1)S(1)} %get-tuple-element.50), channel_id=1, source_target_pairs={{0,4},{2,6},{4,0},{6,2},{8,12},{10,14},{12,8},{14,10},{1,5},{3,7},... | collective-permute-start | bytes 1572872 | tf_op jit(solution)/shard_map/ppermute | solution.py:21
  35.8 0.0 collective-permute-done.6.refs_0_
  35.8 1.5 %collective-permute-start.7 = (bf16[1,1024,128]{2,1,0:T(8,128)(2,1)S(1)}, bf16[1,1024,128]{2,1,0:T(8,128)(2,1)S(1)}, u32[]{:S(2)}, u32[]{:S(2)}) collective-permute-start(bf16[1,1024,128]{2,1,0:T(8,128)(2,1)S(1)} %collective-permute-done.6.refs_0_), channel_id=1, source_target_pairs={{0,2},{2,0},{4,6},{6,4},{8,10},{10,8},{12,14},{14,12},{1,3},{3,1},... | collective-permute-start | bytes 786440 | tf_op jit(solution)/shard_map/ppermute | solution.py:21
  37.3 4.8 %attend.9 = (f32[1,1024,128]{2,1,0:T(8,128)S(1)}, f32[1,16,128]{2,1,0:T(8,128)S(1)}, f32[1,1024,128]{2,1,0:T(8,128)S(1)}, f32[1,16,128]{2,1,0:T(8,128)S(1)}) custom-call(s32[1]{0:T(128)} %bitcast.owner_ref, s32[3,2]{1,0:T(4,128)S(1)} %get-tuple-element.33.seen_ref, s32[8]{0:T(128)S(1)} %copy-done, bf16[1,1024,128]{2,1,0:T(8,128)(2,1)S(1)} %get-tuple-element.65.refs_0_, ...), custom_call_target="tpu_custom_call" | custom-call | flops 1207959552 | bytes 589824 | tf_op jit(solution)/shard_map/attend/pallas_call | solution.py:364
  42.1 0.0 collective-permute-done.11.refs_3_
  42.2 0.1 collective-permute-start.3
  42.3 0.0 collective-permute-done.10.refs_1_
  42.3 6.7 %attend.10 = (f32[1,1024,128]{2,1,0:T(8,128)S(1)}, f32[1,16,128]{2,1,0:T(8,128)S(1)}, bf16[1,1072,128]{2,1,0:T(8,128)(2,1)S(1)}) custom-call(s32[1]{0:T(128)} %bitcast.owner_ref, s32[3,2]{1,0:T(4,128)S(1)} %get-tuple-element.33.seen_ref, s32[8]{0:T(128)S(1)} %copy-done, bf16[1,1024,128]{2,1,0:T(8,128)(2,1)S(1)} %collective-permute-done.9.refs_0_, ...), custom_call_target="tpu_custom_call" | custom-call | flops 2147483648 | bytes 1048576 | tf_op jit(solution)/shard_map/attend/pallas_call | solution.py:364
  49.0 0.6 collective-permute-start.14
  49.6 0.0 collective-permute-done.8.refs_3_
  49.6 0.0 collective-permute-done.7.refs_1_
  49.6 6.9 %attend.11 = (f32[1,1024,128]{2,1,0:T(8,128)S(1)}, f32[1,16,128]{2,1,0:T(8,128)S(1)}, bf16[1,1072,128]{2,1,0:T(8,128)(2,1)S(1)}) custom-call(s32[1]{0:T(128)} %bitcast.owner_ref, s32[3,2]{1,0:T(4,128)S(1)} %get-tuple-element.33.seen_ref, s32[8]{0:T(128)S(1)} %copy-done, bf16[1,1024,128]{2,1,0:T(8,128)(2,1)S(1)} %collective-permute-done.6.refs_0_, ...), custom_call_target="tpu_custom_call" | custom-call | flops 2147483648 | bytes 1048576 | tf_op jit(solution)/shard_map/attend/pallas_call | solution.py:364
  56.5 1.6 %collective-permute-start.12 = (bf16[1,1072,128]{2,1,0:T(8,128)(2,1)S(1)}, bf16[1,1072,128]{2,1,0:T(8,128)(2,1)S(1)}, u32[]{:S(2)}, u32[]{:S(2)}) collective-permute-start(bf16[1,1072,128]{2,1,0:T(8,128)(2,1)S(1)} %get-tuple-element.49), channel_id=1, source_target_pairs={{0,2},{2,0},{4,6},{6,4},{8,10},{10,8},{12,14},{14,12},{1,3},{3,1},... | collective-permute-start | bytes 823304 | tf_op jit(solution)/shard_map/ppermute | solution.py:21
  58.0 0.5 collective-permute-start.1
  58.6 1.9 %collective-permute-start = (bf16[1,2,2,128,128]{4,3,2,1,0:T(8,128)(2,1)S(1)}, bf16[1,2,2,128,128]{4,3,2,1,0:T(8,128)(2,1)S(1)}, u32[]{:S(2)}, u32[]{:S(2)}) collective-permute-start(bf16[1,2,2,128,128]{4,3,2,1,0:T(8,128)(2,1)S(1)} %get-tuple-element.34), channel_id=1, source_target_pairs={{0,4},{2,6},{4,0},{6,2},{8,12},{10,14},{12,8},{14,10},{1,5},{3,7},... | collective-permute-start | bytes 393224 | tf_op jit(solution)/shard_map/ppermute | solution.py:21
  60.5 0.4 join_packed.2.refs_7_
  60.9 0.1 collective-permute-start.18
  61.0 4.3 %attend.12 = (f32[1,1024,128]{2,1,0:T(8,128)S(1)}, f32[1,16,128]{2,1,0:T(8,128)S(1)}, bf16[1,1072,128]{2,1,0:T(8,128)(2,1)S(1)}) custom-call(s32[1]{0:T(128)} %bitcast.owner_ref, s32[3,2]{1,0:T(4,128)S(1)} %get-tuple-element.33.seen_ref, s32[8]{0:T(128)S(1)} %copy-done, bf16[1,1024,128]{2,1,0:T(8,128)(2,1)S(1)} %get-tuple-element.64.refs_0_, ...), custom_call_target="tpu_custom_call" | custom-call | flops 1073741824 | bytes 524288 | tf_op jit(solution)/shard_map/attend/pallas_call | solution.py:364
  65.3 1.6 %collective-permute-start.17 = (bf16[1,1072,128]{2,1,0:T(8,128)(2,1)S(1)}, bf16[1,1072,128]{2,1,0:T(8,128)(2,1)S(1)}, u32[]{:S(2)}, u32[]{:S(2)}) collective-permute-start(bf16[1,1072,128]{2,1,0:T(8,128)(2,1)S(1)} %get-tuple-element.62), channel_id=1, source_target_pairs={{0,2},{2,0},{4,6},{6,4},{8,10},{10,8},{12,14},{14,12},{1,3},{3,1},... | collective-permute-start | bytes 823304 | tf_op jit(solution)/shard_map/ppermute | solution.py:21
  66.9 0.4 join_packed.3.refs_4_
  67.3 2.0 %collective-permute-done.3.refs_1_ = bf16[1,6,2,128,128]{4,3,2,1,0:T(8,128)(2,1)S(1)} collective-permute-done((bf16[1,6,2,128,128]{4,3,2,1,0:T(8,128)(2,1)S(1)}, bf16[1,6,2,128,128]{4,3,2,1,0:T(8,128)(2,1)S(1)}, u32[]{:S(2)}, u32[]{:S(2)}) %collective-permute-start.3) | collective-permute-done | bytes 393248 | tf_op jit(solution)/shard_map/ppermute | solution.py:21
  69.3 2.2 %attend.13.refs_4_ = bf16[1,1072,128]{2,1,0:T(8,128)(2,1)S(1)} custom-call(s32[1]{0:T(128)} %bitcast.owner_ref, s32[3,2]{1,0:T(4,128)S(1)} %get-tuple-element.33.seen_ref, s32[8]{0:T(128)S(1)} %copy-done, bf16[1,1024,128]{2,1,0:T(8,128)(2,1)S(1)} %collective-permute-done.4.refs_1_.refs_0_, bf16[1,6,2,128,128]{4,3,2,1,0:T(8,128)(2,1)S(1)} %collective-permute-done.3.refs_1_, ...), custom_call_target="tpu_custom_call" | custom-call | flops 402653184 | bytes 393216 | tf_op jit(solution)/shard_map/attend/pallas_call | solution.py:364
  71.5 0.1 collective-permute-start.15
  71.5 0.0 collective-permute-done.1
  71.6 1.5 %collective-permute-start.16 = (bf16[1,1072,128]{2,1,0:T(8,128)(2,1)S(1)}, bf16[1,1072,128]{2,1,0:T(8,128)(2,1)S(1)}, u32[]{:S(2)}, u32[]{:S(2)}) collective-permute-start(bf16[1,1072,128]{2,1,0:T(8,128)(2,1)S(1)} %join_packed.3.refs_4_), channel_id=1, source_target_pairs={{0,8},{2,10},{4,12},{6,14},{8,0},{10,2},{12,4},{14,6},{1,9},{3,11}... | collective-permute-start | bytes 823304 | tf_op jit(solution)/shard_map/ppermute | solution.py:21
  73.1 2.5 %collective-permute-start.2 = (bf16[1,2,2,128,128]{4,3,2,1,0:T(8,128)(2,1)S(1)}, bf16[1,2,2,128,128]{4,3,2,1,0:T(8,128)(2,1)S(1)}, u32[]{:S(2)}, u32[]{:S(2)}) collective-permute-start(bf16[1,2,2,128,128]{4,3,2,1,0:T(8,128)(2,1)S(1)} %collective-permute-done.1), channel_id=1, source_target_pairs={{0,4},{2,6},{4,0},{6,2},{8,12},{10,14},{12,8},{14,10},{1,5},{3,7},... | collective-permute-start | bytes 393224 | tf_op jit(solution)/shard_map/ppermute | solution.py:21
  75.5 2.1 %attend.14 = (f32[1,1024,128]{2,1,0:T(8,128)S(1)}, f32[1,16,128]{2,1,0:T(8,128)S(1)}) custom-call(s32[1]{0:T(128)} %bitcast.owner_ref, s32[3,2]{1,0:T(4,128)S(1)} %get-tuple-element.33.seen_ref, s32[8]{0:T(128)S(1)} %copy-done, bf16[1,1024,128]{2,1,0:T(8,128)(2,1)S(1)} %get-tuple-element.65.refs_0_, ...), custom_call_target="tpu_custom_call" | custom-call | flops 402653184 | bytes 393216 | tf_op jit(solution)/shard_map/attend/pallas_call | solution.py:364
  77.7 1.9 %collective-permute-done.2.refs_2_ = bf16[1,2,2,128,128]{4,3,2,1,0:T(8,128)(2,1)S(1)} collective-permute-done((bf16[1,2,2,128,128]{4,3,2,1,0:T(8,128)(2,1)S(1)}, bf16[1,2,2,128,128]{4,3,2,1,0:T(8,128)(2,1)S(1)}, u32[]{:S(2)}, u32[]{:S(2)}) %collective-permute-start.2) | collective-permute-done | bytes 131104 | tf_op jit(solution)/shard_map/ppermute | solution.py:21
  79.6 1.7 %attend.15 = (f32[1,1024,128]{2,1,0:T(8,128)S(1)}, f32[1,16,128]{2,1,0:T(8,128)S(1)}) custom-call(s32[1]{0:T(128)} %bitcast.owner_ref, s32[3,2]{1,0:T(4,128)S(1)} %get-tuple-element.33.seen_ref, s32[8]{0:T(128)S(1)} %copy-done, bf16[1,1024,128]{2,1,0:T(8,128)(2,1)S(1)} %get-tuple-element.65.refs_0_, ...), custom_call_target="tpu_custom_call" | custom-call | flops 268435456 | bytes 262144 | tf_op jit(solution)/shard_map/attend/pallas_call | solution.py:364
  81.3 0.0 collective-permute-done.17.refs_0_
  81.4 1.2 %join_out.2.refs_2_ = bf16[128,16,128]{2,1,0:T(8,128)(2,1)} custom-call(f32[1,1024,128]{2,1,0:T(8,128)S(1)} %get-tuple-element.61.own_mixed, f32[1,16,128]{2,1,0:T(8,128)S(1)} %get-tuple-element.56.refs_1_.own_table, bf16[1,1072,128]{2,1,0:T(8,128)(2,1)S(1)} %collective-permute-done.17.refs_0_, bf16[1,1072,128]{2,1,0:T(8,128)(2,1)S(1)} %collective-permute-done.18.refs_1_), custom_call_target="tpu_custom_call" | custom-call | tf_op jit(solution)/shard_map/join_out/pallas_call | solution.py:459
  82.6 0.0 collective-permute-done.15.refs_0_
  82.6 3.4 %collective-permute-done.16.refs_1_ = bf16[1,1072,128]{2,1,0:T(8,128)(2,1)S(1)} collective-permute-done((bf16[1,1072,128]{2,1,0:T(8,128)(2,1)S(1)}, bf16[1,1072,128]{2,1,0:T(8,128)(2,1)S(1)}, u32[]{:S(2)}, u32[]{:S(2)}) %collective-permute-start.16) | collective-permute-done | bytes 274464 | tf_op jit(solution)/shard_map/ppermute | solution.py:21
  86.0 1.2 %join_out.3 = bf16[128,16,128]{2,1,0:T(8,128)(2,1)} custom-call(f32[1,1024,128]{2,1,0:T(8,128)S(1)} %get-tuple-element.59.own_mixed, f32[1,16,128]{2,1,0:T(8,128)S(1)} %get-tuple-element.60.own_table, bf16[1,1072,128]{2,1,0:T(8,128)(2,1)S(1)} %collective-permute-done.15.refs_0_, ...), custom_call_target="tpu_custom_call", output_to_operand_aliasing={{}: (4, {})} | custom-call | tf_op jit(solution)/shard_map/join_out/pallas_call | solution.py:459
  (10 shorter events, 0.0 us)
Async XLA Ops:
  0.6 11.6 %copy-start.1 = (bf16[128,2,2,128]{3,2,1,0:T(2,128)(2,1)S(1)}, bf16[128,2,2,128]{3,2,1,0:T(2,128)(2,1)}, u32[]{:S(2)}) copy-start(bf16[128,2,2,128]{3,2,1,0:T(2,128)(2,1)} %param.7) | copy-start | bytes 393220
  1.7 15.5 %collective-permute-start.5 = (bf16[1,1024,128]{2,1,0:T(8,128)(2,1)S(1)}, bf16[1,1024,128]{2,1,0:T(8,128)(2,1)S(1)}, u32[]{:S(2)}, u32[]{:S(2)}) collective-permute-start(bf16[1,1024,128]{2,1,0:T(8,128)(2,1)S(1)} %get-tuple-element.64.refs_0_), channel_id=1, source_target_pairs={{0,2},{2,0},{4,6},{6,4},{8,10},{10,8},{12,14},{14,12},{1,3},{3,1},... | collective-permute-start | bytes 786440 | tf_op jit(solution)/shard_map/ppermute | solution.py:21
  4.8 22.4 %copy-start = (s32[8]{0:T(128)S(1)}, s32[8]{0:T(128)}, u32[]{:S(2)}) copy-start(s32[8]{0:T(128)} %fresh_ref.15) | copy-start | bytes 100
  7.1 35.0 %collective-permute-start.11 = (bf16[1,8,2,128,128]{4,3,2,1,0:T(8,128)(2,1)S(1)}, bf16[1,8,2,128,128]{4,3,2,1,0:T(8,128)(2,1)S(1)}, u32[]{:S(2)}, u32[]{:S(2)}) collective-permute-start(bf16[1,8,2,128,128]{4,3,2,1,0:T(8,128)(2,1)S(1)} %gather_pages.3), channel_id=1, source_target_pairs={{0,4},{2,6},{4,0},{6,2},{8,12},{10,14},{12,8},{14,10},{1,5},{3,7},... | collective-permute-start | bytes 1572872 | tf_op jit(solution)/shard_map/ppermute | solution.py:21
  8.8 18.0 %collective-permute-start.9 = (bf16[1,1024,128]{2,1,0:T(8,128)(2,1)S(1)}, bf16[1,1024,128]{2,1,0:T(8,128)(2,1)S(1)}, u32[]{:S(2)}, u32[]{:S(2)}) collective-permute-start(bf16[1,1024,128]{2,1,0:T(8,128)(2,1)S(1)} %get-tuple-element.64.refs_0_), channel_id=1, source_target_pairs={{0,8},{2,10},{4,12},{6,14},{8,0},{10,2},{12,4},{14,6},{1,9},{3,11}... | collective-permute-start | bytes 786440 | tf_op jit(solution)/shard_map/ppermute | solution.py:21
  11.4 20.8 %collective-permute-start.4 = (bf16[1,1024,128]{2,1,0:T(8,128)(2,1)S(1)}, bf16[1,1024,128]{2,1,0:T(8,128)(2,1)S(1)}, u32[]{:S(2)}, u32[]{:S(2)}) collective-permute-start(bf16[1,1024,128]{2,1,0:T(8,128)(2,1)S(1)} %get-tuple-element.65.refs_0_), channel_id=1, source_target_pairs={{0,2},{2,0},{4,6},{6,4},{8,10},{10,8},{12,14},{14,12},{1,3},{3,1},... | collective-permute-start | bytes 786440 | tf_op jit(solution)/shard_map/ppermute | solution.py:21
  11.9 23.9 %collective-permute-start.6 = (bf16[1,1024,128]{2,1,0:T(8,128)(2,1)S(1)}, bf16[1,1024,128]{2,1,0:T(8,128)(2,1)S(1)}, u32[]{:S(2)}, u32[]{:S(2)}) collective-permute-start(bf16[1,1024,128]{2,1,0:T(8,128)(2,1)S(1)} %get-tuple-element.65.refs_0_), channel_id=1, source_target_pairs={{0,8},{2,10},{4,12},{6,14},{8,0},{10,2},{12,4},{14,6},{1,9},{3,11}... | collective-permute-start | bytes 786440 | tf_op jit(solution)/shard_map/ppermute | solution.py:21
  17.3 32.3 %collective-permute-start.8 = (bf16[1,8,2,128,128]{4,3,2,1,0:T(8,128)(2,1)S(1)}, bf16[1,8,2,128,128]{4,3,2,1,0:T(8,128)(2,1)S(1)}, u32[]{:S(2)}, u32[]{:S(2)}) collective-permute-start(bf16[1,8,2,128,128]{4,3,2,1,0:T(8,128)(2,1)S(1)} %get-tuple-element.44), channel_id=1, source_target_pairs={{0,4},{2,6},{4,0},{6,2},{8,12},{10,14},{12,8},{14,10},{1,5},{3,7},... | collective-permute-start | bytes 1572872 | tf_op jit(solution)/shard_map/ppermute | solution.py:21
  26.7 15.6 %collective-permute-start.10 = (bf16[1,1024,128]{2,1,0:T(8,128)(2,1)S(1)}, bf16[1,1024,128]{2,1,0:T(8,128)(2,1)S(1)}, u32[]{:S(2)}, u32[]{:S(2)}) collective-permute-start(bf16[1,1024,128]{2,1,0:T(8,128)(2,1)S(1)} %collective-permute-done.9.refs_0_), channel_id=1, source_target_pairs={{0,2},{2,0},{4,6},{6,4},{8,10},{10,8},{12,14},{14,12},{1,3},{3,1},... | collective-permute-start | bytes 786440 | tf_op jit(solution)/shard_map/ppermute | solution.py:21
  32.2 28.7 %collective-permute-start.13 = (bf16[1,8,2,128,128]{4,3,2,1,0:T(8,128)(2,1)S(1)}, bf16[1,8,2,128,128]{4,3,2,1,0:T(8,128)(2,1)S(1)}, u32[]{:S(2)}, u32[]{:S(2)}) collective-permute-start(bf16[1,8,2,128,128]{4,3,2,1,0:T(8,128)(2,1)S(1)} %get-tuple-element.50), channel_id=1, source_target_pairs={{0,4},{2,6},{4,0},{6,2},{8,12},{10,14},{12,8},{14,10},{1,5},{3,7},... | collective-permute-start | bytes 1572872 | tf_op jit(solution)/shard_map/ppermute | solution.py:21
  35.8 13.8 %collective-permute-start.7 = (bf16[1,1024,128]{2,1,0:T(8,128)(2,1)S(1)}, bf16[1,1024,128]{2,1,0:T(8,128)(2,1)S(1)}, u32[]{:S(2)}, u32[]{:S(2)}) collective-permute-start(bf16[1,1024,128]{2,1,0:T(8,128)(2,1)S(1)} %collective-permute-done.6.refs_0_), channel_id=1, source_target_pairs={{0,2},{2,0},{4,6},{6,4},{8,10},{10,8},{12,14},{14,12},{1,3},{3,1},... | collective-permute-start | bytes 786440 | tf_op jit(solution)/shard_map/ppermute | solution.py:21
  42.2 27.2 %collective-permute-start.3 = (bf16[1,6,2,128,128]{4,3,2,1,0:T(8,128)(2,1)S(1)}, bf16[1,6,2,128,128]{4,3,2,1,0:T(8,128)(2,1)S(1)}, u32[]{:S(2)}, u32[]{:S(2)}) collective-permute-start(bf16[1,6,2,128,128]{4,3,2,1,0:T(8,128)(2,1)S(1)} %get-tuple-element.35), channel_id=1, source_target_pairs={{0,4},{2,6},{4,0},{6,2},{8,12},{10,14},{12,8},{14,10},{1,5},{3,7},... | collective-permute-start | bytes 1179656 | tf_op jit(solution)/shard_map/ppermute | solution.py:21
  49.0 9.6 %collective-permute-start.14 = (bf16[1,1072,128]{2,1,0:T(8,128)(2,1)S(1)}, bf16[1,1072,128]{2,1,0:T(8,128)(2,1)S(1)}, u32[]{:S(2)}, u32[]{:S(2)}) collective-permute-start(bf16[1,1072,128]{2,1,0:T(8,128)(2,1)S(1)} %get-tuple-element.55), channel_id=1, source_target_pairs={{0,2},{2,0},{4,6},{6,4},{8,10},{10,8},{12,14},{14,12},{1,3},{3,1},... | collective-permute-start | bytes 823304 | tf_op jit(solution)/shard_map/ppermute | solution.py:21
  56.5 8.8 %collective-permute-start.12 = (bf16[1,1072,128]{2,1,0:T(8,128)(2,1)S(1)}, bf16[1,1072,128]{2,1,0:T(8,128)(2,1)S(1)}, u32[]{:S(2)}, u32[]{:S(2)}) collective-permute-start(bf16[1,1072,128]{2,1,0:T(8,128)(2,1)S(1)} %get-tuple-element.49), channel_id=1, source_target_pairs={{0,2},{2,0},{4,6},{6,4},{8,10},{10,8},{12,14},{14,12},{1,3},{3,1},... | collective-permute-start | bytes 823304 | tf_op jit(solution)/shard_map/ppermute | solution.py:21
  58.0 13.5 %collective-permute-start.1 = (bf16[1,2,2,128,128]{4,3,2,1,0:T(8,128)(2,1)S(1)}, bf16[1,2,2,128,128]{4,3,2,1,0:T(8,128)(2,1)S(1)}, u32[]{:S(2)}, u32[]{:S(2)}) collective-permute-start(bf16[1,2,2,128,128]{4,3,2,1,0:T(8,128)(2,1)S(1)} %get-tuple-element.34), channel_id=1, source_target_pairs={{0,2},{2,0},{4,6},{6,4},{8,10},{10,8},{12,14},{14,12},{1,3},{3,1},... | collective-permute-start | bytes 393224 | tf_op jit(solution)/shard_map/ppermute | solution.py:21
  58.6 14.5 %collective-permute-start = (bf16[1,2,2,128,128]{4,3,2,1,0:T(8,128)(2,1)S(1)}, bf16[1,2,2,128,128]{4,3,2,1,0:T(8,128)(2,1)S(1)}, u32[]{:S(2)}, u32[]{:S(2)}) collective-permute-start(bf16[1,2,2,128,128]{4,3,2,1,0:T(8,128)(2,1)S(1)} %get-tuple-element.34), channel_id=1, source_target_pairs={{0,4},{2,6},{4,0},{6,2},{8,12},{10,14},{12,8},{14,10},{1,5},{3,7},... | collective-permute-start | bytes 393224 | tf_op jit(solution)/shard_map/ppermute | solution.py:21
  60.9 20.5 %collective-permute-start.18 = (bf16[1,1072,128]{2,1,0:T(8,128)(2,1)S(1)}, bf16[1,1072,128]{2,1,0:T(8,128)(2,1)S(1)}, u32[]{:S(2)}, u32[]{:S(2)}) collective-permute-start(bf16[1,1072,128]{2,1,0:T(8,128)(2,1)S(1)} %join_packed.2.refs_7_), channel_id=1, source_target_pairs={{0,8},{2,10},{4,12},{6,14},{8,0},{10,2},{12,4},{14,6},{1,9},{3,11}... | collective-permute-start | bytes 823304 | tf_op jit(solution)/shard_map/ppermute | solution.py:21
  65.3 16.0 %collective-permute-start.17 = (bf16[1,1072,128]{2,1,0:T(8,128)(2,1)S(1)}, bf16[1,1072,128]{2,1,0:T(8,128)(2,1)S(1)}, u32[]{:S(2)}, u32[]{:S(2)}) collective-permute-start(bf16[1,1072,128]{2,1,0:T(8,128)(2,1)S(1)} %get-tuple-element.62), channel_id=1, source_target_pairs={{0,2},{2,0},{4,6},{6,4},{8,10},{10,8},{12,14},{14,12},{1,3},{3,1},... | collective-permute-start | bytes 823304 | tf_op jit(solution)/shard_map/ppermute | solution.py:21
  71.5 11.1 %collective-permute-start.15 = (bf16[1,1072,128]{2,1,0:T(8,128)(2,1)S(1)}, bf16[1,1072,128]{2,1,0:T(8,128)(2,1)S(1)}, u32[]{:S(2)}, u32[]{:S(2)}) collective-permute-start(bf16[1,1072,128]{2,1,0:T(8,128)(2,1)S(1)} %attend.13.refs_4_), channel_id=1, source_target_pairs={{0,2},{2,0},{4,6},{6,4},{8,10},{10,8},{12,14},{14,12},{1,3},{3,1},... | collective-permute-start | bytes 823304 | tf_op jit(solution)/shard_map/ppermute | solution.py:21
  71.6 14.4 %collective-permute-start.16 = (bf16[1,1072,128]{2,1,0:T(8,128)(2,1)S(1)}, bf16[1,1072,128]{2,1,0:T(8,128)(2,1)S(1)}, u32[]{:S(2)}, u32[]{:S(2)}) collective-permute-start(bf16[1,1072,128]{2,1,0:T(8,128)(2,1)S(1)} %join_packed.3.refs_4_), channel_id=1, source_target_pairs={{0,8},{2,10},{4,12},{6,14},{8,0},{10,2},{12,4},{14,6},{1,9},{3,11}... | collective-permute-start | bytes 823304 | tf_op jit(solution)/shard_map/ppermute | solution.py:21
  73.1 6.5 %collective-permute-start.2 = (bf16[1,2,2,128,128]{4,3,2,1,0:T(8,128)(2,1)S(1)}, bf16[1,2,2,128,128]{4,3,2,1,0:T(8,128)(2,1)S(1)}, u32[]{:S(2)}, u32[]{:S(2)}) collective-permute-start(bf16[1,2,2,128,128]{4,3,2,1,0:T(8,128)(2,1)S(1)} %collective-permute-done.1), channel_id=1, source_target_pairs={{0,4},{2,6},{4,0},{6,2},{8,12},{10,14},{12,8},{14,10},{1,5},{3,7},... | collective-permute-start | bytes 393224 | tf_op jit(solution)/shard_map/ppermute | solution.py:21

commit v8 on v7

--- a/solution.py
+++ b/solution.py
@@ -56,7 +56,7 @@
 
 
 def last_pages(cap):
-    return max(1, cap // 4)
+    return max(1, 3 * cap // 8)
 
 
 def gather_body(owner_ref, table_ref, length_ref, pool_ref, *refs, near, waits, ranges, cap):
@@ -554,6 +554,8 @@
     for k in each:
         joined = join_packed(*far[k], scale, after=after)
         back.append(moved(joined, pairs))
+        after = [joined]
+    for k in each:
         mine, mine_table, theirs, theirs_table = started[k]
         near_keys = [(a, 0) for a in got_near[k]]
         near_at = [(0, i, 0) for i in range(1, near)]
@@ -569,7 +571,7 @@
                 group,
                 1,
                 prev=[mine, theirs],
-                after=[joined],
+                after=after,
             )
             own_part = results[:2]
             other_part = results[2]
@@ -586,7 +588,7 @@
                 group,
                 1,
                 prev=[theirs],
-                after=[joined],
+                after=after,
             )
             early = attend(
                 scalars,

time: 87.5 us -> 88.6 us (1.013)
  waiting for transfers between devices: 16.7 us -> 20.1 us
  starting transfers between devices: 24.4 us -> 21.7 us
    ppermute x19, waiting for transfers between devices: 16.7 us -> 20.1 us  [moved(): return lax.ppermute(array, 'pool', [(i, i ^ apart) for i in range(count)])]
    ppermute x19, starting transfers between devices: 24.4 us -> 21.7 us  [moved(): return lax.ppermute(array, 'pool', [(i, i ^ apart) for i in range(count)])]
  transfers between devices with their start and end apart: 19 -> 19, of which waited for: 4 -> 6; matrix products, arithmetic and copies ran while one was open for 0% -> 0% of each run, Pallas kernels for 49% -> 49%
where the time goes in v8:
time: 88.6 us; the launch traced here: 88.3 us
  Pallas kernels  44.5 us (50%)
  starting transfers between devices  21.7 us (24%)
  waiting for transfers between devices  20.1 us (23%)
  local copies, waits for them, and re-layouts  1.13 us (1%)
    pallas_call x8, Pallas kernels, attend(): pl.pallas_call(functools.partial(attend_body, halves=halves, seen_at=seen...  34 us
    ppermute x19, starting transfers between devices, moved(): return lax.ppermute(array, 'pool', [(i, i ^ apart) for i in range(count)])  21.7 us
    ppermute x19, waiting for transfers between devices, moved(): return lax.ppermute(array, 'pool', [(i, i ^ apart) for i in range(count)])  20.1 us
    pallas_call x2, Pallas kernels, gather_pages(): pl.pallas_call(functools.partial(gather_body, near=near, waits=len(after)...  7.36 us
    pallas_call x2, Pallas kernels, join_out(): pl.pallas_call(functools.partial(join_body, scale=scale, packs=False, wai...  2.44 us
  transfers between devices with their start and end apart: 19, of which 6 were waited for; matrix products, arithmetic and copies ran while one was open for 0% of the time, Pallas kernels for 49%

profile of v8, /device:TPU:0, one launch (start us, length us, event | category | flops | bytes accessed | tf_op | source)
XLA Modules:
  0.0 88.3 jit_solution(1642060535124412274)
XLA Ops:
  0.6 1.1 %slice_bitcast_fusion = (bf16[1,1024,128]{2,1,0:T(8,128)(2,1)S(1)}, bf16[1,1024,128]{2,1,0:T(8,128)(2,1)S(1)}) fusion(bf16[128,16,128]{2,1,0:T(8,128)(2,1)} %param.6), kind=kLoop, calls=%fused_computation | loop fusion | bytes 1048576 | tf_op jit(solution)/shard_map/reshape | solution.py:486
  1.7 3.1 %collective-permute-start.5 = (bf16[1,1024,128]{2,1,0:T(8,128)(2,1)S(1)}, bf16[1,1024,128]{2,1,0:T(8,128)(2,1)S(1)}, u32[]{:S(2)}, u32[]{:S(2)}) collective-permute-start(bf16[1,1024,128]{2,1,0:T(8,128)(2,1)S(1)} %get-tuple-element.64.refs_0_), channel_id=1, source_target_pairs={{0,2},{2,0},{4,6},{6,4},{8,10},{10,8},{12,14},{14,12},{1,3},{3,1},... | collective-permute-start | bytes 786440 | tf_op jit(solution)/shard_map/ppermute | solution.py:21
  4.8 2.6 %collective-permute-start.10 = (bf16[1,1024,128]{2,1,0:T(8,128)(2,1)S(1)}, bf16[1,1024,128]{2,1,0:T(8,128)(2,1)S(1)}, u32[]{:S(2)}, u32[]{:S(2)}) collective-permute-start(bf16[1,1024,128]{2,1,0:T(8,128)(2,1)S(1)} %get-tuple-element.64.refs_0_), channel_id=1, source_target_pairs={{0,8},{2,10},{4,12},{6,14},{8,0},{10,2},{12,4},{14,6},{1,9},{3,11}... | collective-permute-start | bytes 786440 | tf_op jit(solution)/shard_map/ppermute | solution.py:21
  7.4 2.3 %gather_pages.3 = bf16[1,8,2,128,128]{4,3,2,1,0:T(8,128)(2,1)S(1)} custom-call(s32[1]{0:T(128)} %bitcast.owner_ref, s32[4,64]{1,0:T(4,128)} %table_ref.3, s32[4]{0:T(128)} %length_ref.3, bf16[33,2,2,128,128]{4,3,2,1,0:T(8,128)(2,1)} %pool_ref.3), custom_call_target="tpu_custom_call" | custom-call | tf_op jit(solution)/shard_map/gather_pages/pallas_call | solution.py:127
  9.7 1.6 %collective-permute-start.12 = (bf16[1,8,2,128,128]{4,3,2,1,0:T(8,128)(2,1)S(1)}, bf16[1,8,2,128,128]{4,3,2,1,0:T(8,128)(2,1)S(1)}, u32[]{:S(2)}, u32[]{:S(2)}) collective-permute-start(bf16[1,8,2,128,128]{4,3,2,1,0:T(8,128)(2,1)S(1)} %gather_pages.3), channel_id=1, source_target_pairs={{0,4},{2,6},{4,0},{6,2},{8,12},{10,14},{12,8},{14,10},{1,5},{3,7},... | collective-permute-start | bytes 1572872 | tf_op jit(solution)/shard_map/ppermute | solution.py:21
  11.3 0.5 collective-permute-start.4
  11.9 0.3 collective-permute-start.7
  12.2 5.1 %gather_pages.2 = (bf16[1,8,2,128,128]{4,3,2,1,0:T(8,128)(2,1)S(1)}, bf16[1,8,2,128,128]{4,3,2,1,0:T(8,128)(2,1)S(1)}, bf16[1,5,2,128,128]{4,3,2,1,0:T(8,128)(2,...) custom-call(s32[1]{0:T(128)} %bitcast.owner_ref, ...), custom_call_target="tpu_custom_call" | custom-call | tf_op jit(solution)/shard_map/gather_pages/pallas_call | solution.py:127
  17.3 0.0 collective-permute-done.5.refs_1_
  17.3 0.2 collective-permute-start.9
  17.5 2.8 %collective-permute-done.10.refs_0_ = bf16[1,1024,128]{2,1,0:T(8,128)(2,1)S(1)} collective-permute-done((bf16[1,1024,128]{2,1,0:T(8,128)(2,1)S(1)}, bf16[1,1024,128]{2,1,0:T(8,128)(2,1)S(1)}, u32[]{:S(2)}, u32[]{:S(2)}) %collective-permute-start.10) | collective-permute-done | bytes 262176 | tf_op jit(solution)/shard_map/ppermute | solution.py:21
  20.3 0.5 collective-permute-start.11
  20.8 4.9 %attend.8 = (f32[1,1024,128]{2,1,0:T(8,128)S(1)}, f32[1,16,128]{2,1,0:T(8,128)S(1)}, f32[1,1024,128]{2,1,0:T(8,128)S(1)}, f32[1,16,128]{2,1,0:T(8,128)S(1)}, bf16[33,2,2,128,128]{4,3,2,1,0:T(8,128)(2,1)}) custom-call(s32[1]{0:T(128)} %bitcast.owner_ref, s32[3,2]{1,0:T(4,128)S(1)} %get-tuple-element.33.seen_ref, s32[8]{0:T(128)S(1)} %copy-done, ...), custom_call_target="tpu_custom_call" | custom-call | flops 1207959552 | bytes 589824 | tf_op jit(solution)/shard_map/attend/pallas_call | solution.py:364
  25.7 0.0 collective-permute-done.4.refs_1_.refs_0_
  25.7 0.2 collective-permute-start.6
  25.9 5.0 %collective-permute-done.7.refs_0_ = bf16[1,1024,128]{2,1,0:T(8,128)(2,1)S(1)} collective-permute-done((bf16[1,1024,128]{2,1,0:T(8,128)(2,1)S(1)}, bf16[1,1024,128]{2,1,0:T(8,128)(2,1)S(1)}, u32[]{:S(2)}, u32[]{:S(2)}) %collective-permute-start.7) | collective-permute-done | bytes 262176 | tf_op jit(solution)/shard_map/ppermute | solution.py:21
  31.0 0.5 collective-permute-start.8
  31.5 4.8 %attend.9 = (f32[1,1024,128]{2,1,0:T(8,128)S(1)}, f32[1,16,128]{2,1,0:T(8,128)S(1)}, f32[1,1024,128]{2,1,0:T(8,128)S(1)}, f32[1,16,128]{2,1,0:T(8,128)S(1)}) custom-call(s32[1]{0:T(128)} %bitcast.owner_ref, s32[3,2]{1,0:T(4,128)S(1)} %get-tuple-element.33.seen_ref, s32[8]{0:T(128)S(1)} %copy-done, bf16[1,1024,128]{2,1,0:T(8,128)(2,1)S(1)} %get-tuple-element.65.refs_0_, ...), custom_call_target="tpu_custom_call" | custom-call | flops 1207959552 | bytes 589824 | tf_op jit(solution)/shard_map/attend/pallas_call | solution.py:364
  36.3 0.0 collective-permute-done.12.refs_3_
  36.3 0.0 collective-permute-done.11.refs_1_
  36.3 6.7 %attend.10 = (f32[1,1024,128]{2,1,0:T(8,128)S(1)}, f32[1,16,128]{2,1,0:T(8,128)S(1)}, bf16[1,1072,128]{2,1,0:T(8,128)(2,1)S(1)}) custom-call(s32[1]{0:T(128)} %bitcast.owner_ref, s32[3,2]{1,0:T(4,128)S(1)} %get-tuple-element.33.seen_ref, s32[8]{0:T(128)S(1)} %copy-done, bf16[1,1024,128]{2,1,0:T(8,128)(2,1)S(1)} %collective-permute-done.10.refs_0_, ...), custom_call_target="tpu_custom_call" | custom-call | flops 2147483648 | bytes 1048576 | tf_op jit(solution)/shard_map/attend/pallas_call | solution.py:364
  43.0 1.6 %collective-permute-start.14 = (bf16[1,1072,128]{2,1,0:T(8,128)(2,1)S(1)}, bf16[1,1072,128]{2,1,0:T(8,128)(2,1)S(1)}, u32[]{:S(2)}, u32[]{:S(2)}) collective-permute-start(bf16[1,1072,128]{2,1,0:T(8,128)(2,1)S(1)} %get-tuple-element.55), channel_id=1, source_target_pairs={{0,2},{2,0},{4,6},{6,4},{8,10},{10,8},{12,14},{14,12},{1,3},{3,1},... | collective-permute-start | bytes 823304 | tf_op jit(solution)/shard_map/ppermute | solution.py:21
  44.6 1.3 %collective-permute-done.9.refs_3_ = bf16[1,8,2,128,128]{4,3,2,1,0:T(8,128)(2,1)S(1)} collective-permute-done((bf16[1,8,2,128,128]{4,3,2,1,0:T(8,128)(2,1)S(1)}, bf16[1,8,2,128,128]{4,3,2,1,0:T(8,128)(2,1)S(1)}, u32[]{:S(2)}, u32[]{:S(2)}) %collective-permute-start.9) | collective-permute-done | bytes 524320 | tf_op jit(solution)/shard_map/ppermute | solution.py:21
  45.9 0.0 collective-permute-done.8.refs_1_
  45.9 6.9 %attend.11 = (f32[1,1024,128]{2,1,0:T(8,128)S(1)}, f32[1,16,128]{2,1,0:T(8,128)S(1)}, bf16[1,1072,128]{2,1,0:T(8,128)(2,1)S(1)}) custom-call(s32[1]{0:T(128)} %bitcast.owner_ref, s32[3,2]{1,0:T(4,128)S(1)} %get-tuple-element.33.seen_ref, s32[8]{0:T(128)S(1)} %copy-done, bf16[1,1024,128]{2,1,0:T(8,128)(2,1)S(1)} %collective-permute-done.7.refs_0_, ...), custom_call_target="tpu_custom_call" | custom-call | flops 2147483648 | bytes 1048576 | tf_op jit(solution)/shard_map/attend/pallas_call | solution.py:364
  52.8 0.5 collective-permute-start.13
  53.3 1.1 %collective-permute-start.3 = (bf16[1,5,2,128,128]{4,3,2,1,0:T(8,128)(2,1)S(1)}, bf16[1,5,2,128,128]{4,3,2,1,0:T(8,128)(2,1)S(1)}, u32[]{:S(2)}, u32[]{:S(2)}) collective-permute-start(bf16[1,5,2,128,128]{4,3,2,1,0:T(8,128)(2,1)S(1)} %get-tuple-element.35), channel_id=1, source_target_pairs={{0,4},{2,6},{4,0},{6,2},{8,12},{10,14},{12,8},{14,10},{1,5},{3,7},... | collective-permute-start | bytes 983048 | tf_op jit(solution)/shard_map/ppermute | solution.py:21
  54.4 1.5 %collective-permute-start.1 = (bf16[1,3,2,128,128]{4,3,2,1,0:T(8,128)(2,1)S(1)}, bf16[1,3,2,128,128]{4,3,2,1,0:T(8,128)(2,1)S(1)}, u32[]{:S(2)}, u32[]{:S(2)}) collective-permute-start(bf16[1,3,2,128,128]{4,3,2,1,0:T(8,128)(2,1)S(1)} %get-tuple-element.34), channel_id=1, source_target_pairs={{0,2},{2,0},{4,6},{6,4},{8,10},{10,8},{12,14},{14,12},{1,3},{3,1},... | collective-permute-start | bytes 589832 | tf_op jit(solution)/shard_map/ppermute | solution.py:21
  55.9 1.0 %collective-permute-start = (bf16[1,3,2,128,128]{4,3,2,1,0:T(8,128)(2,1)S(1)}, bf16[1,3,2,128,128]{4,3,2,1,0:T(8,128)(2,1)S(1)}, u32[]{:S(2)}, u32[]{:S(2)}) collective-permute-start(bf16[1,3,2,128,128]{4,3,2,1,0:T(8,128)(2,1)S(1)} %get-tuple-element.34), channel_id=1, source_target_pairs={{0,4},{2,6},{4,0},{6,2},{8,12},{10,14},{12,8},{14,10},{1,5},{3,7},... | collective-permute-start | bytes 589832 | tf_op jit(solution)/shard_map/ppermute | solution.py:21
  56.9 0.4 join_packed.2.refs_1_
  57.3 2.9 %collective-permute-done.13.refs_0_ = bf16[1,1072,128]{2,1,0:T(8,128)(2,1)S(1)} collective-permute-done((bf16[1,1072,128]{2,1,0:T(8,128)(2,1)S(1)}, bf16[1,1072,128]{2,1,0:T(8,128)(2,1)S(1)}, u32[]{:S(2)}, u32[]{:S(2)}) %collective-permute-start.13) | collective-permute-done | bytes 274464 | tf_op jit(solution)/shard_map/ppermute | solution.py:21
  60.2 2.0 %collective-permute-start.18 = (bf16[1,1072,128]{2,1,0:T(8,128)(2,1)S(1)}, bf16[1,1072,128]{2,1,0:T(8,128)(2,1)S(1)}, u32[]{:S(2)}, u32[]{:S(2)}) collective-permute-start(bf16[1,1072,128]{2,1,0:T(8,128)(2,1)S(1)} %join_packed.2.refs_1_), channel_id=1, source_target_pairs={{0,8},{2,10},{4,12},{6,14},{8,0},{10,2},{12,4},{14,6},{1,9},{3,11}... | collective-permute-start | bytes 823304 | tf_op jit(solution)/shard_map/ppermute | solution.py:21
  62.2 0.4 join_packed.3.refs_7_
  62.6 4.3 %attend.12 = (f32[1,1024,128]{2,1,0:T(8,128)S(1)}, f32[1,16,128]{2,1,0:T(8,128)S(1)}, bf16[1,1072,128]{2,1,0:T(8,128)(2,1)S(1)}) custom-call(s32[1]{0:T(128)} %bitcast.owner_ref, s32[3,2]{1,0:T(4,128)S(1)} %get-tuple-element.33.seen_ref, s32[8]{0:T(128)S(1)} %copy-done, bf16[1,1024,128]{2,1,0:T(8,128)(2,1)S(1)} %get-tuple-element.64.refs_0_, ...), custom_call_target="tpu_custom_call" | custom-call | flops 1073741824 | bytes 524288 | tf_op jit(solution)/shard_map/attend/pallas_call | solution.py:364
  66.9 0.6 collective-permute-start.17
  67.5 2.1 %collective-permute-done.3.refs_1_ = bf16[1,5,2,128,128]{4,3,2,1,0:T(8,128)(2,1)S(1)} collective-permute-done((bf16[1,5,2,128,128]{4,3,2,1,0:T(8,128)(2,1)S(1)}, bf16[1,5,2,128,128]{4,3,2,1,0:T(8,128)(2,1)S(1)}, u32[]{:S(2)}, u32[]{:S(2)}) %collective-permute-start.3) | collective-permute-done | bytes 327712 | tf_op jit(solution)/shard_map/ppermute | solution.py:21
  69.6 2.2 %attend.13.refs_4_ = bf16[1,1072,128]{2,1,0:T(8,128)(2,1)S(1)} custom-call(s32[1]{0:T(128)} %bitcast.owner_ref, s32[3,2]{1,0:T(4,128)S(1)} %get-tuple-element.33.seen_ref, s32[8]{0:T(128)S(1)} %copy-done, bf16[1,1024,128]{2,1,0:T(8,128)(2,1)S(1)} %collective-permute-done.4.refs_1_.refs_0_, bf16[1,5,2,128,128]{4,3,2,1,0:T(8,128)(2,1)S(1)} %collective-permute-done.3.refs_1_, ...), custom_call_target="tpu_custom_call" | custom-call | flops 335544320 | bytes 327680 | tf_op jit(solution)/shard_map/attend/pallas_call | solution.py:364
  71.8 1.4 %collective-permute-start.15 = (bf16[1,1072,128]{2,1,0:T(8,128)(2,1)S(1)}, bf16[1,1072,128]{2,1,0:T(8,128)(2,1)S(1)}, u32[]{:S(2)}, u32[]{:S(2)}) collective-permute-start(bf16[1,1072,128]{2,1,0:T(8,128)(2,1)S(1)} %attend.13.refs_4_), channel_id=1, source_target_pairs={{0,2},{2,0},{4,6},{6,4},{8,10},{10,8},{12,14},{14,12},{1,3},{3,1},... | collective-permute-start | bytes 823304 | tf_op jit(solution)/shard_map/ppermute | solution.py:21
  73.2 0.1 collective-permute-start.16
  73.3 2.5 %collective-permute-start.2 = (bf16[1,3,2,128,128]{4,3,2,1,0:T(8,128)(2,1)S(1)}, bf16[1,3,2,128,128]{4,3,2,1,0:T(8,128)(2,1)S(1)}, u32[]{:S(2)}, u32[]{:S(2)}) collective-permute-start(bf16[1,3,2,128,128]{4,3,2,1,0:T(8,128)(2,1)S(1)} %collective-permute-done.1), channel_id=1, source_target_pairs={{0,4},{2,6},{4,0},{6,2},{8,12},{10,14},{12,8},{14,10},{1,5},{3,7},... | collective-permute-start | bytes 589832 | tf_op jit(solution)/shard_map/ppermute | solution.py:21
  75.7 2.1 %attend.14 = (f32[1,1024,128]{2,1,0:T(8,128)S(1)}, f32[1,16,128]{2,1,0:T(8,128)S(1)}) custom-call(s32[1]{0:T(128)} %bitcast.owner_ref, s32[3,2]{1,0:T(4,128)S(1)} %get-tuple-element.33.seen_ref, s32[8]{0:T(128)S(1)} %copy-done, bf16[1,1024,128]{2,1,0:T(8,128)(2,1)S(1)} %get-tuple-element.65.refs_0_, ...), custom_call_target="tpu_custom_call" | custom-call | flops 335544320 | bytes 327680 | tf_op jit(solution)/shard_map/attend/pallas_call | solution.py:364
  77.9 5.8 %collective-permute-done.2.refs_2_ = bf16[1,3,2,128,128]{4,3,2,1,0:T(8,128)(2,1)S(1)} collective-permute-done((bf16[1,3,2,128,128]{4,3,2,1,0:T(8,128)(2,1)S(1)}, bf16[1,3,2,128,128]{4,3,2,1,0:T(8,128)(2,1)S(1)}, u32[]{:S(2)}, u32[]{:S(2)}) %collective-permute-start.2) | collective-permute-done | bytes 196640 | tf_op jit(solution)/shard_map/ppermute | solution.py:21
  83.7 2.1 %attend.15 = (f32[1,1024,128]{2,1,0:T(8,128)S(1)}, f32[1,16,128]{2,1,0:T(8,128)S(1)}) custom-call(s32[1]{0:T(128)} %bitcast.owner_ref, s32[3,2]{1,0:T(4,128)S(1)} %get-tuple-element.33.seen_ref, s32[8]{0:T(128)S(1)} %copy-done, bf16[1,1024,128]{2,1,0:T(8,128)(2,1)S(1)} %get-tuple-element.65.refs_0_, ...), custom_call_target="tpu_custom_call" | custom-call | flops 402653184 | bytes 393216 | tf_op jit(solution)/shard_map/attend/pallas_call | solution.py:364
  85.8 0.0 collective-permute-done.17.refs_0_
  85.8 0.0 collective-permute-done.18.refs_1_
  85.9 1.2 %join_out.2.refs_2_ = bf16[128,16,128]{2,1,0:T(8,128)(2,1)} custom-call(f32[1,1024,128]{2,1,0:T(8,128)S(1)} %get-tuple-element.61.own_mixed, f32[1,16,128]{2,1,0:T(8,128)S(1)} %get-tuple-element.56.refs_4_.own_table, bf16[1,1072,128]{2,1,0:T(8,128)(2,1)S(1)} %collective-permute-done.17.refs_0_, bf16[1,1072,128]{2,1,0:T(8,128)(2,1)S(1)} %collective-permute-done.18.refs_1_), custom_call_target="tpu_custom_call" | custom-call | tf_op jit(solution)/shard_map/join_out/pallas_call | solution.py:459
  87.1 0.0 collective-permute-done.16.refs_1_
  87.1 1.2 %join_out.3 = bf16[128,16,128]{2,1,0:T(8,128)(2,1)} custom-call(f32[1,1024,128]{2,1,0:T(8,128)S(1)} %get-tuple-element.59.own_mixed, f32[1,16,128]{2,1,0:T(8,128)S(1)} %get-tuple-element.60.own_table, bf16[1,1072,128]{2,1,0:T(8,128)(2,1)S(1)} %collective-permute-done.15.refs_0_, ...), custom_call_target="tpu_custom_call", output_to_operand_aliasing={{}: (4, {})} | custom-call | tf_op jit(solution)/shard_map/join_out/pallas_call | solution.py:459
  (10 shorter events, 0.0 us)
Async XLA Ops:
  0.6 11.6 %copy-start.1 = (bf16[128,2,2,128]{3,2,1,0:T(2,128)(2,1)S(1)}, bf16[128,2,2,128]{3,2,1,0:T(2,128)(2,1)}, u32[]{:S(2)}) copy-start(bf16[128,2,2,128]{3,2,1,0:T(2,128)(2,1)} %param.7) | copy-start | bytes 393220
  1.7 15.5 %collective-permute-start.5 = (bf16[1,1024,128]{2,1,0:T(8,128)(2,1)S(1)}, bf16[1,1024,128]{2,1,0:T(8,128)(2,1)S(1)}, u32[]{:S(2)}, u32[]{:S(2)}) collective-permute-start(bf16[1,1024,128]{2,1,0:T(8,128)(2,1)S(1)} %get-tuple-element.64.refs_0_), channel_id=1, source_target_pairs={{0,2},{2,0},{4,6},{6,4},{8,10},{10,8},{12,14},{14,12},{1,3},{3,1},... | collective-permute-start | bytes 786440 | tf_op jit(solution)/shard_map/ppermute | solution.py:21
  4.8 15.5 %collective-permute-start.10 = (bf16[1,1024,128]{2,1,0:T(8,128)(2,1)S(1)}, bf16[1,1024,128]{2,1,0:T(8,128)(2,1)S(1)}, u32[]{:S(2)}, u32[]{:S(2)}) collective-permute-start(bf16[1,1024,128]{2,1,0:T(8,128)(2,1)S(1)} %get-tuple-element.64.refs_0_), channel_id=1, source_target_pairs={{0,8},{2,10},{4,12},{6,14},{8,0},{10,2},{12,4},{14,6},{1,9},{3,11}... | collective-permute-start | bytes 786440 | tf_op jit(solution)/shard_map/ppermute | solution.py:21
  7.4 13.4 %copy-start = (s32[8]{0:T(128)S(1)}, s32[8]{0:T(128)}, u32[]{:S(2)}) copy-start(s32[8]{0:T(128)} %fresh_ref.15) | copy-start | bytes 100
  9.7 26.6 %collective-permute-start.12 = (bf16[1,8,2,128,128]{4,3,2,1,0:T(8,128)(2,1)S(1)}, bf16[1,8,2,128,128]{4,3,2,1,0:T(8,128)(2,1)S(1)}, u32[]{:S(2)}, u32[]{:S(2)}) collective-permute-start(bf16[1,8,2,128,128]{4,3,2,1,0:T(8,128)(2,1)S(1)} %gather_pages.3), channel_id=1, source_target_pairs={{0,4},{2,6},{4,0},{6,2},{8,12},{10,14},{12,8},{14,10},{1,5},{3,7},... | collective-permute-start | bytes 1572872 | tf_op jit(solution)/shard_map/ppermute | solution.py:21
  11.3 14.3 %collective-permute-start.4 = (bf16[1,1024,128]{2,1,0:T(8,128)(2,1)S(1)}, bf16[1,1024,128]{2,1,0:T(8,128)(2,1)S(1)}, u32[]{:S(2)}, u32[]{:S(2)}) collective-permute-start(bf16[1,1024,128]{2,1,0:T(8,128)(2,1)S(1)} %get-tuple-element.65.refs_0_), channel_id=1, source_target_pairs={{0,2},{2,0},{4,6},{6,4},{8,10},{10,8},{12,14},{14,12},{1,3},{3,1},... | collective-permute-start | bytes 786440 | tf_op jit(solution)/shard_map/ppermute | solution.py:21
  11.9 19.1 %collective-permute-start.7 = (bf16[1,1024,128]{2,1,0:T(8,128)(2,1)S(1)}, bf16[1,1024,128]{2,1,0:T(8,128)(2,1)S(1)}, u32[]{:S(2)}, u32[]{:S(2)}) collective-permute-start(bf16[1,1024,128]{2,1,0:T(8,128)(2,1)S(1)} %get-tuple-element.65.refs_0_), channel_id=1, source_target_pairs={{0,8},{2,10},{4,12},{6,14},{8,0},{10,2},{12,4},{14,6},{1,9},{3,11}... | collective-permute-start | bytes 786440 | tf_op jit(solution)/shard_map/ppermute | solution.py:21
  17.3 28.6 %collective-permute-start.9 = (bf16[1,8,2,128,128]{4,3,2,1,0:T(8,128)(2,1)S(1)}, bf16[1,8,2,128,128]{4,3,2,1,0:T(8,128)(2,1)S(1)}, u32[]{:S(2)}, u32[]{:S(2)}) collective-permute-start(bf16[1,8,2,128,128]{4,3,2,1,0:T(8,128)(2,1)S(1)} %get-tuple-element.48), channel_id=1, source_target_pairs={{0,4},{2,6},{4,0},{6,2},{8,12},{10,14},{12,8},{14,10},{1,5},{3,7},... | collective-permute-start | bytes 1572872 | tf_op jit(solution)/shard_map/ppermute | solution.py:21
  20.3 16.0 %collective-permute-start.11 = (bf16[1,1024,128]{2,1,0:T(8,128)(2,1)S(1)}, bf16[1,1024,128]{2,1,0:T(8,128)(2,1)S(1)}, u32[]{:S(2)}, u32[]{:S(2)}) collective-permute-start(bf16[1,1024,128]{2,1,0:T(8,128)(2,1)S(1)} %collective-permute-done.10.refs_0_), channel_id=1, source_target_pairs={{0,2},{2,0},{4,6},{6,4},{8,10},{10,8},{12,14},{14,12},{1,3},{3,1},... | collective-permute-start | bytes 786440 | tf_op jit(solution)/shard_map/ppermute | solution.py:21
  25.7 36.9 %collective-permute-start.6 = (bf16[1,8,2,128,128]{4,3,2,1,0:T(8,128)(2,1)S(1)}, bf16[1,8,2,128,128]{4,3,2,1,0:T(8,128)(2,1)S(1)}, u32[]{:S(2)}, u32[]{:S(2)}) collective-permute-start(bf16[1,8,2,128,128]{4,3,2,1,0:T(8,128)(2,1)S(1)} %get-tuple-element.43), channel_id=1, source_target_pairs={{0,4},{2,6},{4,0},{6,2},{8,12},{10,14},{12,8},{14,10},{1,5},{3,7},... | collective-permute-start | bytes 1572872 | tf_op jit(solution)/shard_map/ppermute | solution.py:21
  31.0 14.9 %collective-permute-start.8 = (bf16[1,1024,128]{2,1,0:T(8,128)(2,1)S(1)}, bf16[1,1024,128]{2,1,0:T(8,128)(2,1)S(1)}, u32[]{:S(2)}, u32[]{:S(2)}) collective-permute-start(bf16[1,1024,128]{2,1,0:T(8,128)(2,1)S(1)} %collective-permute-done.7.refs_0_), channel_id=1, source_target_pairs={{0,2},{2,0},{4,6},{6,4},{8,10},{10,8},{12,14},{14,12},{1,3},{3,1},... | collective-permute-start | bytes 786440 | tf_op jit(solution)/shard_map/ppermute | solution.py:21
  43.0 12.9 %collective-permute-start.14 = (bf16[1,1072,128]{2,1,0:T(8,128)(2,1)S(1)}, bf16[1,1072,128]{2,1,0:T(8,128)(2,1)S(1)}, u32[]{:S(2)}, u32[]{:S(2)}) collective-permute-start(bf16[1,1072,128]{2,1,0:T(8,128)(2,1)S(1)} %get-tuple-element.55), channel_id=1, source_target_pairs={{0,2},{2,0},{4,6},{6,4},{8,10},{10,8},{12,14},{14,12},{1,3},{3,1},... | collective-permute-start | bytes 823304 | tf_op jit(solution)/shard_map/ppermute | solution.py:21
  52.8 7.4 %collective-permute-start.13 = (bf16[1,1072,128]{2,1,0:T(8,128)(2,1)S(1)}, bf16[1,1072,128]{2,1,0:T(8,128)(2,1)S(1)}, u32[]{:S(2)}, u32[]{:S(2)}) collective-permute-start(bf16[1,1072,128]{2,1,0:T(8,128)(2,1)S(1)} %get-tuple-element.53), channel_id=1, source_target_pairs={{0,2},{2,0},{4,6},{6,4},{8,10},{10,8},{12,14},{14,12},{1,3},{3,1},... | collective-permute-start | bytes 823304 | tf_op jit(solution)/shard_map/ppermute | solution.py:21
  53.3 16.3 %collective-permute-start.3 = (bf16[1,5,2,128,128]{4,3,2,1,0:T(8,128)(2,1)S(1)}, bf16[1,5,2,128,128]{4,3,2,1,0:T(8,128)(2,1)S(1)}, u32[]{:S(2)}, u32[]{:S(2)}) collective-permute-start(bf16[1,5,2,128,128]{4,3,2,1,0:T(8,128)(2,1)S(1)} %get-tuple-element.35), channel_id=1, source_target_pairs={{0,4},{2,6},{4,0},{6,2},{8,12},{10,14},{12,8},{14,10},{1,5},{3,7},... | collective-permute-start | bytes 983048 | tf_op jit(solution)/shard_map/ppermute | solution.py:21
  54.4 18.8 %collective-permute-start.1 = (bf16[1,3,2,128,128]{4,3,2,1,0:T(8,128)(2,1)S(1)}, bf16[1,3,2,128,128]{4,3,2,1,0:T(8,128)(2,1)S(1)}, u32[]{:S(2)}, u32[]{:S(2)}) collective-permute-start(bf16[1,3,2,128,128]{4,3,2,1,0:T(8,128)(2,1)S(1)} %get-tuple-element.34), channel_id=1, source_target_pairs={{0,2},{2,0},{4,6},{6,4},{8,10},{10,8},{12,14},{14,12},{1,3},{3,1},... | collective-permute-start | bytes 589832 | tf_op jit(solution)/shard_map/ppermute | solution.py:21
  55.9 17.4 %collective-permute-start = (bf16[1,3,2,128,128]{4,3,2,1,0:T(8,128)(2,1)S(1)}, bf16[1,3,2,128,128]{4,3,2,1,0:T(8,128)(2,1)S(1)}, u32[]{:S(2)}, u32[]{:S(2)}) collective-permute-start(bf16[1,3,2,128,128]{4,3,2,1,0:T(8,128)(2,1)S(1)} %get-tuple-element.34), channel_id=1, source_target_pairs={{0,4},{2,6},{4,0},{6,2},{8,12},{10,14},{12,8},{14,10},{1,5},{3,7},... | collective-permute-start | bytes 589832 | tf_op jit(solution)/shard_map/ppermute | solution.py:21
  60.2 25.6 %collective-permute-start.18 = (bf16[1,1072,128]{2,1,0:T(8,128)(2,1)S(1)}, bf16[1,1072,128]{2,1,0:T(8,128)(2,1)S(1)}, u32[]{:S(2)}, u32[]{:S(2)}) collective-permute-start(bf16[1,1072,128]{2,1,0:T(8,128)(2,1)S(1)} %join_packed.2.refs_1_), channel_id=1, source_target_pairs={{0,8},{2,10},{4,12},{6,14},{8,0},{10,2},{12,4},{14,6},{1,9},{3,11}... | collective-permute-start | bytes 823304 | tf_op jit(solution)/shard_map/ppermute | solution.py:21
  66.9 18.9 %collective-permute-start.17 = (bf16[1,1072,128]{2,1,0:T(8,128)(2,1)S(1)}, bf16[1,1072,128]{2,1,0:T(8,128)(2,1)S(1)}, u32[]{:S(2)}, u32[]{:S(2)}) collective-permute-start(bf16[1,1072,128]{2,1,0:T(8,128)(2,1)S(1)} %get-tuple-element.62), channel_id=1, source_target_pairs={{0,2},{2,0},{4,6},{6,4},{8,10},{10,8},{12,14},{14,12},{1,3},{3,1},... | collective-permute-start | bytes 823304 | tf_op jit(solution)/shard_map/ppermute | solution.py:21
  71.8 15.3 %collective-permute-start.15 = (bf16[1,1072,128]{2,1,0:T(8,128)(2,1)S(1)}, bf16[1,1072,128]{2,1,0:T(8,128)(2,1)S(1)}, u32[]{:S(2)}, u32[]{:S(2)}) collective-permute-start(bf16[1,1072,128]{2,1,0:T(8,128)(2,1)S(1)} %attend.13.refs_4_), channel_id=1, source_target_pairs={{0,2},{2,0},{4,6},{6,4},{8,10},{10,8},{12,14},{14,12},{1,3},{3,1},... | collective-permute-start | bytes 823304 | tf_op jit(solution)/shard_map/ppermute | solution.py:21
  73.2 13.9 %collective-permute-start.16 = (bf16[1,1072,128]{2,1,0:T(8,128)(2,1)S(1)}, bf16[1,1072,128]{2,1,0:T(8,128)(2,1)S(1)}, u32[]{:S(2)}, u32[]{:S(2)}) collective-permute-start(bf16[1,1072,128]{2,1,0:T(8,128)(2,1)S(1)} %join_packed.3.refs_7_), channel_id=1, source_target_pairs={{0,8},{2,10},{4,12},{6,14},{8,0},{10,2},{12,4},{14,6},{1,9},{3,11}... | collective-permute-start | bytes 823304 | tf_op jit(solution)/shard_map/ppermute | solution.py:21
  73.3 10.5 %collective-permute-start.2 = (bf16[1,3,2,128,128]{4,3,2,1,0:T(8,128)(2,1)S(1)}, bf16[1,3,2,128,128]{4,3,2,1,0:T(8,128)(2,1)S(1)}, u32[]{:S(2)}, u32[]{:S(2)}) collective-permute-start(bf16[1,3,2,128,128]{4,3,2,1,0:T(8,128)(2,1)S(1)} %collective-permute-done.1), channel_id=1, source_target_pairs={{0,4},{2,6},{4,0},{6,2},{8,12},{10,14},{12,8},{14,10},{1,5},{3,7},... | collective-permute-start | bytes 589832 | tf_op jit(solution)/shard_map/ppermute | solution.py:21

commit v9 on v7

--- a/solution.py
+++ b/solution.py
@@ -94,13 +94,13 @@
             copy.start()
             copies.append(copy)
     if near:
-        asked = [(t, s) for t in range(3) for s in range(near)]
+        asked = [(t, s) for t in range(2) for s in range(near)]
 
         def count(j, seen):
             following = []
             for (t, s), so_far in zip(asked, seen):
-                request = pair ^ (near if t == 1 else 0)
-                _, there = held(request, owner ^ (2 * s + t // 2), j)
+                request = pair ^ (t * near)
+                _, there = held(request, owner ^ (2 * s), j)
                 inside = jnp.clip(length_ref[request] - j * page_len, 0, page_len)
                 following.append(so_far + jnp.where(there, inside, 0))
             return tuple(following)
@@ -122,7 +122,7 @@
     list_count = len({which for which, _, _, _ in ranges})
     specs = [pl.BlockSpec(memory_space=pltpu.VMEM)] * len(outs)
     if near:
-        outs.append(jax.ShapeDtypeStruct((3, near), jnp.int32))
+        outs.append(jax.ShapeDtypeStruct((2, near), jnp.int32))
         specs.append(pl.BlockSpec(memory_space=pltpu.SMEM))
     results = pl.pallas_call(
         functools.partial(gather_body, near=near, waits=len(after), ranges=ranges, cap=cap),
@@ -314,8 +314,8 @@
     rows = queries[0][0].shape[1]
     size = 2 * (rows // block_rows)
     step_rows = min(rows, 1024 // halves)
-    tile_rows = min(step_rows, 256)
     key_count = sum(s.shape[1] * s.shape[3] for s, _ in sources)
+    tile_rows = min(step_rows, 512 if key_count <= 2 * block_rows else 256)
 
     def per_rows(offset):
         return pl.BlockSpec((1, step_rows, lanes), lambda k, i, *_: (k + offset, i, 0))
@@ -506,9 +506,7 @@
 
     got_far = [exchanged(near, k, 0) for k in each]
     got_near = [exchanged(0, k, 0) for k in each]
-    got_late = [moved(pages[i, last, cut], 2 * i) for i in ring]
-    theirs_late = [moved(pages[i, last, cut], 1) for i in ring]
-    got_late += [moved(part, 2 * i) for i, part in zip(ring, theirs_late)]
+    got_late = exchanged(0, last, cut)
     local, local_far = [[pages[i, k, 0] for k in each] for i in (0, near)]
     scalars = (owner_list, seen, new_slots)
 
@@ -575,41 +573,41 @@
             other_part = results[2]
         else:
             late_keys = [(a, 0) for a in got_late]
-            late_at = [(t, i, cut * page_len) for t in (0, 2) for i in ring]
-            (other_part,) = attend(
+            late_at = [(0, i, cut * page_len) for i in range(1, near)]
+            early = attend(
                 scalars,
                 [(other[k], 0)],
                 near_keys,
                 near_at,
-                (True,),
+                (False,),
                 scale,
                 group,
                 1,
                 prev=[theirs],
                 after=[joined],
             )
-            early = attend(
+            (other_part,) = attend(
+                scalars,
+                [(other[k], 0)],
+                late_keys,
+                late_at,
+                (True,),
+                scale,
+                group,
+                1,
+                prev=[(*early, 0)],
+            )
+            own_part = attend(
                 scalars,
                 [(split[k], 0)],
-                near_keys,
-                near_at,
+                near_keys + late_keys,
+                near_at + late_at,
                 (False,),
                 scale,
                 group,
                 1,
                 prev=[mine],
                 after=[other_part],
-            )
-            own_part = attend(
-                scalars,
-                [(split[k], 0)],
-                late_keys,
-                late_at,
-                (False,),
-                scale,
-                group,
-                1,
-                prev=[(*early, 0)],
             )
         ready.append((own_part, moved(other_part, 1)))
         after = [own_part[1]]

time: 87.5 us -> 88.6 us (1.013)
  waiting for transfers between devices: 16.7 us -> 22 us
  starting transfers between devices: 24.4 us -> 20.9 us
    ppermute x19 -> x17, waiting for transfers between devices: 16.7 us -> 22 us  [moved(): return lax.ppermute(array, 'pool', [(i, i ^ apart) for i in range(count)])]
    ppermute x19 -> x17, starting transfers between devices: 24.4 us -> 20.9 us  [moved(): return lax.ppermute(array, 'pool', [(i, i ^ apart) for i in range(count)])]
  transfers between devices with their start and end apart: 19 -> 17, of which waited for: 4 -> 4; matrix products, arithmetic and copies ran while one was open for 0% -> 0% of each run, Pallas kernels for 49% -> 48%
where the time goes in v9:
time: 88.6 us; the launch traced here: 88.3 us
  Pallas kernels  43.6 us (49%)
  waiting for transfers between devices  22 us (25%)
  starting transfers between devices  20.9 us (24%)
  local copies, waits for them, and re-layouts  1.13 us (1%)
    pallas_call x8, Pallas kernels, attend(): pl.pallas_call(functools.partial(attend_body, halves=halves, seen_at=seen...  33.1 us
    ppermute x17, waiting for transfers between devices, moved(): return lax.ppermute(array, 'pool', [(i, i ^ apart) for i in range(count)])  22 us
    ppermute x17, starting transfers between devices, moved(): return lax.ppermute(array, 'pool', [(i, i ^ apart) for i in range(count)])  20.9 us
    pallas_call x2, Pallas kernels, gather_pages(): pl.pallas_call(functools.partial(gather_body, near=near, waits=len(after)...  7.35 us
    pallas_call x2, Pallas kernels, join_out(): pl.pallas_call(functools.partial(join_body, scale=scale, packs=False, wai...  2.43 us
  transfers between devices with their start and end apart: 17, of which 4 were waited for; matrix products, arithmetic and copies ran while one was open for 0% of the time, Pallas kernels for 48%

profile of v9, /device:TPU:0, one launch (start us, length us, event | category | flops | bytes accessed | tf_op | source)
XLA Modules:
  0.0 88.3 jit_solution(17796669259509531803)
XLA Ops:
  0.6 1.1 %slice_bitcast_fusion = (bf16[1,1024,128]{2,1,0:T(8,128)(2,1)S(1)}, bf16[1,1024,128]{2,1,0:T(8,128)(2,1)S(1)}) fusion(bf16[128,16,128]{2,1,0:T(8,128)(2,1)} %param.6), kind=kLoop, calls=%fused_computation | loop fusion | bytes 1048576 | tf_op jit(solution)/shard_map/reshape | solution.py:486
  1.7 3.1 %collective-permute-start.3 = (bf16[1,1024,128]{2,1,0:T(8,128)(2,1)S(1)}, bf16[1,1024,128]{2,1,0:T(8,128)(2,1)S(1)}, u32[]{:S(2)}, u32[]{:S(2)}) collective-permute-start(bf16[1,1024,128]{2,1,0:T(8,128)(2,1)S(1)} %get-tuple-element.64.refs_0_), channel_id=1, source_target_pairs={{0,2},{2,0},{4,6},{6,4},{8,10},{10,8},{12,14},{14,12},{1,3},{3,1},... | collective-permute-start | bytes 786440 | tf_op jit(solution)/shard_map/ppermute | solution.py:21
  4.8 2.3 %gather_pages.3 = bf16[1,8,2,128,128]{4,3,2,1,0:T(8,128)(2,1)S(1)} custom-call(s32[1]{0:T(128)} %bitcast.owner_ref, s32[4,64]{1,0:T(4,128)} %table_ref.3, s32[4]{0:T(128)} %length_ref.3, bf16[33,2,2,128,128]{4,3,2,1,0:T(8,128)(2,1)} %pool_ref.3), custom_call_target="tpu_custom_call" | custom-call | tf_op jit(solution)/shard_map/gather_pages/pallas_call | solution.py:127
  7.1 1.6 %collective-permute-start.9 = (bf16[1,8,2,128,128]{4,3,2,1,0:T(8,128)(2,1)S(1)}, bf16[1,8,2,128,128]{4,3,2,1,0:T(8,128)(2,1)S(1)}, u32[]{:S(2)}, u32[]{:S(2)}) collective-permute-start(bf16[1,8,2,128,128]{4,3,2,1,0:T(8,128)(2,1)S(1)} %gather_pages.3), channel_id=1, source_target_pairs={{0,4},{2,6},{4,0},{6,2},{8,12},{10,14},{12,8},{14,10},{1,5},{3,7},... | collective-permute-start | bytes 1572872 | tf_op jit(solution)/shard_map/ppermute | solution.py:21
  8.8 2.6 %collective-permute-start.7 = (bf16[1,1024,128]{2,1,0:T(8,128)(2,1)S(1)}, bf16[1,1024,128]{2,1,0:T(8,128)(2,1)S(1)}, u32[]{:S(2)}, u32[]{:S(2)}) collective-permute-start(bf16[1,1024,128]{2,1,0:T(8,128)(2,1)S(1)} %get-tuple-element.64.refs_0_), channel_id=1, source_target_pairs={{0,8},{2,10},{4,12},{6,14},{8,0},{10,2},{12,4},{14,6},{1,9},{3,11}... | collective-permute-start | bytes 786440 | tf_op jit(solution)/shard_map/ppermute | solution.py:21
  11.4 0.5 collective-permute-start.2
  11.9 0.3 collective-permute-start.4
  12.2 5.0 %gather_pages.2 = (bf16[1,8,2,128,128]{4,3,2,1,0:T(8,128)(2,1)S(1)}, bf16[1,8,2,128,128]{4,3,2,1,0:T(8,128)(2,1)S(1)}, bf16[1,6,2,128,128]{4,3,2,1,0:T(8,128)(2,...) custom-call(s32[1]{0:T(128)} %bitcast.owner_ref, ...), custom_call_target="tpu_custom_call" | custom-call | tf_op jit(solution)/shard_map/gather_pages/pallas_call | solution.py:127
  17.3 0.0 collective-permute-done.3.refs_1_
  17.3 0.2 collective-permute-start.6
  17.5 9.3 %collective-permute-done.7.refs_0_ = bf16[1,1024,128]{2,1,0:T(8,128)(2,1)S(1)} collective-permute-done((bf16[1,1024,128]{2,1,0:T(8,128)(2,1)S(1)}, bf16[1,1024,128]{2,1,0:T(8,128)(2,1)S(1)}, u32[]{:S(2)}, u32[]{:S(2)}) %collective-permute-start.7) | collective-permute-done | bytes 262176 | tf_op jit(solution)/shard_map/ppermute | solution.py:21
  26.7 0.5 collective-permute-start.8
  27.2 4.9 %attend.8 = (f32[1,1024,128]{2,1,0:T(8,128)S(1)}, f32[1,16,128]{2,1,0:T(8,128)S(1)}, f32[1,1024,128]{2,1,0:T(8,128)S(1)}, f32[1,16,128]{2,1,0:T(8,128)S(1)}, bf16[33,2,2,128,128]{4,3,2,1,0:T(8,128)(2,1)}) custom-call(s32[1]{0:T(128)} %bitcast.owner_ref, s32[2,2]{1,0:T(2,128)S(1)} %get-tuple-element.33.seen_ref, s32[8]{0:T(128)S(1)} %copy-done, ...), custom_call_target="tpu_custom_call" | custom-call | flops 1207959552 | bytes 589824 | tf_op jit(solution)/shard_map/attend/pallas_call | solution.py:364
  32.1 0.0 collective-permute-done.2.refs_1_.refs_0_
  32.2 3.6 %collective-permute-start.11 = (bf16[1,8,2,128,128]{4,3,2,1,0:T(8,128)(2,1)S(1)}, bf16[1,8,2,128,128]{4,3,2,1,0:T(8,128)(2,1)S(1)}, u32[]{:S(2)}, u32[]{:S(2)}) collective-permute-start(bf16[1,8,2,128,128]{4,3,2,1,0:T(8,128)(2,1)S(1)} %get-tuple-element.50), channel_id=1, source_target_pairs={{0,4},{2,6},{4,0},{6,2},{8,12},{10,14},{12,8},{14,10},{1,5},{3,7},... | collective-permute-start | bytes 1572872 | tf_op jit(solution)/shard_map/ppermute | solution.py:21
  35.8 0.0 collective-permute-done.4.refs_0_
  35.8 1.5 %collective-permute-start.5 = (bf16[1,1024,128]{2,1,0:T(8,128)(2,1)S(1)}, bf16[1,1024,128]{2,1,0:T(8,128)(2,1)S(1)}, u32[]{:S(2)}, u32[]{:S(2)}) collective-permute-start(bf16[1,1024,128]{2,1,0:T(8,128)(2,1)S(1)} %collective-permute-done.4.refs_0_), channel_id=1, source_target_pairs={{0,2},{2,0},{4,6},{6,4},{8,10},{10,8},{12,14},{14,12},{1,3},{3,1},... | collective-permute-start | bytes 786440 | tf_op jit(solution)/shard_map/ppermute | solution.py:21
  37.3 4.8 %attend.9 = (f32[1,1024,128]{2,1,0:T(8,128)S(1)}, f32[1,16,128]{2,1,0:T(8,128)S(1)}, f32[1,1024,128]{2,1,0:T(8,128)S(1)}, f32[1,16,128]{2,1,0:T(8,128)S(1)}) custom-call(s32[1]{0:T(128)} %bitcast.owner_ref, s32[2,2]{1,0:T(2,128)S(1)} %get-tuple-element.33.seen_ref, s32[8]{0:T(128)S(1)} %copy-done, bf16[1,1024,128]{2,1,0:T(8,128)(2,1)S(1)} %get-tuple-element.65.refs_0_, ...), custom_call_target="tpu_custom_call" | custom-call | flops 1207959552 | bytes 589824 | tf_op jit(solution)/shard_map/attend/pallas_call | solution.py:364
  42.1 0.0 collective-permute-done.9.refs_3_
  42.1 0.1 collective-permute-start
  42.3 0.0 collective-permute-done.8.refs_1_
  42.3 6.5 %attend.10 = (f32[1,1024,128]{2,1,0:T(8,128)S(1)}, f32[1,16,128]{2,1,0:T(8,128)S(1)}, bf16[1,1072,128]{2,1,0:T(8,128)(2,1)S(1)}) custom-call(s32[1]{0:T(128)} %bitcast.owner_ref, s32[2,2]{1,0:T(2,128)S(1)} %get-tuple-element.33.seen_ref, s32[8]{0:T(128)S(1)} %copy-done, bf16[1,1024,128]{2,1,0:T(8,128)(2,1)S(1)} %collective-permute-done.7.refs_0_, ...), custom_call_target="tpu_custom_call" | custom-call | flops 2147483648 | bytes 1048576 | tf_op jit(solution)/shard_map/attend/pallas_call | solution.py:364
  48.8 0.6 collective-permute-start.12
  49.4 0.0 collective-permute-done.6.refs_3_
  49.4 0.0 collective-permute-done.5.refs_1_
  49.4 6.8 %attend.11 = (f32[1,1024,128]{2,1,0:T(8,128)S(1)}, f32[1,16,128]{2,1,0:T(8,128)S(1)}, bf16[1,1072,128]{2,1,0:T(8,128)(2,1)S(1)}) custom-call(s32[1]{0:T(128)} %bitcast.owner_ref, s32[2,2]{1,0:T(2,128)S(1)} %get-tuple-element.33.seen_ref, s32[8]{0:T(128)S(1)} %copy-done, bf16[1,1024,128]{2,1,0:T(8,128)(2,1)S(1)} %collective-permute-done.4.refs_0_, ...), custom_call_target="tpu_custom_call" | custom-call | flops 2147483648 | bytes 1048576 | tf_op jit(solution)/shard_map/attend/pallas_call | solution.py:364
  56.2 1.6 %collective-permute-start.10 = (bf16[1,1072,128]{2,1,0:T(8,128)(2,1)S(1)}, bf16[1,1072,128]{2,1,0:T(8,128)(2,1)S(1)}, u32[]{:S(2)}, u32[]{:S(2)}) collective-permute-start(bf16[1,1072,128]{2,1,0:T(8,128)(2,1)S(1)} %get-tuple-element.49), channel_id=1, source_target_pairs={{0,2},{2,0},{4,6},{6,4},{8,10},{10,8},{12,14},{14,12},{1,3},{3,1},... | collective-permute-start | bytes 823304 | tf_op jit(solution)/shard_map/ppermute | solution.py:21
  57.8 1.9 %collective-permute-start.1 = (bf16[1,2,2,128,128]{4,3,2,1,0:T(8,128)(2,1)S(1)}, bf16[1,2,2,128,128]{4,3,2,1,0:T(8,128)(2,1)S(1)}, u32[]{:S(2)}, u32[]{:S(2)}) collective-permute-start(bf16[1,2,2,128,128]{4,3,2,1,0:T(8,128)(2,1)S(1)} %get-tuple-element.35), channel_id=1, source_target_pairs={{0,4},{2,6},{4,0},{6,2},{8,12},{10,14},{12,8},{14,10},{1,5},{3,7},... | collective-permute-start | bytes 393224 | tf_op jit(solution)/shard_map/ppermute | solution.py:21
  59.7 0.0 collective-permute-done.12.refs_0_
  59.7 0.4 join_packed.2.refs_7_
  60.1 0.1 collective-permute-start.16
  60.2 0.0 collective-permute-done.11.refs_2_
  60.2 4.2 %attend.12 = (f32[1,1024,128]{2,1,0:T(8,128)S(1)}, f32[1,16,128]{2,1,0:T(8,128)S(1)}, bf16[1,1072,128]{2,1,0:T(8,128)(2,1)S(1)}) custom-call(s32[1]{0:T(128)} %bitcast.owner_ref, s32[2,2]{1,0:T(2,128)S(1)} %get-tuple-element.33.seen_ref, s32[8]{0:T(128)S(1)} %copy-done, bf16[1,1024,128]{2,1,0:T(8,128)(2,1)S(1)} %get-tuple-element.64.refs_0_, ...), custom_call_target="tpu_custom_call" | custom-call | flops 1073741824 | bytes 524288 | tf_op jit(solution)/shard_map/attend/pallas_call | solution.py:364
  64.4 0.6 collective-permute-start.15
  65.0 0.0 collective-permute-done.10.refs_0_
  65.0 0.4 join_packed.3.refs_4_
  65.4 4.6 %collective-permute-done.refs_1_ = bf16[1,6,2,128,128]{4,3,2,1,0:T(8,128)(2,1)S(1)} collective-permute-done((bf16[1,6,2,128,128]{4,3,2,1,0:T(8,128)(2,1)S(1)}, bf16[1,6,2,128,128]{4,3,2,1,0:T(8,128)(2,1)S(1)}, u32[]{:S(2)}, u32[]{:S(2)}) %collective-permute-start) | collective-permute-done | bytes 393248 | tf_op jit(solution)/shard_map/ppermute | solution.py:21
  70.0 2.1 %attend.13 = (f32[1,1024,128]{2,1,0:T(8,128)S(1)}, f32[1,16,128]{2,1,0:T(8,128)S(1)}) custom-call(s32[1]{0:T(128)} %bitcast.owner_ref, s32[2,2]{1,0:T(2,128)S(1)} %get-tuple-element.33.seen_ref, s32[8]{0:T(128)S(1)} %copy-done, bf16[1,1024,128]{2,1,0:T(8,128)(2,1)S(1)} %collective-permute-done.2.refs_1_.refs_0_, ...), custom_call_target="tpu_custom_call" | custom-call | flops 402653184 | bytes 393216 | tf_op jit(solution)/shard_map/attend/pallas_call | solution.py:364
  72.1 0.0 collective-permute-done.1.refs_1_.refs_2_
  72.1 1.4 %attend.14.refs_5_ = bf16[1,1072,128]{2,1,0:T(8,128)(2,1)S(1)} custom-call(s32[1]{0:T(128)} %bitcast.owner_ref, s32[2,2]{1,0:T(2,128)S(1)} %get-tuple-element.33.seen_ref, s32[8]{0:T(128)S(1)} %copy-done, bf16[1,1024,128]{2,1,0:T(8,128)(2,1)S(1)} %collective-permute-done.2.refs_1_.refs_0_, ...), custom_call_target="tpu_custom_call" | custom-call | flops 134217728 | bytes 131072 | tf_op jit(solution)/shard_map/attend/pallas_call | solution.py:364
  73.4 0.1 collective-permute-start.13
  73.6 1.9 %collective-permute-start.14 = (bf16[1,1072,128]{2,1,0:T(8,128)(2,1)S(1)}, bf16[1,1072,128]{2,1,0:T(8,128)(2,1)S(1)}, u32[]{:S(2)}, u32[]{:S(2)}) collective-permute-start(bf16[1,1072,128]{2,1,0:T(8,128)(2,1)S(1)} %join_packed.3.refs_4_), channel_id=1, source_target_pairs={{0,8},{2,10},{4,12},{6,14},{8,0},{10,2},{12,4},{14,6},{1,9},{3,11}... | collective-permute-start | bytes 823304 | tf_op jit(solution)/shard_map/ppermute | solution.py:21
  75.4 2.4 %attend.15 = (f32[1,1024,128]{2,1,0:T(8,128)S(1)}, f32[1,16,128]{2,1,0:T(8,128)S(1)}) custom-call(s32[1]{0:T(128)} %bitcast.owner_ref, s32[2,2]{1,0:T(2,128)S(1)} %get-tuple-element.33.seen_ref, s32[8]{0:T(128)S(1)} %copy-done, bf16[1,1024,128]{2,1,0:T(8,128)(2,1)S(1)} %get-tuple-element.65.refs_0_, ...), custom_call_target="tpu_custom_call" | custom-call | flops 536870912 | bytes 524288 | tf_op jit(solution)/shard_map/attend/pallas_call | solution.py:364
  77.8 0.0 collective-permute-done.16.refs_1_
  77.8 1.2 %join_out.2.refs_2_ = bf16[128,16,128]{2,1,0:T(8,128)(2,1)} custom-call(f32[1,1024,128]{2,1,0:T(8,128)S(1)} %get-tuple-element.61.own_mixed, f32[1,16,128]{2,1,0:T(8,128)S(1)} %get-tuple-element.56.refs_1_.own_table, bf16[1,1072,128]{2,1,0:T(8,128)(2,1)S(1)} %collective-permute-done.15.refs_0_, bf16[1,1072,128]{2,1,0:T(8,128)(2,1)S(1)} %collective-permute-done.16.refs_1_), custom_call_target="tpu_custom_call" | custom-call | tf_op jit(solution)/shard_map/join_out/pallas_call | solution.py:459
  79.1 0.9 %collective-permute-done.13.refs_0_ = bf16[1,1072,128]{2,1,0:T(8,128)(2,1)S(1)} collective-permute-done((bf16[1,1072,128]{2,1,0:T(8,128)(2,1)S(1)}, bf16[1,1072,128]{2,1,0:T(8,128)(2,1)S(1)}, u32[]{:S(2)}, u32[]{:S(2)}) %collective-permute-start.13) | collective-permute-done | bytes 274464 | tf_op jit(solution)/shard_map/ppermute | solution.py:21
  80.0 7.1 %collective-permute-done.14.refs_1_ = bf16[1,1072,128]{2,1,0:T(8,128)(2,1)S(1)} collective-permute-done((bf16[1,1072,128]{2,1,0:T(8,128)(2,1)S(1)}, bf16[1,1072,128]{2,1,0:T(8,128)(2,1)S(1)}, u32[]{:S(2)}, u32[]{:S(2)}) %collective-permute-start.14) | collective-permute-done | bytes 274464 | tf_op jit(solution)/shard_map/ppermute | solution.py:21
  87.1 1.2 %join_out.3 = bf16[128,16,128]{2,1,0:T(8,128)(2,1)} custom-call(f32[1,1024,128]{2,1,0:T(8,128)S(1)} %get-tuple-element.59.own_mixed, f32[1,16,128]{2,1,0:T(8,128)S(1)} %get-tuple-element.60.own_table, bf16[1,1072,128]{2,1,0:T(8,128)(2,1)S(1)} %collective-permute-done.13.refs_0_, ...), custom_call_target="tpu_custom_call", output_to_operand_aliasing={{}: (4, {})} | custom-call | tf_op jit(solution)/shard_map/join_out/pallas_call | solution.py:459
  (6 shorter events, 0.0 us)
Async XLA Ops:
  0.6 11.6 %copy-start.1 = (bf16[128,2,2,128]{3,2,1,0:T(2,128)(2,1)S(1)}, bf16[128,2,2,128]{3,2,1,0:T(2,128)(2,1)}, u32[]{:S(2)}) copy-start(bf16[128,2,2,128]{3,2,1,0:T(2,128)(2,1)} %param.7) | copy-start | bytes 393220
  1.7 15.5 %collective-permute-start.3 = (bf16[1,1024,128]{2,1,0:T(8,128)(2,1)S(1)}, bf16[1,1024,128]{2,1,0:T(8,128)(2,1)S(1)}, u32[]{:S(2)}, u32[]{:S(2)}) collective-permute-start(bf16[1,1024,128]{2,1,0:T(8,128)(2,1)S(1)} %get-tuple-element.64.refs_0_), channel_id=1, source_target_pairs={{0,2},{2,0},{4,6},{6,4},{8,10},{10,8},{12,14},{14,12},{1,3},{3,1},... | collective-permute-start | bytes 786440 | tf_op jit(solution)/shard_map/ppermute | solution.py:21
  4.8 22.4 %copy-start = (s32[8]{0:T(128)S(1)}, s32[8]{0:T(128)}, u32[]{:S(2)}) copy-start(s32[8]{0:T(128)} %fresh_ref.15) | copy-start | bytes 100
  7.1 35.0 %collective-permute-start.9 = (bf16[1,8,2,128,128]{4,3,2,1,0:T(8,128)(2,1)S(1)}, bf16[1,8,2,128,128]{4,3,2,1,0:T(8,128)(2,1)S(1)}, u32[]{:S(2)}, u32[]{:S(2)}) collective-permute-start(bf16[1,8,2,128,128]{4,3,2,1,0:T(8,128)(2,1)S(1)} %gather_pages.3), channel_id=1, source_target_pairs={{0,4},{2,6},{4,0},{6,2},{8,12},{10,14},{12,8},{14,10},{1,5},{3,7},... | collective-permute-start | bytes 1572872 | tf_op jit(solution)/shard_map/ppermute | solution.py:21
  8.8 18.0 %collective-permute-start.7 = (bf16[1,1024,128]{2,1,0:T(8,128)(2,1)S(1)}, bf16[1,1024,128]{2,1,0:T(8,128)(2,1)S(1)}, u32[]{:S(2)}, u32[]{:S(2)}) collective-permute-start(bf16[1,1024,128]{2,1,0:T(8,128)(2,1)S(1)} %get-tuple-element.64.refs_0_), channel_id=1, source_target_pairs={{0,8},{2,10},{4,12},{6,14},{8,0},{10,2},{12,4},{14,6},{1,9},{3,11}... | collective-permute-start | bytes 786440 | tf_op jit(solution)/shard_map/ppermute | solution.py:21
  11.4 20.8 %collective-permute-start.2 = (bf16[1,1024,128]{2,1,0:T(8,128)(2,1)S(1)}, bf16[1,1024,128]{2,1,0:T(8,128)(2,1)S(1)}, u32[]{:S(2)}, u32[]{:S(2)}) collective-permute-start(bf16[1,1024,128]{2,1,0:T(8,128)(2,1)S(1)} %get-tuple-element.65.refs_0_), channel_id=1, source_target_pairs={{0,2},{2,0},{4,6},{6,4},{8,10},{10,8},{12,14},{14,12},{1,3},{3,1},... | collective-permute-start | bytes 786440 | tf_op jit(solution)/shard_map/ppermute | solution.py:21
  11.9 23.9 %collective-permute-start.4 = (bf16[1,1024,128]{2,1,0:T(8,128)(2,1)S(1)}, bf16[1,1024,128]{2,1,0:T(8,128)(2,1)S(1)}, u32[]{:S(2)}, u32[]{:S(2)}) collective-permute-start(bf16[1,1024,128]{2,1,0:T(8,128)(2,1)S(1)} %get-tuple-element.65.refs_0_), channel_id=1, source_target_pairs={{0,8},{2,10},{4,12},{6,14},{8,0},{10,2},{12,4},{14,6},{1,9},{3,11}... | collective-permute-start | bytes 786440 | tf_op jit(solution)/shard_map/ppermute | solution.py:21
  17.3 32.1 %collective-permute-start.6 = (bf16[1,8,2,128,128]{4,3,2,1,0:T(8,128)(2,1)S(1)}, bf16[1,8,2,128,128]{4,3,2,1,0:T(8,128)(2,1)S(1)}, u32[]{:S(2)}, u32[]{:S(2)}) collective-permute-start(bf16[1,8,2,128,128]{4,3,2,1,0:T(8,128)(2,1)S(1)} %get-tuple-element.44), channel_id=1, source_target_pairs={{0,4},{2,6},{4,0},{6,2},{8,12},{10,14},{12,8},{14,10},{1,5},{3,7},... | collective-permute-start | bytes 1572872 | tf_op jit(solution)/shard_map/ppermute | solution.py:21
  26.7 15.5 %collective-permute-start.8 = (bf16[1,1024,128]{2,1,0:T(8,128)(2,1)S(1)}, bf16[1,1024,128]{2,1,0:T(8,128)(2,1)S(1)}, u32[]{:S(2)}, u32[]{:S(2)}) collective-permute-start(bf16[1,1024,128]{2,1,0:T(8,128)(2,1)S(1)} %collective-permute-done.7.refs_0_), channel_id=1, source_target_pairs={{0,2},{2,0},{4,6},{6,4},{8,10},{10,8},{12,14},{14,12},{1,3},{3,1},... | collective-permute-start | bytes 786440 | tf_op jit(solution)/shard_map/ppermute | solution.py:21
  32.2 28.0 %collective-permute-start.11 = (bf16[1,8,2,128,128]{4,3,2,1,0:T(8,128)(2,1)S(1)}, bf16[1,8,2,128,128]{4,3,2,1,0:T(8,128)(2,1)S(1)}, u32[]{:S(2)}, u32[]{:S(2)}) collective-permute-start(bf16[1,8,2,128,128]{4,3,2,1,0:T(8,128)(2,1)S(1)} %get-tuple-element.50), channel_id=1, source_target_pairs={{0,4},{2,6},{4,0},{6,2},{8,12},{10,14},{12,8},{14,10},{1,5},{3,7},... | collective-permute-start | bytes 1572872 | tf_op jit(solution)/shard_map/ppermute | solution.py:21
  35.8 13.6 %collective-permute-start.5 = (bf16[1,1024,128]{2,1,0:T(8,128)(2,1)S(1)}, bf16[1,1024,128]{2,1,0:T(8,128)(2,1)S(1)}, u32[]{:S(2)}, u32[]{:S(2)}) collective-permute-start(bf16[1,1024,128]{2,1,0:T(8,128)(2,1)S(1)} %collective-permute-done.4.refs_0_), channel_id=1, source_target_pairs={{0,2},{2,0},{4,6},{6,4},{8,10},{10,8},{12,14},{14,12},{1,3},{3,1},... | collective-permute-start | bytes 786440 | tf_op jit(solution)/shard_map/ppermute | solution.py:21
  42.1 27.9 %collective-permute-start = (bf16[1,6,2,128,128]{4,3,2,1,0:T(8,128)(2,1)S(1)}, bf16[1,6,2,128,128]{4,3,2,1,0:T(8,128)(2,1)S(1)}, u32[]{:S(2)}, u32[]{:S(2)}) collective-permute-start(bf16[1,6,2,128,128]{4,3,2,1,0:T(8,128)(2,1)S(1)} %get-tuple-element.34), channel_id=1, source_target_pairs={{0,4},{2,6},{4,0},{6,2},{8,12},{10,14},{12,8},{14,10},{1,5},{3,7},... | collective-permute-start | bytes 1179656 | tf_op jit(solution)/shard_map/ppermute | solution.py:21
  48.8 10.9 %collective-permute-start.12 = (bf16[1,1072,128]{2,1,0:T(8,128)(2,1)S(1)}, bf16[1,1072,128]{2,1,0:T(8,128)(2,1)S(1)}, u32[]{:S(2)}, u32[]{:S(2)}) collective-permute-start(bf16[1,1072,128]{2,1,0:T(8,128)(2,1)S(1)} %get-tuple-element.55), channel_id=1, source_target_pairs={{0,2},{2,0},{4,6},{6,4},{8,10},{10,8},{12,14},{14,12},{1,3},{3,1},... | collective-permute-start | bytes 823304 | tf_op jit(solution)/shard_map/ppermute | solution.py:21
  56.2 8.8 %collective-permute-start.10 = (bf16[1,1072,128]{2,1,0:T(8,128)(2,1)S(1)}, bf16[1,1072,128]{2,1,0:T(8,128)(2,1)S(1)}, u32[]{:S(2)}, u32[]{:S(2)}) collective-permute-start(bf16[1,1072,128]{2,1,0:T(8,128)(2,1)S(1)} %get-tuple-element.49), channel_id=1, source_target_pairs={{0,2},{2,0},{4,6},{6,4},{8,10},{10,8},{12,14},{14,12},{1,3},{3,1},... | collective-permute-start | bytes 823304 | tf_op jit(solution)/shard_map/ppermute | solution.py:21
  57.8 14.3 %collective-permute-start.1 = (bf16[1,2,2,128,128]{4,3,2,1,0:T(8,128)(2,1)S(1)}, bf16[1,2,2,128,128]{4,3,2,1,0:T(8,128)(2,1)S(1)}, u32[]{:S(2)}, u32[]{:S(2)}) collective-permute-start(bf16[1,2,2,128,128]{4,3,2,1,0:T(8,128)(2,1)S(1)} %get-tuple-element.35), channel_id=1, source_target_pairs={{0,4},{2,6},{4,0},{6,2},{8,12},{10,14},{12,8},{14,10},{1,5},{3,7},... | collective-permute-start | bytes 393224 | tf_op jit(solution)/shard_map/ppermute | solution.py:21
  60.1 17.7 %collective-permute-start.16 = (bf16[1,1072,128]{2,1,0:T(8,128)(2,1)S(1)}, bf16[1,1072,128]{2,1,0:T(8,128)(2,1)S(1)}, u32[]{:S(2)}, u32[]{:S(2)}) collective-permute-start(bf16[1,1072,128]{2,1,0:T(8,128)(2,1)S(1)} %join_packed.2.refs_7_), channel_id=1, source_target_pairs={{0,8},{2,10},{4,12},{6,14},{8,0},{10,2},{12,4},{14,6},{1,9},{3,11}... | collective-permute-start | bytes 823304 | tf_op jit(solution)/shard_map/ppermute | solution.py:21
  64.4 13.4 %collective-permute-start.15 = (bf16[1,1072,128]{2,1,0:T(8,128)(2,1)S(1)}, bf16[1,1072,128]{2,1,0:T(8,128)(2,1)S(1)}, u32[]{:S(2)}, u32[]{:S(2)}) collective-permute-start(bf16[1,1072,128]{2,1,0:T(8,128)(2,1)S(1)} %get-tuple-element.62), channel_id=1, source_target_pairs={{0,2},{2,0},{4,6},{6,4},{8,10},{10,8},{12,14},{14,12},{1,3},{3,1},... | collective-permute-start | bytes 823304 | tf_op jit(solution)/shard_map/ppermute | solution.py:21
  73.4 6.6 %collective-permute-start.13 = (bf16[1,1072,128]{2,1,0:T(8,128)(2,1)S(1)}, bf16[1,1072,128]{2,1,0:T(8,128)(2,1)S(1)}, u32[]{:S(2)}, u32[]{:S(2)}) collective-permute-start(bf16[1,1072,128]{2,1,0:T(8,128)(2,1)S(1)} %attend.14.refs_5_), channel_id=1, source_target_pairs={{0,2},{2,0},{4,6},{6,4},{8,10},{10,8},{12,14},{14,12},{1,3},{3,1},... | collective-permute-start | bytes 823304 | tf_op jit(solution)/shard_map/ppermute | solution.py:21
  73.6 13.5 %collective-permute-start.14 = (bf16[1,1072,128]{2,1,0:T(8,128)(2,1)S(1)}, bf16[1,1072,128]{2,1,0:T(8,128)(2,1)S(1)}, u32[]{:S(2)}, u32[]{:S(2)}) collective-permute-start(bf16[1,1072,128]{2,1,0:T(8,128)(2,1)S(1)} %join_packed.3.refs_4_), channel_id=1, source_target_pairs={{0,8},{2,10},{4,12},{6,14},{8,0},{10,2},{12,4},{14,6},{1,9},{3,11}... | collective-permute-start | bytes 823304 | tf_op jit(solution)/shard_map/ppermute | solution.py:21
